TPU v7x, 32 devices: a whole 2x2x4 slice. The times are simulated.
32 devices in a mesh: row: 2 (over core), col: 16 (over z, y, x).
Axes of the slice: x: 2, y: 2, z: 4, core: 2. Of those that a mesh axis runs over, the one named last changes fastest.
Arguments:
- object_field: float32 [2, 2, 512, 4096], P(None, None, 'row', 'col'), may hold values from -5 to 5
- probe: float32 [2, 256, 256], replicated, may hold values from -5 to 5
- phase: float32 [256, 256], replicated, may hold values from -3.140625 to 3.140625
- amplitudes: float32 [2, 16, 1, 256, 256], P('row', 'col'), may hold values from 0.2 to 3
- offsets: int32 [2, 16, 1, 2], P('row', 'col'), may hold values from 0 to 128, as said below
Outputs:
- object_grad: float32 [2, 2, 512, 4096], P(None, None, 'row', 'col')
- probe_grad: float32 [2, 256, 256], replicated
Inputs may be any that keep to these rules, and one draw needn't show every extreme that they name: `offsets`: every offset lies between 0 and 128; in every draw some offset is 0 and some offset is 128.
All inputs are finite; a program needn't handle non-finite values.
Results may differ from a plain program's by a relative error of at most 0.0003.
Values sent between devices are 32-bit elements; how exact they have to be, the bound alone decides.
No kernel may reach another device: no remote copies, remote signals or barrier semaphores. Data moves between devices by JAX's collectives and lax.ppermute only.
A program may use at most 64 MiB of HBM per device.

v0:
```python
import functools

import jax
import jax.numpy as jnp
import numpy as np
from jax import lax
from jax.experimental import pallas as pl
from jax.experimental.pallas import tpu as pltpu
from jax.sharding import PartitionSpec as P

EPS_AMP = 0.5
F32 = jnp.float32
BF16 = jnp.bfloat16
VMEM = pl.BlockSpec(memory_space=pltpu.VMEM)
SMEM = pl.BlockSpec(memory_space=pltpu.SMEM)


def split_np(table):
    high = table.astype(BF16)
    low = (table - high.astype(np.float64)).astype(BF16)
    return [high, low]


def dft_constants(n):
    h = n // 2
    k = np.arange(h)
    angle = 2.0 * np.pi * ((k[:, None] * k[None, :]) % h) / h
    scale = 1.0 / np.sqrt(n)
    c, s = np.cos(angle) * scale, np.sin(angle) * scale
    d = np.block([[c, s], [-s, c]])
    mats = np.stack(split_np(d) + split_np(d.T))
    w = np.exp(-2j * np.pi * k / n)
    tw_left = np.stack([np.tile(w.real[:, None], (1, h)), np.tile(w.imag[:, None], (1, h))])
    tw_right = np.stack([np.tile(w.real[None], (8, 1)), np.tile(w.imag[None], (8, 1))])
    order = np.zeros((n, n))
    order[2 * k, k] = 1.0
    order[2 * k + 1, h + k] = 1.0
    return (
        mats,
        tw_left.astype(np.float32),
        tw_right.astype(np.float32),
        np.stack([order.T, order]).astype(BF16),
    )


def split(x):
    high = x.astype(BF16)
    return high, (x - high.astype(F32)).astype(BF16)


def dot(a, b):
    return jnp.dot(a, b, preferred_element_type=F32)


def left_dot(mats, which, x):
    high, low = split(x)
    return dot(mats[which], high) + (dot(mats[which], low) + dot(mats[which + 1], high))


def right_dot(x, mats, which):
    high, low = split(x)
    return dot(high, mats[which]) + (dot(low, mats[which]) + dot(high, mats[which + 1]))


def cat(parts, axis):
    return jnp.concatenate(parts, axis=axis)


def product(a, b):
    return (a[0] * b[0] - a[1] * b[1], a[0] * b[1] + a[1] * b[0])


def conj_product(a, b):
    return (a[0] * b[0] + a[1] * b[1], a[0] * b[1] - a[1] * b[0])


class Dft:
    def __init__(self, mats, tw_left, tw_right, n):
        self.mats, self.n, self.h = mats, n, n // 2
        self.wl = [cat([tw_left[i], tw_left[i]], 1) for i in range(2)]
        self.wr = [tw_right[i, 0:1] for i in range(2)]

    def forward(self, x):
        n, h = self.n, self.h
        total = [p[:h] + p[h:] for p in x]
        odd = product([p[:h] - p[h:] for p in x], self.wl)
        y = left_dot(self.mats, 0, cat([cat(total, 0), cat(odd, 0)], 1))
        x = [cat([y[:h, :n], y[:h, n:]], 0), cat([y[h:, :n], y[h:, n:]], 0)]
        total = [p[:, :h] + p[:, h:] for p in x]
        odd = product([p[:, :h] - p[:, h:] for p in x], self.wr)
        y = right_dot(cat([cat(total, 1), cat(odd, 1)], 0), self.mats, 2)
        return [cat([y[:n, :h], y[n:, :h]], 1), cat([y[:n, h:], y[n:, h:]], 1)]

    def inverse(self, x):
        n, h = self.n, self.h
        y = cat([cat([p[:, :h] for p in x], 1), cat([p[:, h:] for p in x], 1)], 0)
        y = right_dot(y, self.mats, 0)
        even = [y[:n, :h], y[:n, h:]]
        odd = conj_product(self.wr, [y[n:, :h], y[n:, h:]])
        x = [cat([e + o, e - o], 1) for e, o in zip(even, odd)]
        y = cat([cat([p[:h] for p in x], 0), cat([p[h:] for p in x], 0)], 1)
        y = left_dot(self.mats, 2, y)
        even = [y[:h, :n], y[h:, :n]]
        odd = conj_product(self.wl, [y[:h, n:], y[h:, n:]])
        return [cat([e + o, e - o], 0) for e, o in zip(even, odd)]


def iota(shape, dim):
    return lax.broadcasted_iota(jnp.int32, shape, dim)


def half_roll(x):
    return pltpu.roll(x, x.shape[-1] // 2, axis=x.ndim - 1)


def pack_cols(re, im):
    h = re.shape[1] // 2
    front = iota((re.shape[0], h), 1) < h // 2
    low = jnp.where(front, re[:, :h], half_roll(im[:, :h]))
    high = jnp.where(front, half_roll(im[:, h:]), re[:, h:])
    return low, high


def pack_kernel(n_row, obj, *refs):
    halos, outs = refs[:n_row], refs[n_row:]
    even = lax.axis_index("col") % 2 == 0
    for s in range(2):
        sources = [obj] + list(halos)
        at = 0
        for source in sources:
            rows = source.shape[1]
            low, high = pack_cols(source[2 * s], source[2 * s + 1])
            outs[2 * s][at : at + rows] = jnp.where(even, high, low)
            outs[2 * s + 1][at : at + rows] = jnp.where(even, low, high)
            at += rows


def dyn_roll(x, shift, axis):
    return pltpu.roll(x, shift, axis=axis)


def prep_kernel(margin, phase, amps, probe, offs, order, kr, ki, am, pr):
    n = phase.shape[0]

    def thirds(x):
        a = x.astype(BF16)
        rest = x - a.astype(F32)
        return (a,) + split(rest)

    def reorder(ref):
        a, b, c = thirds(ref[...])
        rows = dot(order[0], a) + (dot(order[0], b) + dot(order[0], c))
        a, b, c = thirds(rows)
        return dot(a, order[1]) + (dot(b, order[1]) + dot(c, order[1]))

    angle = reorder(phase)
    kr[...] = jnp.cos(angle)
    ki[...] = jnp.sin(angle)
    am[...] = reorder(amps)
    sy = (offs[0, 0] - margin + n) % n
    sx = (offs[0, 1] - margin + n) % n
    for i in range(2):
        pr[i] = dyn_roll(dyn_roll(probe[i], sy, 0), sx, 1)


def merge_cols(own, low, high, ox, margin):
    n = own[0].shape[1]
    h = n // 2
    lane = iota((own[0].shape[0], h), 1)
    from_high = lane < ox - margin
    from_low = lane + h >= ox + n - margin
    out = []
    for i in range(2):
        strip_high = high if i == 0 else half_roll(high)
        strip_low = low if i == 0 else half_roll(low)
        out.append(
            cat(
                [
                    jnp.where(from_high, strip_high, own[i][:, :h]),
                    jnp.where(from_low, strip_low, own[i][:, h:]),
                ],
                1,
            )
        )
    return out


def window_of(obj, s, halos, strip_e, strip_o, offs, margin):
    n = obj.shape[1]
    oy, ox = offs[0, 0], offs[0, 1]
    col_even = lax.axis_index("col") % 2 == 0
    row_even = lax.axis_index("row") % 2 == 0
    blocks = []
    at = 0
    for source in [obj] + list(halos):
        rows = source.shape[1]
        e, o = strip_e[at : at + rows], strip_o[at : at + rows]
        high, low = jnp.where(col_even, e, o), jnp.where(col_even, o, e)
        blocks.append(merge_cols([source[2 * s], source[2 * s + 1]], low, high, ox, margin))
        at += rows
    row = iota((margin, n), 0)
    take_high = row < oy - margin
    take_low = row + n - margin >= oy + n - margin
    out = []
    for i in range(2):
        main = blocks[0][i]
        if len(blocks) == 3:
            e, o = blocks[1][i], blocks[2][i]
            high, low = jnp.where(row_even, e, o), jnp.where(row_even, o, e)
        else:
            e = blocks[1][i]
            zero = jnp.zeros_like(e)
            high, low = jnp.where(row_even, e, zero), jnp.where(row_even, zero, e)
        out.append(
            cat(
                [
                    jnp.where(take_high, high, main[:margin]),
                    main[margin : n - margin],
                    jnp.where(take_low, low, main[n - margin :]),
                ],
                0,
            )
        )
    return out


def arrive_kernel(n_row, margin, *refs):
    obj, halos = refs[0], refs[1 : 1 + n_row]
    e1, o1, offs, pr, kr, ki, mats, twl, twr, w1, arrive = refs[1 + n_row :]
    n = obj.shape[1]
    dft = Dft(mats, twl[...], twr[...], n)
    win = window_of(obj, 0, halos, e1, o1, offs, margin)
    w1[0], w1[1] = win
    x = dft.forward(product([pr[0], pr[1]], win))
    x = dft.inverse(product([kr[...], ki[...]], x))
    arrive[0], arrive[1] = x


def split_grad(grad, offs, margin, own, strip, sends):
    n = grad[0].shape[0]
    h = n // 2
    oy, ox = offs[0, 0], offs[0, 1]
    row_even = lax.axis_index("row") % 2 == 0
    lane = iota((1, h), 1)
    to_high, to_low = lane < ox - margin, lane + h >= ox + n - margin
    front = lane < h // 2
    spill = jnp.where(front, to_high.astype(jnp.int32), to_low.astype(jnp.int32)) != 0
    for i in range(2):
        g = grad[i]
        row = iota((n, h), 0)
        high_rows = row < oy - margin
        low_rows = row >= oy + n - margin
        inner = jnp.logical_not(jnp.logical_or(high_rows, low_rows))
        left = jnp.where(to_high, 0.0, g[:, :h])
        right = jnp.where(to_low, 0.0, g[:, h:])
        side = jnp.where(spill, jnp.where(front, g[:, :h], g[:, h:]), 0.0)
        pieces = [left, right, side]
        own[i, :, :h] = jnp.where(inner, left, 0.0)
        own[i, :, h:] = jnp.where(inner, right, 0.0)
        strip[i] = jnp.where(inner, side, 0.0)
        for j, piece in enumerate(pieces):
            top = jnp.where(high_rows[:margin], piece[:margin], 0.0)
            bottom = jnp.where(low_rows[n - margin :], piece[n - margin :], 0.0)
            for which, send in enumerate(sends):
                first = row_even if which == 0 else jnp.logical_not(row_even)
                send[i, :, j * h : (j + 1) * h] = jnp.where(first, top, bottom)


def back_kernel(n_row, margin, *refs):
    obj, halos = refs[0], refs[1 : 1 + n_row]
    e2, o2, offs, pr, kr, ki, am, w1, arrive, mats, twl, twr = refs[1 + n_row : 13 + n_row]
    outs = refs[13 + n_row :]
    keep, give = outs[:2]
    n = obj.shape[1]
    dft = Dft(mats, twl[...], twr[...], n)
    win = window_of(obj, 1, halos, e2, o2, offs, margin)
    arr = [arrive[0], arrive[1]]
    far = dft.forward(product(arr, win))
    modulus = jnp.sqrt(far[0] * far[0] + far[1] * far[1] + EPS_AMP)
    factor = 2.0 * (1.0 - am[...] / modulus)
    back_far = dft.inverse([factor * far[0], factor * far[1]])
    rest = outs[2:]
    split_grad(conj_product(arr, back_far), offs, margin, rest[0], rest[1], rest[2 : 2 + n_row])
    x = dft.forward(conj_product(win, back_far))
    x = dft.inverse(conj_product([kr[...], ki[...]], x))
    rest = rest[2 + n_row :]
    split_grad(
        conj_product([pr[0], pr[1]], x), offs, margin, rest[0], rest[1], rest[2 : 2 + n_row]
    )
    grad = conj_product([w1[0], w1[1]], x)
    sy = (margin - offs[0, 0] + n) % n
    sx = (margin - offs[0, 1] + n) % n
    grad = [dyn_roll(dyn_roll(g, sy, 0), sx, 1) for g in grad]
    even = lax.axis_index("row") % 2 == 0
    keep[...] = jnp.where(even, grad[0], grad[1])
    give[...] = jnp.where(even, grad[1], grad[0])


def fold_rows_kernel(n_row, margin, *refs):
    ins, outs = refs[: 2 * (2 + n_row)], refs[2 * (2 + n_row) :]
    row_even = lax.axis_index("row") % 2 == 0
    col_even = lax.axis_index("col") % 2 == 0
    for s in range(2):
        own, strip = ins[s * (2 + n_row) : s * (2 + n_row) + 2]
        got = ins[s * (2 + n_row) + 2 : (s + 1) * (2 + n_row)]
        total, send_e, send_o = outs[3 * s : 3 * s + 3]
        n = own.shape[1]
        h = n // 2
        strips = []
        for i in range(2):
            total[i] = own[i]
            r = got[0][i]
            if n_row == 2:
                q = got[1][i]
            else:
                q = jnp.zeros_like(r)
            top, bottom = jnp.where(row_even, q, r), jnp.where(row_even, r, q)
            total[i, :margin] += top[:, :n]
            total[i, n - margin :] += bottom[:, :n]
            st = strip[i]
            strips.append(
                cat(
                    [
                        st[:margin] + top[:, n:],
                        st[margin : n - margin],
                        st[n - margin :] + bottom[:, n:],
                    ],
                    0,
                )
            )
        front = iota((n, h), 1) < h // 2
        moved = half_roll(strips[1])
        to_high = jnp.where(front, strips[0], moved)
        to_low = jnp.where(front, moved, strips[0])
        send_e[...] = jnp.where(col_even, to_high, to_low)
        send_o[...] = jnp.where(col_even, to_low, to_high)


def fold_cols_kernel(t1, e1, o1, t2, e2, o2, out):
    col_even = lax.axis_index("col") % 2 == 0
    for s, (t, e, o) in enumerate(((t1, e1, o1), (t2, e2, o2))):
        n = t.shape[1]
        h = n // 2
        front = iota((n, h), 1) < h // 2
        high = jnp.where(col_even, e[...], o[...])
        low = jnp.where(col_even, o[...], e[...])
        for i in range(2):
            a = low if i == 0 else half_roll(low)
            b = high if i == 0 else half_roll(high)
            out[2 * s + i, :, :h] = t[i, :, :h] + jnp.where(front, a, 0.0)
            out[2 * s + i, :, h:] = t[i, :, h:] + jnp.where(front, 0.0, b)


def call(kernel, shapes, in_specs, *args):
    return pl.pallas_call(
        kernel,
        out_shape=[jax.ShapeDtypeStruct(s, F32) for s in shapes],
        in_specs=in_specs,
        out_specs=[VMEM] * len(shapes),
        compiler_params=pltpu.CompilerParams(vmem_limit_bytes=48 * 1024 * 1024),
    )(*args)


def edges(axis):
    count = lax.axis_size(axis)
    rounds = []
    for first in (0, 1):
        pairs = [(i, i + 1) for i in range(first, count - 1, 2)]
        pairs += [(b, a) for a, b in pairs]
        if pairs:
            rounds.append(pairs)
    return rounds


def swap(value, axis, distance):
    count = lax.axis_size(axis)
    return lax.ppermute(value, axis, [(i, i ^ distance) for i in range(count)])


def stages(axis, start):
    count = lax.axis_size(axis)
    out = []
    stride = start
    while stride < count:
        width = min(4, count // stride)
        out.append((axis, stride, width))
        stride *= width
    return out


def pair_sum(parts):
    while len(parts) > 1:
        parts = [parts[i] + parts[i + 1] for i in range(0, len(parts), 2)]
    return parts[0]


def reduce_probe(keep, give):
    rows = lax.axis_size("row")
    cols = lax.axis_size("col")
    n = keep.shape[0]
    mine = keep + swap(give, "row", 1)
    quad = min(4, cols)
    place = lax.axis_index("col") % quad
    chunk = n // quad
    parts = [
        lax.dynamic_slice_in_dim(mine, (place ^ j) * chunk, chunk, 0) for j in range(quad)
    ]
    total = pair_sum([parts[0]] + [swap(parts[j], "col", j) for j in range(1, quad)])
    for axis, stride, width in stages("col", quad) + stages("row", 2):
        total = pair_sum([total] + [swap(total, axis, stride * j) for j in range(1, width)])
    full = jnp.zeros((quad, chunk, n), F32)
    for j in range(quad):
        part = total if j == 0 else swap(total, "col", j)
        full = lax.dynamic_update_slice(full, part[None], (place ^ j, 0, 0))
    full = full.reshape(n, n)
    other = swap(full, "row", 1)
    even = lax.axis_index("row") % 2 == 0
    return jnp.stack([jnp.where(even, full, other), jnp.where(even, other, full)])


def body(object_field, probe, phase, amplitudes, offsets):
    tile = object_field.shape[2]
    n = probe.shape[1]
    h = n // 2
    margin = n // 4
    obj = object_field.reshape(4, tile, tile)
    offs = offsets.reshape(1, 2)
    amps = amplitudes.reshape(n, n)
    mats, tw_left, tw_right, order = [jnp.asarray(t) for t in dft_constants(n)]

    row_rounds, col_rounds = edges("row"), edges("col")
    n_row = len(row_rounds)
    row_even = lax.axis_index("row") % 2 == 0
    halos = []
    for which, pairs in enumerate(row_rounds):
        last = row_even if which == 0 else jnp.logical_not(row_even)
        strip = lax.dynamic_slice_in_dim(obj, jnp.where(last, tile - margin, 0), margin, 1)
        halos.append(lax.ppermute(strip, "row", pairs))
    length = tile + margin * n_row

    packed = call(
        functools.partial(pack_kernel, n_row),
        [(length, h)] * 4,
        [VMEM] * (1 + n_row),
        obj,
        *halos,
    )
    strips = [lax.ppermute(packed[i], "col", col_rounds[i % 2]) for i in range(4)]
    kr, ki, am, pr = call(
        functools.partial(prep_kernel, margin),
        [(n, n), (n, n), (n, n), (2, n, n)],
        [VMEM, VMEM, VMEM, SMEM, VMEM],
        phase,
        amps,
        probe,
        offs,
        order,
    )
    w1, arrive = call(
        functools.partial(arrive_kernel, n_row, margin),
        [(2, n, n), (2, n, n)],
        [VMEM] * (1 + n_row) + [VMEM, VMEM, SMEM] + [VMEM] * 6,
        obj,
        *halos,
        strips[0],
        strips[1],
        offs,
        pr,
        kr,
        ki,
        mats,
        tw_left,
        tw_right,
    )
    per_slice = [(2, n, n), (2, n, h)] + [(2, margin, n + h)] * n_row
    outs = call(
        functools.partial(back_kernel, n_row, margin),
        [(n, n), (n, n)] + per_slice * 2,
        [VMEM] * (1 + n_row) + [VMEM, VMEM, SMEM] + [VMEM] * 9,
        obj,
        *halos,
        strips[2],
        strips[3],
        offs,
        pr,
        kr,
        ki,
        am,
        w1,
        arrive,
        mats,
        tw_left,
        tw_right,
    )
    keep, give = outs[:2]
    probe_grad = reduce_probe(keep, give)
    second, first = outs[2 : 4 + n_row], outs[4 + n_row :]
    ins = []
    for part in (first, second):
        ins += list(part[:2])
        ins += [lax.ppermute(part[2 + i], "row", row_rounds[i]) for i in range(n_row)]
    folded = call(
        functools.partial(fold_rows_kernel, n_row, margin),
        [(2, n, n), (n, h), (n, h)] * 2,
        [VMEM] * len(ins),
        *ins,
    )
    folded = [
        f if i % 3 == 0 else lax.ppermute(f, "col", col_rounds[i % 3 - 1])
        for i, f in enumerate(folded)
    ]
    (grad,) = call(fold_cols_kernel, [(4, n, n)], [VMEM] * 6, *folded)
    return (grad.reshape(2, 2, tile, tile), probe_grad)


def solution(mesh):
    placed = (
        P(None, None, "row", "col"),
        P(),
        P(),
        P("row", "col", None, None, None),
        P("row", "col", None, None),
    )
    return jax.shard_map(
        body,
        mesh=mesh,
        in_specs=placed,
        out_specs=(P(None, None, "row", "col"), P()),
        check_vma=False,
    )
```

profile of v0, /device:TPU:0, one launch (start us, length us, event | category | flops | bytes accessed | tf_op | source)
XLA Modules:
  0.0 75.7 jit_solution(8322500510099961139)
XLA Ops:
  0.7 1.0 %constant_dynamic-slice_fusion.3 = f32[4,64,256]{2,1,0:T(8,128)S(1)} fusion(f32[4,256,256]{2,1,0:T(8,128)} %bitcast.19, s32[]{:T(128)S(6)} %select_n.55), kind=kLoop, calls=%fused_computation.12 | loop fusion | bytes 524292 | tf_op jit(solution)/shard_map/dynamic_slice | solution.py:437
  2.2 1.2 %collective-permute-done.refs_0_.refs_1_ = f32[4,64,256]{2,1,0:T(8,128)S(1)} collective-permute-done((f32[4,64,256]{2,1,0:T(8,128)S(1)}, f32[4,64,256]{2,1,0:T(8,128)S(1)}, u32[]{:S(2)}, u32[]{:S(2)}) %collective-permute-start) | collective-permute-done | bytes 262176 | tf_op jit(solution)/shard_map/ppermute | solution.py:438
  3.4 1.2 %copy-done = f32[2,2,256,256]{3,2,1,0:T(8,128)S(1)} copy-done((f32[2,2,256,256]{3,2,1,0:T(8,128)S(1)}, f32[2,2,256,256]{3,2,1,0:T(8,128)}, u32[]{:S(2)}) %copy-start) | copy-done | bytes 1048600
  4.9 2.9 %collective-permute-start.3 = (f32[320,128]{1,0:T(8,128)S(1)}, f32[320,128]{1,0:T(8,128)S(1)}, u32[]{:S(2)}, u32[]{:S(2)}) collective-permute-start(f32[320,128]{1,0:T(8,128)S(1)} %get-tuple-element.32), channel_id=1, source_target_pairs={{0,1},{2,3},{4,5},{6,7},{8,9},{10,11},{12,13},{14,15},{1,0},{3,2},... | collective-permute-start | bytes 491528 | tf_op jit(solution)/shard_map/ppermute | solution.py:448
  8.5 4.3 %collective-permute-start.1 = (f32[320,128]{1,0:T(8,128)S(1)}, f32[320,128]{1,0:T(8,128)S(1)}, u32[]{:S(2)}, u32[]{:S(2)}) collective-permute-start(f32[320,128]{1,0:T(8,128)S(1)} %get-tuple-element.26), channel_id=1, source_target_pairs={{0,1},{2,3},{4,5},{6,7},{8,9},{10,11},{12,13},{14,15},{1,0},{3,2},... | collective-permute-start | bytes 491528 | tf_op jit(solution)/shard_map/ppermute | solution.py:448
  14.1 0.9 %copy-done.6 = f32[1,1,1,256,256]{4,3,2,1,0:T(8,128)S(1)} copy-done((f32[1,1,1,256,256]{4,3,2,1,0:T(8,128)S(1)}, f32[1,1,1,256,256]{4,3,2,1,0:T(8,128)}, u32[]{:S(2)}) %copy-start.6) | copy-done | bytes 262168
  15.0 0.9 %copy-done.7 = bf16[2,256,256]{2,1,0:T(8,128)(2,1)S(1)} copy-done((bf16[2,256,256]{2,1,0:T(8,128)(2,1)S(1)}, bf16[2,256,256]{2,1,0:T(8,128)(2,1)}, u32[]{:S(2)}) %copy-start.7) | copy-done | bytes 262168
  16.0 2.4 %shard_map.105 = (f32[256,256]{1,0:T(8,128)S(1)}, f32[256,256]{1,0:T(8,128)S(1)}, f32[256,256]{1,0:T(8,128)S(1)}, f32[2,256,256]{2,1,0:T(8,128)S(1)}) custom-call(f32[256,256]{1,0:T(8,128)S(1)} %copy-done.5, f32[256,256]{1,0:T(8,128)S(1)} %bitcast.23, f32[2,256,256]{2,1,0:T(8,128)S(1)} %copy-done.3, s32[1,2]{1,0:T(1,128)S(1)} %bitcast.24, ...), custom_call_target="tpu_custom_call" | custom-call | tf_op jit(solution)/shard_map/pallas_call | solution.py:355
  18.4 2.4 %shard_map.106 = (f32[2,256,256]{2,1,0:T(8,128)S(1)}, f32[2,256,256]{2,1,0:T(8,128)S(1)}) custom-call(f32[4,256,256]{2,1,0:T(8,128)S(1)} %bitcast.22, f32[4,64,256]{2,1,0:T(8,128)S(1)} %collective-permute-done.refs_0_.refs_1_, f32[320,128]{1,0:T(8,128)S(1)} %collective-permute-done.3.refs_2_, f32[320,128]{1,0:T(8,128)S(1)} %collective-permute-done.4.refs_3_, ...), custom_call_target="tpu_custom_call" | custom-call | tf_op jit(solution)/shard_map/pallas_call | solution.py:355
  20.8 1.7 %collective-permute-done.1.refs_2_ = f32[320,128]{1,0:T(8,128)S(1)} collective-permute-done((f32[320,128]{1,0:T(8,128)S(1)}, f32[320,128]{1,0:T(8,128)S(1)}, u32[]{:S(2)}, u32[]{:S(2)}) %collective-permute-start.1) | collective-permute-done | bytes 163872 | tf_op jit(solution)/shard_map/ppermute | solution.py:448
  22.6 5.6 %shard_map.107 = (f32[256,256]{1,0:T(8,128)S(1)}, f32[256,256]{1,0:T(8,128)S(1)}, f32[2,256,256]{2,1,0:T(8,128)S(1)}, f32[2,256,128]{2,1,0:T(8,128)S(1)}, f32[2,...) custom-call(f32[4,256,256]{2,1,0:T(8,128)} %bitcast.20, ...), custom_call_target="tpu_custom_call" | custom-call | tf_op jit(solution)/shard_map/pallas_call | solution.py:355
  28.3 1.5 %collective-permute-done.11 = f32[256,256]{1,0:T(8,128)S(1)} collective-permute-done((f32[256,256]{1,0:T(8,128)S(1)}, f32[256,256]{1,0:T(8,128)S(1)}, u32[]{:S(2)}, u32[]{:S(2)}) %collective-permute-start.11) | collective-permute-done | bytes 262176 | tf_op jit(solution)/shard_map/ppermute | solution.py:377
  29.8 3.0 %collective-permute-start.12 = (f32[64,256]{1,0:T(8,128)S(1)}, f32[64,256]{1,0:T(8,128)S(1)}, u32[]{:S(2)}, u32[]{:S(2)}) collective-permute-start(f32[64,256]{1,0:T(8,128)S(1)} %get-tuple-element.54), channel_id=1, source_target_pairs={{0,1},{1,0},{2,3},{3,2},{4,5},{5,4},{6,7},{7,6},{8,9},{9,8},{10,11... | collective-permute-start | bytes 196616 | tf_op jit(solution)/shard_map/ppermute | solution.py:377
  32.9 1.1 %collective-permute-start.13 = (f32[64,256]{1,0:T(8,128)S(1)}, f32[64,256]{1,0:T(8,128)S(1)}, u32[]{:S(2)}, u32[]{:S(2)}) collective-permute-start(f32[64,256]{1,0:T(8,128)S(1)} %get-tuple-element.56), channel_id=1, source_target_pairs={{0,2},{1,3},{2,0},{3,1},{4,6},{5,7},{6,4},{7,5},{8,10},{9,11},{10,... | collective-permute-start | bytes 196616 | tf_op jit(solution)/shard_map/ppermute | solution.py:377
  34.4 0.9 %collective-permute-done.12 = f32[64,256]{1,0:T(8,128)S(1)} collective-permute-done((f32[64,256]{1,0:T(8,128)S(1)}, f32[64,256]{1,0:T(8,128)S(1)}, u32[]{:S(2)}, u32[]{:S(2)}) %collective-permute-start.12) | collective-permute-done | bytes 65568 | tf_op jit(solution)/shard_map/ppermute | solution.py:377
  35.3 2.6 %collective-permute-done.13 = f32[64,256]{1,0:T(8,128)S(1)} collective-permute-done((f32[64,256]{1,0:T(8,128)S(1)}, f32[64,256]{1,0:T(8,128)S(1)}, u32[]{:S(2)}, u32[]{:S(2)}) %collective-permute-start.13) | collective-permute-done | bytes 65568 | tf_op jit(solution)/shard_map/ppermute | solution.py:377
  37.8 1.3 %collective-permute-done.14 = f32[64,256]{1,0:T(8,128)S(1)} collective-permute-done((f32[64,256]{1,0:T(8,128)S(1)}, f32[64,256]{1,0:T(8,128)S(1)}, u32[]{:S(2)}, u32[]{:S(2)}) %collective-permute-start.14) | collective-permute-done | bytes 65568 | tf_op jit(solution)/shard_map/ppermute | solution.py:377
  39.1 1.6 %collective-permute-start.15 = (f32[64,256]{1,0:T(8,128)S(1)}, f32[64,256]{1,0:T(8,128)S(1)}, u32[]{:S(2)}, u32[]{:S(2)}) collective-permute-start(f32[64,256]{1,0:T(8,128)S(1)} %add_add_fusion.1), channel_id=1, source_target_pairs={{0,4},{1,5},{2,6},{3,7},{4,0},{5,1},{6,2},{7,3},{8,12},{9,13},{10,... | collective-permute-start | bytes 196616 | tf_op jit(solution)/shard_map/ppermute | solution.py:377
  40.8 1.8 %collective-permute-start.16 = (f32[64,256]{1,0:T(8,128)S(1)}, f32[64,256]{1,0:T(8,128)S(1)}, u32[]{:S(2)}, u32[]{:S(2)}) collective-permute-start(f32[64,256]{1,0:T(8,128)S(1)} %add_add_fusion.1), channel_id=1, source_target_pairs={{0,8},{1,9},{2,10},{3,11},{4,12},{5,13},{6,14},{7,15},{8,0},{9,1},... | collective-permute-start | bytes 196616 | tf_op jit(solution)/shard_map/ppermute | solution.py:377
  42.6 1.0 %collective-permute-start.17 = (f32[64,256]{1,0:T(8,128)S(1)}, f32[64,256]{1,0:T(8,128)S(1)}, u32[]{:S(2)}, u32[]{:S(2)}) collective-permute-start(f32[64,256]{1,0:T(8,128)S(1)} %add_add_fusion.1), channel_id=1, source_target_pairs={{0,12},{1,13},{2,14},{3,15},{4,8},{5,9},{6,10},{7,11},{8,4},{9,5},... | collective-permute-start | bytes 196616 | tf_op jit(solution)/shard_map/ppermute | solution.py:377
  43.8 3.3 %collective-permute-done.16 = f32[64,256]{1,0:T(8,128)S(1)} collective-permute-done((f32[64,256]{1,0:T(8,128)S(1)}, f32[64,256]{1,0:T(8,128)S(1)}, u32[]{:S(2)}, u32[]{:S(2)}) %collective-permute-start.16) | collective-permute-done | bytes 65568 | tf_op jit(solution)/shard_map/ppermute | solution.py:377
  47.2 1.5 %collective-permute-done.17 = f32[64,256]{1,0:T(8,128)S(1)} collective-permute-done((f32[64,256]{1,0:T(8,128)S(1)}, f32[64,256]{1,0:T(8,128)S(1)}, u32[]{:S(2)}, u32[]{:S(2)}) %collective-permute-start.17) | collective-permute-done | bytes 65568 | tf_op jit(solution)/shard_map/ppermute | solution.py:377
  48.7 1.3 %collective-permute-start.18 = (f32[64,256]{1,0:T(8,128)S(1)}, f32[64,256]{1,0:T(8,128)S(1)}, u32[]{:S(2)}, u32[]{:S(2)}) collective-permute-start(f32[64,256]{1,0:T(8,128)S(1)} %get-tuple-element.51), channel_id=1, source_target_pairs={{0,1},{1,0},{2,3},{3,2},{4,5},{5,4},{6,7},{7,6},{8,9},{9,8},{10,11... | collective-permute-start | bytes 196616 | tf_op jit(solution)/shard_map/ppermute | solution.py:377
  51.1 1.7 %collective-permute-start.20 = (f32[64,256]{1,0:T(8,128)S(1)}, f32[64,256]{1,0:T(8,128)S(1)}, u32[]{:S(2)}, u32[]{:S(2)}) collective-permute-start(f32[64,256]{1,0:T(8,128)S(1)} %get-tuple-element.51), channel_id=1, source_target_pairs={{0,3},{1,2},{2,1},{3,0},{4,7},{5,6},{6,5},{7,4},{8,11},{9,10},{10,... | collective-permute-start | bytes 196616 | tf_op jit(solution)/shard_map/ppermute | solution.py:377
  53.0 2.5 %collective-permute-done.19 = f32[64,256]{1,0:T(8,128)S(1)} collective-permute-done((f32[64,256]{1,0:T(8,128)S(1)}, f32[64,256]{1,0:T(8,128)S(1)}, u32[]{:S(2)}, u32[]{:S(2)}) %collective-permute-start.19) | collective-permute-done | bytes 65568 | tf_op jit(solution)/shard_map/ppermute | solution.py:377
  55.5 0.7 collective-permute-done.20
  57.2 4.2 %collective-permute-start.7 = (f32[256,128]{1,0:T(8,128)S(1)}, f32[256,128]{1,0:T(8,128)S(1)}, u32[]{:S(2)}, u32[]{:S(2)}) collective-permute-start(f32[256,128]{1,0:T(8,128)S(1)} %get-tuple-element.43), channel_id=1, source_target_pairs={{0,1},{2,3},{4,5},{6,7},{8,9},{10,11},{12,13},{14,15},{1,0},{3,2},... | collective-permute-start | bytes 393224 | tf_op jit(solution)/shard_map/ppermute | solution.py:509
  62.1 3.2 %collective-permute-start.9 = (f32[256,128]{1,0:T(8,128)S(1)}, f32[256,128]{1,0:T(8,128)S(1)}, u32[]{:S(2)}, u32[]{:S(2)}) collective-permute-start(f32[256,128]{1,0:T(8,128)S(1)} %get-tuple-element.46), channel_id=1, source_target_pairs={{0,1},{2,3},{4,5},{6,7},{8,9},{10,11},{12,13},{14,15},{1,0},{3,2},... | collective-permute-start | bytes 393224 | tf_op jit(solution)/shard_map/ppermute | solution.py:509
  65.4 4.9 %collective-permute-done.7.e1 = f32[256,128]{1,0:T(8,128)S(1)} collective-permute-done((f32[256,128]{1,0:T(8,128)S(1)}, f32[256,128]{1,0:T(8,128)S(1)}, u32[]{:S(2)}, u32[]{:S(2)}) %collective-permute-start.7) | collective-permute-done | bytes 131104 | tf_op jit(solution)/shard_map/ppermute | solution.py:509
  70.3 3.4 %collective-permute-done.9.e2 = f32[256,128]{1,0:T(8,128)S(1)} collective-permute-done((f32[256,128]{1,0:T(8,128)S(1)}, f32[256,128]{1,0:T(8,128)S(1)}, u32[]{:S(2)}, u32[]{:S(2)}) %collective-permute-start.9) | collective-permute-done | bytes 131104 | tf_op jit(solution)/shard_map/ppermute | solution.py:509
  73.7 1.2 %shard_map.109 = f32[4,256,256]{2,1,0:T(8,128)} custom-call(f32[2,256,256]{2,1,0:T(8,128)S(1)} %get-tuple-element.42.t1, f32[256,128]{1,0:T(8,128)S(1)} %collective-permute-done.7.e1, f32[256,128]{1,0:T(8,128)S(1)} %collective-permute-done.8.o1, f32[2,256,256]{2,1,0:T(8,128)S(1)} %get-tuple-element.45.t2, f32[256,128]{1,0:T(8,128)S(1)} %collective-permute-done.9.e2, ...), custom_call_target="tpu_custom_call" | custom-call | tf_op jit(solution)/shard_map/pallas_call | solution.py:355
  74.9 0.8 %pad_maximum_fusion = f32[2,256,256]{2,1,0:T(8,128)} fusion(f32[1,256,256]{2,1,0:T(8,128)S(1)} %get-tuple-element.53, f32[1,256,256]{2,1,0:T(8,128)S(1)} %get-tuple-element.52), kind=kLoop, calls=%fused_computation | loop fusion | flops 131072 | bytes 1048576 | tf_op jit(solution)/shard_map/stack | solution.py:418
  (49 shorter events, 6.6 us)
Async XLA Ops:
  0.6 12.8 %copy-start.3 = (f32[2,256,256]{2,1,0:T(8,128)S(1)}, f32[2,256,256]{2,1,0:T(8,128)}, u32[]{:S(2)}) copy-start(f32[2,256,256]{2,1,0:T(8,128)} %probe.1) | copy-start | bytes 1572868
  1.7 1.7 %collective-permute-start = (f32[4,64,256]{2,1,0:T(8,128)S(1)}, f32[4,64,256]{2,1,0:T(8,128)S(1)}, u32[]{:S(2)}, u32[]{:S(2)}) collective-permute-start(f32[4,64,256]{2,1,0:T(8,128)S(1)} %constant_dynamic-slice_fusion.3), channel_id=1, source_target_pairs={{0,16},{16,0},{1,17},{17,1},{2,18},{18,2},{3,19},{19,3},{4,20},{20... | collective-permute-start | bytes 786440 | tf_op jit(solution)/shard_map/ppermute | solution.py:438
  3.4 1.2 %copy-start = (f32[2,2,256,256]{3,2,1,0:T(8,128)S(1)}, f32[2,2,256,256]{3,2,1,0:T(8,128)}, u32[]{:S(2)}) copy-start(f32[2,2,256,256]{3,2,1,0:T(8,128)} %param.9) | copy-start | bytes 3145732
  4.6 8.8 %copy-start.5 = (f32[256,256]{1,0:T(8,128)S(1)}, f32[256,256]{1,0:T(8,128)}, u32[]{:S(2)}) copy-start(f32[256,256]{1,0:T(8,128)} %phase.1) | copy-start | bytes 786436
  4.6 13.7 %copy-start.1 = (f32[2,2,256,256]{3,2,1,0:T(8,128)S(1)}, f32[2,2,256,256]{3,2,1,0:T(8,128)}, u32[]{:S(2)}) copy-start(f32[2,2,256,256]{3,2,1,0:T(8,128)} %param.9) | copy-start | bytes 3145732
  4.9 13.5 %collective-permute-start.3 = (f32[320,128]{1,0:T(8,128)S(1)}, f32[320,128]{1,0:T(8,128)S(1)}, u32[]{:S(2)}, u32[]{:S(2)}) collective-permute-start(f32[320,128]{1,0:T(8,128)S(1)} %get-tuple-element.32), channel_id=1, source_target_pairs={{0,1},{2,3},{4,5},{6,7},{8,9},{10,11},{12,13},{14,15},{1,0},{3,2},... | collective-permute-start | bytes 491528 | tf_op jit(solution)/shard_map/ppermute | solution.py:448
  7.8 10.6 %collective-permute-start.4 = (f32[320,128]{1,0:T(8,128)S(1)}, f32[320,128]{1,0:T(8,128)S(1)}, u32[]{:S(2)}, u32[]{:S(2)}) collective-permute-start(f32[320,128]{1,0:T(8,128)S(1)} %get-tuple-element.33), channel_id=1, source_target_pairs={{1,2},{3,4},{5,6},{7,8},{9,10},{11,12},{13,14},{2,1},{4,3},{6,5},{... | collective-permute-start | bytes 491528 | tf_op jit(solution)/shard_map/ppermute | solution.py:448
  8.5 14.1 %collective-permute-start.1 = (f32[320,128]{1,0:T(8,128)S(1)}, f32[320,128]{1,0:T(8,128)S(1)}, u32[]{:S(2)}, u32[]{:S(2)}) collective-permute-start(f32[320,128]{1,0:T(8,128)S(1)} %get-tuple-element.26), channel_id=1, source_target_pairs={{0,1},{2,3},{4,5},{6,7},{8,9},{10,11},{12,13},{14,15},{1,0},{3,2},... | collective-permute-start | bytes 491528 | tf_op jit(solution)/shard_map/ppermute | solution.py:448
  12.8 9.8 %collective-permute-start.2 = (f32[320,128]{1,0:T(8,128)S(1)}, f32[320,128]{1,0:T(8,128)S(1)}, u32[]{:S(2)}, u32[]{:S(2)}) collective-permute-start(f32[320,128]{1,0:T(8,128)S(1)} %get-tuple-element.27), channel_id=1, source_target_pairs={{1,2},{3,4},{5,6},{7,8},{9,10},{11,12},{13,14},{2,1},{4,3},{6,5},{... | collective-permute-start | bytes 491528 | tf_op jit(solution)/shard_map/ppermute | solution.py:448
  13.4 0.7 copy-start.9
  14.1 0.9 %copy-start.6 = (f32[1,1,1,256,256]{4,3,2,1,0:T(8,128)S(1)}, f32[1,1,1,256,256]{4,3,2,1,0:T(8,128)}, u32[]{:S(2)}) copy-start(f32[1,1,1,256,256]{4,3,2,1,0:T(8,128)} %param.12) | copy-start | bytes 786436
  15.0 0.9 %copy-start.7 = (bf16[2,256,256]{2,1,0:T(8,128)(2,1)S(1)}, bf16[2,256,256]{2,1,0:T(8,128)(2,1)}, u32[]{:S(2)}) copy-start(bf16[2,256,256]{2,1,0:T(8,128)(2,1)} %constant.57.clone.order) | copy-start | bytes 786436
  16.0 2.4 %copy-start.2 = (bf16[4,256,256]{2,1,0:T(8,128)(2,1)S(1)}, bf16[4,256,256]{2,1,0:T(8,128)(2,1)}, u32[]{:S(2)}) copy-start(bf16[4,256,256]{2,1,0:T(8,128)(2,1)} %constant.54.clone.refs_8_.refs_11_) | copy-start | bytes 1572868
  16.0 2.4 %copy-start.4 = (f32[2,128,128]{2,1,0:T(8,128)S(1)}, f32[2,128,128]{2,1,0:T(8,128)}, u32[]{:S(2)}) copy-start(f32[2,128,128]{2,1,0:T(8,128)} %constant.55.clone.refs_9_.refs_12_) | copy-start | bytes 393220
  16.0 2.4 %copy-start.8 = (f32[2,8,128]{2,1,0:T(8,128)S(1)}, f32[2,8,128]{2,1,0:T(8,128)}, u32[]{:S(2)}) copy-start(f32[2,8,128]{2,1,0:T(8,128)} %constant.56.clone.refs_10_.refs_13_) | copy-start | bytes 24580
  28.2 1.6 %collective-permute-start.11 = (f32[256,256]{1,0:T(8,128)S(1)}, f32[256,256]{1,0:T(8,128)S(1)}, u32[]{:S(2)}, u32[]{:S(2)}) collective-permute-start(f32[256,256]{1,0:T(8,128)S(1)} %get-tuple-element.49), channel_id=1, source_target_pairs={{0,16},{16,0},{1,17},{17,1},{2,18},{18,2},{3,19},{19,3},{4,20},{20... | collective-permute-start | bytes 786440 | tf_op jit(solution)/shard_map/ppermute | solution.py:377
  29.8 5.4 %collective-permute-start.12 = (f32[64,256]{1,0:T(8,128)S(1)}, f32[64,256]{1,0:T(8,128)S(1)}, u32[]{:S(2)}, u32[]{:S(2)}) collective-permute-start(f32[64,256]{1,0:T(8,128)S(1)} %get-tuple-element.54), channel_id=1, source_target_pairs={{0,1},{1,0},{2,3},{3,2},{4,5},{5,4},{6,7},{7,6},{8,9},{9,8},{10,11... | collective-permute-start | bytes 196616 | tf_op jit(solution)/shard_map/ppermute | solution.py:377
  32.9 5.0 %collective-permute-start.13 = (f32[64,256]{1,0:T(8,128)S(1)}, f32[64,256]{1,0:T(8,128)S(1)}, u32[]{:S(2)}, u32[]{:S(2)}) collective-permute-start(f32[64,256]{1,0:T(8,128)S(1)} %get-tuple-element.56), channel_id=1, source_target_pairs={{0,2},{1,3},{2,0},{3,1},{4,6},{5,7},{6,4},{7,5},{8,10},{9,11},{10,... | collective-permute-start | bytes 196616 | tf_op jit(solution)/shard_map/ppermute | solution.py:377
  33.9 5.2 %collective-permute-start.14 = (f32[64,256]{1,0:T(8,128)S(1)}, f32[64,256]{1,0:T(8,128)S(1)}, u32[]{:S(2)}, u32[]{:S(2)}) collective-permute-start(f32[64,256]{1,0:T(8,128)S(1)} %get-tuple-element.55), channel_id=1, source_target_pairs={{0,3},{1,2},{2,1},{3,0},{4,7},{5,6},{6,5},{7,4},{8,11},{9,10},{10,... | collective-permute-start | bytes 196616 | tf_op jit(solution)/shard_map/ppermute | solution.py:377
  39.1 4.7 %collective-permute-start.15 = (f32[64,256]{1,0:T(8,128)S(1)}, f32[64,256]{1,0:T(8,128)S(1)}, u32[]{:S(2)}, u32[]{:S(2)}) collective-permute-start(f32[64,256]{1,0:T(8,128)S(1)} %add_add_fusion.1), channel_id=1, source_target_pairs={{0,4},{1,5},{2,6},{3,7},{4,0},{5,1},{6,2},{7,3},{8,12},{9,13},{10,... | collective-permute-start | bytes 196616 | tf_op jit(solution)/shard_map/ppermute | solution.py:377
  40.8 6.4 %collective-permute-start.16 = (f32[64,256]{1,0:T(8,128)S(1)}, f32[64,256]{1,0:T(8,128)S(1)}, u32[]{:S(2)}, u32[]{:S(2)}) collective-permute-start(f32[64,256]{1,0:T(8,128)S(1)} %add_add_fusion.1), channel_id=1, source_target_pairs={{0,8},{1,9},{2,10},{3,11},{4,12},{5,13},{6,14},{7,15},{8,0},{9,1},... | collective-permute-start | bytes 196616 | tf_op jit(solution)/shard_map/ppermute | solution.py:377
  42.6 6.1 %collective-permute-start.17 = (f32[64,256]{1,0:T(8,128)S(1)}, f32[64,256]{1,0:T(8,128)S(1)}, u32[]{:S(2)}, u32[]{:S(2)}) collective-permute-start(f32[64,256]{1,0:T(8,128)S(1)} %add_add_fusion.1), channel_id=1, source_target_pairs={{0,12},{1,13},{2,14},{3,15},{4,8},{5,9},{6,10},{7,11},{8,4},{9,5},... | collective-permute-start | bytes 196616 | tf_op jit(solution)/shard_map/ppermute | solution.py:377
  48.7 4.3 %collective-permute-start.18 = (f32[64,256]{1,0:T(8,128)S(1)}, f32[64,256]{1,0:T(8,128)S(1)}, u32[]{:S(2)}, u32[]{:S(2)}) collective-permute-start(f32[64,256]{1,0:T(8,128)S(1)} %get-tuple-element.51), channel_id=1, source_target_pairs={{0,1},{1,0},{2,3},{3,2},{4,5},{5,4},{6,7},{7,6},{8,9},{9,8},{10,11... | collective-permute-start | bytes 196616 | tf_op jit(solution)/shard_map/ppermute | solution.py:377
  50.0 6.3 %collective-permute-start.5 = (f32[2,64,384]{2,1,0:T(8,128)S(1)}, f32[2,64,384]{2,1,0:T(8,128)S(1)}, u32[]{:S(2)}, u32[]{:S(2)}) collective-permute-start(f32[2,64,384]{2,1,0:T(8,128)S(1)} %get-tuple-element.38), channel_id=1, source_target_pairs={{0,16},{16,0},{1,17},{17,1},{2,18},{18,2},{3,19},{19,3},{4,20},{20... | collective-permute-start | bytes 589832 | tf_op jit(solution)/shard_map/ppermute | solution.py:501
  50.0 6.3 %collective-permute-start.6 = (f32[2,64,384]{2,1,0:T(8,128)S(1)}, f32[2,64,384]{2,1,0:T(8,128)S(1)}, u32[]{:S(2)}, u32[]{:S(2)}) collective-permute-start(f32[2,64,384]{2,1,0:T(8,128)S(1)} %get-tuple-element.41), channel_id=1, source_target_pairs={{0,16},{16,0},{1,17},{17,1},{2,18},{18,2},{3,19},{19,3},{4,20},{20... | collective-permute-start | bytes 589832 | tf_op jit(solution)/shard_map/ppermute | solution.py:501
  50.5 5.0 %collective-permute-start.19 = (f32[64,256]{1,0:T(8,128)S(1)}, f32[64,256]{1,0:T(8,128)S(1)}, u32[]{:S(2)}, u32[]{:S(2)}) collective-permute-start(f32[64,256]{1,0:T(8,128)S(1)} %get-tuple-element.51), channel_id=1, source_target_pairs={{0,2},{1,3},{2,0},{3,1},{4,6},{5,7},{6,4},{7,5},{8,10},{9,11},{10,... | collective-permute-start | bytes 196616 | tf_op jit(solution)/shard_map/ppermute | solution.py:377
  51.1 5.2 %collective-permute-start.20 = (f32[64,256]{1,0:T(8,128)S(1)}, f32[64,256]{1,0:T(8,128)S(1)}, u32[]{:S(2)}, u32[]{:S(2)}) collective-permute-start(f32[64,256]{1,0:T(8,128)S(1)} %get-tuple-element.51), channel_id=1, source_target_pairs={{0,3},{1,2},{2,1},{3,0},{4,7},{5,6},{6,5},{7,4},{8,11},{9,10},{10,... | collective-permute-start | bytes 196616 | tf_op jit(solution)/shard_map/ppermute | solution.py:377
  56.3 18.6 %collective-permute-start.21 = (f32[256,256]{1,0:T(8,128)S(1)}, f32[256,256]{1,0:T(8,128)S(1)}, u32[]{:S(2)}, u32[]{:S(2)}) collective-permute-start(f32[256,256]{1,0:T(8,128)S(1)} %bitcast.28), channel_id=1, source_target_pairs={{0,16},{16,0},{1,17},{17,1},{2,18},{18,2},{3,19},{19,3},{4,20},{20... | collective-permute-start | bytes 786440 | tf_op jit(solution)/shard_map/ppermute | solution.py:377
  56.5 8.8 %collective-permute-start.10 = (f32[256,128]{1,0:T(8,128)S(1)}, f32[256,128]{1,0:T(8,128)S(1)}, u32[]{:S(2)}, u32[]{:S(2)}) collective-permute-start(f32[256,128]{1,0:T(8,128)S(1)} %get-tuple-element.47), channel_id=1, source_target_pairs={{1,2},{3,4},{5,6},{7,8},{9,10},{11,12},{13,14},{2,1},{4,3},{6,5},{... | collective-permute-start | bytes 393224 | tf_op jit(solution)/shard_map/ppermute | solution.py:509
  57.2 13.0 %collective-permute-start.7 = (f32[256,128]{1,0:T(8,128)S(1)}, f32[256,128]{1,0:T(8,128)S(1)}, u32[]{:S(2)}, u32[]{:S(2)}) collective-permute-start(f32[256,128]{1,0:T(8,128)S(1)} %get-tuple-element.43), channel_id=1, source_target_pairs={{0,1},{2,3},{4,5},{6,7},{8,9},{10,11},{12,13},{14,15},{1,0},{3,2},... | collective-permute-start | bytes 393224 | tf_op jit(solution)/shard_map/ppermute | solution.py:509
  61.5 8.8 %collective-permute-start.8 = (f32[256,128]{1,0:T(8,128)S(1)}, f32[256,128]{1,0:T(8,128)S(1)}, u32[]{:S(2)}, u32[]{:S(2)}) collective-permute-start(f32[256,128]{1,0:T(8,128)S(1)} %get-tuple-element.44), channel_id=1, source_target_pairs={{1,2},{3,4},{5,6},{7,8},{9,10},{11,12},{13,14},{2,1},{4,3},{6,5},{... | collective-permute-start | bytes 393224 | tf_op jit(solution)/shard_map/ppermute | solution.py:509
  62.1 11.5 %collective-permute-start.9 = (f32[256,128]{1,0:T(8,128)S(1)}, f32[256,128]{1,0:T(8,128)S(1)}, u32[]{:S(2)}, u32[]{:S(2)}) collective-permute-start(f32[256,128]{1,0:T(8,128)S(1)} %get-tuple-element.46), channel_id=1, source_target_pairs={{0,1},{2,3},{4,5},{6,7},{8,9},{10,11},{12,13},{14,15},{1,0},{3,2},... | collective-permute-start | bytes 393224 | tf_op jit(solution)/shard_map/ppermute | solution.py:509
where the time goes:
time: 76.1 us; the launch traced here: 75.7 us
  starting transfers between devices  31.1 us (41%)
  waiting for transfers between devices  25.9 us (34%)
  Pallas kernels  12 us (16%)
  local copies, waits for them, and re-layouts  4.88 us (6%)
  other arithmetic  0.94 us (1%)
  between operations  0.92 us (1%)
    ppermute x11, waiting for transfers between devices, swap(): return lax.ppermute(value, axis, [(i, i ^ distance) for i in range(count)])  14.7 us
    ppermute x11, starting transfers between devices, swap(): return lax.ppermute(value, axis, [(i, i ^ distance) for i in range(count)])  12.7 us
    pallas_call x6, Pallas kernels, call(): pl.pallas_call(kernel, out_shape=[jax.ShapeDtypeStruct(s, F32) for s in s...  12 us
    ppermute x4, starting transfers between devices, body(): lax.ppermute(f, 'col', col_rounds[i % 3 - 1])  8.81 us
    ppermute x4, starting transfers between devices, body(): lax.ppermute(packed[i], 'col', col_rounds[i % 2])  8.52 us
    ppermute x4, waiting for transfers between devices, body(): lax.ppermute(f, 'col', col_rounds[i % 3 - 1])  8.29 us
    unnamed x20, local copies, waits for them, and re-layouts  3.78 us
    ppermute x4, waiting for transfers between devices, body(): lax.ppermute(packed[i], 'col', col_rounds[i % 2])  1.74 us
  transfers between devices with their start and end apart: 22, of which 14 were waited for; matrix products, arithmetic and copies ran while one was open for 0% of the time, Pallas kernels for 8%

commit v1 on v0

--- a/solution.py
+++ b/solution.py
@@ -8,11 +8,13 @@
 from jax.experimental.pallas import tpu as pltpu
 from jax.sharding import PartitionSpec as P
 
+
 EPS_AMP = 0.5
 F32 = jnp.float32
 BF16 = jnp.bfloat16
 VMEM = pl.BlockSpec(memory_space=pltpu.VMEM)
 SMEM = pl.BlockSpec(memory_space=pltpu.SMEM)
+HBM = pl.BlockSpec(memory_space=pltpu.HBM)
 
 
 def split_np(table):
@@ -121,6 +123,27 @@
     return low, high
 
 
+def load_kernel(n_row, margin, obj_hbm, offs_hbm, *refs):
+    strips, (obj, offs, sems) = refs[:n_row], refs[n_row:]
+    n = obj.shape[1]
+    even = lax.axis_index("row") % 2 == 0
+    copies = []
+    for which, strip in enumerate(strips):
+        last = even if which == 0 else jnp.logical_not(even)
+        start = pl.multiple_of(jnp.where(last, n - margin, 0), 8)
+        copies.append(
+            pltpu.make_async_copy(
+                obj_hbm.at[:, pl.ds(start, margin), :], strip, sems.at[which + 1]
+            )
+        )
+    copies.append(pltpu.make_async_copy(obj_hbm, obj, sems.at[0]))
+    copies.append(pltpu.make_async_copy(offs_hbm, offs, sems.at[n_row + 1]))
+    for copy in copies:
+        copy.start()
+    for copy in copies:
+        copy.wait()
+
+
 def pack_kernel(n_row, obj, *refs):
     halos, outs = refs[:n_row], refs[n_row:]
     even = lax.axis_index("col") % 2 == 0
@@ -139,8 +162,15 @@
     return pltpu.roll(x, shift, axis=axis)
 
 
-def prep_kernel(margin, phase, amps, probe, offs, order, kr, ki, am, pr):
+def prep_kernel(margin, offs, *refs):
+    hbm, outs, scratch, sems = refs[:7], refs[7:14], refs[14:18], refs[18]
+    kr, ki, am, pr = outs[:4]
+    phase, amps, probe, order = scratch
     n = phase.shape[0]
+    places = list(scratch) + list(outs[4:])
+    copies = [pltpu.make_async_copy(a, b, sems.at[i]) for i, (a, b) in enumerate(zip(hbm, places))]
+    for copy in copies:
+        copy.start()
 
     def thirds(x):
         a = x.astype(BF16)
@@ -153,14 +183,20 @@
         a, b, c = thirds(rows)
         return dot(a, order[1]) + (dot(b, order[1]) + dot(c, order[1]))
 
+    copies[0].wait()
+    copies[3].wait()
     angle = reorder(phase)
     kr[...] = jnp.cos(angle)
     ki[...] = jnp.sin(angle)
+    copies[1].wait()
     am[...] = reorder(amps)
     sy = (offs[0, 0] - margin + n) % n
     sx = (offs[0, 1] - margin + n) % n
+    copies[2].wait()
     for i in range(2):
         pr[i] = dyn_roll(dyn_roll(probe[i], sy, 0), sx, 1)
+    for copy in copies[4:]:
+        copy.wait()
 
 
 def merge_cols(own, low, high, ox, margin):
@@ -236,7 +272,7 @@
     arrive[0], arrive[1] = x
 
 
-def split_grad(grad, offs, margin, own, strip, sends):
+def split_grad(grad, s, offs, margin, own, strip, sends):
     n = grad[0].shape[0]
     h = n // 2
     oy, ox = offs[0, 0], offs[0, 1]
@@ -255,15 +291,15 @@
         right = jnp.where(to_low, 0.0, g[:, h:])
         side = jnp.where(spill, jnp.where(front, g[:, :h], g[:, h:]), 0.0)
         pieces = [left, right, side]
-        own[i, :, :h] = jnp.where(inner, left, 0.0)
-        own[i, :, h:] = jnp.where(inner, right, 0.0)
-        strip[i] = jnp.where(inner, side, 0.0)
+        own[2 * s + i, :, :h] = jnp.where(inner, left, 0.0)
+        own[2 * s + i, :, h:] = jnp.where(inner, right, 0.0)
+        strip[2 * s + i] = jnp.where(inner, side, 0.0)
         for j, piece in enumerate(pieces):
             top = jnp.where(high_rows[:margin], piece[:margin], 0.0)
             bottom = jnp.where(low_rows[n - margin :], piece[n - margin :], 0.0)
             for which, send in enumerate(sends):
                 first = row_even if which == 0 else jnp.logical_not(row_even)
-                send[i, :, j * h : (j + 1) * h] = jnp.where(first, top, bottom)
+                send[2 * s + i, :, j * h : (j + 1) * h] = jnp.where(first, top, bottom)
 
 
 def back_kernel(n_row, margin, *refs):
@@ -279,14 +315,11 @@
     modulus = jnp.sqrt(far[0] * far[0] + far[1] * far[1] + EPS_AMP)
     factor = 2.0 * (1.0 - am[...] / modulus)
     back_far = dft.inverse([factor * far[0], factor * far[1]])
-    rest = outs[2:]
-    split_grad(conj_product(arr, back_far), offs, margin, rest[0], rest[1], rest[2 : 2 + n_row])
+    own, strip, sends = outs[2], outs[3], outs[4:]
+    split_grad(conj_product(arr, back_far), 1, offs, margin, own, strip, sends)
     x = dft.forward(conj_product(win, back_far))
     x = dft.inverse(conj_product([kr[...], ki[...]], x))
-    rest = rest[2 + n_row :]
-    split_grad(
-        conj_product([pr[0], pr[1]], x), offs, margin, rest[0], rest[1], rest[2 : 2 + n_row]
-    )
+    split_grad(conj_product([pr[0], pr[1]], x), 0, offs, margin, own, strip, sends)
     grad = conj_product([w1[0], w1[1]], x)
     sy = (margin - offs[0, 0] + n) % n
     sx = (margin - offs[0, 1] + n) % n
@@ -296,24 +329,19 @@
     give[...] = jnp.where(even, grad[1], grad[0])
 
 
-def fold_rows_kernel(n_row, margin, *refs):
-    ins, outs = refs[: 2 * (2 + n_row)], refs[2 * (2 + n_row) :]
+def fold_rows_kernel(n_row, margin, own, strip, *refs):
+    got, (total, send_e, send_o) = refs[:n_row], refs[n_row:]
     row_even = lax.axis_index("row") % 2 == 0
     col_even = lax.axis_index("col") % 2 == 0
+    n = own.shape[1]
+    h = n // 2
+    front = iota((n, h), 1) < h // 2
     for s in range(2):
-        own, strip = ins[s * (2 + n_row) : s * (2 + n_row) + 2]
-        got = ins[s * (2 + n_row) + 2 : (s + 1) * (2 + n_row)]
-        total, send_e, send_o = outs[3 * s : 3 * s + 3]
-        n = own.shape[1]
-        h = n // 2
         strips = []
-        for i in range(2):
+        for i in range(2 * s, 2 * s + 2):
             total[i] = own[i]
             r = got[0][i]
-            if n_row == 2:
-                q = got[1][i]
-            else:
-                q = jnp.zeros_like(r)
+            q = got[1][i] if n_row == 2 else jnp.zeros_like(r)
             top, bottom = jnp.where(row_even, q, r), jnp.where(row_even, r, q)
             total[i, :margin] += top[:, :n]
             total[i, n - margin :] += bottom[:, :n]
@@ -328,36 +356,42 @@
                     0,
                 )
             )
-        front = iota((n, h), 1) < h // 2
         moved = half_roll(strips[1])
         to_high = jnp.where(front, strips[0], moved)
         to_low = jnp.where(front, moved, strips[0])
-        send_e[...] = jnp.where(col_even, to_high, to_low)
-        send_o[...] = jnp.where(col_even, to_low, to_high)
-
-
-def fold_cols_kernel(t1, e1, o1, t2, e2, o2, out):
+        send_e[s] = jnp.where(col_even, to_high, to_low)
+        send_o[s] = jnp.where(col_even, to_low, to_high)
+
+
+def fold_cols_kernel(total, e, o, out):
     col_even = lax.axis_index("col") % 2 == 0
-    for s, (t, e, o) in enumerate(((t1, e1, o1), (t2, e2, o2))):
-        n = t.shape[1]
-        h = n // 2
-        front = iota((n, h), 1) < h // 2
-        high = jnp.where(col_even, e[...], o[...])
-        low = jnp.where(col_even, o[...], e[...])
+    n = total.shape[1]
+    h = n // 2
+    front = iota((n, h), 1) < h // 2
+    for s in range(2):
+        high = jnp.where(col_even, e[s], o[s])
+        low = jnp.where(col_even, o[s], e[s])
         for i in range(2):
             a = low if i == 0 else half_roll(low)
             b = high if i == 0 else half_roll(high)
-            out[2 * s + i, :, :h] = t[i, :, :h] + jnp.where(front, a, 0.0)
-            out[2 * s + i, :, h:] = t[i, :, h:] + jnp.where(front, 0.0, b)
-
-
-def call(kernel, shapes, in_specs, *args):
+            at = 2 * s + i
+            out[at, :, :h] = total[at, :, :h] + jnp.where(front, a, 0.0)
+            out[at, :, h:] = total[at, :, h:] + jnp.where(front, 0.0, b)
+
+
+def in_hbm(x):
+    return pltpu.with_memory_space_constraint(x, pltpu.HBM)
+
+
+def call(kernel, shapes, in_specs, *args, scratch=(), mib=16):
+    shapes = [s if isinstance(s, jax.ShapeDtypeStruct) else jax.ShapeDtypeStruct(s, F32) for s in shapes]
     return pl.pallas_call(
         kernel,
-        out_shape=[jax.ShapeDtypeStruct(s, F32) for s in shapes],
+        out_shape=shapes,
         in_specs=in_specs,
-        out_specs=[VMEM] * len(shapes),
-        compiler_params=pltpu.CompilerParams(vmem_limit_bytes=48 * 1024 * 1024),
+        out_specs=[VMEM if s.dtype != jnp.int32 else SMEM for s in shapes],
+        scratch_shapes=list(scratch),
+        compiler_params=pltpu.CompilerParams(vmem_limit_bytes=mib << 20),
     )(*args)
 
 
@@ -395,19 +429,25 @@
 
 
 def reduce_probe(keep, give):
-    rows = lax.axis_size("row")
     cols = lax.axis_size("col")
     n = keep.shape[0]
-    mine = keep + swap(give, "row", 1)
+    other = swap(give, "row", 1)
+    mine = keep + other
     quad = min(4, cols)
     place = lax.axis_index("col") % quad
     chunk = n // quad
     parts = [
         lax.dynamic_slice_in_dim(mine, (place ^ j) * chunk, chunk, 0) for j in range(quad)
     ]
-    total = pair_sum([parts[0]] + [swap(parts[j], "col", j) for j in range(1, quad)])
+    sums = [parts[0]]
+    for j in range(1, quad):
+        sums.append(swap(parts[j], "col", j))
+    total = pair_sum(sums)
     for axis, stride, width in stages("col", quad) + stages("row", 2):
-        total = pair_sum([total] + [swap(total, axis, stride * j) for j in range(1, width)])
+        sums = [total]
+        for j in range(1, width):
+            sums.append(swap(total, axis, stride * j))
+        total = pair_sum(sums)
     full = jnp.zeros((quad, chunk, n), F32)
     for j in range(quad):
         part = total if j == 0 else swap(total, "col", j)
@@ -418,26 +458,26 @@
     return jnp.stack([jnp.where(even, full, other), jnp.where(even, other, full)])
 
 
-def body(object_field, probe, phase, amplitudes, offsets):
+def whole(object_field, probe, phase, amplitudes, offsets):
     tile = object_field.shape[2]
     n = probe.shape[1]
     h = n // 2
     margin = n // 4
-    obj = object_field.reshape(4, tile, tile)
-    offs = offsets.reshape(1, 2)
-    amps = amplitudes.reshape(n, n)
-    mats, tw_left, tw_right, order = [jnp.asarray(t) for t in dft_constants(n)]
+    tables = [jnp.asarray(t) for t in dft_constants(n)]
+    mats, tw_left, tw_right, order = tables
 
     row_rounds, col_rounds = edges("row"), edges("col")
     n_row = len(row_rounds)
-    row_even = lax.axis_index("row") % 2 == 0
-    halos = []
-    for which, pairs in enumerate(row_rounds):
-        last = row_even if which == 0 else jnp.logical_not(row_even)
-        strip = lax.dynamic_slice_in_dim(obj, jnp.where(last, tile - margin, 0), margin, 1)
-        halos.append(lax.ppermute(strip, "row", pairs))
+    *halos, obj, offs = call(
+        functools.partial(load_kernel, n_row, margin),
+        [(4, margin, n)] * n_row + [(4, n, n), jax.ShapeDtypeStruct((1, 2), jnp.int32)],
+        [HBM, HBM],
+        in_hbm(object_field.reshape(4, tile, tile)),
+        in_hbm(offsets.reshape(1, 2)),
+        scratch=[pltpu.SemaphoreType.DMA((n_row + 2,))],
+    )
+    halos = [lax.ppermute(x, "row", pairs) for x, pairs in zip(halos, row_rounds)]
     length = tile + margin * n_row
-
     packed = call(
         functools.partial(pack_kernel, n_row),
         [(length, h)] * 4,
@@ -445,16 +485,24 @@
         obj,
         *halos,
     )
-    strips = [lax.ppermute(packed[i], "col", col_rounds[i % 2]) for i in range(4)]
-    kr, ki, am, pr = call(
+    strips = []
+    for i in range(4):
+        strips.append(lax.ppermute(packed[i], "col", col_rounds[i % 2]))
+    kr, ki, am, pr, mats, tw_left, tw_right = call(
         functools.partial(prep_kernel, margin),
-        [(n, n), (n, n), (n, n), (2, n, n)],
-        [VMEM, VMEM, VMEM, SMEM, VMEM],
-        phase,
-        amps,
-        probe,
+        [(n, n), (n, n), (n, n), (2, n, n)]
+        + [jax.ShapeDtypeStruct(t.shape, t.dtype) for t in tables[:3]],
+        [SMEM] + [HBM] * 7,
         offs,
-        order,
+        *[in_hbm(x) for x in (phase, amplitudes.reshape(n, n), probe, order)],
+        *[in_hbm(x) for x in (mats, tw_left, tw_right)],
+        scratch=[
+            pltpu.VMEM((n, n), F32),
+            pltpu.VMEM((n, n), F32),
+            pltpu.VMEM((2, n, n), F32),
+            pltpu.VMEM((2, n, n), BF16),
+            pltpu.SemaphoreType.DMA((7,)),
+        ],
     )
     w1, arrive = call(
         functools.partial(arrive_kernel, n_row, margin),
@@ -472,10 +520,9 @@
         tw_left,
         tw_right,
     )
-    per_slice = [(2, n, n), (2, n, h)] + [(2, margin, n + h)] * n_row
-    outs = call(
+    keep, give, own, strip, *sends = call(
         functools.partial(back_kernel, n_row, margin),
-        [(n, n), (n, n)] + per_slice * 2,
+        [(n, n), (n, n), (4, n, n), (4, n, h)] + [(4, margin, n + h)] * n_row,
         [VMEM] * (1 + n_row) + [VMEM, VMEM, SMEM] + [VMEM] * 9,
         obj,
         *halos,
@@ -491,25 +538,23 @@
         mats,
         tw_left,
         tw_right,
-    )
-    keep, give = outs[:2]
+        mib=40,
+    )
     probe_grad = reduce_probe(keep, give)
-    second, first = outs[2 : 4 + n_row], outs[4 + n_row :]
-    ins = []
-    for part in (first, second):
-        ins += list(part[:2])
-        ins += [lax.ppermute(part[2 + i], "row", row_rounds[i]) for i in range(n_row)]
-    folded = call(
+    got = []
+    for i, pairs in enumerate(row_rounds):
+        got.append(lax.ppermute(sends[i], "row", pairs))
+    total, send_e, send_o = call(
         functools.partial(fold_rows_kernel, n_row, margin),
-        [(2, n, n), (n, h), (n, h)] * 2,
-        [VMEM] * len(ins),
-        *ins,
-    )
-    folded = [
-        f if i % 3 == 0 else lax.ppermute(f, "col", col_rounds[i % 3 - 1])
-        for i, f in enumerate(folded)
-    ]
-    (grad,) = call(fold_cols_kernel, [(4, n, n)], [VMEM] * 6, *folded)
+        [(4, n, n), (2, n, h), (2, n, h)],
+        [VMEM] * (2 + n_row),
+        own,
+        strip,
+        *got,
+    )
+    send_e = lax.ppermute(send_e, "col", col_rounds[0])
+    send_o = lax.ppermute(send_o, "col", col_rounds[1])
+    (grad,) = call(fold_cols_kernel, [(4, n, n)], [VMEM] * 3, total, send_e, send_o)
     return (grad.reshape(2, 2, tile, tile), probe_grad)
 
 
@@ -522,7 +567,7 @@
         P("row", "col", None, None),
     )
     return jax.shard_map(
-        body,
+        whole,
         mesh=mesh,
         in_specs=placed,
         out_specs=(P(None, None, "row", "col"), P()),

time: 76.1 us -> 66.6 us (0.88)
  starting transfers between devices: 31.1 us -> 23.3 us
  waiting for transfers between devices: 25.9 us -> 21.1 us
  Pallas kernels: 12 us -> 15.1 us
  other arithmetic: 0.94 us -> 2.53 us
  local copies, waits for them, and re-layouts: 4.88 us -> 3.5 us
    ppermute x11 -> x8, starting transfers between devices: 18.4 us -> 10.8 us  [the longest x4 8.52 us: whole(): strips.append(lax.ppermute(packed[i], 'col', col_rounds[i % 2]))]
    unnamed x20 -> x0, local copies, waits for them, and re-layouts: 3.78 us -> none
    pallas_call x6 -> x7, Pallas kernels: 12 us -> 15.1 us  [call(): pl.pallas_call(kernel, out_shape=shapes, in_specs=in_specs, out_specs=[VM...]
    dynamic_update_slice x3, local copies, waits for them, and re-layouts: 0.02 us -> 2.75 us  [reduce_probe(): full = lax.dynamic_update_slice(full, part[None], (place ^ j, 0, 0))]
    ppermute x11 -> x8, waiting for transfers between devices: 11.2 us -> 8.5 us  [the longest x1 4.84 us: whole(): send_e = lax.ppermute(send_e, 'col', col_rounds[0])]
    ppermute x11, waiting for transfers between devices: 14.7 us -> 12.6 us  [swap(): return lax.ppermute(value, axis, [(i, i ^ distance) for i in range(count)])]
    dynamic_slice x1 -> x0, local copies, waits for them, and re-layouts: 1.03 us -> none  [body(): lax.dynamic_slice_in_dim(obj, jnp.where(last, tile - margin, 0), margin, 1)]
    another operation x2, other arithmetic: 0.87 us -> 1.82 us  [reduce_probe(): jnp.stack([jnp.where(even, full, other), jnp.where(even, other, full)])]
  transfers between devices with their start and end apart: 22 -> 19, of which waited for: 14 -> 11; matrix products, arithmetic and copies ran while one was open for 0% -> 6% of each run, Pallas kernels for 8% -> 12%
where the time goes in v1:
time: 66.6 us; the launch traced here: 66.3 us
  starting transfers between devices  23.3 us (35%)
  waiting for transfers between devices  21.1 us (32%)
  Pallas kernels  15.1 us (23%)
  local copies, waits for them, and re-layouts  3.5 us (5%)
  other arithmetic  2.53 us (4%)
  between operations  0.79 us (1%)
    pallas_call x7, Pallas kernels, call(): pl.pallas_call(kernel, out_shape=shapes, in_specs=in_specs, out_specs=[VM...  15.1 us
    ppermute x11, waiting for transfers between devices, swap(): return lax.ppermute(value, axis, [(i, i ^ distance) for i in range(count)])  12.6 us
    ppermute x11, starting transfers between devices, swap(): return lax.ppermute(value, axis, [(i, i ^ distance) for i in range(count)])  12.5 us
    ppermute x4, starting transfers between devices, whole(): strips.append(lax.ppermute(packed[i], 'col', col_rounds[i % 2]))  8.52 us
    ppermute x1, waiting for transfers between devices, whole(): send_e = lax.ppermute(send_e, 'col', col_rounds[0])  4.84 us
    dynamic_update_slice x3, local copies, waits for them, and re-layouts, reduce_probe(): full = lax.dynamic_update_slice(full, part[None], (place ^ j, 0, 0))  2.75 us
    ppermute x4, waiting for transfers between devices, whole(): strips.append(lax.ppermute(packed[i], 'col', col_rounds[i % 2]))  2.49 us
    another operation x2, other arithmetic, reduce_probe(): jnp.stack([jnp.where(even, full, other), jnp.where(even, other, full)])  1.82 us
  transfers between devices with their start and end apart: 19, of which 11 were waited for; matrix products, arithmetic and copies ran while one was open for 6% of the time, Pallas kernels for 12%

profile of v1, /device:TPU:0, one launch (start us, length us, event | category | flops | bytes accessed | tf_op | source)
XLA Modules:
  0.0 66.3 jit_solution(1407424673064400481)
XLA Ops:
  0.6 2.0 %shard_map.104 = (f32[4,64,256]{2,1,0:T(8,128)S(1)}, f32[4,256,256]{2,1,0:T(8,128)S(1)}, s32[1,2]{1,0:T(1,128)S(1)}) custom-call(f32[4,256,256]{2,1,0:T(8,128)} %bitcast.19, s32[1,2]{1,0:T(1,128)} %bitcast.22), custom_call_target="tpu_custom_call" | custom-call | tf_op jit(solution)/shard_map/pallas_call | solution.py:388
  3.2 1.2 %collective-permute-done.refs_0_.refs_1_ = f32[4,64,256]{2,1,0:T(8,128)S(1)} collective-permute-done((f32[4,64,256]{2,1,0:T(8,128)S(1)}, f32[4,64,256]{2,1,0:T(8,128)S(1)}, u32[]{:S(2)}, u32[]{:S(2)}) %collective-permute-start) | collective-permute-done | bytes 262176 | tf_op jit(solution)/shard_map/ppermute | solution.py:479
  4.6 2.9 %collective-permute-start.3 = (f32[320,128]{1,0:T(8,128)S(1)}, f32[320,128]{1,0:T(8,128)S(1)}, u32[]{:S(2)}, u32[]{:S(2)}) collective-permute-start(f32[320,128]{1,0:T(8,128)S(1)} %get-tuple-element.35), channel_id=1, source_target_pairs={{0,1},{2,3},{4,5},{6,7},{8,9},{10,11},{12,13},{14,15},{1,0},{3,2},... | collective-permute-start | bytes 491528 | tf_op jit(solution)/shard_map/ppermute | solution.py:490
  7.5 0.7 collective-permute-start.4
  8.1 4.3 %collective-permute-start.1 = (f32[320,128]{1,0:T(8,128)S(1)}, f32[320,128]{1,0:T(8,128)S(1)}, u32[]{:S(2)}, u32[]{:S(2)}) collective-permute-start(f32[320,128]{1,0:T(8,128)S(1)} %get-tuple-element.28), channel_id=1, source_target_pairs={{0,1},{2,3},{4,5},{6,7},{8,9},{10,11},{12,13},{14,15},{1,0},{3,2},... | collective-permute-start | bytes 491528 | tf_op jit(solution)/shard_map/ppermute | solution.py:490
  13.1 4.2 %shard_map.106 = (f32[256,256]{1,0:T(8,128)S(1)}, f32[256,256]{1,0:T(8,128)S(1)}, f32[256,256]{1,0:T(8,128)S(1)}, f32[2,256,256]{2,1,0:T(8,128)S(1)}, bf16[4,256...) custom-call(s32[1,2]{1,0:T(1,128)S(1)} %get-tuple-element.30.offs.refs_4_, ...), custom_call_target="tpu_custom_call" | custom-call | tf_op jit(solution)/shard_map/pallas_call | solution.py:388
  17.3 2.4 %shard_map.107 = (f32[2,256,256]{2,1,0:T(8,128)S(1)}, f32[2,256,256]{2,1,0:T(8,128)S(1)}) custom-call(f32[4,256,256]{2,1,0:T(8,128)S(1)} %get-tuple-element.26.obj.refs_0_, f32[4,64,256]{2,1,0:T(8,128)S(1)} %collective-permute-done.refs_0_.refs_1_, f32[320,128]{1,0:T(8,128)S(1)} %collective-permute-done.3.refs_2_, ...), custom_call_target="tpu_custom_call" | custom-call | tf_op jit(solution)/shard_map/pallas_call | solution.py:388
  19.8 2.5 %collective-permute-done.1.refs_2_ = f32[320,128]{1,0:T(8,128)S(1)} collective-permute-done((f32[320,128]{1,0:T(8,128)S(1)}, f32[320,128]{1,0:T(8,128)S(1)}, u32[]{:S(2)}, u32[]{:S(2)}) %collective-permute-start.1) | collective-permute-done | bytes 163872 | tf_op jit(solution)/shard_map/ppermute | solution.py:490
  22.2 4.9 %shard_map.108 = (f32[256,256]{1,0:T(8,128)S(1)}, f32[256,256]{1,0:T(8,128)S(1)}, f32[4,256,256]{2,1,0:T(8,128)S(1)}, f32[4,256,128]{2,1,0:T(8,128)S(1)}, f32[4,64,384]{2,1,0:T(8,128)S(1)}) custom-call(f32[4,256,256]{2,1,0:T(8,128)S(1)} %get-tuple-element.26.obj.refs_0_, f32[4,64,256]{2,1,0:T(8,128)S(1)} %collective-permute-done.refs_0_.refs_1_, ...), custom_call_target="tpu_custom_call" | custom-call | tf_op jit(solution)/shard_map/pallas_call | solution.py:388
  27.3 1.5 %collective-permute-done.8 = f32[256,256]{1,0:T(8,128)S(1)} collective-permute-done((f32[256,256]{1,0:T(8,128)S(1)}, f32[256,256]{1,0:T(8,128)S(1)}, u32[]{:S(2)}, u32[]{:S(2)}) %collective-permute-start.8) | collective-permute-done | bytes 262176 | tf_op jit(solution)/shard_map/ppermute | solution.py:411
  28.8 2.6 %collective-permute-start.10 = (f32[64,256]{1,0:T(8,128)S(1)}, f32[64,256]{1,0:T(8,128)S(1)}, u32[]{:S(2)}, u32[]{:S(2)}) collective-permute-start(f32[64,256]{1,0:T(8,128)S(1)} %get-tuple-element.56), channel_id=1, source_target_pairs={{0,2},{1,3},{2,0},{3,1},{4,6},{5,7},{6,4},{7,5},{8,10},{9,11},{10,... | collective-permute-start | bytes 196616 | tf_op jit(solution)/shard_map/ppermute | solution.py:411
  31.4 1.9 %collective-permute-start.11 = (f32[64,256]{1,0:T(8,128)S(1)}, f32[64,256]{1,0:T(8,128)S(1)}, u32[]{:S(2)}, u32[]{:S(2)}) collective-permute-start(f32[64,256]{1,0:T(8,128)S(1)} %get-tuple-element.55), channel_id=1, source_target_pairs={{0,3},{1,2},{2,1},{3,0},{4,7},{5,6},{6,5},{7,4},{8,11},{9,10},{10,... | collective-permute-start | bytes 196616 | tf_op jit(solution)/shard_map/ppermute | solution.py:411
  33.3 1.3 %collective-permute-done.10 = f32[64,256]{1,0:T(8,128)S(1)} collective-permute-done((f32[64,256]{1,0:T(8,128)S(1)}, f32[64,256]{1,0:T(8,128)S(1)}, u32[]{:S(2)}, u32[]{:S(2)}) %collective-permute-start.10) | collective-permute-done | bytes 65568 | tf_op jit(solution)/shard_map/ppermute | solution.py:411
  34.6 2.2 %collective-permute-done.11 = f32[64,256]{1,0:T(8,128)S(1)} collective-permute-done((f32[64,256]{1,0:T(8,128)S(1)}, f32[64,256]{1,0:T(8,128)S(1)}, u32[]{:S(2)}, u32[]{:S(2)}) %collective-permute-start.11) | collective-permute-done | bytes 65568 | tf_op jit(solution)/shard_map/ppermute | solution.py:411
  36.8 0.7 %collective-permute-done.9 = f32[64,256]{1,0:T(8,128)S(1)} collective-permute-done((f32[64,256]{1,0:T(8,128)S(1)}, f32[64,256]{1,0:T(8,128)S(1)}, u32[]{:S(2)}, u32[]{:S(2)}) %collective-permute-start.9) | collective-permute-done | bytes 65568 | tf_op jit(solution)/shard_map/ppermute | solution.py:411
  37.6 1.6 %collective-permute-start.12 = (f32[64,256]{1,0:T(8,128)S(1)}, f32[64,256]{1,0:T(8,128)S(1)}, u32[]{:S(2)}, u32[]{:S(2)}) collective-permute-start(f32[64,256]{1,0:T(8,128)S(1)} %add_add_fusion.1), channel_id=1, source_target_pairs={{0,4},{1,5},{2,6},{3,7},{4,0},{5,1},{6,2},{7,3},{8,12},{9,13},{10,... | collective-permute-start | bytes 196616 | tf_op jit(solution)/shard_map/ppermute | solution.py:411
  39.2 2.6 %collective-permute-start.13 = (f32[64,256]{1,0:T(8,128)S(1)}, f32[64,256]{1,0:T(8,128)S(1)}, u32[]{:S(2)}, u32[]{:S(2)}) collective-permute-start(f32[64,256]{1,0:T(8,128)S(1)} %add_add_fusion.1), channel_id=1, source_target_pairs={{0,8},{1,9},{2,10},{3,11},{4,12},{5,13},{6,14},{7,15},{8,0},{9,1},... | collective-permute-start | bytes 196616 | tf_op jit(solution)/shard_map/ppermute | solution.py:411
  42.5 3.3 %collective-permute-done.13 = f32[64,256]{1,0:T(8,128)S(1)} collective-permute-done((f32[64,256]{1,0:T(8,128)S(1)}, f32[64,256]{1,0:T(8,128)S(1)}, u32[]{:S(2)}, u32[]{:S(2)}) %collective-permute-start.13) | collective-permute-done | bytes 65568 | tf_op jit(solution)/shard_map/ppermute | solution.py:411
  45.8 2.1 %collective-permute-done.14 = f32[64,256]{1,0:T(8,128)S(1)} collective-permute-done((f32[64,256]{1,0:T(8,128)S(1)}, f32[64,256]{1,0:T(8,128)S(1)}, u32[]{:S(2)}, u32[]{:S(2)}) %collective-permute-start.14) | collective-permute-done | bytes 65568 | tf_op jit(solution)/shard_map/ppermute | solution.py:411
  47.9 0.7 %broadcast_in_dim.15 = f32[4,64,256]{2,1,0:T(8,128)} broadcast(f32[]{:T(128)} %constant.43.clone.1), dimensions={} | broadcast | bytes 262148 | tf_op jit(solution)/shard_map/broadcast_in_dim | solution.py:451
  48.6 0.7 %bitcast_dynamic-update-slice_fusion.3 = (f32[4,64,256]{2,1,0:T(8,128)}, f32[64,256]{1,0:T(8,128)}) fusion(f32[4,64,256]{2,1,0:T(8,128)} %broadcast_in_dim.15, s32[]{:T(128)S(6)} %select_n.54, f32[64,256]{1,0:T(8,128)S(1)} %collective-permute-done.13, f32[64,256]{1,0:T(8,128)S(1)} %collective-permute-done.14, f32[64,256]{1,0:T(8,128)S(1)} %add_add_fusion.1, ...), kind=kLoop, calls=%fused_computation.6 | loop fusion | flops 49152 | bytes 393220 | tf_op jit(solution)/shard_map/dynamic_update_slice | solution.py:454
  49.3 1.0 %collective-permute-start.15 = (f32[64,256]{1,0:T(8,128)}, f32[64,256]{1,0:T(8,128)}, u32[]{:S(2)}, u32[]{:S(2)}) collective-permute-start(f32[64,256]{1,0:T(8,128)} %get-tuple-element.51), channel_id=1, source_target_pairs={{0,1},{1,0},{2,3},{3,2},{4,5},{5,4},{6,7},{7,6},{8,9},{9,8},{10,11... | collective-permute-start | bytes 196616 | tf_op jit(solution)/shard_map/ppermute | solution.py:411
  50.3 0.8 %collective-permute-start.16 = (f32[64,256]{1,0:T(8,128)}, f32[64,256]{1,0:T(8,128)S(1)}, u32[]{:S(2)}, u32[]{:S(2)}) collective-permute-start(f32[64,256]{1,0:T(8,128)} %get-tuple-element.51), channel_id=1, source_target_pairs={{0,2},{1,3},{2,0},{3,1},{4,6},{5,7},{6,4},{7,5},{8,10},{9,11},{10,... | collective-permute-start | bytes 196616 | tf_op jit(solution)/shard_map/ppermute | solution.py:411
  51.0 1.7 %collective-permute-start.17 = (f32[64,256]{1,0:T(8,128)}, f32[64,256]{1,0:T(8,128)S(1)}, u32[]{:S(2)}, u32[]{:S(2)}) collective-permute-start(f32[64,256]{1,0:T(8,128)} %get-tuple-element.51), channel_id=1, source_target_pairs={{0,3},{1,2},{2,1},{3,0},{4,7},{5,6},{6,5},{7,4},{8,11},{9,10},{10,... | collective-permute-start | bytes 196616 | tf_op jit(solution)/shard_map/ppermute | solution.py:411
  52.9 1.1 %collective-permute-start.6 = (f32[2,256,128]{2,1,0:T(8,128)S(1)}, f32[2,256,128]{2,1,0:T(8,128)S(1)}, u32[]{:S(2)}, u32[]{:S(2)}) collective-permute-start(f32[2,256,128]{2,1,0:T(8,128)S(1)} %get-tuple-element.46), channel_id=1, source_target_pairs={{0,1},{2,3},{4,5},{6,7},{8,9},{10,11},{12,13},{14,15},{1,0},{3,2},... | collective-permute-start | bytes 786440 | tf_op jit(solution)/shard_map/ppermute | solution.py:555
  54.0 0.7 %collective-permute-start.7 = (f32[2,256,128]{2,1,0:T(8,128)S(1)}, f32[2,256,128]{2,1,0:T(8,128)S(1)}, u32[]{:S(2)}, u32[]{:S(2)}) collective-permute-start(f32[2,256,128]{2,1,0:T(8,128)S(1)} %get-tuple-element.47), channel_id=1, source_target_pairs={{1,2},{3,4},{5,6},{7,8},{9,10},{11,12},{13,14},{2,1},{4,3},{6,5},{... | collective-permute-start | bytes 786440 | tf_op jit(solution)/shard_map/ppermute | solution.py:556
  54.7 1.5 %bitcast_dynamic-update-slice_fusion.2 = f32[4,64,256]{2,1,0:T(8,128)} fusion(f32[4,64,256]{2,1,0:T(8,128)} %get-tuple-element.50, s32[]{:T(128)S(6)} %select_n.55, f32[64,256]{1,0:T(8,128)} %collective-permute-done.15), kind=kLoop, calls=%fused_computation.5 | loop fusion | bytes 131076 | tf_op jit(solution)/shard_map/dynamic_update_slice | solution.py:454
  56.8 1.0 %collective-permute-done.17 = f32[64,256]{1,0:T(8,128)S(1)} collective-permute-done((f32[64,256]{1,0:T(8,128)}, f32[64,256]{1,0:T(8,128)S(1)}, u32[]{:S(2)}, u32[]{:S(2)}) %collective-permute-start.17) | collective-permute-done | bytes 65568 | tf_op jit(solution)/shard_map/ppermute | solution.py:411
  58.5 4.8 %collective-permute-done.6.e = f32[2,256,128]{2,1,0:T(8,128)S(1)} collective-permute-done((f32[2,256,128]{2,1,0:T(8,128)S(1)}, f32[2,256,128]{2,1,0:T(8,128)S(1)}, u32[]{:S(2)}, u32[]{:S(2)}) %collective-permute-start.6) | collective-permute-done | bytes 262176 | tf_op jit(solution)/shard_map/ppermute | solution.py:555
  63.3 1.2 %shard_map.110 = f32[4,256,256]{2,1,0:T(8,128)} custom-call(f32[4,256,256]{2,1,0:T(8,128)S(1)} %get-tuple-element.45.total, f32[2,256,128]{2,1,0:T(8,128)S(1)} %collective-permute-done.6.e, f32[2,256,128]{2,1,0:T(8,128)S(1)} %collective-permute-done.7.o), custom_call_target="tpu_custom_call" | custom-call | tf_op jit(solution)/shard_map/pallas_call | solution.py:388
  64.5 1.0 %select_bitcast_fusion.1 = (f32[1,256,256]{2,1,0:T(8,128)S(1)}, f32[1,256,256]{2,1,0:T(8,128)S(1)}) fusion(f32[256,256]{1,0:T(8,128)S(1)} %collective-permute-done.18, pred[]{:T(512)S(6)} %eq.6, f32[4,64,256]{2,1,0:T(8,128)} %bitcast_dynamic-update-slice_fusion), kind=kLoop, calls=%fused_computation.2 | loop fusion | flops 131072 | bytes 1048577 | tf_op jit(solution)/shard_map/stack | solution.py:458
  65.5 0.8 %pad_maximum_fusion = f32[2,256,256]{2,1,0:T(8,128)} fusion(f32[1,256,256]{2,1,0:T(8,128)S(1)} %get-tuple-element.53, f32[1,256,256]{2,1,0:T(8,128)S(1)} %get-tuple-element.52), kind=kLoop, calls=%fused_computation | loop fusion | flops 131072 | bytes 1048576 | tf_op jit(solution)/shard_map/stack | solution.py:458
  (23 shorter events, 3.8 us)
Async XLA Ops:
  2.6 1.7 %collective-permute-start = (f32[4,64,256]{2,1,0:T(8,128)S(1)}, f32[4,64,256]{2,1,0:T(8,128)S(1)}, u32[]{:S(2)}, u32[]{:S(2)}) collective-permute-start(f32[4,64,256]{2,1,0:T(8,128)S(1)} %get-tuple-element.27), channel_id=1, source_target_pairs={{0,16},{16,0},{1,17},{17,1},{2,18},{18,2},{3,19},{19,3},{4,20},{20... | collective-permute-start | bytes 786440 | tf_op jit(solution)/shard_map/ppermute | solution.py:479
  4.6 12.8 %collective-permute-start.3 = (f32[320,128]{1,0:T(8,128)S(1)}, f32[320,128]{1,0:T(8,128)S(1)}, u32[]{:S(2)}, u32[]{:S(2)}) collective-permute-start(f32[320,128]{1,0:T(8,128)S(1)} %get-tuple-element.35), channel_id=1, source_target_pairs={{0,1},{2,3},{4,5},{6,7},{8,9},{10,11},{12,13},{14,15},{1,0},{3,2},... | collective-permute-start | bytes 491528 | tf_op jit(solution)/shard_map/ppermute | solution.py:490
  7.5 9.9 %collective-permute-start.4 = (f32[320,128]{1,0:T(8,128)S(1)}, f32[320,128]{1,0:T(8,128)S(1)}, u32[]{:S(2)}, u32[]{:S(2)}) collective-permute-start(f32[320,128]{1,0:T(8,128)S(1)} %get-tuple-element.36), channel_id=1, source_target_pairs={{1,2},{3,4},{5,6},{7,8},{9,10},{11,12},{13,14},{2,1},{4,3},{6,5},{... | collective-permute-start | bytes 491528 | tf_op jit(solution)/shard_map/ppermute | solution.py:490
  8.1 14.1 %collective-permute-start.1 = (f32[320,128]{1,0:T(8,128)S(1)}, f32[320,128]{1,0:T(8,128)S(1)}, u32[]{:S(2)}, u32[]{:S(2)}) collective-permute-start(f32[320,128]{1,0:T(8,128)S(1)} %get-tuple-element.28), channel_id=1, source_target_pairs={{0,1},{2,3},{4,5},{6,7},{8,9},{10,11},{12,13},{14,15},{1,0},{3,2},... | collective-permute-start | bytes 491528 | tf_op jit(solution)/shard_map/ppermute | solution.py:490
  12.4 9.8 %collective-permute-start.2 = (f32[320,128]{1,0:T(8,128)S(1)}, f32[320,128]{1,0:T(8,128)S(1)}, u32[]{:S(2)}, u32[]{:S(2)}) collective-permute-start(f32[320,128]{1,0:T(8,128)S(1)} %get-tuple-element.29), channel_id=1, source_target_pairs={{1,2},{3,4},{5,6},{7,8},{9,10},{11,12},{13,14},{2,1},{4,3},{6,5},{... | collective-permute-start | bytes 491528 | tf_op jit(solution)/shard_map/ppermute | solution.py:490
  27.1 1.6 %collective-permute-start.8 = (f32[256,256]{1,0:T(8,128)S(1)}, f32[256,256]{1,0:T(8,128)S(1)}, u32[]{:S(2)}, u32[]{:S(2)}) collective-permute-start(f32[256,256]{1,0:T(8,128)S(1)} %get-tuple-element.49), channel_id=1, source_target_pairs={{0,16},{16,0},{1,17},{17,1},{2,18},{18,2},{3,19},{19,3},{4,20},{20... | collective-permute-start | bytes 786440 | tf_op jit(solution)/shard_map/ppermute | solution.py:411
  28.8 5.8 %collective-permute-start.10 = (f32[64,256]{1,0:T(8,128)S(1)}, f32[64,256]{1,0:T(8,128)S(1)}, u32[]{:S(2)}, u32[]{:S(2)}) collective-permute-start(f32[64,256]{1,0:T(8,128)S(1)} %get-tuple-element.56), channel_id=1, source_target_pairs={{0,2},{1,3},{2,0},{3,1},{4,6},{5,7},{6,4},{7,5},{8,10},{9,11},{10,... | collective-permute-start | bytes 196616 | tf_op jit(solution)/shard_map/ppermute | solution.py:411
  31.4 5.5 %collective-permute-start.11 = (f32[64,256]{1,0:T(8,128)S(1)}, f32[64,256]{1,0:T(8,128)S(1)}, u32[]{:S(2)}, u32[]{:S(2)}) collective-permute-start(f32[64,256]{1,0:T(8,128)S(1)} %get-tuple-element.55), channel_id=1, source_target_pairs={{0,3},{1,2},{2,1},{3,0},{4,7},{5,6},{6,5},{7,4},{8,11},{9,10},{10,... | collective-permute-start | bytes 196616 | tf_op jit(solution)/shard_map/ppermute | solution.py:411
  33.3 4.3 %collective-permute-start.9 = (f32[64,256]{1,0:T(8,128)S(1)}, f32[64,256]{1,0:T(8,128)S(1)}, u32[]{:S(2)}, u32[]{:S(2)}) collective-permute-start(f32[64,256]{1,0:T(8,128)S(1)} %get-tuple-element.54), channel_id=1, source_target_pairs={{0,1},{1,0},{2,3},{3,2},{4,5},{5,4},{6,7},{7,6},{8,9},{9,8},{10,11... | collective-permute-start | bytes 196616 | tf_op jit(solution)/shard_map/ppermute | solution.py:411
  33.3 19.5 %collective-permute-start.5 = (f32[4,64,384]{2,1,0:T(8,128)S(1)}, f32[4,64,384]{2,1,0:T(8,128)S(1)}, u32[]{:S(2)}, u32[]{:S(2)}) collective-permute-start(f32[4,64,384]{2,1,0:T(8,128)S(1)} %get-tuple-element.44), channel_id=1, source_target_pairs={{0,16},{16,0},{1,17},{17,1},{2,18},{18,2},{3,19},{19,3},{4,20},{20... | collective-permute-start | bytes 1179656 | tf_op jit(solution)/shard_map/ppermute | solution.py:546
  37.6 4.9 %collective-permute-start.12 = (f32[64,256]{1,0:T(8,128)S(1)}, f32[64,256]{1,0:T(8,128)S(1)}, u32[]{:S(2)}, u32[]{:S(2)}) collective-permute-start(f32[64,256]{1,0:T(8,128)S(1)} %add_add_fusion.1), channel_id=1, source_target_pairs={{0,4},{1,5},{2,6},{3,7},{4,0},{5,1},{6,2},{7,3},{8,12},{9,13},{10,... | collective-permute-start | bytes 196616 | tf_op jit(solution)/shard_map/ppermute | solution.py:411
  39.2 6.6 %collective-permute-start.13 = (f32[64,256]{1,0:T(8,128)S(1)}, f32[64,256]{1,0:T(8,128)S(1)}, u32[]{:S(2)}, u32[]{:S(2)}) collective-permute-start(f32[64,256]{1,0:T(8,128)S(1)} %add_add_fusion.1), channel_id=1, source_target_pairs={{0,8},{1,9},{2,10},{3,11},{4,12},{5,13},{6,14},{7,15},{8,0},{9,1},... | collective-permute-start | bytes 196616 | tf_op jit(solution)/shard_map/ppermute | solution.py:411
  41.8 6.1 %collective-permute-start.14 = (f32[64,256]{1,0:T(8,128)S(1)}, f32[64,256]{1,0:T(8,128)S(1)}, u32[]{:S(2)}, u32[]{:S(2)}) collective-permute-start(f32[64,256]{1,0:T(8,128)S(1)} %add_add_fusion.1), channel_id=1, source_target_pairs={{0,12},{1,13},{2,14},{3,15},{4,8},{5,9},{6,10},{7,11},{8,4},{9,5},... | collective-permute-start | bytes 196616 | tf_op jit(solution)/shard_map/ppermute | solution.py:411
  49.3 5.4 %collective-permute-start.15 = (f32[64,256]{1,0:T(8,128)}, f32[64,256]{1,0:T(8,128)}, u32[]{:S(2)}, u32[]{:S(2)}) collective-permute-start(f32[64,256]{1,0:T(8,128)} %get-tuple-element.51), channel_id=1, source_target_pairs={{0,1},{1,0},{2,3},{3,2},{4,5},{5,4},{6,7},{7,6},{8,9},{9,8},{10,11... | collective-permute-start | bytes 196616 | tf_op jit(solution)/shard_map/ppermute | solution.py:411
  50.3 5.9 %collective-permute-start.16 = (f32[64,256]{1,0:T(8,128)}, f32[64,256]{1,0:T(8,128)S(1)}, u32[]{:S(2)}, u32[]{:S(2)}) collective-permute-start(f32[64,256]{1,0:T(8,128)} %get-tuple-element.51), channel_id=1, source_target_pairs={{0,2},{1,3},{2,0},{3,1},{4,6},{5,7},{6,4},{7,5},{8,10},{9,11},{10,... | collective-permute-start | bytes 196616 | tf_op jit(solution)/shard_map/ppermute | solution.py:411
  51.0 6.8 %collective-permute-start.17 = (f32[64,256]{1,0:T(8,128)}, f32[64,256]{1,0:T(8,128)S(1)}, u32[]{:S(2)}, u32[]{:S(2)}) collective-permute-start(f32[64,256]{1,0:T(8,128)} %get-tuple-element.51), channel_id=1, source_target_pairs={{0,3},{1,2},{2,1},{3,0},{4,7},{5,6},{6,5},{7,4},{8,11},{9,10},{10,... | collective-permute-start | bytes 196616 | tf_op jit(solution)/shard_map/ppermute | solution.py:411
  52.9 10.4 %collective-permute-start.6 = (f32[2,256,128]{2,1,0:T(8,128)S(1)}, f32[2,256,128]{2,1,0:T(8,128)S(1)}, u32[]{:S(2)}, u32[]{:S(2)}) collective-permute-start(f32[2,256,128]{2,1,0:T(8,128)S(1)} %get-tuple-element.46), channel_id=1, source_target_pairs={{0,1},{2,3},{4,5},{6,7},{8,9},{10,11},{12,13},{14,15},{1,0},{3,2},... | collective-permute-start | bytes 786440 | tf_op jit(solution)/shard_map/ppermute | solution.py:555
  54.0 9.3 %collective-permute-start.7 = (f32[2,256,128]{2,1,0:T(8,128)S(1)}, f32[2,256,128]{2,1,0:T(8,128)S(1)}, u32[]{:S(2)}, u32[]{:S(2)}) collective-permute-start(f32[2,256,128]{2,1,0:T(8,128)S(1)} %get-tuple-element.47), channel_id=1, source_target_pairs={{1,2},{3,4},{5,6},{7,8},{9,10},{11,12},{13,14},{2,1},{4,3},{6,5},{... | collective-permute-start | bytes 786440 | tf_op jit(solution)/shard_map/ppermute | solution.py:556
  58.5 6.1 %collective-permute-start.18 = (f32[256,256]{1,0:T(8,128)}, f32[256,256]{1,0:T(8,128)S(1)}, u32[]{:S(2)}, u32[]{:S(2)}) collective-permute-start(f32[256,256]{1,0:T(8,128)} %bitcast.8), channel_id=1, source_target_pairs={{0,16},{16,0},{1,17},{17,1},{2,18},{18,2},{3,19},{19,3},{4,20},{20... | collective-permute-start | bytes 786440 | tf_op jit(solution)/shard_map/ppermute | solution.py:411

commit v2 on v1

--- a/solution.py
+++ b/solution.py
@@ -123,24 +123,31 @@
     return low, high
 
 
-def load_kernel(n_row, margin, obj_hbm, offs_hbm, *refs):
-    strips, (obj, offs, sems) = refs[:n_row], refs[n_row:]
+def copy_all(sources, places, sems):
+    copies = [
+        pltpu.make_async_copy(a, b, sems.at[i]) for i, (a, b) in enumerate(zip(sources, places))
+    ]
+    for copy in copies:
+        copy.start()
+    return copies
+
+
+def strips_kernel(margin, obj, offs_hbm, *refs):
+    offs, strips, sems = refs[0], refs[1:-1], refs[-1]
     n = obj.shape[1]
     even = lax.axis_index("row") % 2 == 0
-    copies = []
-    for which, strip in enumerate(strips):
+    sources = [offs_hbm]
+    for which in range(len(strips)):
         last = even if which == 0 else jnp.logical_not(even)
         start = pl.multiple_of(jnp.where(last, n - margin, 0), 8)
-        copies.append(
-            pltpu.make_async_copy(
-                obj_hbm.at[:, pl.ds(start, margin), :], strip, sems.at[which + 1]
-            )
-        )
-    copies.append(pltpu.make_async_copy(obj_hbm, obj, sems.at[0]))
-    copies.append(pltpu.make_async_copy(offs_hbm, offs, sems.at[n_row + 1]))
-    for copy in copies:
-        copy.start()
-    for copy in copies:
+        sources.append(obj.at[:, pl.ds(start, margin), :])
+    for copy in copy_all(sources, [offs, *strips], sems):
+        copy.wait()
+
+
+def load_kernel(*refs):
+    half = len(refs) // 2
+    for copy in copy_all(refs[:half], refs[half:-1], refs[-1]):
         copy.wait()
 
 
@@ -162,41 +169,33 @@
     return pltpu.roll(x, shift, axis=axis)
 
 
-def prep_kernel(margin, offs, *refs):
-    hbm, outs, scratch, sems = refs[:7], refs[7:14], refs[14:18], refs[18]
-    kr, ki, am, pr = outs[:4]
-    phase, amps, probe, order = scratch
+def reorder(x, order):
+    def thirds(y):
+        a = y.astype(BF16)
+        return (a,) + split(y - a.astype(F32))
+
+    a, b, c = thirds(x)
+    a, b, c = thirds(dot(order[0], a) + (dot(order[0], b) + dot(order[0], c)))
+    return dot(a, order[1]) + (dot(b, order[1]) + dot(c, order[1]))
+
+
+def prep_kernel(margin, phase, probe, order, offs, amps_hbm, mats_hbm, twl_hbm, twr_hbm, *refs):
+    kr, ki, pr, amps, mats, twl, twr, sems = refs
     n = phase.shape[0]
-    places = list(scratch) + list(outs[4:])
-    copies = [pltpu.make_async_copy(a, b, sems.at[i]) for i, (a, b) in enumerate(zip(hbm, places))]
-    for copy in copies:
-        copy.start()
-
-    def thirds(x):
-        a = x.astype(BF16)
-        rest = x - a.astype(F32)
-        return (a,) + split(rest)
-
-    def reorder(ref):
-        a, b, c = thirds(ref[...])
-        rows = dot(order[0], a) + (dot(order[0], b) + dot(order[0], c))
-        a, b, c = thirds(rows)
-        return dot(a, order[1]) + (dot(b, order[1]) + dot(c, order[1]))
-
-    copies[0].wait()
-    copies[3].wait()
-    angle = reorder(phase)
+    copies = copy_all((mats_hbm, twl_hbm, twr_hbm, amps_hbm), (mats, twl, twr, amps), sems)
+    angle = reorder(phase[...], order)
     kr[...] = jnp.cos(angle)
     ki[...] = jnp.sin(angle)
-    copies[1].wait()
-    am[...] = reorder(amps)
     sy = (offs[0, 0] - margin + n) % n
     sx = (offs[0, 1] - margin + n) % n
-    copies[2].wait()
     for i in range(2):
         pr[i] = dyn_roll(dyn_roll(probe[i], sy, 0), sx, 1)
-    for copy in copies[4:]:
+    for copy in copies:
         copy.wait()
+
+
+def reorder_kernel(x, order, after, out):
+    out[...] = reorder(x[...], order)
 
 
 def merge_cols(own, low, high, ox, margin):
@@ -428,34 +427,57 @@
     return parts[0]
 
 
+def share_kernel(quad, keep, other, *parts):
+    place = lax.axis_index("col") % quad
+    chunk = keep.shape[0] // quad
+    for j, part in enumerate(parts):
+        rows = pl.ds(pl.multiple_of((place ^ j) * chunk, 8), chunk)
+        part[...] = keep[rows, :] + other[rows, :]
+
+
+def sum_kernel(*refs):
+    refs[-1][...] = pair_sum([r[...] for r in refs[:-1]])
+
+
+def join_kernel(*refs):
+    parts, full = refs[:-1], refs[-1]
+    quad, chunk = len(parts), parts[0].shape[0]
+    place = lax.axis_index("col") % quad
+    for j, part in enumerate(parts):
+        full[pl.ds(pl.multiple_of((place ^ j) * chunk, 8), chunk), :] = part[...]
+
+
+def both_kernel(full, other, out):
+    even = lax.axis_index("row") % 2 == 0
+    out[0] = jnp.where(even, full[...], other[...])
+    out[1] = jnp.where(even, other[...], full[...])
+
+
 def reduce_probe(keep, give):
     cols = lax.axis_size("col")
     n = keep.shape[0]
     other = swap(give, "row", 1)
-    mine = keep + other
     quad = min(4, cols)
-    place = lax.axis_index("col") % quad
     chunk = n // quad
-    parts = [
-        lax.dynamic_slice_in_dim(mine, (place ^ j) * chunk, chunk, 0) for j in range(quad)
-    ]
+    parts = call(
+        functools.partial(share_kernel, quad), [(chunk, n)] * quad, [VMEM] * 2, keep, other
+    )
     sums = [parts[0]]
     for j in range(1, quad):
         sums.append(swap(parts[j], "col", j))
-    total = pair_sum(sums)
+    (total,) = call(sum_kernel, [(chunk, n)], [VMEM] * quad, *sums)
     for axis, stride, width in stages("col", quad) + stages("row", 2):
         sums = [total]
         for j in range(1, width):
             sums.append(swap(total, axis, stride * j))
-        total = pair_sum(sums)
-    full = jnp.zeros((quad, chunk, n), F32)
-    for j in range(quad):
-        part = total if j == 0 else swap(total, "col", j)
-        full = lax.dynamic_update_slice(full, part[None], (place ^ j, 0, 0))
-    full = full.reshape(n, n)
+        (total,) = call(sum_kernel, [(chunk, n)], [VMEM] * width, *sums)
+    parts = [total]
+    for j in range(1, quad):
+        parts.append(swap(total, "col", j))
+    (full,) = call(join_kernel, [(n, n)], [VMEM] * quad, *parts)
     other = swap(full, "row", 1)
-    even = lax.axis_index("row") % 2 == 0
-    return jnp.stack([jnp.where(even, full, other), jnp.where(even, other, full)])
+    (grad,) = call(both_kernel, [(2, n, n)], [VMEM] * 2, full, other)
+    return grad
 
 
 def whole(object_field, probe, phase, amplitudes, offsets):
@@ -468,15 +490,24 @@
 
     row_rounds, col_rounds = edges("row"), edges("col")
     n_row = len(row_rounds)
-    *halos, obj, offs = call(
-        functools.partial(load_kernel, n_row, margin),
-        [(4, margin, n)] * n_row + [(4, n, n), jax.ShapeDtypeStruct((1, 2), jnp.int32)],
+    whole_tile = in_hbm(object_field.reshape(4, tile, tile))
+    offs, *halos = call(
+        functools.partial(strips_kernel, margin),
+        [jax.ShapeDtypeStruct((1, 2), jnp.int32)] + [(4, margin, n)] * n_row,
         [HBM, HBM],
-        in_hbm(object_field.reshape(4, tile, tile)),
+        whole_tile,
         in_hbm(offsets.reshape(1, 2)),
-        scratch=[pltpu.SemaphoreType.DMA((n_row + 2,))],
+        scratch=[pltpu.SemaphoreType.DMA((n_row + 1,))],
     )
     halos = [lax.ppermute(x, "row", pairs) for x, pairs in zip(halos, row_rounds)]
+    first = [whole_tile] + [in_hbm(x) for x in (phase, probe, order)]
+    obj, phase, probe, order = call(
+        load_kernel,
+        [jax.ShapeDtypeStruct(x.shape, x.dtype) for x in first],
+        [HBM] * len(first),
+        *first,
+        scratch=[pltpu.SemaphoreType.DMA((len(first),))],
+    )
     length = tile + margin * n_row
     packed = call(
         functools.partial(pack_kernel, n_row),
@@ -488,21 +519,18 @@
     strips = []
     for i in range(4):
         strips.append(lax.ppermute(packed[i], "col", col_rounds[i % 2]))
-    kr, ki, am, pr, mats, tw_left, tw_right = call(
+    later = [in_hbm(x) for x in (amplitudes.reshape(n, n), mats, tw_left, tw_right)]
+    kr, ki, pr, am, mats, tw_left, tw_right = call(
         functools.partial(prep_kernel, margin),
-        [(n, n), (n, n), (n, n), (2, n, n)]
-        + [jax.ShapeDtypeStruct(t.shape, t.dtype) for t in tables[:3]],
-        [SMEM] + [HBM] * 7,
+        [(n, n), (n, n), (2, n, n)]
+        + [jax.ShapeDtypeStruct(x.shape, x.dtype) for x in later],
+        [VMEM, VMEM, VMEM, SMEM] + [HBM] * 4,
+        phase,
+        probe,
+        order,
         offs,
-        *[in_hbm(x) for x in (phase, amplitudes.reshape(n, n), probe, order)],
-        *[in_hbm(x) for x in (mats, tw_left, tw_right)],
-        scratch=[
-            pltpu.VMEM((n, n), F32),
-            pltpu.VMEM((n, n), F32),
-            pltpu.VMEM((2, n, n), F32),
-            pltpu.VMEM((2, n, n), BF16),
-            pltpu.SemaphoreType.DMA((7,)),
-        ],
+        *later,
+        scratch=[pltpu.SemaphoreType.DMA((4,))],
     )
     w1, arrive = call(
         functools.partial(arrive_kernel, n_row, margin),
@@ -520,6 +548,7 @@
         tw_left,
         tw_right,
     )
+    (am,) = call(reorder_kernel, [(n, n)], [VMEM] * 3, am, order, arrive)
     keep, give, own, strip, *sends = call(
         functools.partial(back_kernel, n_row, margin),
         [(n, n), (n, n), (4, n, n), (4, n, h)] + [(4, margin, n + h)] * n_row,

time: 66.6 us -> 63.7 us (0.956)
  local copies, waits for them, and re-layouts: 3.5 us -> 0 us
  other arithmetic: 2.53 us -> 0 us
  waiting for transfers between devices: 21.1 us -> 22.7 us
  Pallas kernels: 15.1 us -> 15.8 us
    dynamic_update_slice x3 -> x0, local copies, waits for them, and re-layouts: 2.75 us -> none  [reduce_probe(): full = lax.dynamic_update_slice(full, part[None], (place ^ j, 0, 0))]
    ppermute x1, waiting for transfers between devices: 4.84 us -> 7.21 us  [whole(): send_e = lax.ppermute(send_e, 'col', col_rounds[0])]
    another operation x2 -> x0, other arithmetic: 1.82 us -> none  [reduce_probe(): jnp.stack([jnp.where(even, full, other), jnp.where(even, other, full)])]
    ppermute x4, waiting for transfers between devices: 2.49 us -> 4.2 us  [whole(): strips.append(lax.ppermute(packed[i], 'col', col_rounds[i % 2]))]
    ppermute x11, waiting for transfers between devices: 12.6 us -> 11.3 us  [swap(): return lax.ppermute(value, axis, [(i, i ^ distance) for i in range(count)])]
    ppermute x1, waiting for transfers between devices: 1.16 us -> 0.01 us  [whole(): lax.ppermute(x, 'row', pairs)]
    pallas_call x7 -> x14, Pallas kernels: 15.1 us -> 15.8 us  [call(): pl.pallas_call(kernel, out_shape=shapes, in_specs=in_specs, out_specs=[VM...]
    broadcast_in_dim x1 -> x0, local copies, waits for them, and re-layouts: 0.72 us -> none  [reduce_probe(): full = jnp.zeros((quad, chunk, n), F32)]
  transfers between devices with their start and end apart: 19 -> 19, of which waited for: 11 -> 9; matrix products, arithmetic and copies ran while one was open for 6% -> 0% of each run, Pallas kernels for 12% -> 13%
where the time goes in v2:
time: 63.7 us; the launch traced here: 63.3 us
  starting transfers between devices  23.9 us (38%)
  waiting for transfers between devices  22.7 us (36%)
  Pallas kernels  15.8 us (25%)
  between operations  0.78 us (1%)
    pallas_call x14, Pallas kernels, call(): pl.pallas_call(kernel, out_shape=shapes, in_specs=in_specs, out_specs=[VM...  15.8 us
    ppermute x11, starting transfers between devices, swap(): return lax.ppermute(value, axis, [(i, i ^ distance) for i in range(count)])  12.7 us
    ppermute x11, waiting for transfers between devices, swap(): return lax.ppermute(value, axis, [(i, i ^ distance) for i in range(count)])  11.3 us
    ppermute x4, starting transfers between devices, whole(): strips.append(lax.ppermute(packed[i], 'col', col_rounds[i % 2]))  8.16 us
    ppermute x1, waiting for transfers between devices, whole(): send_e = lax.ppermute(send_e, 'col', col_rounds[0])  7.21 us
    ppermute x4, waiting for transfers between devices, whole(): strips.append(lax.ppermute(packed[i], 'col', col_rounds[i % 2]))  4.2 us
    ppermute x1, starting transfers between devices, whole(): send_e = lax.ppermute(send_e, 'col', col_rounds[0])  1.35 us
  transfers between devices with their start and end apart: 19, of which 9 were waited for; matrix products, arithmetic and copies ran while one was open for 0% of the time, Pallas kernels for 13%

profile of v2, /device:TPU:0, one launch (start us, length us, event | category | flops | bytes accessed | tf_op | source)
XLA Modules:
  0.0 63.3 jit_solution(2603510145721484164)
XLA Ops:
  0.6 1.6 %shard_map.105 = (s32[1,2]{1,0:T(1,128)S(1)}, f32[4,64,256]{2,1,0:T(8,128)S(1)}) custom-call(f32[4,256,256]{2,1,0:T(8,128)} %bitcast.4, s32[1,2]{1,0:T(1,128)} %bitcast.8), custom_call_target="tpu_custom_call" | custom-call | tf_op jit(solution)/shard_map/pallas_call | solution.py:387
  2.2 0.6 collective-permute-start
  2.8 1.5 %shard_map.104 = (f32[4,256,256]{2,1,0:T(8,128)S(1)}, f32[256,256]{1,0:T(8,128)S(1)}, f32[2,256,256]{2,1,0:T(8,128)S(1)}, bf16[2,256,256]{2,1,0:T(8,128)(2,1)S(1)}) custom-call(f32[4,256,256]{2,1,0:T(8,128)} %bitcast.5, f32[256,256]{1,0:T(8,128)} %refs_1_.1, f32[2,256,256]{2,1,0:T(8,128)} %refs_2_.1, bf16[2,256,256]{2,1,0:T(8,128)(2,1)} %constant.11.clone.refs_3_), custom_call_target="tpu_custom_call" | custom-call | tf_op jit(solution)/shard_map/pallas_call | solution.py:387
  4.6 2.6 %collective-permute-start.3 = (f32[320,128]{1,0:T(8,128)S(1)}, f32[320,128]{1,0:T(8,128)S(1)}, u32[]{:S(2)}, u32[]{:S(2)}) collective-permute-start(f32[320,128]{1,0:T(8,128)S(1)} %get-tuple-element.45), channel_id=1, source_target_pairs={{0,1},{2,3},{4,5},{6,7},{8,9},{10,11},{12,13},{14,15},{1,0},{3,2},... | collective-permute-start | bytes 491528 | tf_op jit(solution)/shard_map/ppermute | solution.py:521
  7.1 0.7 %collective-permute-start.4 = (f32[320,128]{1,0:T(8,128)S(1)}, f32[320,128]{1,0:T(8,128)S(1)}, u32[]{:S(2)}, u32[]{:S(2)}) collective-permute-start(f32[320,128]{1,0:T(8,128)S(1)} %get-tuple-element.46), channel_id=1, source_target_pairs={{1,2},{3,4},{5,6},{7,8},{9,10},{11,12},{13,14},{2,1},{4,3},{6,5},{... | collective-permute-start | bytes 491528 | tf_op jit(solution)/shard_map/ppermute | solution.py:521
  7.8 4.3 %collective-permute-start.1 = (f32[320,128]{1,0:T(8,128)S(1)}, f32[320,128]{1,0:T(8,128)S(1)}, u32[]{:S(2)}, u32[]{:S(2)}) collective-permute-start(f32[320,128]{1,0:T(8,128)S(1)} %get-tuple-element.35), channel_id=1, source_target_pairs={{0,1},{2,3},{4,5},{6,7},{8,9},{10,11},{12,13},{14,15},{1,0},{3,2},... | collective-permute-start | bytes 491528 | tf_op jit(solution)/shard_map/ppermute | solution.py:521
  12.1 0.7 %collective-permute-start.2 = (f32[320,128]{1,0:T(8,128)S(1)}, f32[320,128]{1,0:T(8,128)S(1)}, u32[]{:S(2)}, u32[]{:S(2)}) collective-permute-start(f32[320,128]{1,0:T(8,128)S(1)} %get-tuple-element.36), channel_id=1, source_target_pairs={{1,2},{3,4},{5,6},{7,8},{9,10},{11,12},{13,14},{2,1},{4,3},{6,5},{... | collective-permute-start | bytes 491528 | tf_op jit(solution)/shard_map/ppermute | solution.py:521
  12.8 2.2 %shard_map.107 = (f32[256,256]{1,0:T(8,128)S(1)}, f32[256,256]{1,0:T(8,128)S(1)}, f32[2,256,256]{2,1,0:T(8,128)S(1)}, f32[256,256]{1,0:T(8,128)S(1)}, bf16[4,256...) custom-call(f32[256,256]{1,0:T(8,128)S(1)} %get-tuple-element.38.phase, ...), custom_call_target="tpu_custom_call" | custom-call | tf_op jit(solution)/shard_map/pallas_call | solution.py:387
  15.0 2.4 %shard_map.108 = (f32[2,256,256]{2,1,0:T(8,128)S(1)}, f32[2,256,256]{2,1,0:T(8,128)S(1)}) custom-call(f32[4,256,256]{2,1,0:T(8,128)S(1)} %get-tuple-element.33.obj.refs_0_, f32[4,64,256]{2,1,0:T(8,128)S(1)} %collective-permute-done.refs_0_.refs_1_, f32[320,128]{1,0:T(8,128)S(1)} %collective-permute-done.3.refs_2_, ...), custom_call_target="tpu_custom_call" | custom-call | tf_op jit(solution)/shard_map/pallas_call | solution.py:387
  17.4 0.6 shard_map.109.refs_8_
  18.1 4.2 %collective-permute-done.1.refs_2_ = f32[320,128]{1,0:T(8,128)S(1)} collective-permute-done((f32[320,128]{1,0:T(8,128)S(1)}, f32[320,128]{1,0:T(8,128)S(1)}, u32[]{:S(2)}, u32[]{:S(2)}) %collective-permute-start.1) | collective-permute-done | bytes 163872 | tf_op jit(solution)/shard_map/ppermute | solution.py:521
  22.3 4.9 %shard_map.110 = (f32[256,256]{1,0:T(8,128)S(1)}, f32[256,256]{1,0:T(8,128)S(1)}, f32[4,256,256]{2,1,0:T(8,128)S(1)}, f32[4,256,128]{2,1,0:T(8,128)S(1)}, f32[4,64,384]{2,1,0:T(8,128)S(1)}) custom-call(f32[4,256,256]{2,1,0:T(8,128)S(1)} %get-tuple-element.33.obj.refs_0_, f32[4,64,256]{2,1,0:T(8,128)S(1)} %collective-permute-done.refs_0_.refs_1_, ...), custom_call_target="tpu_custom_call" | custom-call | tf_op jit(solution)/shard_map/pallas_call | solution.py:387
  27.2 0.5 collective-permute-start.5
  27.7 1.0 %collective-permute-done.8.other = f32[256,256]{1,0:T(8,128)S(1)} collective-permute-done((f32[256,256]{1,0:T(8,128)S(1)}, f32[256,256]{1,0:T(8,128)S(1)}, u32[]{:S(2)}, u32[]{:S(2)}) %collective-permute-start.8) | collective-permute-done | bytes 262176 | tf_op jit(solution)/shard_map/ppermute | solution.py:410
  28.8 3.0 %collective-permute-start.9 = (f32[64,256]{1,0:T(8,128)S(1)}, f32[64,256]{1,0:T(8,128)S(1)}, u32[]{:S(2)}, u32[]{:S(2)}) collective-permute-start(f32[64,256]{1,0:T(8,128)S(1)} %get-tuple-element.61), channel_id=1, source_target_pairs={{0,1},{1,0},{2,3},{3,2},{4,5},{5,4},{6,7},{7,6},{8,9},{9,8},{10,11... | collective-permute-start | bytes 196616 | tf_op jit(solution)/shard_map/ppermute | solution.py:410
  31.8 1.5 %collective-permute-start.11 = (f32[64,256]{1,0:T(8,128)S(1)}, f32[64,256]{1,0:T(8,128)S(1)}, u32[]{:S(2)}, u32[]{:S(2)}) collective-permute-start(f32[64,256]{1,0:T(8,128)S(1)} %get-tuple-element.63), channel_id=1, source_target_pairs={{0,3},{1,2},{2,1},{3,0},{4,7},{5,6},{6,5},{7,4},{8,11},{9,10},{10,... | collective-permute-start | bytes 196616 | tf_op jit(solution)/shard_map/ppermute | solution.py:410
  33.4 0.9 %collective-permute-done.9.refs_1_ = f32[64,256]{1,0:T(8,128)S(1)} collective-permute-done((f32[64,256]{1,0:T(8,128)S(1)}, f32[64,256]{1,0:T(8,128)S(1)}, u32[]{:S(2)}, u32[]{:S(2)}) %collective-permute-start.9) | collective-permute-done | bytes 65568 | tf_op jit(solution)/shard_map/ppermute | solution.py:410
  34.2 3.1 %collective-permute-done.10.refs_2_ = f32[64,256]{1,0:T(8,128)S(1)} collective-permute-done((f32[64,256]{1,0:T(8,128)S(1)}, f32[64,256]{1,0:T(8,128)S(1)}, u32[]{:S(2)}, u32[]{:S(2)}) %collective-permute-start.10) | collective-permute-done | bytes 65568 | tf_op jit(solution)/shard_map/ppermute | solution.py:410
  37.3 3.7 %collective-permute-start.14 = (f32[64,256]{1,0:T(8,128)S(1)}, f32[64,256]{1,0:T(8,128)S(1)}, u32[]{:S(2)}, u32[]{:S(2)}) collective-permute-start(f32[64,256]{1,0:T(8,128)S(1)} %shard_map.114.refs_0_), channel_id=1, source_target_pairs={{0,12},{1,13},{2,14},{3,15},{4,8},{5,9},{6,10},{7,11},{8,4},{9,5},... | collective-permute-start | bytes 196616 | tf_op jit(solution)/shard_map/ppermute | solution.py:410
  41.0 0.8 %collective-permute-start.12 = (f32[64,256]{1,0:T(8,128)S(1)}, f32[64,256]{1,0:T(8,128)S(1)}, u32[]{:S(2)}, u32[]{:S(2)}) collective-permute-start(f32[64,256]{1,0:T(8,128)S(1)} %shard_map.114.refs_0_), channel_id=1, source_target_pairs={{0,4},{1,5},{2,6},{3,7},{4,0},{5,1},{6,2},{7,3},{8,12},{9,13},{10,... | collective-permute-start | bytes 196616 | tf_op jit(solution)/shard_map/ppermute | solution.py:410
  41.7 1.7 %collective-permute-done.14.refs_3_ = f32[64,256]{1,0:T(8,128)S(1)} collective-permute-done((f32[64,256]{1,0:T(8,128)S(1)}, f32[64,256]{1,0:T(8,128)S(1)}, u32[]{:S(2)}, u32[]{:S(2)}) %collective-permute-start.14) | collective-permute-done | bytes 65568 | tf_op jit(solution)/shard_map/ppermute | solution.py:410
  43.4 2.7 %collective-permute-done.13.refs_2_ = f32[64,256]{1,0:T(8,128)S(1)} collective-permute-done((f32[64,256]{1,0:T(8,128)S(1)}, f32[64,256]{1,0:T(8,128)S(1)}, u32[]{:S(2)}, u32[]{:S(2)}) %collective-permute-start.13) | collective-permute-done | bytes 65568 | tf_op jit(solution)/shard_map/ppermute | solution.py:410
  46.1 1.5 %collective-permute-start.17 = (f32[64,256]{1,0:T(8,128)S(1)}, f32[64,256]{1,0:T(8,128)S(1)}, u32[]{:S(2)}, u32[]{:S(2)}) collective-permute-start(f32[64,256]{1,0:T(8,128)S(1)} %shard_map.115.refs_0_), channel_id=1, source_target_pairs={{0,3},{1,2},{2,1},{3,0},{4,7},{5,6},{6,5},{7,4},{8,11},{9,10},{10,... | collective-permute-start | bytes 196616 | tf_op jit(solution)/shard_map/ppermute | solution.py:410
  47.6 1.3 %collective-permute-start.16 = (f32[64,256]{1,0:T(8,128)S(1)}, f32[64,256]{1,0:T(8,128)S(1)}, u32[]{:S(2)}, u32[]{:S(2)}) collective-permute-start(f32[64,256]{1,0:T(8,128)S(1)} %shard_map.115.refs_0_), channel_id=1, source_target_pairs={{0,2},{1,3},{2,0},{3,1},{4,6},{5,7},{6,4},{7,5},{8,10},{9,11},{10,... | collective-permute-start | bytes 196616 | tf_op jit(solution)/shard_map/ppermute | solution.py:410
  49.0 0.7 %collective-permute-start.15 = (f32[64,256]{1,0:T(8,128)S(1)}, f32[64,256]{1,0:T(8,128)S(1)}, u32[]{:S(2)}, u32[]{:S(2)}) collective-permute-start(f32[64,256]{1,0:T(8,128)S(1)} %shard_map.115.refs_0_), channel_id=1, source_target_pairs={{0,1},{1,0},{2,3},{3,2},{4,5},{5,4},{6,7},{7,6},{8,9},{9,8},{10,11... | collective-permute-start | bytes 196616 | tf_op jit(solution)/shard_map/ppermute | solution.py:410
  49.9 1.3 %collective-permute-start.6 = (f32[2,256,128]{2,1,0:T(8,128)S(1)}, f32[2,256,128]{2,1,0:T(8,128)S(1)}, u32[]{:S(2)}, u32[]{:S(2)}) collective-permute-start(f32[2,256,128]{2,1,0:T(8,128)S(1)} %get-tuple-element.56), channel_id=1, source_target_pairs={{0,1},{2,3},{4,5},{6,7},{8,9},{10,11},{12,13},{14,15},{1,0},{3,2},... | collective-permute-start | bytes 786440 | tf_op jit(solution)/shard_map/ppermute | solution.py:584
  51.2 0.7 %collective-permute-start.7 = (f32[2,256,128]{2,1,0:T(8,128)S(1)}, f32[2,256,128]{2,1,0:T(8,128)S(1)}, u32[]{:S(2)}, u32[]{:S(2)}) collective-permute-start(f32[2,256,128]{2,1,0:T(8,128)S(1)} %get-tuple-element.57), channel_id=1, source_target_pairs={{1,2},{3,4},{5,6},{7,8},{9,10},{11,12},{13,14},{2,1},{4,3},{6,5},{... | collective-permute-start | bytes 786440 | tf_op jit(solution)/shard_map/ppermute | solution.py:585
  51.9 0.3 collective-permute-done.16.refs_2_
  52.2 1.7 %collective-permute-done.15.refs_1_ = f32[64,256]{1,0:T(8,128)S(1)} collective-permute-done((f32[64,256]{1,0:T(8,128)S(1)}, f32[64,256]{1,0:T(8,128)S(1)}, u32[]{:S(2)}, u32[]{:S(2)}) %collective-permute-start.15) | collective-permute-done | bytes 65568 | tf_op jit(solution)/shard_map/ppermute | solution.py:410
  54.0 7.2 %collective-permute-done.6.e = f32[2,256,128]{2,1,0:T(8,128)S(1)} collective-permute-done((f32[2,256,128]{2,1,0:T(8,128)S(1)}, f32[2,256,128]{2,1,0:T(8,128)S(1)}, u32[]{:S(2)}, u32[]{:S(2)}) %collective-permute-start.6) | collective-permute-done | bytes 262176 | tf_op jit(solution)/shard_map/ppermute | solution.py:584
  61.2 1.2 %shard_map.112 = f32[4,256,256]{2,1,0:T(8,128)} custom-call(f32[4,256,256]{2,1,0:T(8,128)S(1)} %get-tuple-element.55.total, f32[2,256,128]{2,1,0:T(8,128)S(1)} %collective-permute-done.6.e, f32[2,256,128]{2,1,0:T(8,128)S(1)} %collective-permute-done.7.o), custom_call_target="tpu_custom_call" | custom-call | tf_op jit(solution)/shard_map/pallas_call | solution.py:387
  62.5 0.9 %shard_map.117 = f32[2,256,256]{2,1,0:T(8,128)} custom-call(f32[256,256]{1,0:T(8,128)S(1)} %shard_map.116.full, f32[256,256]{1,0:T(8,128)S(1)} %collective-permute-done.18.other), custom_call_target="tpu_custom_call" | custom-call | tf_op jit(solution)/shard_map/pallas_call | solution.py:387
  (20 shorter events, 0.7 us)
Async XLA Ops:
  2.2 2.1 %collective-permute-start = (f32[4,64,256]{2,1,0:T(8,128)S(1)}, f32[4,64,256]{2,1,0:T(8,128)S(1)}, u32[]{:S(2)}, u32[]{:S(2)}) collective-permute-start(f32[4,64,256]{2,1,0:T(8,128)S(1)} %get-tuple-element.34), channel_id=1, source_target_pairs={{0,16},{16,0},{1,17},{17,1},{2,18},{18,2},{3,19},{19,3},{4,20},{20... | collective-permute-start | bytes 786440 | tf_op jit(solution)/shard_map/ppermute | solution.py:502
  4.6 10.4 %collective-permute-start.3 = (f32[320,128]{1,0:T(8,128)S(1)}, f32[320,128]{1,0:T(8,128)S(1)}, u32[]{:S(2)}, u32[]{:S(2)}) collective-permute-start(f32[320,128]{1,0:T(8,128)S(1)} %get-tuple-element.45), channel_id=1, source_target_pairs={{0,1},{2,3},{4,5},{6,7},{8,9},{10,11},{12,13},{14,15},{1,0},{3,2},... | collective-permute-start | bytes 491528 | tf_op jit(solution)/shard_map/ppermute | solution.py:521
  7.1 7.9 %collective-permute-start.4 = (f32[320,128]{1,0:T(8,128)S(1)}, f32[320,128]{1,0:T(8,128)S(1)}, u32[]{:S(2)}, u32[]{:S(2)}) collective-permute-start(f32[320,128]{1,0:T(8,128)S(1)} %get-tuple-element.46), channel_id=1, source_target_pairs={{1,2},{3,4},{5,6},{7,8},{9,10},{11,12},{13,14},{2,1},{4,3},{6,5},{... | collective-permute-start | bytes 491528 | tf_op jit(solution)/shard_map/ppermute | solution.py:521
  7.8 14.5 %collective-permute-start.1 = (f32[320,128]{1,0:T(8,128)S(1)}, f32[320,128]{1,0:T(8,128)S(1)}, u32[]{:S(2)}, u32[]{:S(2)}) collective-permute-start(f32[320,128]{1,0:T(8,128)S(1)} %get-tuple-element.35), channel_id=1, source_target_pairs={{0,1},{2,3},{4,5},{6,7},{8,9},{10,11},{12,13},{14,15},{1,0},{3,2},... | collective-permute-start | bytes 491528 | tf_op jit(solution)/shard_map/ppermute | solution.py:521
  12.1 10.2 %collective-permute-start.2 = (f32[320,128]{1,0:T(8,128)S(1)}, f32[320,128]{1,0:T(8,128)S(1)}, u32[]{:S(2)}, u32[]{:S(2)}) collective-permute-start(f32[320,128]{1,0:T(8,128)S(1)} %get-tuple-element.36), channel_id=1, source_target_pairs={{1,2},{3,4},{5,6},{7,8},{9,10},{11,12},{13,14},{2,1},{4,3},{6,5},{... | collective-permute-start | bytes 491528 | tf_op jit(solution)/shard_map/ppermute | solution.py:521
  27.1 1.6 %collective-permute-start.8 = (f32[256,256]{1,0:T(8,128)S(1)}, f32[256,256]{1,0:T(8,128)S(1)}, u32[]{:S(2)}, u32[]{:S(2)}) collective-permute-start(f32[256,256]{1,0:T(8,128)S(1)} %get-tuple-element.59), channel_id=1, source_target_pairs={{0,16},{16,0},{1,17},{17,1},{2,18},{18,2},{3,19},{19,3},{4,20},{20... | collective-permute-start | bytes 786440 | tf_op jit(solution)/shard_map/ppermute | solution.py:410
  27.2 22.5 %collective-permute-start.5 = (f32[4,64,384]{2,1,0:T(8,128)S(1)}, f32[4,64,384]{2,1,0:T(8,128)S(1)}, u32[]{:S(2)}, u32[]{:S(2)}) collective-permute-start(f32[4,64,384]{2,1,0:T(8,128)S(1)} %get-tuple-element.54), channel_id=1, source_target_pairs={{0,16},{16,0},{1,17},{17,1},{2,18},{18,2},{3,19},{19,3},{4,20},{20... | collective-permute-start | bytes 1179656 | tf_op jit(solution)/shard_map/ppermute | solution.py:575
  28.8 5.4 %collective-permute-start.9 = (f32[64,256]{1,0:T(8,128)S(1)}, f32[64,256]{1,0:T(8,128)S(1)}, u32[]{:S(2)}, u32[]{:S(2)}) collective-permute-start(f32[64,256]{1,0:T(8,128)S(1)} %get-tuple-element.61), channel_id=1, source_target_pairs={{0,1},{1,0},{2,3},{3,2},{4,5},{5,4},{6,7},{7,6},{8,9},{9,8},{10,11... | collective-permute-start | bytes 196616 | tf_op jit(solution)/shard_map/ppermute | solution.py:410
  31.8 5.5 %collective-permute-start.10 = (f32[64,256]{1,0:T(8,128)S(1)}, f32[64,256]{1,0:T(8,128)S(1)}, u32[]{:S(2)}, u32[]{:S(2)}) collective-permute-start(f32[64,256]{1,0:T(8,128)S(1)} %get-tuple-element.62), channel_id=1, source_target_pairs={{0,2},{1,3},{2,0},{3,1},{4,6},{5,7},{6,4},{7,5},{8,10},{9,11},{10,... | collective-permute-start | bytes 196616 | tf_op jit(solution)/shard_map/ppermute | solution.py:410
  31.8 5.5 %collective-permute-start.11 = (f32[64,256]{1,0:T(8,128)S(1)}, f32[64,256]{1,0:T(8,128)S(1)}, u32[]{:S(2)}, u32[]{:S(2)}) collective-permute-start(f32[64,256]{1,0:T(8,128)S(1)} %get-tuple-element.63), channel_id=1, source_target_pairs={{0,3},{1,2},{2,1},{3,0},{4,7},{5,6},{6,5},{7,4},{8,11},{9,10},{10,... | collective-permute-start | bytes 196616 | tf_op jit(solution)/shard_map/ppermute | solution.py:410
  37.3 6.1 %collective-permute-start.14 = (f32[64,256]{1,0:T(8,128)S(1)}, f32[64,256]{1,0:T(8,128)S(1)}, u32[]{:S(2)}, u32[]{:S(2)}) collective-permute-start(f32[64,256]{1,0:T(8,128)S(1)} %shard_map.114.refs_0_), channel_id=1, source_target_pairs={{0,12},{1,13},{2,14},{3,15},{4,8},{5,9},{6,10},{7,11},{8,4},{9,5},... | collective-permute-start | bytes 196616 | tf_op jit(solution)/shard_map/ppermute | solution.py:410
  41.0 5.2 %collective-permute-start.13 = (f32[64,256]{1,0:T(8,128)S(1)}, f32[64,256]{1,0:T(8,128)S(1)}, u32[]{:S(2)}, u32[]{:S(2)}) collective-permute-start(f32[64,256]{1,0:T(8,128)S(1)} %shard_map.114.refs_0_), channel_id=1, source_target_pairs={{0,8},{1,9},{2,10},{3,11},{4,12},{5,13},{6,14},{7,15},{8,0},{9,1},... | collective-permute-start | bytes 196616 | tf_op jit(solution)/shard_map/ppermute | solution.py:410
  41.0 5.2 %collective-permute-start.12 = (f32[64,256]{1,0:T(8,128)S(1)}, f32[64,256]{1,0:T(8,128)S(1)}, u32[]{:S(2)}, u32[]{:S(2)}) collective-permute-start(f32[64,256]{1,0:T(8,128)S(1)} %shard_map.114.refs_0_), channel_id=1, source_target_pairs={{0,4},{1,5},{2,6},{3,7},{4,0},{5,1},{6,2},{7,3},{8,12},{9,13},{10,... | collective-permute-start | bytes 196616 | tf_op jit(solution)/shard_map/ppermute | solution.py:410
  46.1 5.8 %collective-permute-start.17 = (f32[64,256]{1,0:T(8,128)S(1)}, f32[64,256]{1,0:T(8,128)S(1)}, u32[]{:S(2)}, u32[]{:S(2)}) collective-permute-start(f32[64,256]{1,0:T(8,128)S(1)} %shard_map.115.refs_0_), channel_id=1, source_target_pairs={{0,3},{1,2},{2,1},{3,0},{4,7},{5,6},{6,5},{7,4},{8,11},{9,10},{10,... | collective-permute-start | bytes 196616 | tf_op jit(solution)/shard_map/ppermute | solution.py:410
  47.6 4.6 %collective-permute-start.16 = (f32[64,256]{1,0:T(8,128)S(1)}, f32[64,256]{1,0:T(8,128)S(1)}, u32[]{:S(2)}, u32[]{:S(2)}) collective-permute-start(f32[64,256]{1,0:T(8,128)S(1)} %shard_map.115.refs_0_), channel_id=1, source_target_pairs={{0,2},{1,3},{2,0},{3,1},{4,6},{5,7},{6,4},{7,5},{8,10},{9,11},{10,... | collective-permute-start | bytes 196616 | tf_op jit(solution)/shard_map/ppermute | solution.py:410
  49.0 5.0 %collective-permute-start.15 = (f32[64,256]{1,0:T(8,128)S(1)}, f32[64,256]{1,0:T(8,128)S(1)}, u32[]{:S(2)}, u32[]{:S(2)}) collective-permute-start(f32[64,256]{1,0:T(8,128)S(1)} %shard_map.115.refs_0_), channel_id=1, source_target_pairs={{0,1},{1,0},{2,3},{3,2},{4,5},{5,4},{6,7},{7,6},{8,9},{9,8},{10,11... | collective-permute-start | bytes 196616 | tf_op jit(solution)/shard_map/ppermute | solution.py:410
  49.9 11.3 %collective-permute-start.6 = (f32[2,256,128]{2,1,0:T(8,128)S(1)}, f32[2,256,128]{2,1,0:T(8,128)S(1)}, u32[]{:S(2)}, u32[]{:S(2)}) collective-permute-start(f32[2,256,128]{2,1,0:T(8,128)S(1)} %get-tuple-element.56), channel_id=1, source_target_pairs={{0,1},{2,3},{4,5},{6,7},{8,9},{10,11},{12,13},{14,15},{1,0},{3,2},... | collective-permute-start | bytes 786440 | tf_op jit(solution)/shard_map/ppermute | solution.py:584
  51.2 10.0 %collective-permute-start.7 = (f32[2,256,128]{2,1,0:T(8,128)S(1)}, f32[2,256,128]{2,1,0:T(8,128)S(1)}, u32[]{:S(2)}, u32[]{:S(2)}) collective-permute-start(f32[2,256,128]{2,1,0:T(8,128)S(1)} %get-tuple-element.57), channel_id=1, source_target_pairs={{1,2},{3,4},{5,6},{7,8},{9,10},{11,12},{13,14},{2,1},{4,3},{6,5},{... | collective-permute-start | bytes 786440 | tf_op jit(solution)/shard_map/ppermute | solution.py:585
  54.0 8.5 %collective-permute-start.18 = (f32[256,256]{1,0:T(8,128)S(1)}, f32[256,256]{1,0:T(8,128)S(1)}, u32[]{:S(2)}, u32[]{:S(2)}) collective-permute-start(f32[256,256]{1,0:T(8,128)S(1)} %shard_map.116.full), channel_id=1, source_target_pairs={{0,16},{16,0},{1,17},{17,1},{2,18},{18,2},{3,19},{19,3},{4,20},{20... | collective-permute-start | bytes 786440 | tf_op jit(solution)/shard_map/ppermute | solution.py:410

commit v3 on v2

--- a/solution.py
+++ b/solution.py
@@ -111,6 +111,10 @@
     return lax.broadcasted_iota(jnp.int32, shape, dim)
 
 
+def dyn_roll(x, shift, axis):
+    return pltpu.roll(x, shift, axis=axis)
+
+
 def half_roll(x):
     return pltpu.roll(x, x.shape[-1] // 2, axis=x.ndim - 1)
 
@@ -132,41 +136,34 @@
     return copies
 
 
-def strips_kernel(margin, obj, offs_hbm, *refs):
-    offs, strips, sems = refs[0], refs[1:-1], refs[-1]
+def row_start(which, n, margin):
+    even = lax.axis_index("row") % 2 == 0
+    last = even if which == 0 else jnp.logical_not(even)
+    return pl.multiple_of(jnp.where(last, n - margin, 0), 8)
+
+
+def pack_kernel(margin, obj_hbm, offs_hbm, obj, offs, *refs):
+    strips, rows, sems = refs[:4], refs[4:-1], refs[-1]
     n = obj.shape[1]
-    even = lax.axis_index("row") % 2 == 0
-    sources = [offs_hbm]
-    for which in range(len(strips)):
-        last = even if which == 0 else jnp.logical_not(even)
-        start = pl.multiple_of(jnp.where(last, n - margin, 0), 8)
-        sources.append(obj.at[:, pl.ds(start, margin), :])
-    for copy in copy_all(sources, [offs, *strips], sems):
-        copy.wait()
-
-
-def load_kernel(*refs):
-    half = len(refs) // 2
-    for copy in copy_all(refs[:half], refs[half:-1], refs[-1]):
-        copy.wait()
-
-
-def pack_kernel(n_row, obj, *refs):
-    halos, outs = refs[:n_row], refs[n_row:]
+    copies = copy_all(
+        (obj_hbm.at[0:2], obj_hbm.at[2:4], offs_hbm), (obj.at[0:2], obj.at[2:4], offs), sems
+    )
     even = lax.axis_index("col") % 2 == 0
     for s in range(2):
-        sources = [obj] + list(halos)
-        at = 0
-        for source in sources:
-            rows = source.shape[1]
-            low, high = pack_cols(source[2 * s], source[2 * s + 1])
-            outs[2 * s][at : at + rows] = jnp.where(even, high, low)
-            outs[2 * s + 1][at : at + rows] = jnp.where(even, low, high)
-            at += rows
-
-
-def dyn_roll(x, shift, axis):
-    return pltpu.roll(x, shift, axis=axis)
+        copies[s].wait()
+        low, high = pack_cols(obj[2 * s], obj[2 * s + 1])
+        strips[2 * s][...] = jnp.where(even, high, low)
+        strips[2 * s + 1][...] = jnp.where(even, low, high)
+    for which, out in enumerate(rows):
+        out[...] = obj[:, pl.ds(row_start(which, n, margin), margin), :]
+    copies[2].wait()
+
+
+def corner_kernel(margin, e, o, after, *outs):
+    for which, out in enumerate(outs):
+        rows = pl.ds(row_start(which, e.shape[0], margin), margin)
+        out[0] = e[rows, :]
+        out[1] = o[rows, :]
 
 
 def reorder(x, order):
@@ -179,19 +176,25 @@
     return dot(a, order[1]) + (dot(b, order[1]) + dot(c, order[1]))
 
 
-def prep_kernel(margin, phase, probe, order, offs, amps_hbm, mats_hbm, twl_hbm, twr_hbm, *refs):
-    kr, ki, pr, amps, mats, twl, twr, sems = refs
-    n = phase.shape[0]
-    copies = copy_all((mats_hbm, twl_hbm, twr_hbm, amps_hbm), (mats, twl, twr, amps), sems)
-    angle = reorder(phase[...], order)
+def prep_kernel(*refs):
+    hbm, (kr, ki), loaded = refs[:7], refs[7:9], refs[9:15]
+    phase, sems = refs[15:]
+    copies = copy_all(hbm, (phase,) + loaded, sems)
+    copies[0].wait()
+    copies[1].wait()
+    angle = reorder(phase[...], loaded[0])
     kr[...] = jnp.cos(angle)
     ki[...] = jnp.sin(angle)
+    for copy in copies[2:]:
+        copy.wait()
+
+
+def roll_kernel(margin, offs, probe, pr):
+    n = probe.shape[1]
     sy = (offs[0, 0] - margin + n) % n
     sx = (offs[0, 1] - margin + n) % n
     for i in range(2):
         pr[i] = dyn_roll(dyn_roll(probe[i], sy, 0), sx, 1)
-    for copy in copies:
-        copy.wait()
 
 
 def reorder_kernel(x, order, after, out):
@@ -220,19 +223,17 @@
     return out
 
 
-def window_of(obj, s, halos, strip_e, strip_o, offs, margin):
+def window_of(obj, s, halos, corners, strip_e, strip_o, offs, margin):
     n = obj.shape[1]
     oy, ox = offs[0, 0], offs[0, 1]
     col_even = lax.axis_index("col") % 2 == 0
     row_even = lax.axis_index("row") % 2 == 0
     blocks = []
-    at = 0
-    for source in [obj] + list(halos):
-        rows = source.shape[1]
-        e, o = strip_e[at : at + rows], strip_o[at : at + rows]
+    sides = [(strip_e, strip_o)] + [(c.at[0], c.at[1]) for c in corners]
+    for source, (e, o) in zip([obj] + list(halos), sides):
+        e, o = e[...], o[...]
         high, low = jnp.where(col_even, e, o), jnp.where(col_even, o, e)
         blocks.append(merge_cols([source[2 * s], source[2 * s + 1]], low, high, ox, margin))
-        at += rows
     row = iota((margin, n), 0)
     take_high = row < oy - margin
     take_low = row + n - margin >= oy + n - margin
@@ -259,12 +260,16 @@
     return out
 
 
+def unpack(n_row, refs):
+    return refs[0], refs[1 : 1 + n_row], refs[1 + n_row : 1 + 2 * n_row], refs[1 + 2 * n_row :]
+
+
 def arrive_kernel(n_row, margin, *refs):
-    obj, halos = refs[0], refs[1 : 1 + n_row]
-    e1, o1, offs, pr, kr, ki, mats, twl, twr, w1, arrive = refs[1 + n_row :]
+    obj, halos, corners, refs = unpack(n_row, refs)
+    e1, o1, offs, pr, kr, ki, mats, twl, twr, w1, arrive = refs
     n = obj.shape[1]
     dft = Dft(mats, twl[...], twr[...], n)
-    win = window_of(obj, 0, halos, e1, o1, offs, margin)
+    win = window_of(obj, 0, halos, corners, e1, o1, offs, margin)
     w1[0], w1[1] = win
     x = dft.forward(product([pr[0], pr[1]], win))
     x = dft.inverse(product([kr[...], ki[...]], x))
@@ -302,13 +307,13 @@
 
 
 def back_kernel(n_row, margin, *refs):
-    obj, halos = refs[0], refs[1 : 1 + n_row]
-    e2, o2, offs, pr, kr, ki, am, w1, arrive, mats, twl, twr = refs[1 + n_row : 13 + n_row]
-    outs = refs[13 + n_row :]
+    obj, halos, corners, refs = unpack(n_row, refs)
+    e2, o2, offs, pr, kr, ki, am, w1, arrive, mats, twl, twr = refs[:12]
+    outs = refs[12:]
     keep, give = outs[:2]
     n = obj.shape[1]
     dft = Dft(mats, twl[...], twr[...], n)
-    win = window_of(obj, 1, halos, e2, o2, offs, margin)
+    win = window_of(obj, 1, halos, corners, e2, o2, offs, margin)
     arr = [arrive[0], arrive[1]]
     far = dft.forward(product(arr, win))
     modulus = jnp.sqrt(far[0] * far[0] + far[1] * far[1] + EPS_AMP)
@@ -410,14 +415,17 @@
     return lax.ppermute(value, axis, [(i, i ^ distance) for i in range(count)])
 
 
-def stages(axis, start):
-    count = lax.axis_size(axis)
+def groups():
+    cols = [("col", 1 << b) for b in range(lax.axis_size("col").bit_length() - 1)]
+    rows = [("row", 1 << b) for b in range(1, lax.axis_size("row").bit_length() - 1)]
+    first, rest = cols[:2], cols[2:]
+    pairs = [first]
+    for bits in (rest, rows):
+        pairs += [bits[i : i + 2] for i in range(0, len(bits), 2)]
     out = []
-    stride = start
-    while stride < count:
-        width = min(4, count // stride)
-        out.append((axis, stride, width))
-        stride *= width
+    for pair in pairs:
+        axis, masks = pair[0][0], [m for _, m in pair]
+        out.append((axis, [0] + masks + ([sum(masks)] if len(masks) == 2 else [])))
     return out
 
 
@@ -427,8 +435,8 @@
     return parts[0]
 
 
-def share_kernel(quad, keep, other, *parts):
-    place = lax.axis_index("col") % quad
+def share_kernel(quad, stride, keep, other, *parts):
+    place = lax.axis_index("col") // stride % quad
     chunk = keep.shape[0] // quad
     for j, part in enumerate(parts):
         rows = pl.ds(pl.multiple_of((place ^ j) * chunk, 8), chunk)
@@ -439,10 +447,10 @@
     refs[-1][...] = pair_sum([r[...] for r in refs[:-1]])
 
 
-def join_kernel(*refs):
+def join_kernel(stride, *refs):
     parts, full = refs[:-1], refs[-1]
     quad, chunk = len(parts), parts[0].shape[0]
-    place = lax.axis_index("col") % quad
+    place = lax.axis_index("col") // stride % quad
     for j, part in enumerate(parts):
         full[pl.ds(pl.multiple_of((place ^ j) * chunk, 8), chunk), :] = part[...]
 
@@ -454,27 +462,33 @@
 
 
 def reduce_probe(keep, give):
-    cols = lax.axis_size("col")
     n = keep.shape[0]
+    (_, offsets), *rest = groups()
+    quad, stride = len(offsets), offsets[1]
+    chunk = n // quad
     other = swap(give, "row", 1)
-    quad = min(4, cols)
-    chunk = n // quad
     parts = call(
-        functools.partial(share_kernel, quad), [(chunk, n)] * quad, [VMEM] * 2, keep, other
+        functools.partial(share_kernel, quad, stride),
+        [(chunk, n)] * quad,
+        [VMEM] * 2,
+        keep,
+        other,
     )
     sums = [parts[0]]
     for j in range(1, quad):
-        sums.append(swap(parts[j], "col", j))
+        sums.append(swap(parts[j], "col", offsets[j]))
     (total,) = call(sum_kernel, [(chunk, n)], [VMEM] * quad, *sums)
-    for axis, stride, width in stages("col", quad) + stages("row", 2):
+    for axis, masks in rest:
         sums = [total]
-        for j in range(1, width):
-            sums.append(swap(total, axis, stride * j))
-        (total,) = call(sum_kernel, [(chunk, n)], [VMEM] * width, *sums)
+        for mask in masks[1:]:
+            sums.append(swap(total, axis, mask))
+        (total,) = call(sum_kernel, [(chunk, n)], [VMEM] * len(sums), *sums)
     parts = [total]
     for j in range(1, quad):
-        parts.append(swap(total, "col", j))
-    (full,) = call(join_kernel, [(n, n)], [VMEM] * quad, *parts)
+        parts.append(swap(total, "col", offsets[j]))
+    (full,) = call(
+        functools.partial(join_kernel, stride), [(n, n)], [VMEM] * quad, *parts
+    )
     other = swap(full, "row", 1)
     (grad,) = call(both_kernel, [(2, n, n)], [VMEM] * 2, full, other)
     return grad
@@ -490,54 +504,50 @@
 
     row_rounds, col_rounds = edges("row"), edges("col")
     n_row = len(row_rounds)
-    whole_tile = in_hbm(object_field.reshape(4, tile, tile))
-    offs, *halos = call(
-        functools.partial(strips_kernel, margin),
-        [jax.ShapeDtypeStruct((1, 2), jnp.int32)] + [(4, margin, n)] * n_row,
+    obj, offs, *packed = call(
+        functools.partial(pack_kernel, margin),
+        [(4, n, n), jax.ShapeDtypeStruct((1, 2), jnp.int32)]
+        + [(n, h)] * 4
+        + [(4, margin, n)] * n_row,
         [HBM, HBM],
-        whole_tile,
+        in_hbm(object_field.reshape(4, tile, tile)),
         in_hbm(offsets.reshape(1, 2)),
-        scratch=[pltpu.SemaphoreType.DMA((n_row + 1,))],
-    )
-    halos = [lax.ppermute(x, "row", pairs) for x, pairs in zip(halos, row_rounds)]
-    first = [whole_tile] + [in_hbm(x) for x in (phase, probe, order)]
-    obj, phase, probe, order = call(
-        load_kernel,
-        [jax.ShapeDtypeStruct(x.shape, x.dtype) for x in first],
-        [HBM] * len(first),
-        *first,
-        scratch=[pltpu.SemaphoreType.DMA((len(first),))],
-    )
-    length = tile + margin * n_row
-    packed = call(
-        functools.partial(pack_kernel, n_row),
-        [(length, h)] * 4,
-        [VMEM] * (1 + n_row),
-        obj,
-        *halos,
-    )
-    strips = []
+        scratch=[pltpu.SemaphoreType.DMA((3,))],
+    )
+    strips, halos, corners = [], [], [[], []]
     for i in range(4):
         strips.append(lax.ppermute(packed[i], "col", col_rounds[i % 2]))
-    later = [in_hbm(x) for x in (amplitudes.reshape(n, n), mats, tw_left, tw_right)]
-    kr, ki, pr, am, mats, tw_left, tw_right = call(
-        functools.partial(prep_kernel, margin),
-        [(n, n), (n, n), (2, n, n)]
-        + [jax.ShapeDtypeStruct(x.shape, x.dtype) for x in later],
-        [VMEM, VMEM, VMEM, SMEM] + [HBM] * 4,
-        phase,
-        probe,
-        order,
-        offs,
-        *later,
-        scratch=[pltpu.SemaphoreType.DMA((4,))],
-    )
+    for i, pairs in enumerate(row_rounds):
+        halos.append(lax.ppermute(packed[4 + i], "row", pairs))
+
+    def cut(s, after):
+        parts = call(
+            functools.partial(corner_kernel, margin),
+            [(2, margin, h)] * n_row,
+            [VMEM] * 3,
+            *strips[2 * s : 2 * s + 2],
+            after,
+        )
+        for i, pairs in enumerate(row_rounds):
+            corners[s].append(lax.ppermute(parts[i], "row", pairs))
+
+    loads = (phase, order, mats, tw_left, tw_right, probe, amplitudes.reshape(n, n))
+    kr, ki, order, mats, tw_left, tw_right, pr, am = call(
+        prep_kernel,
+        [(n, n), (n, n)] + [jax.ShapeDtypeStruct(x.shape, x.dtype) for x in loads[1:]],
+        [HBM] * len(loads),
+        *[in_hbm(x) for x in loads],
+        scratch=[pltpu.VMEM((n, n), F32), pltpu.SemaphoreType.DMA((len(loads),))],
+    )
+    cut(0, kr)
+    (pr,) = call(functools.partial(roll_kernel, margin), [(2, n, n)], [SMEM, VMEM], offs, pr)
     w1, arrive = call(
         functools.partial(arrive_kernel, n_row, margin),
         [(2, n, n), (2, n, n)],
-        [VMEM] * (1 + n_row) + [VMEM, VMEM, SMEM] + [VMEM] * 6,
+        [VMEM] * (3 + 2 * n_row) + [SMEM] + [VMEM] * 6,
         obj,
         *halos,
+        *corners[0],
         strips[0],
         strips[1],
         offs,
@@ -548,13 +558,15 @@
         tw_left,
         tw_right,
     )
+    cut(1, arrive)
     (am,) = call(reorder_kernel, [(n, n)], [VMEM] * 3, am, order, arrive)
     keep, give, own, strip, *sends = call(
         functools.partial(back_kernel, n_row, margin),
         [(n, n), (n, n), (4, n, n), (4, n, h)] + [(4, margin, n + h)] * n_row,
-        [VMEM] * (1 + n_row) + [VMEM, VMEM, SMEM] + [VMEM] * 9,
+        [VMEM] * (3 + 2 * n_row) + [SMEM] + [VMEM] * 9,
         obj,
         *halos,
+        *corners[1],
         strips[2],
         strips[3],
         offs,

time: 63.7 us -> 62.7 us (0.984)
  waiting for transfers between devices: 22.7 us -> 21.7 us
    ppermute x4, waiting for transfers between devices: 4.2 us -> 0.97 us  [whole(): strips.append(lax.ppermute(packed[i], 'col', col_rounds[i % 2]))]
    ppermute x1 -> x3, waiting for transfers between devices: 0.01 us -> 1.07 us  [the longest x2 1.06 us: cut(): corners[s].append(lax.ppermute(parts[i], 'row', pairs))]
    ppermute x1, waiting for transfers between devices: 7.21 us -> 8.06 us  [whole(): send_e = lax.ppermute(send_e, 'col', col_rounds[0])]
    pallas_call x14 -> x15, Pallas kernels: 15.8 us -> 15.6 us  [call(): pl.pallas_call(kernel, out_shape=shapes, in_specs=in_specs, out_specs=[VM...]
  transfers between devices with their start and end apart: 19 -> 21, of which waited for: 9 -> 14; matrix products, arithmetic and copies ran while one was open for 0% -> 0% of each run, Pallas kernels for 13% -> 13%
where the time goes in v3:
time: 62.7 us; the launch traced here: 62.3 us
  starting transfers between devices  24.2 us (39%)
  waiting for transfers between devices  21.7 us (35%)
  Pallas kernels  15.6 us (25%)
  between operations  0.78 us (1%)
    pallas_call x15, Pallas kernels, call(): pl.pallas_call(kernel, out_shape=shapes, in_specs=in_specs, out_specs=[VM...  15.6 us
    ppermute x11, starting transfers between devices, swap(): return lax.ppermute(value, axis, [(i, i ^ distance) for i in range(count)])  13.2 us
    ppermute x11, waiting for transfers between devices, swap(): return lax.ppermute(value, axis, [(i, i ^ distance) for i in range(count)])  11.6 us
    ppermute x4, starting transfers between devices, whole(): strips.append(lax.ppermute(packed[i], 'col', col_rounds[i % 2]))  8.15 us
    ppermute x1, waiting for transfers between devices, whole(): send_e = lax.ppermute(send_e, 'col', col_rounds[0])  8.06 us
  transfers between devices with their start and end apart: 21, of which 14 were waited for; matrix products, arithmetic and copies ran while one was open for 0% of the time, Pallas kernels for 13%

profile of v3, /device:TPU:0, one launch (start us, length us, event | category | flops | bytes accessed | tf_op | source)
XLA Modules:
  0.0 62.3 jit_solution(8924502883316491070)
XLA Ops:
  0.6 2.0 %shard_map.104 = (f32[4,256,256]{2,1,0:T(8,128)S(1)}, s32[1,2]{1,0:T(1,128)S(1)}, f32[256,128]{1,0:T(8,128)S(1)}, f32[256,128]{1,0:T(8,128)S(1)}, f32[256,128]{1...) custom-call(f32[4,256,256]{2,1,0:T(8,128)} %bitcast.4, s32[1,2]{1,0:T(1,128)} %bitcast.7), custom_call_target="tpu_custom_call" | custom-call | tf_op jit(solution)/shard_map/pallas_call | solution.py:392
  3.2 2.6 %collective-permute-start.3 = (f32[256,128]{1,0:T(8,128)S(1)}, f32[256,128]{1,0:T(8,128)S(1)}, u32[]{:S(2)}, u32[]{:S(2)}) collective-permute-start(f32[256,128]{1,0:T(8,128)S(1)} %get-tuple-element.35), channel_id=1, source_target_pairs={{0,1},{2,3},{4,5},{6,7},{8,9},{10,11},{12,13},{14,15},{1,0},{3,2},... | collective-permute-start | bytes 393224 | tf_op jit(solution)/shard_map/ppermute | solution.py:519
  5.7 0.7 %collective-permute-start.4 = (f32[256,128]{1,0:T(8,128)S(1)}, f32[256,128]{1,0:T(8,128)S(1)}, u32[]{:S(2)}, u32[]{:S(2)}) collective-permute-start(f32[256,128]{1,0:T(8,128)S(1)} %get-tuple-element.36), channel_id=1, source_target_pairs={{1,2},{3,4},{5,6},{7,8},{9,10},{11,12},{13,14},{2,1},{4,3},{6,5},{... | collective-permute-start | bytes 393224 | tf_op jit(solution)/shard_map/ppermute | solution.py:519
  6.4 4.3 %collective-permute-start.1 = (f32[256,128]{1,0:T(8,128)S(1)}, f32[256,128]{1,0:T(8,128)S(1)}, u32[]{:S(2)}, u32[]{:S(2)}) collective-permute-start(f32[256,128]{1,0:T(8,128)S(1)} %get-tuple-element.33), channel_id=1, source_target_pairs={{0,1},{2,3},{4,5},{6,7},{8,9},{10,11},{12,13},{14,15},{1,0},{3,2},... | collective-permute-start | bytes 393224 | tf_op jit(solution)/shard_map/ppermute | solution.py:519
  10.7 0.7 %collective-permute-start.2 = (f32[256,128]{1,0:T(8,128)S(1)}, f32[256,128]{1,0:T(8,128)S(1)}, u32[]{:S(2)}, u32[]{:S(2)}) collective-permute-start(f32[256,128]{1,0:T(8,128)S(1)} %get-tuple-element.34), channel_id=1, source_target_pairs={{1,2},{3,4},{5,6},{7,8},{9,10},{11,12},{13,14},{2,1},{4,3},{6,5},{... | collective-permute-start | bytes 393224 | tf_op jit(solution)/shard_map/ppermute | solution.py:519
  11.3 2.6 %shard_map.105 = (f32[256,256]{1,0:T(8,128)S(1)}, f32[256,256]{1,0:T(8,128)S(1)}, bf16[2,256,256]{2,1,0:T(8,128)(2,1)S(1)}, bf16[4,256,256]{2,1,0:T(8,128)(2,1)S...) custom-call(f32[256,256]{1,0:T(8,128)} %refs_0_.1, ...), custom_call_target="tpu_custom_call" | custom-call | tf_op jit(solution)/shard_map/pallas_call | solution.py:392
  14.1 0.8 %shard_map.107.refs_6_ = f32[2,256,256]{2,1,0:T(8,128)S(1)} custom-call(s32[1,2]{1,0:T(1,128)S(1)} %get-tuple-element.38.offs.refs_5_, f32[2,256,256]{2,1,0:T(8,128)S(1)} %get-tuple-element.39.probe), custom_call_target="tpu_custom_call" | custom-call | tf_op jit(solution)/shard_map/pallas_call | solution.py:392
  15.3 2.4 %shard_map.108 = (f32[2,256,256]{2,1,0:T(8,128)S(1)}, f32[2,256,256]{2,1,0:T(8,128)S(1)}) custom-call(f32[4,256,256]{2,1,0:T(8,128)S(1)} %get-tuple-element.31.refs_0_, f32[4,64,256]{2,1,0:T(8,128)S(1)} %collective-permute-done.refs_1_, f32[2,64,128]{2,1,0:T(8,128)S(1)} %collective-permute-done.5.refs_2_, f32[256,128]{1,0:T(8,128)S(1)} %collective-permute-done.3.e.refs_3_, ...), custom_call_target="tpu_custom_call" | custom-call | tf_op jit(solution)/shard_map/pallas_call | solution.py:392
  17.7 1.0 %collective-permute-done.1.e.refs_3_ = f32[256,128]{1,0:T(8,128)S(1)} collective-permute-done((f32[256,128]{1,0:T(8,128)S(1)}, f32[256,128]{1,0:T(8,128)S(1)}, u32[]{:S(2)}, u32[]{:S(2)}) %collective-permute-start.1) | collective-permute-done | bytes 131104 | tf_op jit(solution)/shard_map/ppermute | solution.py:519
  18.8 0.6 %shard_map.110.refs_9_ = f32[256,256]{1,0:T(8,128)S(1)} custom-call(f32[256,256]{1,0:T(8,128)S(1)} %get-tuple-element.45.x, bf16[2,256,256]{2,1,0:T(8,128)(2,1)S(1)} %get-tuple-element.46.order, f32[2,256,256]{2,1,0:T(8,128)S(1)} %get-tuple-element.44.after.refs_11_), custom_call_target="tpu_custom_call" | custom-call | tf_op jit(solution)/shard_map/pallas_call | solution.py:392
  20.0 4.8 %shard_map.111 = (f32[256,256]{1,0:T(8,128)S(1)}, f32[256,256]{1,0:T(8,128)S(1)}, f32[4,256,256]{2,1,0:T(8,128)S(1)}, f32[4,256,128]{2,1,0:T(8,128)S(1)}, f32[4,64,384]{2,1,0:T(8,128)S(1)}) custom-call(f32[4,256,256]{2,1,0:T(8,128)S(1)} %get-tuple-element.31.refs_0_, f32[4,64,256]{2,1,0:T(8,128)S(1)} %collective-permute-done.refs_1_, ...), custom_call_target="tpu_custom_call" | custom-call | tf_op jit(solution)/shard_map/pallas_call | solution.py:392
  25.4 1.0 %collective-permute-done.10.other = f32[256,256]{1,0:T(8,128)S(1)} collective-permute-done((f32[256,256]{1,0:T(8,128)S(1)}, f32[256,256]{1,0:T(8,128)S(1)}, u32[]{:S(2)}, u32[]{:S(2)}) %collective-permute-start.10) | collective-permute-done | bytes 262176 | tf_op jit(solution)/shard_map/ppermute | solution.py:415
  26.5 3.4 %collective-permute-start.11 = (f32[64,256]{1,0:T(8,128)S(1)}, f32[64,256]{1,0:T(8,128)S(1)}, u32[]{:S(2)}, u32[]{:S(2)}) collective-permute-start(f32[64,256]{1,0:T(8,128)S(1)} %get-tuple-element.57), channel_id=1, source_target_pairs={{0,1},{1,0},{2,3},{3,2},{4,5},{5,4},{6,7},{7,6},{8,9},{9,8},{10,11... | collective-permute-start | bytes 196616 | tf_op jit(solution)/shard_map/ppermute | solution.py:415
  29.9 1.5 %collective-permute-start.12 = (f32[64,256]{1,0:T(8,128)S(1)}, f32[64,256]{1,0:T(8,128)S(1)}, u32[]{:S(2)}, u32[]{:S(2)}) collective-permute-start(f32[64,256]{1,0:T(8,128)S(1)} %get-tuple-element.58), channel_id=1, source_target_pairs={{0,2},{1,3},{2,0},{3,1},{4,6},{5,7},{6,4},{7,5},{8,10},{9,11},{10,... | collective-permute-start | bytes 196616 | tf_op jit(solution)/shard_map/ppermute | solution.py:415
  31.4 0.9 %collective-permute-done.11.refs_1_ = f32[64,256]{1,0:T(8,128)S(1)} collective-permute-done((f32[64,256]{1,0:T(8,128)S(1)}, f32[64,256]{1,0:T(8,128)S(1)}, u32[]{:S(2)}, u32[]{:S(2)}) %collective-permute-start.11) | collective-permute-done | bytes 65568 | tf_op jit(solution)/shard_map/ppermute | solution.py:415
  32.3 1.9 %collective-permute-done.12.refs_2_ = f32[64,256]{1,0:T(8,128)S(1)} collective-permute-done((f32[64,256]{1,0:T(8,128)S(1)}, f32[64,256]{1,0:T(8,128)S(1)}, u32[]{:S(2)}, u32[]{:S(2)}) %collective-permute-start.12) | collective-permute-done | bytes 65568 | tf_op jit(solution)/shard_map/ppermute | solution.py:415
  34.1 2.4 %collective-permute-done.13.refs_3_ = f32[64,256]{1,0:T(8,128)S(1)} collective-permute-done((f32[64,256]{1,0:T(8,128)S(1)}, f32[64,256]{1,0:T(8,128)S(1)}, u32[]{:S(2)}, u32[]{:S(2)}) %collective-permute-start.13) | collective-permute-done | bytes 65568 | tf_op jit(solution)/shard_map/ppermute | solution.py:415
  36.6 1.5 %collective-permute-start.16 = (f32[64,256]{1,0:T(8,128)S(1)}, f32[64,256]{1,0:T(8,128)S(1)}, u32[]{:S(2)}, u32[]{:S(2)}) collective-permute-start(f32[64,256]{1,0:T(8,128)S(1)} %shard_map.115.refs_0_), channel_id=1, source_target_pairs={{0,12},{1,13},{2,14},{3,15},{4,8},{5,9},{6,10},{7,11},{8,4},{9,5},... | collective-permute-start | bytes 196616 | tf_op jit(solution)/shard_map/ppermute | solution.py:415
  38.1 1.6 %collective-permute-start.15 = (f32[64,256]{1,0:T(8,128)S(1)}, f32[64,256]{1,0:T(8,128)S(1)}, u32[]{:S(2)}, u32[]{:S(2)}) collective-permute-start(f32[64,256]{1,0:T(8,128)S(1)} %shard_map.115.refs_0_), channel_id=1, source_target_pairs={{0,8},{1,9},{2,10},{3,11},{4,12},{5,13},{6,14},{7,15},{8,0},{9,1},... | collective-permute-start | bytes 196616 | tf_op jit(solution)/shard_map/ppermute | solution.py:415
  39.7 1.4 %collective-permute-start.14 = (f32[64,256]{1,0:T(8,128)S(1)}, f32[64,256]{1,0:T(8,128)S(1)}, u32[]{:S(2)}, u32[]{:S(2)}) collective-permute-start(f32[64,256]{1,0:T(8,128)S(1)} %shard_map.115.refs_0_), channel_id=1, source_target_pairs={{0,4},{1,5},{2,6},{3,7},{4,0},{5,1},{6,2},{7,3},{8,12},{9,13},{10,... | collective-permute-start | bytes 196616 | tf_op jit(solution)/shard_map/ppermute | solution.py:415
  41.0 2.0 %collective-permute-done.16.refs_3_ = f32[64,256]{1,0:T(8,128)S(1)} collective-permute-done((f32[64,256]{1,0:T(8,128)S(1)}, f32[64,256]{1,0:T(8,128)S(1)}, u32[]{:S(2)}, u32[]{:S(2)}) %collective-permute-start.16) | collective-permute-done | bytes 65568 | tf_op jit(solution)/shard_map/ppermute | solution.py:415
  43.0 0.8 %collective-permute-done.15.refs_2_ = f32[64,256]{1,0:T(8,128)S(1)} collective-permute-done((f32[64,256]{1,0:T(8,128)S(1)}, f32[64,256]{1,0:T(8,128)S(1)}, u32[]{:S(2)}, u32[]{:S(2)}) %collective-permute-start.15) | collective-permute-done | bytes 65568 | tf_op jit(solution)/shard_map/ppermute | solution.py:415
  43.8 0.6 %collective-permute-done.14.refs_1_ = f32[64,256]{1,0:T(8,128)S(1)} collective-permute-done((f32[64,256]{1,0:T(8,128)S(1)}, f32[64,256]{1,0:T(8,128)S(1)}, u32[]{:S(2)}, u32[]{:S(2)}) %collective-permute-start.14) | collective-permute-done | bytes 65568 | tf_op jit(solution)/shard_map/ppermute | solution.py:415
  44.5 1.1 %collective-permute-start.19 = (f32[64,256]{1,0:T(8,128)S(1)}, f32[64,256]{1,0:T(8,128)S(1)}, u32[]{:S(2)}, u32[]{:S(2)}) collective-permute-start(f32[64,256]{1,0:T(8,128)S(1)} %shard_map.116.refs_0_), channel_id=1, source_target_pairs={{0,3},{1,2},{2,1},{3,0},{4,7},{5,6},{6,5},{7,4},{8,11},{9,10},{10,... | collective-permute-start | bytes 196616 | tf_op jit(solution)/shard_map/ppermute | solution.py:415
  45.5 1.5 %collective-permute-start.18 = (f32[64,256]{1,0:T(8,128)S(1)}, f32[64,256]{1,0:T(8,128)S(1)}, u32[]{:S(2)}, u32[]{:S(2)}) collective-permute-start(f32[64,256]{1,0:T(8,128)S(1)} %shard_map.116.refs_0_), channel_id=1, source_target_pairs={{0,2},{1,3},{2,0},{3,1},{4,6},{5,7},{6,4},{7,5},{8,10},{9,11},{10,... | collective-permute-start | bytes 196616 | tf_op jit(solution)/shard_map/ppermute | solution.py:415
  47.1 1.0 %collective-permute-start.17 = (f32[64,256]{1,0:T(8,128)S(1)}, f32[64,256]{1,0:T(8,128)S(1)}, u32[]{:S(2)}, u32[]{:S(2)}) collective-permute-start(f32[64,256]{1,0:T(8,128)S(1)} %shard_map.116.refs_0_), channel_id=1, source_target_pairs={{0,1},{1,0},{2,3},{3,2},{4,5},{5,4},{6,7},{7,6},{8,9},{9,8},{10,11... | collective-permute-start | bytes 196616 | tf_op jit(solution)/shard_map/ppermute | solution.py:415
  48.2 1.1 %collective-permute-start.8 = (f32[2,256,128]{2,1,0:T(8,128)S(1)}, f32[2,256,128]{2,1,0:T(8,128)S(1)}, u32[]{:S(2)}, u32[]{:S(2)}) collective-permute-start(f32[2,256,128]{2,1,0:T(8,128)S(1)} %get-tuple-element.52), channel_id=1, source_target_pairs={{0,1},{2,3},{4,5},{6,7},{8,9},{10,11},{12,13},{14,15},{1,0},{3,2},... | collective-permute-start | bytes 786440 | tf_op jit(solution)/shard_map/ppermute | solution.py:596
  49.3 0.7 %collective-permute-start.9 = (f32[2,256,128]{2,1,0:T(8,128)S(1)}, f32[2,256,128]{2,1,0:T(8,128)S(1)}, u32[]{:S(2)}, u32[]{:S(2)}) collective-permute-start(f32[2,256,128]{2,1,0:T(8,128)S(1)} %get-tuple-element.53), channel_id=1, source_target_pairs={{1,2},{3,4},{5,6},{7,8},{9,10},{11,12},{13,14},{2,1},{4,3},{6,5},{... | collective-permute-start | bytes 786440 | tf_op jit(solution)/shard_map/ppermute | solution.py:597
  50.5 1.6 %collective-permute-done.17.refs_1_ = f32[64,256]{1,0:T(8,128)S(1)} collective-permute-done((f32[64,256]{1,0:T(8,128)S(1)}, f32[64,256]{1,0:T(8,128)S(1)}, u32[]{:S(2)}, u32[]{:S(2)}) %collective-permute-start.17) | collective-permute-done | bytes 65568 | tf_op jit(solution)/shard_map/ppermute | solution.py:415
  52.1 8.1 %collective-permute-done.8.e = f32[2,256,128]{2,1,0:T(8,128)S(1)} collective-permute-done((f32[2,256,128]{2,1,0:T(8,128)S(1)}, f32[2,256,128]{2,1,0:T(8,128)S(1)}, u32[]{:S(2)}, u32[]{:S(2)}) %collective-permute-start.8) | collective-permute-done | bytes 262176 | tf_op jit(solution)/shard_map/ppermute | solution.py:596
  60.2 1.2 %shard_map.113 = f32[4,256,256]{2,1,0:T(8,128)} custom-call(f32[4,256,256]{2,1,0:T(8,128)S(1)} %get-tuple-element.51.total, f32[2,256,128]{2,1,0:T(8,128)S(1)} %collective-permute-done.8.e, f32[2,256,128]{2,1,0:T(8,128)S(1)} %collective-permute-done.9.o), custom_call_target="tpu_custom_call" | custom-call | tf_op jit(solution)/shard_map/pallas_call | solution.py:392
  61.4 0.9 %shard_map.118 = f32[2,256,256]{2,1,0:T(8,128)} custom-call(f32[256,256]{1,0:T(8,128)S(1)} %shard_map.117.full, f32[256,256]{1,0:T(8,128)S(1)} %collective-permute-done.20.other), custom_call_target="tpu_custom_call" | custom-call | tf_op jit(solution)/shard_map/pallas_call | solution.py:392
  (25 shorter events, 3.2 us)
Async XLA Ops:
  2.6 12.7 %collective-permute-start = (f32[4,64,256]{2,1,0:T(8,128)S(1)}, f32[4,64,256]{2,1,0:T(8,128)S(1)}, u32[]{:S(2)}, u32[]{:S(2)}) collective-permute-start(f32[4,64,256]{2,1,0:T(8,128)S(1)} %get-tuple-element.32), channel_id=1, source_target_pairs={{0,16},{16,0},{1,17},{17,1},{2,18},{18,2},{3,19},{19,3},{4,20},{20... | collective-permute-start | bytes 786440 | tf_op jit(solution)/shard_map/ppermute | solution.py:521
  3.2 10.8 %collective-permute-start.3 = (f32[256,128]{1,0:T(8,128)S(1)}, f32[256,128]{1,0:T(8,128)S(1)}, u32[]{:S(2)}, u32[]{:S(2)}) collective-permute-start(f32[256,128]{1,0:T(8,128)S(1)} %get-tuple-element.35), channel_id=1, source_target_pairs={{0,1},{2,3},{4,5},{6,7},{8,9},{10,11},{12,13},{14,15},{1,0},{3,2},... | collective-permute-start | bytes 393224 | tf_op jit(solution)/shard_map/ppermute | solution.py:519
  5.7 8.2 %collective-permute-start.4 = (f32[256,128]{1,0:T(8,128)S(1)}, f32[256,128]{1,0:T(8,128)S(1)}, u32[]{:S(2)}, u32[]{:S(2)}) collective-permute-start(f32[256,128]{1,0:T(8,128)S(1)} %get-tuple-element.36), channel_id=1, source_target_pairs={{1,2},{3,4},{5,6},{7,8},{9,10},{11,12},{13,14},{2,1},{4,3},{6,5},{... | collective-permute-start | bytes 393224 | tf_op jit(solution)/shard_map/ppermute | solution.py:519
  6.4 12.3 %collective-permute-start.1 = (f32[256,128]{1,0:T(8,128)S(1)}, f32[256,128]{1,0:T(8,128)S(1)}, u32[]{:S(2)}, u32[]{:S(2)}) collective-permute-start(f32[256,128]{1,0:T(8,128)S(1)} %get-tuple-element.33), channel_id=1, source_target_pairs={{0,1},{2,3},{4,5},{6,7},{8,9},{10,11},{12,13},{14,15},{1,0},{3,2},... | collective-permute-start | bytes 393224 | tf_op jit(solution)/shard_map/ppermute | solution.py:519
  10.7 8.0 %collective-permute-start.2 = (f32[256,128]{1,0:T(8,128)S(1)}, f32[256,128]{1,0:T(8,128)S(1)}, u32[]{:S(2)}, u32[]{:S(2)}) collective-permute-start(f32[256,128]{1,0:T(8,128)S(1)} %get-tuple-element.34), channel_id=1, source_target_pairs={{1,2},{3,4},{5,6},{7,8},{9,10},{11,12},{13,14},{2,1},{4,3},{6,5},{... | collective-permute-start | bytes 393224 | tf_op jit(solution)/shard_map/ppermute | solution.py:519
  14.0 1.3 %collective-permute-start.5 = (f32[2,64,128]{2,1,0:T(8,128)S(1)}, f32[2,64,128]{2,1,0:T(8,128)S(1)}, u32[]{:S(2)}, u32[]{:S(2)}) collective-permute-start(f32[2,64,128]{2,1,0:T(8,128)S(1)} %shard_map.106), channel_id=1, source_target_pairs={{0,16},{16,0},{1,17},{17,1},{2,18},{18,2},{3,19},{19,3},{4,20},{20... | collective-permute-start | bytes 196616 | tf_op jit(solution)/shard_map/ppermute | solution.py:532
  18.7 1.3 %collective-permute-start.6 = (f32[2,64,128]{2,1,0:T(8,128)S(1)}, f32[2,64,128]{2,1,0:T(8,128)S(1)}, u32[]{:S(2)}, u32[]{:S(2)}) collective-permute-start(f32[2,64,128]{2,1,0:T(8,128)S(1)} %shard_map.109), channel_id=1, source_target_pairs={{0,16},{16,0},{1,17},{17,1},{2,18},{18,2},{3,19},{19,3},{4,20},{20... | collective-permute-start | bytes 196616 | tf_op jit(solution)/shard_map/ppermute | solution.py:532
  24.9 1.6 %collective-permute-start.10 = (f32[256,256]{1,0:T(8,128)S(1)}, f32[256,256]{1,0:T(8,128)S(1)}, u32[]{:S(2)}, u32[]{:S(2)}) collective-permute-start(f32[256,256]{1,0:T(8,128)S(1)} %get-tuple-element.55), channel_id=1, source_target_pairs={{0,16},{16,0},{1,17},{17,1},{2,18},{18,2},{3,19},{19,3},{4,20},{20... | collective-permute-start | bytes 786440 | tf_op jit(solution)/shard_map/ppermute | solution.py:415
  25.1 22.9 %collective-permute-start.7 = (f32[4,64,384]{2,1,0:T(8,128)S(1)}, f32[4,64,384]{2,1,0:T(8,128)S(1)}, u32[]{:S(2)}, u32[]{:S(2)}) collective-permute-start(f32[4,64,384]{2,1,0:T(8,128)S(1)} %get-tuple-element.50), channel_id=1, source_target_pairs={{0,16},{16,0},{1,17},{17,1},{2,18},{18,2},{3,19},{19,3},{4,20},{20... | collective-permute-start | bytes 1179656 | tf_op jit(solution)/shard_map/ppermute | solution.py:587
  26.5 5.8 %collective-permute-start.11 = (f32[64,256]{1,0:T(8,128)S(1)}, f32[64,256]{1,0:T(8,128)S(1)}, u32[]{:S(2)}, u32[]{:S(2)}) collective-permute-start(f32[64,256]{1,0:T(8,128)S(1)} %get-tuple-element.57), channel_id=1, source_target_pairs={{0,1},{1,0},{2,3},{3,2},{4,5},{5,4},{6,7},{7,6},{8,9},{9,8},{10,11... | collective-permute-start | bytes 196616 | tf_op jit(solution)/shard_map/ppermute | solution.py:415
  29.9 4.3 %collective-permute-start.12 = (f32[64,256]{1,0:T(8,128)S(1)}, f32[64,256]{1,0:T(8,128)S(1)}, u32[]{:S(2)}, u32[]{:S(2)}) collective-permute-start(f32[64,256]{1,0:T(8,128)S(1)} %get-tuple-element.58), channel_id=1, source_target_pairs={{0,2},{1,3},{2,0},{3,1},{4,6},{5,7},{6,4},{7,5},{8,10},{9,11},{10,... | collective-permute-start | bytes 196616 | tf_op jit(solution)/shard_map/ppermute | solution.py:415
  31.4 5.2 %collective-permute-start.13 = (f32[64,256]{1,0:T(8,128)S(1)}, f32[64,256]{1,0:T(8,128)S(1)}, u32[]{:S(2)}, u32[]{:S(2)}) collective-permute-start(f32[64,256]{1,0:T(8,128)S(1)} %get-tuple-element.59), channel_id=1, source_target_pairs={{0,3},{1,2},{2,1},{3,0},{4,7},{5,6},{6,5},{7,4},{8,11},{9,10},{10,... | collective-permute-start | bytes 196616 | tf_op jit(solution)/shard_map/ppermute | solution.py:415
  36.6 6.4 %collective-permute-start.16 = (f32[64,256]{1,0:T(8,128)S(1)}, f32[64,256]{1,0:T(8,128)S(1)}, u32[]{:S(2)}, u32[]{:S(2)}) collective-permute-start(f32[64,256]{1,0:T(8,128)S(1)} %shard_map.115.refs_0_), channel_id=1, source_target_pairs={{0,12},{1,13},{2,14},{3,15},{4,8},{5,9},{6,10},{7,11},{8,4},{9,5},... | collective-permute-start | bytes 196616 | tf_op jit(solution)/shard_map/ppermute | solution.py:415
  38.1 5.7 %collective-permute-start.15 = (f32[64,256]{1,0:T(8,128)S(1)}, f32[64,256]{1,0:T(8,128)S(1)}, u32[]{:S(2)}, u32[]{:S(2)}) collective-permute-start(f32[64,256]{1,0:T(8,128)S(1)} %shard_map.115.refs_0_), channel_id=1, source_target_pairs={{0,8},{1,9},{2,10},{3,11},{4,12},{5,13},{6,14},{7,15},{8,0},{9,1},... | collective-permute-start | bytes 196616 | tf_op jit(solution)/shard_map/ppermute | solution.py:415
  39.7 4.8 %collective-permute-start.14 = (f32[64,256]{1,0:T(8,128)S(1)}, f32[64,256]{1,0:T(8,128)S(1)}, u32[]{:S(2)}, u32[]{:S(2)}) collective-permute-start(f32[64,256]{1,0:T(8,128)S(1)} %shard_map.115.refs_0_), channel_id=1, source_target_pairs={{0,4},{1,5},{2,6},{3,7},{4,0},{5,1},{6,2},{7,3},{8,12},{9,13},{10,... | collective-permute-start | bytes 196616 | tf_op jit(solution)/shard_map/ppermute | solution.py:415
  44.5 5.9 %collective-permute-start.19 = (f32[64,256]{1,0:T(8,128)S(1)}, f32[64,256]{1,0:T(8,128)S(1)}, u32[]{:S(2)}, u32[]{:S(2)}) collective-permute-start(f32[64,256]{1,0:T(8,128)S(1)} %shard_map.116.refs_0_), channel_id=1, source_target_pairs={{0,3},{1,2},{2,1},{3,0},{4,7},{5,6},{6,5},{7,4},{8,11},{9,10},{10,... | collective-permute-start | bytes 196616 | tf_op jit(solution)/shard_map/ppermute | solution.py:415
  45.5 4.9 %collective-permute-start.18 = (f32[64,256]{1,0:T(8,128)S(1)}, f32[64,256]{1,0:T(8,128)S(1)}, u32[]{:S(2)}, u32[]{:S(2)}) collective-permute-start(f32[64,256]{1,0:T(8,128)S(1)} %shard_map.116.refs_0_), channel_id=1, source_target_pairs={{0,2},{1,3},{2,0},{3,1},{4,6},{5,7},{6,4},{7,5},{8,10},{9,11},{10,... | collective-permute-start | bytes 196616 | tf_op jit(solution)/shard_map/ppermute | solution.py:415
  47.1 5.0 %collective-permute-start.17 = (f32[64,256]{1,0:T(8,128)S(1)}, f32[64,256]{1,0:T(8,128)S(1)}, u32[]{:S(2)}, u32[]{:S(2)}) collective-permute-start(f32[64,256]{1,0:T(8,128)S(1)} %shard_map.116.refs_0_), channel_id=1, source_target_pairs={{0,1},{1,0},{2,3},{3,2},{4,5},{5,4},{6,7},{7,6},{8,9},{9,8},{10,11... | collective-permute-start | bytes 196616 | tf_op jit(solution)/shard_map/ppermute | solution.py:415
  48.2 12.0 %collective-permute-start.8 = (f32[2,256,128]{2,1,0:T(8,128)S(1)}, f32[2,256,128]{2,1,0:T(8,128)S(1)}, u32[]{:S(2)}, u32[]{:S(2)}) collective-permute-start(f32[2,256,128]{2,1,0:T(8,128)S(1)} %get-tuple-element.52), channel_id=1, source_target_pairs={{0,1},{2,3},{4,5},{6,7},{8,9},{10,11},{12,13},{14,15},{1,0},{3,2},... | collective-permute-start | bytes 786440 | tf_op jit(solution)/shard_map/ppermute | solution.py:596
  49.3 10.9 %collective-permute-start.9 = (f32[2,256,128]{2,1,0:T(8,128)S(1)}, f32[2,256,128]{2,1,0:T(8,128)S(1)}, u32[]{:S(2)}, u32[]{:S(2)}) collective-permute-start(f32[2,256,128]{2,1,0:T(8,128)S(1)} %get-tuple-element.53), channel_id=1, source_target_pairs={{1,2},{3,4},{5,6},{7,8},{9,10},{11,12},{13,14},{2,1},{4,3},{6,5},{... | collective-permute-start | bytes 786440 | tf_op jit(solution)/shard_map/ppermute | solution.py:597
  52.1 9.3 %collective-permute-start.20 = (f32[256,256]{1,0:T(8,128)S(1)}, f32[256,256]{1,0:T(8,128)S(1)}, u32[]{:S(2)}, u32[]{:S(2)}) collective-permute-start(f32[256,256]{1,0:T(8,128)S(1)} %shard_map.117.full), channel_id=1, source_target_pairs={{0,16},{16,0},{1,17},{17,1},{2,18},{18,2},{3,19},{19,3},{4,20},{20... | collective-permute-start | bytes 786440 | tf_op jit(solution)/shard_map/ppermute | solution.py:415

commit v4 on v3

--- a/solution.py
+++ b/solution.py
@@ -1,4 +1,5 @@
 import functools
+import math
 
 import jax
 import jax.numpy as jnp
@@ -107,6 +108,24 @@
         return [cat([e + o, e - o], 0) for e, o in zip(even, odd)]
 
 
+SIN = [(-1.0) ** i / math.factorial(2 * i + 1) for i in range(7)]
+COS = [(-1.0) ** i / math.factorial(2 * i) for i in range(7)]
+
+
+def series(coefficients, z):
+    total = coefficients[-1]
+    for c in coefficients[-2::-1]:
+        total = total * z + c
+    return total
+
+
+def cos_sin(x):
+    y = 0.5 * x
+    z = y * y
+    s, c = y * series(SIN, z), series(COS, z)
+    return 1.0 - 2.0 * (s * s), 2.0 * (s * c)
+
+
 def iota(shape, dim):
     return lax.broadcasted_iota(jnp.int32, shape, dim)
 
@@ -183,8 +202,7 @@
     copies[0].wait()
     copies[1].wait()
     angle = reorder(phase[...], loaded[0])
-    kr[...] = jnp.cos(angle)
-    ki[...] = jnp.sin(angle)
+    kr[...], ki[...] = cos_sin(angle)
     for copy in copies[2:]:
         copy.wait()
 
@@ -276,6 +294,11 @@
     arrive[0], arrive[1] = x
 
 
+def divide_kernel(margin, grads, offs, own, strip, *sends):
+    for s in range(2):
+        split_grad([grads[2 * s], grads[2 * s + 1]], s, offs, margin, own, strip, sends)
+
+
 def split_grad(grad, s, offs, margin, own, strip, sends):
     n = grad[0].shape[0]
     h = n // 2
@@ -310,7 +333,7 @@
     obj, halos, corners, refs = unpack(n_row, refs)
     e2, o2, offs, pr, kr, ki, am, w1, arrive, mats, twl, twr = refs[:12]
     outs = refs[12:]
-    keep, give = outs[:2]
+    keep, give, grads = outs
     n = obj.shape[1]
     dft = Dft(mats, twl[...], twr[...], n)
     win = window_of(obj, 1, halos, corners, e2, o2, offs, margin)
@@ -319,11 +342,10 @@
     modulus = jnp.sqrt(far[0] * far[0] + far[1] * far[1] + EPS_AMP)
     factor = 2.0 * (1.0 - am[...] / modulus)
     back_far = dft.inverse([factor * far[0], factor * far[1]])
-    own, strip, sends = outs[2], outs[3], outs[4:]
-    split_grad(conj_product(arr, back_far), 1, offs, margin, own, strip, sends)
+    grads[2], grads[3] = conj_product(arr, back_far)
     x = dft.forward(conj_product(win, back_far))
     x = dft.inverse(conj_product([kr[...], ki[...]], x))
-    split_grad(conj_product([pr[0], pr[1]], x), 0, offs, margin, own, strip, sends)
+    grads[0], grads[1] = conj_product([pr[0], pr[1]], x)
     grad = conj_product([w1[0], w1[1]], x)
     sy = (margin - offs[0, 0] + n) % n
     sx = (margin - offs[0, 1] + n) % n
@@ -560,9 +582,9 @@
     )
     cut(1, arrive)
     (am,) = call(reorder_kernel, [(n, n)], [VMEM] * 3, am, order, arrive)
-    keep, give, own, strip, *sends = call(
+    keep, give, grads = call(
         functools.partial(back_kernel, n_row, margin),
-        [(n, n), (n, n), (4, n, n), (4, n, h)] + [(4, margin, n + h)] * n_row,
+        [(n, n), (n, n), (4, n, n)],
         [VMEM] * (3 + 2 * n_row) + [SMEM] + [VMEM] * 9,
         obj,
         *halos,
@@ -582,6 +604,13 @@
         mib=40,
     )
     probe_grad = reduce_probe(keep, give)
+    own, strip, *sends = call(
+        functools.partial(divide_kernel, margin),
+        [(4, n, n), (4, n, h)] + [(4, margin, n + h)] * n_row,
+        [VMEM, SMEM],
+        grads,
+        offs,
+    )
     got = []
     for i, pairs in enumerate(row_rounds):
         got.append(lax.ppermute(sends[i], "row", pairs))

time: 62.7 us -> 62 us (0.989)
  starting transfers between devices: 24.2 us -> 23.2 us
    ppermute x4, waiting for transfers between devices: 0.97 us -> 1.61 us  [whole(): strips.append(lax.ppermute(packed[i], 'col', col_rounds[i % 2]))]
    pallas_call x15 -> x16, Pallas kernels: 15.6 us -> 15.6 us  [call(): pl.pallas_call(kernel, out_shape=shapes, in_specs=in_specs, out_specs=[VM...]
  transfers between devices with their start and end apart: 21 -> 21, of which waited for: 14 -> 12; matrix products, arithmetic and copies ran while one was open for 0% -> 0% of each run, Pallas kernels for 13% -> 13%
where the time goes in v4:
time: 62 us; the launch traced here: 61.4 us
  starting transfers between devices  23.2 us (37%)
  waiting for transfers between devices  21.8 us (35%)
  Pallas kernels  15.6 us (25%)
  between operations  0.79 us (1%)
    pallas_call x16, Pallas kernels, call(): pl.pallas_call(kernel, out_shape=shapes, in_specs=in_specs, out_specs=[VM...  15.6 us
    ppermute x11, starting transfers between devices, swap(): return lax.ppermute(value, axis, [(i, i ^ distance) for i in range(count)])  12.6 us
    ppermute x11, waiting for transfers between devices, swap(): return lax.ppermute(value, axis, [(i, i ^ distance) for i in range(count)])  11.2 us
    ppermute x4, starting transfers between devices, whole(): strips.append(lax.ppermute(packed[i], 'col', col_rounds[i % 2]))  8.15 us
    ppermute x1, waiting for transfers between devices, whole(): send_e = lax.ppermute(send_e, 'col', col_rounds[0])  7.84 us
    ppermute x4, waiting for transfers between devices, whole(): strips.append(lax.ppermute(packed[i], 'col', col_rounds[i % 2]))  1.61 us
  transfers between devices with their start and end apart: 21, of which 12 were waited for; matrix products, arithmetic and copies ran while one was open for 0% of the time, Pallas kernels for 13%

profile of v4, /device:TPU:0, one launch (start us, length us, event | category | flops | bytes accessed | tf_op | source)
XLA Modules:
  0.0 61.4 jit_solution(16091778652216835415)
XLA Ops:
  0.6 2.0 %shard_map.104 = (f32[4,256,256]{2,1,0:T(8,128)S(1)}, s32[1,2]{1,0:T(1,128)S(1)}, f32[256,128]{1,0:T(8,128)S(1)}, f32[256,128]{1,0:T(8,128)S(1)}, f32[256,128]{1...) custom-call(f32[4,256,256]{2,1,0:T(8,128)} %bitcast.4, s32[1,2]{1,0:T(1,128)} %bitcast.7), custom_call_target="tpu_custom_call" | custom-call | tf_op jit(solution)/shard_map/pallas_call | solution.py:414
  3.2 2.6 %collective-permute-start.3 = (f32[256,128]{1,0:T(8,128)S(1)}, f32[256,128]{1,0:T(8,128)S(1)}, u32[]{:S(2)}, u32[]{:S(2)}) collective-permute-start(f32[256,128]{1,0:T(8,128)S(1)} %get-tuple-element.36), channel_id=1, source_target_pairs={{0,1},{2,3},{4,5},{6,7},{8,9},{10,11},{12,13},{14,15},{1,0},{3,2},... | collective-permute-start | bytes 393224 | tf_op jit(solution)/shard_map/ppermute | solution.py:541
  5.7 0.7 %collective-permute-start.4 = (f32[256,128]{1,0:T(8,128)S(1)}, f32[256,128]{1,0:T(8,128)S(1)}, u32[]{:S(2)}, u32[]{:S(2)}) collective-permute-start(f32[256,128]{1,0:T(8,128)S(1)} %get-tuple-element.37), channel_id=1, source_target_pairs={{1,2},{3,4},{5,6},{7,8},{9,10},{11,12},{13,14},{2,1},{4,3},{6,5},{... | collective-permute-start | bytes 393224 | tf_op jit(solution)/shard_map/ppermute | solution.py:541
  6.4 4.3 %collective-permute-start.1 = (f32[256,128]{1,0:T(8,128)S(1)}, f32[256,128]{1,0:T(8,128)S(1)}, u32[]{:S(2)}, u32[]{:S(2)}) collective-permute-start(f32[256,128]{1,0:T(8,128)S(1)} %get-tuple-element.34), channel_id=1, source_target_pairs={{0,1},{2,3},{4,5},{6,7},{8,9},{10,11},{12,13},{14,15},{1,0},{3,2},... | collective-permute-start | bytes 393224 | tf_op jit(solution)/shard_map/ppermute | solution.py:541
  10.7 0.7 %collective-permute-start.2 = (f32[256,128]{1,0:T(8,128)S(1)}, f32[256,128]{1,0:T(8,128)S(1)}, u32[]{:S(2)}, u32[]{:S(2)}) collective-permute-start(f32[256,128]{1,0:T(8,128)S(1)} %get-tuple-element.35), channel_id=1, source_target_pairs={{1,2},{3,4},{5,6},{7,8},{9,10},{11,12},{13,14},{2,1},{4,3},{6,5},{... | collective-permute-start | bytes 393224 | tf_op jit(solution)/shard_map/ppermute | solution.py:541
  11.3 2.0 %shard_map.105 = (f32[256,256]{1,0:T(8,128)S(1)}, f32[256,256]{1,0:T(8,128)S(1)}, bf16[2,256,256]{2,1,0:T(8,128)(2,1)S(1)}, bf16[4,256,256]{2,1,0:T(8,128)(2,1)S...) custom-call(f32[256,256]{1,0:T(8,128)} %refs_0_.1, ...), custom_call_target="tpu_custom_call" | custom-call | tf_op jit(solution)/shard_map/pallas_call | solution.py:414
  13.4 0.8 %shard_map.107.refs_6_ = f32[2,256,256]{2,1,0:T(8,128)S(1)} custom-call(s32[1,2]{1,0:T(1,128)S(1)} %get-tuple-element.39.offs.refs_5_, f32[2,256,256]{2,1,0:T(8,128)S(1)} %get-tuple-element.40.probe), custom_call_target="tpu_custom_call" | custom-call | tf_op jit(solution)/shard_map/pallas_call | solution.py:414
  14.7 2.4 %shard_map.108 = (f32[2,256,256]{2,1,0:T(8,128)S(1)}, f32[2,256,256]{2,1,0:T(8,128)S(1)}) custom-call(f32[4,256,256]{2,1,0:T(8,128)S(1)} %get-tuple-element.32.refs_0_, f32[4,64,256]{2,1,0:T(8,128)S(1)} %collective-permute-done.refs_1_, f32[2,64,128]{2,1,0:T(8,128)S(1)} %collective-permute-done.5.refs_2_, f32[256,128]{1,0:T(8,128)S(1)} %collective-permute-done.3.e.refs_3_, ...), custom_call_target="tpu_custom_call" | custom-call | tf_op jit(solution)/shard_map/pallas_call | solution.py:414
  17.1 1.6 %collective-permute-done.1.e.refs_3_ = f32[256,128]{1,0:T(8,128)S(1)} collective-permute-done((f32[256,128]{1,0:T(8,128)S(1)}, f32[256,128]{1,0:T(8,128)S(1)}, u32[]{:S(2)}, u32[]{:S(2)}) %collective-permute-start.1) | collective-permute-done | bytes 131104 | tf_op jit(solution)/shard_map/ppermute | solution.py:541
  18.8 0.6 %shard_map.110.refs_9_ = f32[256,256]{1,0:T(8,128)S(1)} custom-call(f32[256,256]{1,0:T(8,128)S(1)} %get-tuple-element.46.x, bf16[2,256,256]{2,1,0:T(8,128)(2,1)S(1)} %get-tuple-element.47.order, f32[2,256,256]{2,1,0:T(8,128)S(1)} %get-tuple-element.45.after.refs_11_), custom_call_target="tpu_custom_call" | custom-call | tf_op jit(solution)/shard_map/pallas_call | solution.py:414
  19.4 0.6 collective-permute-done.6.refs_2_
  20.0 4.7 %shard_map.111 = (f32[256,256]{1,0:T(8,128)S(1)}, f32[256,256]{1,0:T(8,128)S(1)}, f32[4,256,256]{2,1,0:T(8,128)S(1)}) custom-call(f32[4,256,256]{2,1,0:T(8,128)S(1)} %get-tuple-element.32.refs_0_, f32[4,64,256]{2,1,0:T(8,128)S(1)} %collective-permute-done.refs_1_, f32[2,64,128]{2,1,0:T(8,128)S(1)} %collective-permute-done.6.refs_2_, ...), custom_call_target="tpu_custom_call" | custom-call | tf_op jit(solution)/shard_map/pallas_call | solution.py:414
  24.9 0.9 %shard_map.112 = (f32[4,256,256]{2,1,0:T(8,128)S(1)}, f32[4,256,128]{2,1,0:T(8,128)S(1)}, f32[4,64,384]{2,1,0:T(8,128)S(1)}) custom-call(f32[4,256,256]{2,1,0:T(8,128)S(1)} %get-tuple-element.49.grads, s32[1,2]{1,0:T(1,128)S(1)} %get-tuple-element.39.offs.refs_5_), custom_call_target="tpu_custom_call" | custom-call | tf_op jit(solution)/shard_map/pallas_call | solution.py:414
  26.3 2.7 %collective-permute-start.11 = (f32[64,256]{1,0:T(8,128)S(1)}, f32[64,256]{1,0:T(8,128)S(1)}, u32[]{:S(2)}, u32[]{:S(2)}) collective-permute-start(f32[64,256]{1,0:T(8,128)S(1)} %get-tuple-element.59), channel_id=1, source_target_pairs={{0,1},{1,0},{2,3},{3,2},{4,5},{5,4},{6,7},{7,6},{8,9},{9,8},{10,11... | collective-permute-start | bytes 196616 | tf_op jit(solution)/shard_map/ppermute | solution.py:437
  29.0 1.5 %collective-permute-start.12 = (f32[64,256]{1,0:T(8,128)S(1)}, f32[64,256]{1,0:T(8,128)S(1)}, u32[]{:S(2)}, u32[]{:S(2)}) collective-permute-start(f32[64,256]{1,0:T(8,128)S(1)} %get-tuple-element.60), channel_id=1, source_target_pairs={{0,2},{1,3},{2,0},{3,1},{4,6},{5,7},{6,4},{7,5},{8,10},{9,11},{10,... | collective-permute-start | bytes 196616 | tf_op jit(solution)/shard_map/ppermute | solution.py:437
  30.6 0.9 %collective-permute-done.11.refs_1_ = f32[64,256]{1,0:T(8,128)S(1)} collective-permute-done((f32[64,256]{1,0:T(8,128)S(1)}, f32[64,256]{1,0:T(8,128)S(1)}, u32[]{:S(2)}, u32[]{:S(2)}) %collective-permute-start.11) | collective-permute-done | bytes 65568 | tf_op jit(solution)/shard_map/ppermute | solution.py:437
  31.5 1.9 %collective-permute-done.12.refs_2_ = f32[64,256]{1,0:T(8,128)S(1)} collective-permute-done((f32[64,256]{1,0:T(8,128)S(1)}, f32[64,256]{1,0:T(8,128)S(1)}, u32[]{:S(2)}, u32[]{:S(2)}) %collective-permute-start.12) | collective-permute-done | bytes 65568 | tf_op jit(solution)/shard_map/ppermute | solution.py:437
  33.3 2.4 %collective-permute-done.13.refs_3_ = f32[64,256]{1,0:T(8,128)S(1)} collective-permute-done((f32[64,256]{1,0:T(8,128)S(1)}, f32[64,256]{1,0:T(8,128)S(1)}, u32[]{:S(2)}, u32[]{:S(2)}) %collective-permute-start.13) | collective-permute-done | bytes 65568 | tf_op jit(solution)/shard_map/ppermute | solution.py:437
  35.7 2.2 %collective-permute-start.16 = (f32[64,256]{1,0:T(8,128)S(1)}, f32[64,256]{1,0:T(8,128)S(1)}, u32[]{:S(2)}, u32[]{:S(2)}) collective-permute-start(f32[64,256]{1,0:T(8,128)S(1)} %shard_map.116.refs_0_), channel_id=1, source_target_pairs={{0,12},{1,13},{2,14},{3,15},{4,8},{5,9},{6,10},{7,11},{8,4},{9,5},... | collective-permute-start | bytes 196616 | tf_op jit(solution)/shard_map/ppermute | solution.py:437
  37.9 0.9 %collective-permute-start.15 = (f32[64,256]{1,0:T(8,128)S(1)}, f32[64,256]{1,0:T(8,128)S(1)}, u32[]{:S(2)}, u32[]{:S(2)}) collective-permute-start(f32[64,256]{1,0:T(8,128)S(1)} %shard_map.116.refs_0_), channel_id=1, source_target_pairs={{0,8},{1,9},{2,10},{3,11},{4,12},{5,13},{6,14},{7,15},{8,0},{9,1},... | collective-permute-start | bytes 196616 | tf_op jit(solution)/shard_map/ppermute | solution.py:437
  38.9 1.3 %collective-permute-start.14 = (f32[64,256]{1,0:T(8,128)S(1)}, f32[64,256]{1,0:T(8,128)S(1)}, u32[]{:S(2)}, u32[]{:S(2)}) collective-permute-start(f32[64,256]{1,0:T(8,128)S(1)} %shard_map.116.refs_0_), channel_id=1, source_target_pairs={{0,4},{1,5},{2,6},{3,7},{4,0},{5,1},{6,2},{7,3},{8,12},{9,13},{10,... | collective-permute-start | bytes 196616 | tf_op jit(solution)/shard_map/ppermute | solution.py:437
  40.2 2.4 %collective-permute-done.16.refs_3_ = f32[64,256]{1,0:T(8,128)S(1)} collective-permute-done((f32[64,256]{1,0:T(8,128)S(1)}, f32[64,256]{1,0:T(8,128)S(1)}, u32[]{:S(2)}, u32[]{:S(2)}) %collective-permute-start.16) | collective-permute-done | bytes 65568 | tf_op jit(solution)/shard_map/ppermute | solution.py:437
  42.6 1.6 %collective-permute-done.15.refs_2_ = f32[64,256]{1,0:T(8,128)S(1)} collective-permute-done((f32[64,256]{1,0:T(8,128)S(1)}, f32[64,256]{1,0:T(8,128)S(1)}, u32[]{:S(2)}, u32[]{:S(2)}) %collective-permute-start.15) | collective-permute-done | bytes 65568 | tf_op jit(solution)/shard_map/ppermute | solution.py:437
  44.3 0.7 %collective-permute-start.19 = (f32[64,256]{1,0:T(8,128)S(1)}, f32[64,256]{1,0:T(8,128)S(1)}, u32[]{:S(2)}, u32[]{:S(2)}) collective-permute-start(f32[64,256]{1,0:T(8,128)S(1)} %shard_map.117.refs_0_), channel_id=1, source_target_pairs={{0,3},{1,2},{2,1},{3,0},{4,7},{5,6},{6,5},{7,4},{8,11},{9,10},{10,... | collective-permute-start | bytes 196616 | tf_op jit(solution)/shard_map/ppermute | solution.py:437
  44.9 1.5 %collective-permute-start.18 = (f32[64,256]{1,0:T(8,128)S(1)}, f32[64,256]{1,0:T(8,128)S(1)}, u32[]{:S(2)}, u32[]{:S(2)}) collective-permute-start(f32[64,256]{1,0:T(8,128)S(1)} %shard_map.117.refs_0_), channel_id=1, source_target_pairs={{0,2},{1,3},{2,0},{3,1},{4,6},{5,7},{6,4},{7,5},{8,10},{9,11},{10,... | collective-permute-start | bytes 196616 | tf_op jit(solution)/shard_map/ppermute | solution.py:437
  46.4 1.4 %collective-permute-start.17 = (f32[64,256]{1,0:T(8,128)S(1)}, f32[64,256]{1,0:T(8,128)S(1)}, u32[]{:S(2)}, u32[]{:S(2)}) collective-permute-start(f32[64,256]{1,0:T(8,128)S(1)} %shard_map.117.refs_0_), channel_id=1, source_target_pairs={{0,1},{1,0},{2,3},{3,2},{4,5},{5,4},{6,7},{7,6},{8,9},{9,8},{10,11... | collective-permute-start | bytes 196616 | tf_op jit(solution)/shard_map/ppermute | solution.py:437
  48.0 0.7 %collective-permute-start.8 = (f32[2,256,128]{2,1,0:T(8,128)S(1)}, f32[2,256,128]{2,1,0:T(8,128)S(1)}, u32[]{:S(2)}, u32[]{:S(2)}) collective-permute-start(f32[2,256,128]{2,1,0:T(8,128)S(1)} %get-tuple-element.54), channel_id=1, source_target_pairs={{0,1},{2,3},{4,5},{6,7},{8,9},{10,11},{12,13},{14,15},{1,0},{3,2},... | collective-permute-start | bytes 786440 | tf_op jit(solution)/shard_map/ppermute | solution.py:625
  48.7 0.7 %collective-permute-start.9 = (f32[2,256,128]{2,1,0:T(8,128)S(1)}, f32[2,256,128]{2,1,0:T(8,128)S(1)}, u32[]{:S(2)}, u32[]{:S(2)}) collective-permute-start(f32[2,256,128]{2,1,0:T(8,128)S(1)} %get-tuple-element.55), channel_id=1, source_target_pairs={{1,2},{3,4},{5,6},{7,8},{9,10},{11,12},{13,14},{2,1},{4,3},{6,5},{... | collective-permute-start | bytes 786440 | tf_op jit(solution)/shard_map/ppermute | solution.py:626
  49.9 1.5 %collective-permute-done.17.refs_1_ = f32[64,256]{1,0:T(8,128)S(1)} collective-permute-done((f32[64,256]{1,0:T(8,128)S(1)}, f32[64,256]{1,0:T(8,128)S(1)}, u32[]{:S(2)}, u32[]{:S(2)}) %collective-permute-start.17) | collective-permute-done | bytes 65568 | tf_op jit(solution)/shard_map/ppermute | solution.py:437
  51.5 7.8 %collective-permute-done.8.e = f32[2,256,128]{2,1,0:T(8,128)S(1)} collective-permute-done((f32[2,256,128]{2,1,0:T(8,128)S(1)}, f32[2,256,128]{2,1,0:T(8,128)S(1)}, u32[]{:S(2)}, u32[]{:S(2)}) %collective-permute-start.8) | collective-permute-done | bytes 262176 | tf_op jit(solution)/shard_map/ppermute | solution.py:625
  59.4 1.2 %shard_map.114 = f32[4,256,256]{2,1,0:T(8,128)} custom-call(f32[4,256,256]{2,1,0:T(8,128)S(1)} %get-tuple-element.53.total, f32[2,256,128]{2,1,0:T(8,128)S(1)} %collective-permute-done.8.e, f32[2,256,128]{2,1,0:T(8,128)S(1)} %collective-permute-done.9.o), custom_call_target="tpu_custom_call" | custom-call | tf_op jit(solution)/shard_map/pallas_call | solution.py:414
  60.6 0.9 %shard_map.119 = f32[2,256,256]{2,1,0:T(8,128)} custom-call(f32[256,256]{1,0:T(8,128)S(1)} %shard_map.118.full, f32[256,256]{1,0:T(8,128)S(1)} %collective-permute-done.20.other), custom_call_target="tpu_custom_call" | custom-call | tf_op jit(solution)/shard_map/pallas_call | solution.py:414
  (26 shorter events, 2.8 us)
Async XLA Ops:
  2.6 12.1 %collective-permute-start = (f32[4,64,256]{2,1,0:T(8,128)S(1)}, f32[4,64,256]{2,1,0:T(8,128)S(1)}, u32[]{:S(2)}, u32[]{:S(2)}) collective-permute-start(f32[4,64,256]{2,1,0:T(8,128)S(1)} %get-tuple-element.33), channel_id=1, source_target_pairs={{0,16},{16,0},{1,17},{17,1},{2,18},{18,2},{3,19},{19,3},{4,20},{20... | collective-permute-start | bytes 786440 | tf_op jit(solution)/shard_map/ppermute | solution.py:543
  3.2 10.1 %collective-permute-start.3 = (f32[256,128]{1,0:T(8,128)S(1)}, f32[256,128]{1,0:T(8,128)S(1)}, u32[]{:S(2)}, u32[]{:S(2)}) collective-permute-start(f32[256,128]{1,0:T(8,128)S(1)} %get-tuple-element.36), channel_id=1, source_target_pairs={{0,1},{2,3},{4,5},{6,7},{8,9},{10,11},{12,13},{14,15},{1,0},{3,2},... | collective-permute-start | bytes 393224 | tf_op jit(solution)/shard_map/ppermute | solution.py:541
  5.7 7.6 %collective-permute-start.4 = (f32[256,128]{1,0:T(8,128)S(1)}, f32[256,128]{1,0:T(8,128)S(1)}, u32[]{:S(2)}, u32[]{:S(2)}) collective-permute-start(f32[256,128]{1,0:T(8,128)S(1)} %get-tuple-element.37), channel_id=1, source_target_pairs={{1,2},{3,4},{5,6},{7,8},{9,10},{11,12},{13,14},{2,1},{4,3},{6,5},{... | collective-permute-start | bytes 393224 | tf_op jit(solution)/shard_map/ppermute | solution.py:541
  6.4 12.3 %collective-permute-start.1 = (f32[256,128]{1,0:T(8,128)S(1)}, f32[256,128]{1,0:T(8,128)S(1)}, u32[]{:S(2)}, u32[]{:S(2)}) collective-permute-start(f32[256,128]{1,0:T(8,128)S(1)} %get-tuple-element.34), channel_id=1, source_target_pairs={{0,1},{2,3},{4,5},{6,7},{8,9},{10,11},{12,13},{14,15},{1,0},{3,2},... | collective-permute-start | bytes 393224 | tf_op jit(solution)/shard_map/ppermute | solution.py:541
  10.7 8.0 %collective-permute-start.2 = (f32[256,128]{1,0:T(8,128)S(1)}, f32[256,128]{1,0:T(8,128)S(1)}, u32[]{:S(2)}, u32[]{:S(2)}) collective-permute-start(f32[256,128]{1,0:T(8,128)S(1)} %get-tuple-element.35), channel_id=1, source_target_pairs={{1,2},{3,4},{5,6},{7,8},{9,10},{11,12},{13,14},{2,1},{4,3},{6,5},{... | collective-permute-start | bytes 393224 | tf_op jit(solution)/shard_map/ppermute | solution.py:541
  13.3 1.3 %collective-permute-start.5 = (f32[2,64,128]{2,1,0:T(8,128)S(1)}, f32[2,64,128]{2,1,0:T(8,128)S(1)}, u32[]{:S(2)}, u32[]{:S(2)}) collective-permute-start(f32[2,64,128]{2,1,0:T(8,128)S(1)} %shard_map.106), channel_id=1, source_target_pairs={{0,16},{16,0},{1,17},{17,1},{2,18},{18,2},{3,19},{19,3},{4,20},{20... | collective-permute-start | bytes 196616 | tf_op jit(solution)/shard_map/ppermute | solution.py:554
  18.7 1.3 %collective-permute-start.6 = (f32[2,64,128]{2,1,0:T(8,128)S(1)}, f32[2,64,128]{2,1,0:T(8,128)S(1)}, u32[]{:S(2)}, u32[]{:S(2)}) collective-permute-start(f32[2,64,128]{2,1,0:T(8,128)S(1)} %shard_map.109), channel_id=1, source_target_pairs={{0,16},{16,0},{1,17},{17,1},{2,18},{18,2},{3,19},{19,3},{4,20},{20... | collective-permute-start | bytes 196616 | tf_op jit(solution)/shard_map/ppermute | solution.py:554
  24.7 1.6 %collective-permute-start.10 = (f32[256,256]{1,0:T(8,128)S(1)}, f32[256,256]{1,0:T(8,128)S(1)}, u32[]{:S(2)}, u32[]{:S(2)}) collective-permute-start(f32[256,256]{1,0:T(8,128)S(1)} %get-tuple-element.57), channel_id=1, source_target_pairs={{0,16},{16,0},{1,17},{17,1},{2,18},{18,2},{3,19},{19,3},{4,20},{20... | collective-permute-start | bytes 786440 | tf_op jit(solution)/shard_map/ppermute | solution.py:437
  25.8 22.0 %collective-permute-start.7 = (f32[4,64,384]{2,1,0:T(8,128)S(1)}, f32[4,64,384]{2,1,0:T(8,128)S(1)}, u32[]{:S(2)}, u32[]{:S(2)}) collective-permute-start(f32[4,64,384]{2,1,0:T(8,128)S(1)} %get-tuple-element.52), channel_id=1, source_target_pairs={{0,16},{16,0},{1,17},{17,1},{2,18},{18,2},{3,19},{19,3},{4,20},{20... | collective-permute-start | bytes 1179656 | tf_op jit(solution)/shard_map/ppermute | solution.py:616
  26.3 5.1 %collective-permute-start.11 = (f32[64,256]{1,0:T(8,128)S(1)}, f32[64,256]{1,0:T(8,128)S(1)}, u32[]{:S(2)}, u32[]{:S(2)}) collective-permute-start(f32[64,256]{1,0:T(8,128)S(1)} %get-tuple-element.59), channel_id=1, source_target_pairs={{0,1},{1,0},{2,3},{3,2},{4,5},{5,4},{6,7},{7,6},{8,9},{9,8},{10,11... | collective-permute-start | bytes 196616 | tf_op jit(solution)/shard_map/ppermute | solution.py:437
  29.0 4.3 %collective-permute-start.12 = (f32[64,256]{1,0:T(8,128)S(1)}, f32[64,256]{1,0:T(8,128)S(1)}, u32[]{:S(2)}, u32[]{:S(2)}) collective-permute-start(f32[64,256]{1,0:T(8,128)S(1)} %get-tuple-element.60), channel_id=1, source_target_pairs={{0,2},{1,3},{2,0},{3,1},{4,6},{5,7},{6,4},{7,5},{8,10},{9,11},{10,... | collective-permute-start | bytes 196616 | tf_op jit(solution)/shard_map/ppermute | solution.py:437
  30.6 5.2 %collective-permute-start.13 = (f32[64,256]{1,0:T(8,128)S(1)}, f32[64,256]{1,0:T(8,128)S(1)}, u32[]{:S(2)}, u32[]{:S(2)}) collective-permute-start(f32[64,256]{1,0:T(8,128)S(1)} %get-tuple-element.61), channel_id=1, source_target_pairs={{0,3},{1,2},{2,1},{3,0},{4,7},{5,6},{6,5},{7,4},{8,11},{9,10},{10,... | collective-permute-start | bytes 196616 | tf_op jit(solution)/shard_map/ppermute | solution.py:437
  35.7 6.9 %collective-permute-start.16 = (f32[64,256]{1,0:T(8,128)S(1)}, f32[64,256]{1,0:T(8,128)S(1)}, u32[]{:S(2)}, u32[]{:S(2)}) collective-permute-start(f32[64,256]{1,0:T(8,128)S(1)} %shard_map.116.refs_0_), channel_id=1, source_target_pairs={{0,12},{1,13},{2,14},{3,15},{4,8},{5,9},{6,10},{7,11},{8,4},{9,5},... | collective-permute-start | bytes 196616 | tf_op jit(solution)/shard_map/ppermute | solution.py:437
  37.9 6.3 %collective-permute-start.15 = (f32[64,256]{1,0:T(8,128)S(1)}, f32[64,256]{1,0:T(8,128)S(1)}, u32[]{:S(2)}, u32[]{:S(2)}) collective-permute-start(f32[64,256]{1,0:T(8,128)S(1)} %shard_map.116.refs_0_), channel_id=1, source_target_pairs={{0,8},{1,9},{2,10},{3,11},{4,12},{5,13},{6,14},{7,15},{8,0},{9,1},... | collective-permute-start | bytes 196616 | tf_op jit(solution)/shard_map/ppermute | solution.py:437
  38.9 5.4 %collective-permute-start.14 = (f32[64,256]{1,0:T(8,128)S(1)}, f32[64,256]{1,0:T(8,128)S(1)}, u32[]{:S(2)}, u32[]{:S(2)}) collective-permute-start(f32[64,256]{1,0:T(8,128)S(1)} %shard_map.116.refs_0_), channel_id=1, source_target_pairs={{0,4},{1,5},{2,6},{3,7},{4,0},{5,1},{6,2},{7,3},{8,12},{9,13},{10,... | collective-permute-start | bytes 196616 | tf_op jit(solution)/shard_map/ppermute | solution.py:437
  44.3 5.4 %collective-permute-start.19 = (f32[64,256]{1,0:T(8,128)S(1)}, f32[64,256]{1,0:T(8,128)S(1)}, u32[]{:S(2)}, u32[]{:S(2)}) collective-permute-start(f32[64,256]{1,0:T(8,128)S(1)} %shard_map.117.refs_0_), channel_id=1, source_target_pairs={{0,3},{1,2},{2,1},{3,0},{4,7},{5,6},{6,5},{7,4},{8,11},{9,10},{10,... | collective-permute-start | bytes 196616 | tf_op jit(solution)/shard_map/ppermute | solution.py:437
  44.9 5.0 %collective-permute-start.18 = (f32[64,256]{1,0:T(8,128)S(1)}, f32[64,256]{1,0:T(8,128)S(1)}, u32[]{:S(2)}, u32[]{:S(2)}) collective-permute-start(f32[64,256]{1,0:T(8,128)S(1)} %shard_map.117.refs_0_), channel_id=1, source_target_pairs={{0,2},{1,3},{2,0},{3,1},{4,6},{5,7},{6,4},{7,5},{8,10},{9,11},{10,... | collective-permute-start | bytes 196616 | tf_op jit(solution)/shard_map/ppermute | solution.py:437
  46.4 5.0 %collective-permute-start.17 = (f32[64,256]{1,0:T(8,128)S(1)}, f32[64,256]{1,0:T(8,128)S(1)}, u32[]{:S(2)}, u32[]{:S(2)}) collective-permute-start(f32[64,256]{1,0:T(8,128)S(1)} %shard_map.117.refs_0_), channel_id=1, source_target_pairs={{0,1},{1,0},{2,3},{3,2},{4,5},{5,4},{6,7},{7,6},{8,9},{9,8},{10,11... | collective-permute-start | bytes 196616 | tf_op jit(solution)/shard_map/ppermute | solution.py:437
  48.0 11.3 %collective-permute-start.8 = (f32[2,256,128]{2,1,0:T(8,128)S(1)}, f32[2,256,128]{2,1,0:T(8,128)S(1)}, u32[]{:S(2)}, u32[]{:S(2)}) collective-permute-start(f32[2,256,128]{2,1,0:T(8,128)S(1)} %get-tuple-element.54), channel_id=1, source_target_pairs={{0,1},{2,3},{4,5},{6,7},{8,9},{10,11},{12,13},{14,15},{1,0},{3,2},... | collective-permute-start | bytes 786440 | tf_op jit(solution)/shard_map/ppermute | solution.py:625
  48.7 10.6 %collective-permute-start.9 = (f32[2,256,128]{2,1,0:T(8,128)S(1)}, f32[2,256,128]{2,1,0:T(8,128)S(1)}, u32[]{:S(2)}, u32[]{:S(2)}) collective-permute-start(f32[2,256,128]{2,1,0:T(8,128)S(1)} %get-tuple-element.55), channel_id=1, source_target_pairs={{1,2},{3,4},{5,6},{7,8},{9,10},{11,12},{13,14},{2,1},{4,3},{6,5},{... | collective-permute-start | bytes 786440 | tf_op jit(solution)/shard_map/ppermute | solution.py:626
  51.4 9.1 %collective-permute-start.20 = (f32[256,256]{1,0:T(8,128)S(1)}, f32[256,256]{1,0:T(8,128)S(1)}, u32[]{:S(2)}, u32[]{:S(2)}) collective-permute-start(f32[256,256]{1,0:T(8,128)S(1)} %shard_map.118.full), channel_id=1, source_target_pairs={{0,16},{16,0},{1,17},{17,1},{2,18},{18,2},{3,19},{19,3},{4,20},{20... | collective-permute-start | bytes 786440 | tf_op jit(solution)/shard_map/ppermute | solution.py:437

commit v5 on v4

--- a/solution.py
+++ b/solution.py
@@ -80,31 +80,45 @@
 class Dft:
     def __init__(self, mats, tw_left, tw_right, n):
         self.mats, self.n, self.h = mats, n, n // 2
-        self.wl = [cat([tw_left[i], tw_left[i]], 1) for i in range(2)]
-        self.wr = [tw_right[i, 0:1] for i in range(2)]
-
-    def forward(self, x):
-        n, h = self.n, self.h
+        self.tw_left, self.tw_right = tw_left, tw_right
+
+    def wl(self, width):
+        parts = width // self.tw_left.shape[2]
+        return [cat([self.tw_left[i]] * parts, 1) for i in range(2)]
+
+    def wr(self):
+        return [self.tw_right[i, 0:1] for i in range(2)]
+
+    def left(self, x):
+        h, w = self.h, x[0].shape[1]
         total = [p[:h] + p[h:] for p in x]
-        odd = product([p[:h] - p[h:] for p in x], self.wl)
-        y = left_dot(self.mats, 0, cat([cat(total, 0), cat(odd, 0)], 1))
-        x = [cat([y[:h, :n], y[:h, n:]], 0), cat([y[h:, :n], y[h:, n:]], 0)]
+        odd = product([p[:h] - p[h:] for p in x], self.wl(w))
+        u = left_dot(self.mats, 0, cat(total, 0))
+        v = left_dot(self.mats, 0, cat(odd, 0))
+        return [cat([u[:h], v[:h]], 0), cat([u[h:], v[h:]], 0)]
+
+    def right(self, x):
+        h, m = self.h, x[0].shape[0]
         total = [p[:, :h] + p[:, h:] for p in x]
-        odd = product([p[:, :h] - p[:, h:] for p in x], self.wr)
-        y = right_dot(cat([cat(total, 1), cat(odd, 1)], 0), self.mats, 2)
-        return [cat([y[:n, :h], y[n:, :h]], 1), cat([y[:n, h:], y[n:, h:]], 1)]
-
-    def inverse(self, x):
-        n, h = self.n, self.h
-        y = cat([cat([p[:, :h] for p in x], 1), cat([p[:, h:] for p in x], 1)], 0)
-        y = right_dot(y, self.mats, 0)
-        even = [y[:n, :h], y[:n, h:]]
-        odd = conj_product(self.wr, [y[n:, :h], y[n:, h:]])
-        x = [cat([e + o, e - o], 1) for e, o in zip(even, odd)]
-        y = cat([cat([p[:h] for p in x], 0), cat([p[h:] for p in x], 0)], 1)
-        y = left_dot(self.mats, 2, y)
-        even = [y[:h, :n], y[h:, :n]]
-        odd = conj_product(self.wl, [y[:h, n:], y[h:, n:]])
+        odd = product([p[:, :h] - p[:, h:] for p in x], self.wr())
+        u = right_dot(cat(total, 1), self.mats, 2)
+        v = right_dot(cat(odd, 1), self.mats, 2)
+        return [cat([u[:, :h], v[:, :h]], 1), cat([u[:, h:], v[:, h:]], 1)]
+
+    def right_inverse(self, x):
+        h, m = self.h, x[0].shape[0]
+        u = right_dot(cat([p[:, :h] for p in x], 1), self.mats, 0)
+        v = right_dot(cat([p[:, h:] for p in x], 1), self.mats, 0)
+        even = [u[:, :h], u[:, h:]]
+        odd = conj_product(self.wr(), [v[:, :h], v[:, h:]])
+        return [cat([e + o, e - o], 1) for e, o in zip(even, odd)]
+
+    def left_inverse(self, x):
+        h, w = self.h, x[0].shape[1]
+        u = left_dot(self.mats, 2, cat([p[:h] for p in x], 0))
+        v = left_dot(self.mats, 2, cat([p[h:] for p in x], 0))
+        even = [u[:h], u[h:]]
+        odd = conj_product(self.wl(w), [v[:h], v[h:]])
         return [cat([e + o, e - o], 0) for e, o in zip(even, odd)]
 
 
@@ -161,7 +175,7 @@
     return pl.multiple_of(jnp.where(last, n - margin, 0), 8)
 
 
-def pack_kernel(margin, obj_hbm, offs_hbm, obj, offs, *refs):
+def pack_kernel(margin, obj_hbm, offs_hbm, obj, offs, limits, *refs):
     strips, rows, sems = refs[:4], refs[4:-1], refs[-1]
     n = obj.shape[1]
     copies = copy_all(
@@ -176,6 +190,8 @@
     for which, out in enumerate(rows):
         out[...] = obj[:, pl.ds(row_start(which, n, margin), margin), :]
     copies[2].wait()
+    for i in range(2):
+        limits[i] = jnp.full(limits.shape[1:], offs[0, i] - margin, jnp.int32)
 
 
 def corner_kernel(margin, e, o, after, *outs):
@@ -196,14 +212,16 @@
 
 
 def prep_kernel(*refs):
-    hbm, (kr, ki), loaded = refs[:7], refs[7:9], refs[9:15]
-    phase, sems = refs[15:]
-    copies = copy_all(hbm, (phase,) + loaded, sems)
+    hbm, (kr, ki, am), loaded = refs[:7], refs[7:10], refs[10:14]
+    phase, order, amps, sems = refs[14:]
+    copies = copy_all(hbm, (phase, order, amps) + loaded, sems)
     copies[0].wait()
     copies[1].wait()
-    angle = reorder(phase[...], loaded[0])
+    angle = reorder(phase[...], order)
     kr[...], ki[...] = cos_sin(angle)
-    for copy in copies[2:]:
+    copies[2].wait()
+    am[...] = reorder(amps[...], order)
+    for copy in copies[3:]:
         copy.wait()
 
 
@@ -215,16 +233,14 @@
         pr[i] = dyn_roll(dyn_roll(probe[i], sy, 0), sx, 1)
 
 
-def reorder_kernel(x, order, after, out):
-    out[...] = reorder(x[...], order)
-
-
-def merge_cols(own, low, high, ox, margin):
+def merge_cols(own, e, o, limits):
     n = own[0].shape[1]
     h = n // 2
-    lane = iota((own[0].shape[0], h), 1)
-    from_high = lane < ox - margin
-    from_low = lane + h >= ox + n - margin
+    even = lax.axis_index("col") % 2 == 0
+    high, low = jnp.where(even, e, o), jnp.where(even, o, e)
+    lane = iota((1, h), 1)
+    from_high = lane < limits[1, 0:1]
+    from_low = lane >= limits[1, 0:1] + h
     out = []
     for i in range(2):
         strip_high = high if i == 0 else half_roll(high)
@@ -241,36 +257,33 @@
     return out
 
 
-def window_of(obj, s, halos, corners, strip_e, strip_o, offs, margin):
-    n = obj.shape[1]
-    oy, ox = offs[0, 0], offs[0, 1]
-    col_even = lax.axis_index("col") % 2 == 0
+def merge_kernel(s, obj, e, o, limits, out):
+    own = [obj[2 * s], obj[2 * s + 1]]
+    out[0], out[1] = merge_cols(own, e[...], o[...], limits)
+
+
+def window_of(main, s, halos, corners, limits, margin):
+    n = main.shape[1]
     row_even = lax.axis_index("row") % 2 == 0
     blocks = []
-    sides = [(strip_e, strip_o)] + [(c.at[0], c.at[1]) for c in corners]
-    for source, (e, o) in zip([obj] + list(halos), sides):
-        e, o = e[...], o[...]
-        high, low = jnp.where(col_even, e, o), jnp.where(col_even, o, e)
-        blocks.append(merge_cols([source[2 * s], source[2 * s + 1]], low, high, ox, margin))
+    for halo, corner in zip(halos, corners):
+        own = [halo[2 * s], halo[2 * s + 1]]
+        blocks.append(merge_cols(own, corner[0], corner[1], limits))
     row = iota((margin, n), 0)
-    take_high = row < oy - margin
-    take_low = row + n - margin >= oy + n - margin
+    limit = cat([limits[0, 0:1]] * 2, 1)
+    take_high = row < limit
+    take_low = row >= limit + margin
     out = []
     for i in range(2):
-        main = blocks[0][i]
-        if len(blocks) == 3:
-            e, o = blocks[1][i], blocks[2][i]
-            high, low = jnp.where(row_even, e, o), jnp.where(row_even, o, e)
-        else:
-            e = blocks[1][i]
-            zero = jnp.zeros_like(e)
-            high, low = jnp.where(row_even, e, zero), jnp.where(row_even, zero, e)
+        e = blocks[0][i]
+        o = blocks[1][i] if len(blocks) == 2 else jnp.zeros_like(e)
+        high, low = jnp.where(row_even, e, o), jnp.where(row_even, o, e)
         out.append(
             cat(
                 [
-                    jnp.where(take_high, high, main[:margin]),
-                    main[margin : n - margin],
-                    jnp.where(take_low, low, main[n - margin :]),
+                    jnp.where(take_high, high, main[i, :margin]),
+                    main[i, margin : n - margin],
+                    jnp.where(take_low, low, main[i, n - margin :]),
                 ],
                 0,
             )
@@ -282,37 +295,70 @@
     return refs[0], refs[1 : 1 + n_row], refs[1 + n_row : 1 + 2 * n_row], refs[1 + 2 * n_row :]
 
 
+def through(dft, x, re, im):
+    return dft.right_inverse(product([re, im], dft.right(x)))
+
+
 def arrive_kernel(n_row, margin, *refs):
-    obj, halos, corners, refs = unpack(n_row, refs)
-    e1, o1, offs, pr, kr, ki, mats, twl, twr, w1, arrive = refs
-    n = obj.shape[1]
+    main, halos, corners, refs = unpack(n_row, refs)
+    limits, pr, kr, ki, mats, twl, twr, w1, arrive = refs
+    n = main.shape[1]
     dft = Dft(mats, twl[...], twr[...], n)
-    win = window_of(obj, 0, halos, corners, e1, o1, offs, margin)
+    win = window_of(main, 0, halos, corners, limits, margin)
     w1[0], w1[1] = win
-    x = dft.forward(product([pr[0], pr[1]], win))
-    x = dft.inverse(product([kr[...], ki[...]], x))
-    arrive[0], arrive[1] = x
-
-
-def divide_kernel(margin, grads, offs, own, strip, *sends):
+    x = dft.left(product([pr[0], pr[1]], win))
+    x = through(dft, x, kr[...], ki[...])
+    arrive[0], arrive[1] = dft.left_inverse(x)
+
+
+def back_kernel(n_row, margin, *refs):
+    main, halos, corners, refs = unpack(n_row, refs)
+    limits, offs_hbm, pr, kr, ki, am, w1, arrive, mats, twl, twr = refs[:11]
+    keep, give, grads, offs, sem = refs[11:]
+    scalars = pltpu.make_async_copy(offs_hbm, offs, sem)
+    scalars.start()
+    n = main.shape[1]
+    dft = Dft(mats, twl[...], twr[...], n)
+    win = window_of(main, 1, halos, corners, limits, margin)
+    x = dft.left(product([arrive[0], arrive[1]], win))
+    far = dft.right(x)
+    modulus = jnp.sqrt(far[0] * far[0] + far[1] * far[1] + EPS_AMP)
+    factor = 2.0 * (1.0 - am[...] / modulus)
+    x = dft.right_inverse([factor * far[0], factor * far[1]])
+    back_far = dft.left_inverse(x)
+    grads[2], grads[3] = conj_product([arrive[0], arrive[1]], back_far)
+    x = dft.left(conj_product(win, back_far))
+    x = through(dft, x, kr[...], -ki[...])
+    x = dft.left_inverse(x)
+    grads[0], grads[1] = conj_product([pr[0], pr[1]], x)
+    grad = conj_product([w1[0], w1[1]], x)
+    scalars.wait()
+    sy = (margin - offs[0, 0] + n) % n
+    sx = (margin - offs[0, 1] + n) % n
+    grad = [dyn_roll(dyn_roll(g, sy, 0), sx, 1) for g in grad]
+    even = lax.axis_index("row") % 2 == 0
+    keep[...] = jnp.where(even, grad[0], grad[1])
+    give[...] = jnp.where(even, grad[1], grad[0])
+
+
+def divide_kernel(margin, grads, limits, own, strip, *sends):
     for s in range(2):
-        split_grad([grads[2 * s], grads[2 * s + 1]], s, offs, margin, own, strip, sends)
-
-
-def split_grad(grad, s, offs, margin, own, strip, sends):
+        split_grad([grads[2 * s], grads[2 * s + 1]], s, limits, margin, own, strip, sends)
+
+
+def split_grad(grad, s, limits, margin, own, strip, sends):
     n = grad[0].shape[0]
     h = n // 2
-    oy, ox = offs[0, 0], offs[0, 1]
     row_even = lax.axis_index("row") % 2 == 0
     lane = iota((1, h), 1)
-    to_high, to_low = lane < ox - margin, lane + h >= ox + n - margin
+    to_high, to_low = lane < limits[1, 0:1], lane >= limits[1, 0:1] + h
     front = lane < h // 2
     spill = jnp.where(front, to_high.astype(jnp.int32), to_low.astype(jnp.int32)) != 0
     for i in range(2):
         g = grad[i]
         row = iota((n, h), 0)
-        high_rows = row < oy - margin
-        low_rows = row >= oy + n - margin
+        high_rows = row < limits[0, 0:1]
+        low_rows = row >= limits[0, 0:1] + n
         inner = jnp.logical_not(jnp.logical_or(high_rows, low_rows))
         left = jnp.where(to_high, 0.0, g[:, :h])
         right = jnp.where(to_low, 0.0, g[:, h:])
@@ -327,32 +373,6 @@
             for which, send in enumerate(sends):
                 first = row_even if which == 0 else jnp.logical_not(row_even)
                 send[2 * s + i, :, j * h : (j + 1) * h] = jnp.where(first, top, bottom)
-
-
-def back_kernel(n_row, margin, *refs):
-    obj, halos, corners, refs = unpack(n_row, refs)
-    e2, o2, offs, pr, kr, ki, am, w1, arrive, mats, twl, twr = refs[:12]
-    outs = refs[12:]
-    keep, give, grads = outs
-    n = obj.shape[1]
-    dft = Dft(mats, twl[...], twr[...], n)
-    win = window_of(obj, 1, halos, corners, e2, o2, offs, margin)
-    arr = [arrive[0], arrive[1]]
-    far = dft.forward(product(arr, win))
-    modulus = jnp.sqrt(far[0] * far[0] + far[1] * far[1] + EPS_AMP)
-    factor = 2.0 * (1.0 - am[...] / modulus)
-    back_far = dft.inverse([factor * far[0], factor * far[1]])
-    grads[2], grads[3] = conj_product(arr, back_far)
-    x = dft.forward(conj_product(win, back_far))
-    x = dft.inverse(conj_product([kr[...], ki[...]], x))
-    grads[0], grads[1] = conj_product([pr[0], pr[1]], x)
-    grad = conj_product([w1[0], w1[1]], x)
-    sy = (margin - offs[0, 0] + n) % n
-    sx = (margin - offs[0, 1] + n) % n
-    grad = [dyn_roll(dyn_roll(g, sy, 0), sx, 1) for g in grad]
-    even = lax.axis_index("row") % 2 == 0
-    keep[...] = jnp.where(even, grad[0], grad[1])
-    give[...] = jnp.where(even, grad[1], grad[0])
 
 
 def fold_rows_kernel(n_row, margin, own, strip, *refs):
@@ -415,7 +435,7 @@
         kernel,
         out_shape=shapes,
         in_specs=in_specs,
-        out_specs=[VMEM if s.dtype != jnp.int32 else SMEM for s in shapes],
+        out_specs=[SMEM if s.shape == (1, 2) else VMEM for s in shapes],
         scratch_shapes=list(scratch),
         compiler_params=pltpu.CompilerParams(vmem_limit_bytes=mib << 20),
     )(*args)
@@ -526,9 +546,10 @@
 
     row_rounds, col_rounds = edges("row"), edges("col")
     n_row = len(row_rounds)
-    obj, offs, *packed = call(
+    obj, offs, limits, *packed = call(
         functools.partial(pack_kernel, margin),
         [(4, n, n), jax.ShapeDtypeStruct((1, 2), jnp.int32)]
+        + [jax.ShapeDtypeStruct((2, 8, h), jnp.int32)]
         + [(n, h)] * 4
         + [(4, margin, n)] * n_row,
         [HBM, HBM],
@@ -553,26 +574,41 @@
         for i, pairs in enumerate(row_rounds):
             corners[s].append(lax.ppermute(parts[i], "row", pairs))
 
-    loads = (phase, order, mats, tw_left, tw_right, probe, amplitudes.reshape(n, n))
-    kr, ki, order, mats, tw_left, tw_right, pr, am = call(
+    def merge(s):
+        (main,) = call(
+            functools.partial(merge_kernel, s),
+            [(2, n, n)],
+            [VMEM] * 4,
+            obj,
+            *strips[2 * s : 2 * s + 2],
+            limits,
+        )
+        return main
+
+    loads = (phase, order, amplitudes.reshape(n, n), mats, tw_left, tw_right, probe)
+    kr, ki, am, mats, tw_left, tw_right, pr = call(
         prep_kernel,
-        [(n, n), (n, n)] + [jax.ShapeDtypeStruct(x.shape, x.dtype) for x in loads[1:]],
+        [(n, n)] * 3 + [jax.ShapeDtypeStruct(x.shape, x.dtype) for x in loads[3:]],
         [HBM] * len(loads),
         *[in_hbm(x) for x in loads],
-        scratch=[pltpu.VMEM((n, n), F32), pltpu.SemaphoreType.DMA((len(loads),))],
+        scratch=[
+            pltpu.VMEM((n, n), F32),
+            pltpu.VMEM((2, n, n), BF16),
+            pltpu.VMEM((n, n), F32),
+            pltpu.SemaphoreType.DMA((len(loads),)),
+        ],
     )
     cut(0, kr)
     (pr,) = call(functools.partial(roll_kernel, margin), [(2, n, n)], [SMEM, VMEM], offs, pr)
+    main = merge(0)
     w1, arrive = call(
         functools.partial(arrive_kernel, n_row, margin),
         [(2, n, n), (2, n, n)],
-        [VMEM] * (3 + 2 * n_row) + [SMEM] + [VMEM] * 6,
-        obj,
+        [VMEM] * (8 + 2 * n_row),
+        main,
         *halos,
         *corners[0],
-        strips[0],
-        strips[1],
-        offs,
+        limits,
         pr,
         kr,
         ki,
@@ -581,17 +617,16 @@
         tw_right,
     )
     cut(1, arrive)
-    (am,) = call(reorder_kernel, [(n, n)], [VMEM] * 3, am, order, arrive)
+    main = merge(1)
     keep, give, grads = call(
         functools.partial(back_kernel, n_row, margin),
         [(n, n), (n, n), (4, n, n)],
-        [VMEM] * (3 + 2 * n_row) + [SMEM] + [VMEM] * 9,
-        obj,
+        [VMEM] * (2 + 2 * n_row) + [HBM] + [VMEM] * 9,
+        main,
         *halos,
         *corners[1],
-        strips[2],
-        strips[3],
-        offs,
+        limits,
+        in_hbm(offsets.reshape(1, 2)),
         pr,
         kr,
         ki,
@@ -601,15 +636,16 @@
         mats,
         tw_left,
         tw_right,
+        scratch=[pltpu.SMEM((1, 2), jnp.int32), pltpu.SemaphoreType.DMA(())],
         mib=40,
     )
     probe_grad = reduce_probe(keep, give)
     own, strip, *sends = call(
         functools.partial(divide_kernel, margin),
         [(4, n, n), (4, n, h)] + [(4, margin, n + h)] * n_row,
-        [VMEM, SMEM],
+        [VMEM, VMEM],
         grads,
-        offs,
+        limits,
     )
     got = []
     for i, pairs in enumerate(row_rounds):

time: 62 us -> 60.2 us (0.971)
  Pallas kernels: 15.6 us -> 13.4 us
  waiting for transfers between devices: 21.8 us -> 22.5 us
    pallas_call x16 -> x17, Pallas kernels: 15.6 us -> 13.4 us  [call(): pl.pallas_call(kernel, out_shape=shapes, in_specs=in_specs, out_specs=[SM...]
  transfers between devices with their start and end apart: 21 -> 21, of which waited for: 12 -> 12; matrix products, arithmetic and copies ran while one was open for 0% -> 0% of each run, Pallas kernels for 13% -> 12%
where the time goes in v5:
time: 60.2 us; the launch traced here: 59.9 us
  starting transfers between devices  23.2 us (39%)
  waiting for transfers between devices  22.5 us (37%)
  Pallas kernels  13.4 us (22%)
  between operations  0.79 us (1%)
    pallas_call x17, Pallas kernels, call(): pl.pallas_call(kernel, out_shape=shapes, in_specs=in_specs, out_specs=[SM...  13.4 us
    ppermute x11, starting transfers between devices, swap(): return lax.ppermute(value, axis, [(i, i ^ distance) for i in range(count)])  12.4 us
    ppermute x11, waiting for transfers between devices, swap(): return lax.ppermute(value, axis, [(i, i ^ distance) for i in range(count)])  11.8 us
    ppermute x4, starting transfers between devices, whole(): strips.append(lax.ppermute(packed[i], 'col', col_rounds[i % 2]))  8.15 us
    ppermute x1, waiting for transfers between devices, whole(): send_e = lax.ppermute(send_e, 'col', col_rounds[0])  7.47 us
    ppermute x4, waiting for transfers between devices, whole(): strips.append(lax.ppermute(packed[i], 'col', col_rounds[i % 2]))  1.88 us
    ppermute x2, waiting for transfers between devices, cut(): corners[s].append(lax.ppermute(parts[i], 'row', pairs))  1.37 us
  transfers between devices with their start and end apart: 21, of which 12 were waited for; matrix products, arithmetic and copies ran while one was open for 0% of the time, Pallas kernels for 12%

profile of v5, /device:TPU:0, one launch (start us, length us, event | category | flops | bytes accessed | tf_op | source)
XLA Modules:
  0.0 59.9 jit_solution(12554227454953406873)
XLA Ops:
  0.6 2.0 %shard_map.104 = (f32[4,256,256]{2,1,0:T(8,128)S(1)}, s32[1,2]{1,0:T(1,128)S(1)}, s32[2,8,128]{2,1,0:T(8,128)S(1)}, f32[256,128]{1,0:T(8,128)S(1)}, f32[256,128]...) custom-call(f32[4,256,256]{2,1,0:T(8,128)} %bitcast.4, s32[1,2]{1,0:T(1,128)} %bitcast.7), custom_call_target="tpu_custom_call" | custom-call | tf_op jit(solution)/shard_map/pallas_call | solution.py:434
  3.2 2.6 %collective-permute-start.3 = (f32[256,128]{1,0:T(8,128)S(1)}, f32[256,128]{1,0:T(8,128)S(1)}, u32[]{:S(2)}, u32[]{:S(2)}) collective-permute-start(f32[256,128]{1,0:T(8,128)S(1)} %get-tuple-element.37), channel_id=1, source_target_pairs={{0,1},{2,3},{4,5},{6,7},{8,9},{10,11},{12,13},{14,15},{1,0},{3,2},... | collective-permute-start | bytes 393224 | tf_op jit(solution)/shard_map/ppermute | solution.py:562
  5.7 0.7 %collective-permute-start.4 = (f32[256,128]{1,0:T(8,128)S(1)}, f32[256,128]{1,0:T(8,128)S(1)}, u32[]{:S(2)}, u32[]{:S(2)}) collective-permute-start(f32[256,128]{1,0:T(8,128)S(1)} %get-tuple-element.38), channel_id=1, source_target_pairs={{1,2},{3,4},{5,6},{7,8},{9,10},{11,12},{13,14},{2,1},{4,3},{6,5},{... | collective-permute-start | bytes 393224 | tf_op jit(solution)/shard_map/ppermute | solution.py:562
  6.4 4.3 %collective-permute-start = (f32[256,128]{1,0:T(8,128)S(1)}, f32[256,128]{1,0:T(8,128)S(1)}, u32[]{:S(2)}, u32[]{:S(2)}) collective-permute-start(f32[256,128]{1,0:T(8,128)S(1)} %get-tuple-element.33), channel_id=1, source_target_pairs={{0,1},{2,3},{4,5},{6,7},{8,9},{10,11},{12,13},{14,15},{1,0},{3,2},... | collective-permute-start | bytes 393224 | tf_op jit(solution)/shard_map/ppermute | solution.py:562
  10.7 0.7 %collective-permute-start.1 = (f32[256,128]{1,0:T(8,128)S(1)}, f32[256,128]{1,0:T(8,128)S(1)}, u32[]{:S(2)}, u32[]{:S(2)}) collective-permute-start(f32[256,128]{1,0:T(8,128)S(1)} %get-tuple-element.34), channel_id=1, source_target_pairs={{1,2},{3,4},{5,6},{7,8},{9,10},{11,12},{13,14},{2,1},{4,3},{6,5},{... | collective-permute-start | bytes 393224 | tf_op jit(solution)/shard_map/ppermute | solution.py:562
  11.3 2.6 %shard_map.107 = (f32[256,256]{1,0:T(8,128)S(1)}, f32[256,256]{1,0:T(8,128)S(1)}, f32[256,256]{1,0:T(8,128)S(1)}, bf16[4,256,256]{2,1,0:T(8,128)(2,1)S(1)}, f32[...) custom-call(f32[256,256]{1,0:T(8,128)} %refs_0_.1, ...), custom_call_target="tpu_custom_call" | custom-call | tf_op jit(solution)/shard_map/pallas_call | solution.py:434
  14.1 0.8 %shard_map.109.refs_4_.refs_5_ = f32[2,256,256]{2,1,0:T(8,128)S(1)} custom-call(s32[1,2]{1,0:T(1,128)S(1)} %get-tuple-element.40.offs, f32[2,256,256]{2,1,0:T(8,128)S(1)} %get-tuple-element.41.probe), custom_call_target="tpu_custom_call" | custom-call | tf_op jit(solution)/shard_map/pallas_call | solution.py:434
  15.3 1.5 %shard_map.110 = (f32[2,256,256]{2,1,0:T(8,128)S(1)}, f32[2,256,256]{2,1,0:T(8,128)S(1)}) custom-call(f32[2,256,256]{2,1,0:T(8,128)S(1)} %shard_map.106.refs_0_, f32[4,64,256]{2,1,0:T(8,128)S(1)} %collective-permute-done.2.refs_1_, f32[2,64,128]{2,1,0:T(8,128)S(1)} %collective-permute-done.5.refs_2_, s32[2,8,128]{2,1,0:T(8,128)S(1)} %get-tuple-element.35.limits.refs_3_, ...), custom_call_target="tpu_custom_call" | custom-call | tf_op jit(solution)/shard_map/pallas_call | solution.py:434
  16.8 1.9 %collective-permute-done.e = f32[256,128]{1,0:T(8,128)S(1)} collective-permute-done((f32[256,128]{1,0:T(8,128)S(1)}, f32[256,128]{1,0:T(8,128)S(1)}, u32[]{:S(2)}, u32[]{:S(2)}) %collective-permute-start) | collective-permute-done | bytes 131104 | tf_op jit(solution)/shard_map/ppermute | solution.py:562
  18.9 1.1 %collective-permute-done.6.refs_2_ = f32[2,64,128]{2,1,0:T(8,128)S(1)} collective-permute-done((f32[2,64,128]{2,1,0:T(8,128)S(1)}, f32[2,64,128]{2,1,0:T(8,128)S(1)}, u32[]{:S(2)}, u32[]{:S(2)}) %collective-permute-start.6) | collective-permute-done | bytes 65568 | tf_op jit(solution)/shard_map/ppermute | solution.py:575
  20.0 3.5 %shard_map.112 = (f32[256,256]{1,0:T(8,128)S(1)}, f32[256,256]{1,0:T(8,128)S(1)}, f32[4,256,256]{2,1,0:T(8,128)S(1)}) custom-call(f32[2,256,256]{2,1,0:T(8,128)S(1)} %shard_map.105.refs_0_, f32[4,64,256]{2,1,0:T(8,128)S(1)} %collective-permute-done.2.refs_1_, f32[2,64,128]{2,1,0:T(8,128)S(1)} %collective-permute-done.6.refs_2_, ...), custom_call_target="tpu_custom_call" | custom-call | tf_op jit(solution)/shard_map/pallas_call | solution.py:434
  24.6 0.6 collective-permute-done.10.other
  25.2 2.5 %collective-permute-start.11 = (f32[64,256]{1,0:T(8,128)S(1)}, f32[64,256]{1,0:T(8,128)S(1)}, u32[]{:S(2)}, u32[]{:S(2)}) collective-permute-start(f32[64,256]{1,0:T(8,128)S(1)} %get-tuple-element.59), channel_id=1, source_target_pairs={{0,1},{1,0},{2,3},{3,2},{4,5},{5,4},{6,7},{7,6},{8,9},{9,8},{10,11... | collective-permute-start | bytes 196616 | tf_op jit(solution)/shard_map/ppermute | solution.py:457
  27.8 1.4 %collective-permute-start.12 = (f32[64,256]{1,0:T(8,128)S(1)}, f32[64,256]{1,0:T(8,128)S(1)}, u32[]{:S(2)}, u32[]{:S(2)}) collective-permute-start(f32[64,256]{1,0:T(8,128)S(1)} %get-tuple-element.60), channel_id=1, source_target_pairs={{0,2},{1,3},{2,0},{3,1},{4,6},{5,7},{6,4},{7,5},{8,10},{9,11},{10,... | collective-permute-start | bytes 196616 | tf_op jit(solution)/shard_map/ppermute | solution.py:457
  29.3 0.9 %collective-permute-done.11.refs_1_ = f32[64,256]{1,0:T(8,128)S(1)} collective-permute-done((f32[64,256]{1,0:T(8,128)S(1)}, f32[64,256]{1,0:T(8,128)S(1)}, u32[]{:S(2)}, u32[]{:S(2)}) %collective-permute-start.11) | collective-permute-done | bytes 65568 | tf_op jit(solution)/shard_map/ppermute | solution.py:457
  30.2 1.9 %collective-permute-done.12.refs_2_ = f32[64,256]{1,0:T(8,128)S(1)} collective-permute-done((f32[64,256]{1,0:T(8,128)S(1)}, f32[64,256]{1,0:T(8,128)S(1)}, u32[]{:S(2)}, u32[]{:S(2)}) %collective-permute-start.12) | collective-permute-done | bytes 65568 | tf_op jit(solution)/shard_map/ppermute | solution.py:457
  32.0 2.3 %collective-permute-done.13.refs_3_ = f32[64,256]{1,0:T(8,128)S(1)} collective-permute-done((f32[64,256]{1,0:T(8,128)S(1)}, f32[64,256]{1,0:T(8,128)S(1)}, u32[]{:S(2)}, u32[]{:S(2)}) %collective-permute-start.13) | collective-permute-done | bytes 65568 | tf_op jit(solution)/shard_map/ppermute | solution.py:457
  34.4 2.4 %collective-permute-start.16 = (f32[64,256]{1,0:T(8,128)S(1)}, f32[64,256]{1,0:T(8,128)S(1)}, u32[]{:S(2)}, u32[]{:S(2)}) collective-permute-start(f32[64,256]{1,0:T(8,128)S(1)} %shard_map.117.refs_0_), channel_id=1, source_target_pairs={{0,12},{1,13},{2,14},{3,15},{4,8},{5,9},{6,10},{7,11},{8,4},{9,5},... | collective-permute-start | bytes 196616 | tf_op jit(solution)/shard_map/ppermute | solution.py:457
  36.8 0.7 %collective-permute-start.15 = (f32[64,256]{1,0:T(8,128)S(1)}, f32[64,256]{1,0:T(8,128)S(1)}, u32[]{:S(2)}, u32[]{:S(2)}) collective-permute-start(f32[64,256]{1,0:T(8,128)S(1)} %shard_map.117.refs_0_), channel_id=1, source_target_pairs={{0,8},{1,9},{2,10},{3,11},{4,12},{5,13},{6,14},{7,15},{8,0},{9,1},... | collective-permute-start | bytes 196616 | tf_op jit(solution)/shard_map/ppermute | solution.py:457
  37.5 1.3 %collective-permute-start.14 = (f32[64,256]{1,0:T(8,128)S(1)}, f32[64,256]{1,0:T(8,128)S(1)}, u32[]{:S(2)}, u32[]{:S(2)}) collective-permute-start(f32[64,256]{1,0:T(8,128)S(1)} %shard_map.117.refs_0_), channel_id=1, source_target_pairs={{0,4},{1,5},{2,6},{3,7},{4,0},{5,1},{6,2},{7,3},{8,12},{9,13},{10,... | collective-permute-start | bytes 196616 | tf_op jit(solution)/shard_map/ppermute | solution.py:457
  38.8 2.1 %collective-permute-done.16.refs_3_ = f32[64,256]{1,0:T(8,128)S(1)} collective-permute-done((f32[64,256]{1,0:T(8,128)S(1)}, f32[64,256]{1,0:T(8,128)S(1)}, u32[]{:S(2)}, u32[]{:S(2)}) %collective-permute-start.16) | collective-permute-done | bytes 65568 | tf_op jit(solution)/shard_map/ppermute | solution.py:457
  40.9 2.1 %collective-permute-done.15.refs_2_ = f32[64,256]{1,0:T(8,128)S(1)} collective-permute-done((f32[64,256]{1,0:T(8,128)S(1)}, f32[64,256]{1,0:T(8,128)S(1)}, u32[]{:S(2)}, u32[]{:S(2)}) %collective-permute-start.15) | collective-permute-done | bytes 65568 | tf_op jit(solution)/shard_map/ppermute | solution.py:457
  43.0 0.8 %collective-permute-start.19 = (f32[64,256]{1,0:T(8,128)S(1)}, f32[64,256]{1,0:T(8,128)S(1)}, u32[]{:S(2)}, u32[]{:S(2)}) collective-permute-start(f32[64,256]{1,0:T(8,128)S(1)} %shard_map.118.refs_0_), channel_id=1, source_target_pairs={{0,3},{1,2},{2,1},{3,0},{4,7},{5,6},{6,5},{7,4},{8,11},{9,10},{10,... | collective-permute-start | bytes 196616 | tf_op jit(solution)/shard_map/ppermute | solution.py:457
  43.7 1.6 %collective-permute-start.18 = (f32[64,256]{1,0:T(8,128)S(1)}, f32[64,256]{1,0:T(8,128)S(1)}, u32[]{:S(2)}, u32[]{:S(2)}) collective-permute-start(f32[64,256]{1,0:T(8,128)S(1)} %shard_map.118.refs_0_), channel_id=1, source_target_pairs={{0,2},{1,3},{2,0},{3,1},{4,6},{5,7},{6,4},{7,5},{8,10},{9,11},{10,... | collective-permute-start | bytes 196616 | tf_op jit(solution)/shard_map/ppermute | solution.py:457
  45.3 1.2 %collective-permute-start.17 = (f32[64,256]{1,0:T(8,128)S(1)}, f32[64,256]{1,0:T(8,128)S(1)}, u32[]{:S(2)}, u32[]{:S(2)}) collective-permute-start(f32[64,256]{1,0:T(8,128)S(1)} %shard_map.118.refs_0_), channel_id=1, source_target_pairs={{0,1},{1,0},{2,3},{3,2},{4,5},{5,4},{6,7},{7,6},{8,9},{9,8},{10,11... | collective-permute-start | bytes 196616 | tf_op jit(solution)/shard_map/ppermute | solution.py:457
  46.7 0.9 %collective-permute-start.8 = (f32[2,256,128]{2,1,0:T(8,128)S(1)}, f32[2,256,128]{2,1,0:T(8,128)S(1)}, u32[]{:S(2)}, u32[]{:S(2)}) collective-permute-start(f32[2,256,128]{2,1,0:T(8,128)S(1)} %get-tuple-element.54), channel_id=1, source_target_pairs={{0,1},{2,3},{4,5},{6,7},{8,9},{10,11},{12,13},{14,15},{1,0},{3,2},... | collective-permute-start | bytes 786440 | tf_op jit(solution)/shard_map/ppermute | solution.py:661
  47.6 0.7 %collective-permute-start.9 = (f32[2,256,128]{2,1,0:T(8,128)S(1)}, f32[2,256,128]{2,1,0:T(8,128)S(1)}, u32[]{:S(2)}, u32[]{:S(2)}) collective-permute-start(f32[2,256,128]{2,1,0:T(8,128)S(1)} %get-tuple-element.55), channel_id=1, source_target_pairs={{1,2},{3,4},{5,6},{7,8},{9,10},{11,12},{13,14},{2,1},{4,3},{6,5},{... | collective-permute-start | bytes 786440 | tf_op jit(solution)/shard_map/ppermute | solution.py:662
  48.3 0.7 %collective-permute-done.19.refs_3_ = f32[64,256]{1,0:T(8,128)S(1)} collective-permute-done((f32[64,256]{1,0:T(8,128)S(1)}, f32[64,256]{1,0:T(8,128)S(1)}, u32[]{:S(2)}, u32[]{:S(2)}) %collective-permute-start.19) | collective-permute-done | bytes 65568 | tf_op jit(solution)/shard_map/ppermute | solution.py:457
  48.9 1.4 %collective-permute-done.17.refs_1_ = f32[64,256]{1,0:T(8,128)S(1)} collective-permute-done((f32[64,256]{1,0:T(8,128)S(1)}, f32[64,256]{1,0:T(8,128)S(1)}, u32[]{:S(2)}, u32[]{:S(2)}) %collective-permute-start.17) | collective-permute-done | bytes 65568 | tf_op jit(solution)/shard_map/ppermute | solution.py:457
  50.4 7.5 %collective-permute-done.8.e = f32[2,256,128]{2,1,0:T(8,128)S(1)} collective-permute-done((f32[2,256,128]{2,1,0:T(8,128)S(1)}, f32[2,256,128]{2,1,0:T(8,128)S(1)}, u32[]{:S(2)}, u32[]{:S(2)}) %collective-permute-start.8) | collective-permute-done | bytes 262176 | tf_op jit(solution)/shard_map/ppermute | solution.py:661
  57.9 1.2 %shard_map.115 = f32[4,256,256]{2,1,0:T(8,128)} custom-call(f32[4,256,256]{2,1,0:T(8,128)S(1)} %get-tuple-element.53.total, f32[2,256,128]{2,1,0:T(8,128)S(1)} %collective-permute-done.8.e, f32[2,256,128]{2,1,0:T(8,128)S(1)} %collective-permute-done.9.o), custom_call_target="tpu_custom_call" | custom-call | tf_op jit(solution)/shard_map/pallas_call | solution.py:434
  59.1 0.9 %shard_map.120 = f32[2,256,256]{2,1,0:T(8,128)} custom-call(f32[256,256]{1,0:T(8,128)S(1)} %shard_map.119.full, f32[256,256]{1,0:T(8,128)S(1)} %collective-permute-done.20.other), custom_call_target="tpu_custom_call" | custom-call | tf_op jit(solution)/shard_map/pallas_call | solution.py:434
  (27 shorter events, 2.8 us)
Async XLA Ops:
  2.6 12.7 %collective-permute-start.2 = (f32[4,64,256]{2,1,0:T(8,128)S(1)}, f32[4,64,256]{2,1,0:T(8,128)S(1)}, u32[]{:S(2)}, u32[]{:S(2)}) collective-permute-start(f32[4,64,256]{2,1,0:T(8,128)S(1)} %get-tuple-element.36), channel_id=1, source_target_pairs={{0,16},{16,0},{1,17},{17,1},{2,18},{18,2},{3,19},{19,3},{4,20},{20... | collective-permute-start | bytes 786440 | tf_op jit(solution)/shard_map/ppermute | solution.py:564
  3.2 10.8 %collective-permute-start.3 = (f32[256,128]{1,0:T(8,128)S(1)}, f32[256,128]{1,0:T(8,128)S(1)}, u32[]{:S(2)}, u32[]{:S(2)}) collective-permute-start(f32[256,128]{1,0:T(8,128)S(1)} %get-tuple-element.37), channel_id=1, source_target_pairs={{0,1},{2,3},{4,5},{6,7},{8,9},{10,11},{12,13},{14,15},{1,0},{3,2},... | collective-permute-start | bytes 393224 | tf_op jit(solution)/shard_map/ppermute | solution.py:562
  5.7 8.2 %collective-permute-start.4 = (f32[256,128]{1,0:T(8,128)S(1)}, f32[256,128]{1,0:T(8,128)S(1)}, u32[]{:S(2)}, u32[]{:S(2)}) collective-permute-start(f32[256,128]{1,0:T(8,128)S(1)} %get-tuple-element.38), channel_id=1, source_target_pairs={{1,2},{3,4},{5,6},{7,8},{9,10},{11,12},{13,14},{2,1},{4,3},{6,5},{... | collective-permute-start | bytes 393224 | tf_op jit(solution)/shard_map/ppermute | solution.py:562
  6.4 12.3 %collective-permute-start = (f32[256,128]{1,0:T(8,128)S(1)}, f32[256,128]{1,0:T(8,128)S(1)}, u32[]{:S(2)}, u32[]{:S(2)}) collective-permute-start(f32[256,128]{1,0:T(8,128)S(1)} %get-tuple-element.33), channel_id=1, source_target_pairs={{0,1},{2,3},{4,5},{6,7},{8,9},{10,11},{12,13},{14,15},{1,0},{3,2},... | collective-permute-start | bytes 393224 | tf_op jit(solution)/shard_map/ppermute | solution.py:562
  10.7 8.0 %collective-permute-start.1 = (f32[256,128]{1,0:T(8,128)S(1)}, f32[256,128]{1,0:T(8,128)S(1)}, u32[]{:S(2)}, u32[]{:S(2)}) collective-permute-start(f32[256,128]{1,0:T(8,128)S(1)} %get-tuple-element.34), channel_id=1, source_target_pairs={{1,2},{3,4},{5,6},{7,8},{9,10},{11,12},{13,14},{2,1},{4,3},{6,5},{... | collective-permute-start | bytes 393224 | tf_op jit(solution)/shard_map/ppermute | solution.py:562
  14.0 1.3 %collective-permute-start.5 = (f32[2,64,128]{2,1,0:T(8,128)S(1)}, f32[2,64,128]{2,1,0:T(8,128)S(1)}, u32[]{:S(2)}, u32[]{:S(2)}) collective-permute-start(f32[2,64,128]{2,1,0:T(8,128)S(1)} %shard_map.108), channel_id=1, source_target_pairs={{0,16},{16,0},{1,17},{17,1},{2,18},{18,2},{3,19},{19,3},{4,20},{20... | collective-permute-start | bytes 196616 | tf_op jit(solution)/shard_map/ppermute | solution.py:575
  18.7 1.3 %collective-permute-start.6 = (f32[2,64,128]{2,1,0:T(8,128)S(1)}, f32[2,64,128]{2,1,0:T(8,128)S(1)}, u32[]{:S(2)}, u32[]{:S(2)}) collective-permute-start(f32[2,64,128]{2,1,0:T(8,128)S(1)} %shard_map.111), channel_id=1, source_target_pairs={{0,16},{16,0},{1,17},{17,1},{2,18},{18,2},{3,19},{19,3},{4,20},{20... | collective-permute-start | bytes 196616 | tf_op jit(solution)/shard_map/ppermute | solution.py:575
  23.6 1.6 %collective-permute-start.10 = (f32[256,256]{1,0:T(8,128)S(1)}, f32[256,256]{1,0:T(8,128)S(1)}, u32[]{:S(2)}, u32[]{:S(2)}) collective-permute-start(f32[256,256]{1,0:T(8,128)S(1)} %get-tuple-element.57), channel_id=1, source_target_pairs={{0,16},{16,0},{1,17},{17,1},{2,18},{18,2},{3,19},{19,3},{4,20},{20... | collective-permute-start | bytes 786440 | tf_op jit(solution)/shard_map/ppermute | solution.py:457
  24.2 22.4 %collective-permute-start.7 = (f32[4,64,384]{2,1,0:T(8,128)S(1)}, f32[4,64,384]{2,1,0:T(8,128)S(1)}, u32[]{:S(2)}, u32[]{:S(2)}) collective-permute-start(f32[4,64,384]{2,1,0:T(8,128)S(1)} %get-tuple-element.52), channel_id=1, source_target_pairs={{0,16},{16,0},{1,17},{17,1},{2,18},{18,2},{3,19},{19,3},{4,20},{20... | collective-permute-start | bytes 1179656 | tf_op jit(solution)/shard_map/ppermute | solution.py:652
  25.2 5.0 %collective-permute-start.11 = (f32[64,256]{1,0:T(8,128)S(1)}, f32[64,256]{1,0:T(8,128)S(1)}, u32[]{:S(2)}, u32[]{:S(2)}) collective-permute-start(f32[64,256]{1,0:T(8,128)S(1)} %get-tuple-element.59), channel_id=1, source_target_pairs={{0,1},{1,0},{2,3},{3,2},{4,5},{5,4},{6,7},{7,6},{8,9},{9,8},{10,11... | collective-permute-start | bytes 196616 | tf_op jit(solution)/shard_map/ppermute | solution.py:457
  27.8 4.3 %collective-permute-start.12 = (f32[64,256]{1,0:T(8,128)S(1)}, f32[64,256]{1,0:T(8,128)S(1)}, u32[]{:S(2)}, u32[]{:S(2)}) collective-permute-start(f32[64,256]{1,0:T(8,128)S(1)} %get-tuple-element.60), channel_id=1, source_target_pairs={{0,2},{1,3},{2,0},{3,1},{4,6},{5,7},{6,4},{7,5},{8,10},{9,11},{10,... | collective-permute-start | bytes 196616 | tf_op jit(solution)/shard_map/ppermute | solution.py:457
  29.2 5.2 %collective-permute-start.13 = (f32[64,256]{1,0:T(8,128)S(1)}, f32[64,256]{1,0:T(8,128)S(1)}, u32[]{:S(2)}, u32[]{:S(2)}) collective-permute-start(f32[64,256]{1,0:T(8,128)S(1)} %get-tuple-element.61), channel_id=1, source_target_pairs={{0,3},{1,2},{2,1},{3,0},{4,7},{5,6},{6,5},{7,4},{8,11},{9,10},{10,... | collective-permute-start | bytes 196616 | tf_op jit(solution)/shard_map/ppermute | solution.py:457
  34.4 6.5 %collective-permute-start.16 = (f32[64,256]{1,0:T(8,128)S(1)}, f32[64,256]{1,0:T(8,128)S(1)}, u32[]{:S(2)}, u32[]{:S(2)}) collective-permute-start(f32[64,256]{1,0:T(8,128)S(1)} %shard_map.117.refs_0_), channel_id=1, source_target_pairs={{0,12},{1,13},{2,14},{3,15},{4,8},{5,9},{6,10},{7,11},{8,4},{9,5},... | collective-permute-start | bytes 196616 | tf_op jit(solution)/shard_map/ppermute | solution.py:457
  36.8 6.1 %collective-permute-start.15 = (f32[64,256]{1,0:T(8,128)S(1)}, f32[64,256]{1,0:T(8,128)S(1)}, u32[]{:S(2)}, u32[]{:S(2)}) collective-permute-start(f32[64,256]{1,0:T(8,128)S(1)} %shard_map.117.refs_0_), channel_id=1, source_target_pairs={{0,8},{1,9},{2,10},{3,11},{4,12},{5,13},{6,14},{7,15},{8,0},{9,1},... | collective-permute-start | bytes 196616 | tf_op jit(solution)/shard_map/ppermute | solution.py:457
  37.5 5.5 %collective-permute-start.14 = (f32[64,256]{1,0:T(8,128)S(1)}, f32[64,256]{1,0:T(8,128)S(1)}, u32[]{:S(2)}, u32[]{:S(2)}) collective-permute-start(f32[64,256]{1,0:T(8,128)S(1)} %shard_map.117.refs_0_), channel_id=1, source_target_pairs={{0,4},{1,5},{2,6},{3,7},{4,0},{5,1},{6,2},{7,3},{8,12},{9,13},{10,... | collective-permute-start | bytes 196616 | tf_op jit(solution)/shard_map/ppermute | solution.py:457
  43.0 5.9 %collective-permute-start.19 = (f32[64,256]{1,0:T(8,128)S(1)}, f32[64,256]{1,0:T(8,128)S(1)}, u32[]{:S(2)}, u32[]{:S(2)}) collective-permute-start(f32[64,256]{1,0:T(8,128)S(1)} %shard_map.118.refs_0_), channel_id=1, source_target_pairs={{0,3},{1,2},{2,1},{3,0},{4,7},{5,6},{6,5},{7,4},{8,11},{9,10},{10,... | collective-permute-start | bytes 196616 | tf_op jit(solution)/shard_map/ppermute | solution.py:457
  43.7 5.2 %collective-permute-start.18 = (f32[64,256]{1,0:T(8,128)S(1)}, f32[64,256]{1,0:T(8,128)S(1)}, u32[]{:S(2)}, u32[]{:S(2)}) collective-permute-start(f32[64,256]{1,0:T(8,128)S(1)} %shard_map.118.refs_0_), channel_id=1, source_target_pairs={{0,2},{1,3},{2,0},{3,1},{4,6},{5,7},{6,4},{7,5},{8,10},{9,11},{10,... | collective-permute-start | bytes 196616 | tf_op jit(solution)/shard_map/ppermute | solution.py:457
  45.3 5.0 %collective-permute-start.17 = (f32[64,256]{1,0:T(8,128)S(1)}, f32[64,256]{1,0:T(8,128)S(1)}, u32[]{:S(2)}, u32[]{:S(2)}) collective-permute-start(f32[64,256]{1,0:T(8,128)S(1)} %shard_map.118.refs_0_), channel_id=1, source_target_pairs={{0,1},{1,0},{2,3},{3,2},{4,5},{5,4},{6,7},{7,6},{8,9},{9,8},{10,11... | collective-permute-start | bytes 196616 | tf_op jit(solution)/shard_map/ppermute | solution.py:457
  46.7 11.1 %collective-permute-start.8 = (f32[2,256,128]{2,1,0:T(8,128)S(1)}, f32[2,256,128]{2,1,0:T(8,128)S(1)}, u32[]{:S(2)}, u32[]{:S(2)}) collective-permute-start(f32[2,256,128]{2,1,0:T(8,128)S(1)} %get-tuple-element.54), channel_id=1, source_target_pairs={{0,1},{2,3},{4,5},{6,7},{8,9},{10,11},{12,13},{14,15},{1,0},{3,2},... | collective-permute-start | bytes 786440 | tf_op jit(solution)/shard_map/ppermute | solution.py:661
  47.6 10.3 %collective-permute-start.9 = (f32[2,256,128]{2,1,0:T(8,128)S(1)}, f32[2,256,128]{2,1,0:T(8,128)S(1)}, u32[]{:S(2)}, u32[]{:S(2)}) collective-permute-start(f32[2,256,128]{2,1,0:T(8,128)S(1)} %get-tuple-element.55), channel_id=1, source_target_pairs={{1,2},{3,4},{5,6},{7,8},{9,10},{11,12},{13,14},{2,1},{4,3},{6,5},{... | collective-permute-start | bytes 786440 | tf_op jit(solution)/shard_map/ppermute | solution.py:662
  50.3 8.8 %collective-permute-start.20 = (f32[256,256]{1,0:T(8,128)S(1)}, f32[256,256]{1,0:T(8,128)S(1)}, u32[]{:S(2)}, u32[]{:S(2)}) collective-permute-start(f32[256,256]{1,0:T(8,128)S(1)} %shard_map.119.full), channel_id=1, source_target_pairs={{0,16},{16,0},{1,17},{17,1},{2,18},{18,2},{3,19},{19,3},{4,20},{20... | collective-permute-start | bytes 786440 | tf_op jit(solution)/shard_map/ppermute | solution.py:457

commit v6 on v5

--- a/solution.py
+++ b/solution.py
@@ -31,19 +31,11 @@
     scale = 1.0 / np.sqrt(n)
     c, s = np.cos(angle) * scale, np.sin(angle) * scale
     d = np.block([[c, s], [-s, c]])
-    mats = np.stack(split_np(d) + split_np(d.T))
+    mats = np.stack(split_np(d))
     w = np.exp(-2j * np.pi * k / n)
     tw_left = np.stack([np.tile(w.real[:, None], (1, h)), np.tile(w.imag[:, None], (1, h))])
     tw_right = np.stack([np.tile(w.real[None], (8, 1)), np.tile(w.imag[None], (8, 1))])
-    order = np.zeros((n, n))
-    order[2 * k, k] = 1.0
-    order[2 * k + 1, h + k] = 1.0
-    return (
-        mats,
-        tw_left.astype(np.float32),
-        tw_right.astype(np.float32),
-        np.stack([order.T, order]).astype(BF16),
-    )
+    return mats, tw_left.astype(np.float32), tw_right.astype(np.float32)
 
 
 def split(x):
@@ -201,24 +193,40 @@
         out[1] = o[rows, :]
 
 
+def even_odd(n, axis):
+    h = n // 2
+    natural, sorted_ = iota((n, n), axis), iota((n, n), 1 - axis)
+    source = jnp.where(sorted_ < h, 2 * sorted_, 2 * (sorted_ - h) + 1)
+    return (natural == source).astype(F32).astype(BF16)
+
+
 def reorder(x, order):
     def thirds(y):
         a = y.astype(BF16)
         return (a,) + split(y - a.astype(F32))
 
     a, b, c = thirds(x)
-    a, b, c = thirds(dot(order[0], a) + (dot(order[0], b) + dot(order[0], c)))
-    return dot(a, order[1]) + (dot(b, order[1]) + dot(c, order[1]))
+    a, b, c = thirds(dot(order[1], a) + (dot(order[1], b) + dot(order[1], c)))
+    return dot(a, order[0]) + (dot(b, order[0]) + dot(c, order[0]))
 
 
 def prep_kernel(*refs):
-    hbm, (kr, ki, am), loaded = refs[:7], refs[7:10], refs[10:14]
-    phase, order, amps, sems = refs[14:]
-    copies = copy_all(hbm, (phase, order, amps) + loaded, sems)
+    hbm, (kr, ki, am, mats), loaded = refs[:6], refs[6:10], refs[10:13]
+    phase, amps, table, sems = refs[13:]
+    n = phase.shape[0]
+    h = n // 2
+    copies = copy_all(hbm, (phase, table, amps) + loaded, sems)
+    order = [even_odd(n, axis) for axis in range(2)]
     copies[0].wait()
-    copies[1].wait()
     angle = reorder(phase[...], order)
     kr[...], ki[...] = cos_sin(angle)
+    copies[1].wait()
+    for i in range(2):
+        mats[i] = table[i]
+        mats[2 + i, :h, :h] = table[i, :h, :h]
+        mats[2 + i, :h, h:] = -table[i, :h, h:]
+        mats[2 + i, h:, :h] = -table[i, h:, :h]
+        mats[2 + i, h:, h:] = table[i, h:, h:]
     copies[2].wait()
     am[...] = reorder(amps[...], order)
     for copy in copies[3:]:
@@ -497,10 +505,16 @@
         full[pl.ds(pl.multiple_of((place ^ j) * chunk, 8), chunk), :] = part[...]
 
 
-def both_kernel(full, other, out):
-    even = lax.axis_index("row") % 2 == 0
-    out[0] = jnp.where(even, full[...], other[...])
-    out[1] = jnp.where(even, other[...], full[...])
+def half_kernel(full, out, sem):
+    copy = pltpu.make_async_copy(full, out.at[lax.axis_index("row") % 2], sem)
+    copy.start()
+    copy.wait()
+
+
+def other_kernel(started, other, out, sem):
+    copy = pltpu.make_async_copy(other, out.at[1 - lax.axis_index("row") % 2], sem)
+    copy.start()
+    copy.wait()
 
 
 def reduce_probe(keep, give):
@@ -532,8 +546,16 @@
         functools.partial(join_kernel, stride), [(n, n)], [VMEM] * quad, *parts
     )
     other = swap(full, "row", 1)
-    (grad,) = call(both_kernel, [(2, n, n)], [VMEM] * 2, full, other)
-    return grad
+    out = dict(
+        out_shape=jax.ShapeDtypeStruct((2, n, n), F32),
+        out_specs=HBM,
+        scratch_shapes=[pltpu.SemaphoreType.DMA(())],
+        compiler_params=pltpu.CompilerParams(vmem_limit_bytes=16 << 20),
+    )
+    grad = pl.pallas_call(half_kernel, in_specs=[VMEM], **out)(full)
+    return pl.pallas_call(
+        other_kernel, in_specs=[HBM, VMEM], input_output_aliases={0: 0}, **out
+    )(grad, other)
 
 
 def whole(object_field, probe, phase, amplitudes, offsets):
@@ -541,8 +563,7 @@
     n = probe.shape[1]
     h = n // 2
     margin = n // 4
-    tables = [jnp.asarray(t) for t in dft_constants(n)]
-    mats, tw_left, tw_right, order = tables
+    mats, tw_left, tw_right = [jnp.asarray(t) for t in dft_constants(n)]
 
     row_rounds, col_rounds = edges("row"), edges("col")
     n_row = len(row_rounds)
@@ -585,16 +606,18 @@
         )
         return main
 
-    loads = (phase, order, amplitudes.reshape(n, n), mats, tw_left, tw_right, probe)
+    loads = (phase, mats, amplitudes.reshape(n, n), tw_left, tw_right, probe)
     kr, ki, am, mats, tw_left, tw_right, pr = call(
         prep_kernel,
-        [(n, n)] * 3 + [jax.ShapeDtypeStruct(x.shape, x.dtype) for x in loads[3:]],
+        [(n, n)] * 3
+        + [jax.ShapeDtypeStruct((4, n, n), BF16)]
+        + [jax.ShapeDtypeStruct(x.shape, x.dtype) for x in loads[3:]],
         [HBM] * len(loads),
         *[in_hbm(x) for x in loads],
         scratch=[
             pltpu.VMEM((n, n), F32),
+            pltpu.VMEM((n, n), F32),
             pltpu.VMEM((2, n, n), BF16),
-            pltpu.VMEM((n, n), F32),
             pltpu.SemaphoreType.DMA((len(loads),)),
         ],
     )

time: 60.2 us -> 60.1 us (level)
  waiting for transfers between devices: 22.5 us -> 21.8 us
    pallas_call x0 -> x2, Pallas kernels: none -> 1.44 us  [the longest x1 0.73 us: reduce_probe(): grad = pl.pallas_call(half_kernel, in_specs=[VMEM], **out)(full)]
    pallas_call x17 -> x16, Pallas kernels: 13.4 us -> 12.5 us  [call(): pl.pallas_call(kernel, out_shape=shapes, in_specs=in_specs, out_specs=[SM...]
    ppermute x1, waiting for transfers between devices: 7.47 us -> 6.74 us  [whole(): send_e = lax.ppermute(send_e, 'col', col_rounds[0])]
  transfers between devices with their start and end apart: 21 -> 21, of which waited for: 12 -> 12; matrix products, arithmetic and copies ran while one was open for 0% -> 0% of each run, Pallas kernels for 12% -> 13%
where the time goes in v6:
time: 60.1 us; the launch traced here: 59.8 us
  starting transfers between devices  23.2 us (39%)
  waiting for transfers between devices  21.8 us (36%)
  Pallas kernels  14 us (23%)
  between operations  0.8 us (1%)
    pallas_call x16, Pallas kernels, call(): pl.pallas_call(kernel, out_shape=shapes, in_specs=in_specs, out_specs=[SM...  12.5 us
    ppermute x11, starting transfers between devices, swap(): return lax.ppermute(value, axis, [(i, i ^ distance) for i in range(count)])  12.4 us
    ppermute x11, waiting for transfers between devices, swap(): return lax.ppermute(value, axis, [(i, i ^ distance) for i in range(count)])  11.8 us
    ppermute x4, starting transfers between devices, whole(): strips.append(lax.ppermute(packed[i], 'col', col_rounds[i % 2]))  8.15 us
    ppermute x1, waiting for transfers between devices, whole(): send_e = lax.ppermute(send_e, 'col', col_rounds[0])  6.74 us
    ppermute x4, waiting for transfers between devices, whole(): strips.append(lax.ppermute(packed[i], 'col', col_rounds[i % 2]))  1.88 us
    ppermute x2, waiting for transfers between devices, cut(): corners[s].append(lax.ppermute(parts[i], 'row', pairs))  1.37 us
  transfers between devices with their start and end apart: 21, of which 12 were waited for; matrix products, arithmetic and copies ran while one was open for 0% of the time, Pallas kernels for 13%

profile of v6, /device:TPU:0, one launch (start us, length us, event | category | flops | bytes accessed | tf_op | source)
XLA Modules:
  0.0 59.8 jit_solution(9541135799321643415)
XLA Ops:
  0.6 2.0 %shard_map.95 = (f32[4,256,256]{2,1,0:T(8,128)S(1)}, s32[1,2]{1,0:T(1,128)S(1)}, s32[2,8,128]{2,1,0:T(8,128)S(1)}, f32[256,128]{1,0:T(8,128)S(1)}, f32[256,128]{...) custom-call(f32[4,256,256]{2,1,0:T(8,128)} %bitcast.4, s32[1,2]{1,0:T(1,128)} %bitcast.7), custom_call_target="tpu_custom_call" | custom-call | tf_op jit(solution)/shard_map/pallas_call | solution.py:442
  3.2 2.6 %collective-permute-start.3 = (f32[256,128]{1,0:T(8,128)S(1)}, f32[256,128]{1,0:T(8,128)S(1)}, u32[]{:S(2)}, u32[]{:S(2)}) collective-permute-start(f32[256,128]{1,0:T(8,128)S(1)} %get-tuple-element.37), channel_id=1, source_target_pairs={{0,1},{2,3},{4,5},{6,7},{8,9},{10,11},{12,13},{14,15},{1,0},{3,2},... | collective-permute-start | bytes 393224 | tf_op jit(solution)/shard_map/ppermute | solution.py:583
  5.7 0.7 %collective-permute-start.4 = (f32[256,128]{1,0:T(8,128)S(1)}, f32[256,128]{1,0:T(8,128)S(1)}, u32[]{:S(2)}, u32[]{:S(2)}) collective-permute-start(f32[256,128]{1,0:T(8,128)S(1)} %get-tuple-element.38), channel_id=1, source_target_pairs={{1,2},{3,4},{5,6},{7,8},{9,10},{11,12},{13,14},{2,1},{4,3},{6,5},{... | collective-permute-start | bytes 393224 | tf_op jit(solution)/shard_map/ppermute | solution.py:583
  6.4 4.3 %collective-permute-start = (f32[256,128]{1,0:T(8,128)S(1)}, f32[256,128]{1,0:T(8,128)S(1)}, u32[]{:S(2)}, u32[]{:S(2)}) collective-permute-start(f32[256,128]{1,0:T(8,128)S(1)} %get-tuple-element.33), channel_id=1, source_target_pairs={{0,1},{2,3},{4,5},{6,7},{8,9},{10,11},{12,13},{14,15},{1,0},{3,2},... | collective-permute-start | bytes 393224 | tf_op jit(solution)/shard_map/ppermute | solution.py:583
  10.7 0.7 %collective-permute-start.1 = (f32[256,128]{1,0:T(8,128)S(1)}, f32[256,128]{1,0:T(8,128)S(1)}, u32[]{:S(2)}, u32[]{:S(2)}) collective-permute-start(f32[256,128]{1,0:T(8,128)S(1)} %get-tuple-element.34), channel_id=1, source_target_pairs={{1,2},{3,4},{5,6},{7,8},{9,10},{11,12},{13,14},{2,1},{4,3},{6,5},{... | collective-permute-start | bytes 393224 | tf_op jit(solution)/shard_map/ppermute | solution.py:583
  11.3 2.6 %shard_map.98 = (f32[256,256]{1,0:T(8,128)S(1)}, f32[256,256]{1,0:T(8,128)S(1)}, f32[256,256]{1,0:T(8,128)S(1)}, bf16[4,256,256]{2,1,0:T(8,128)(2,1)S(1)}, f32[2...) custom-call(f32[256,256]{1,0:T(8,128)} %refs_0_.1, ...), custom_call_target="tpu_custom_call" | custom-call | tf_op jit(solution)/shard_map/pallas_call | solution.py:442
  14.1 0.8 %shard_map.100.refs_4_.refs_5_ = f32[2,256,256]{2,1,0:T(8,128)S(1)} custom-call(s32[1,2]{1,0:T(1,128)S(1)} %get-tuple-element.40.offs, f32[2,256,256]{2,1,0:T(8,128)S(1)} %get-tuple-element.41.probe), custom_call_target="tpu_custom_call" | custom-call | tf_op jit(solution)/shard_map/pallas_call | solution.py:442
  15.3 1.5 %shard_map.101 = (f32[2,256,256]{2,1,0:T(8,128)S(1)}, f32[2,256,256]{2,1,0:T(8,128)S(1)}) custom-call(f32[2,256,256]{2,1,0:T(8,128)S(1)} %shard_map.97.refs_0_, f32[4,64,256]{2,1,0:T(8,128)S(1)} %collective-permute-done.2.refs_1_, f32[2,64,128]{2,1,0:T(8,128)S(1)} %collective-permute-done.5.refs_2_, s32[2,8,128]{2,1,0:T(8,128)S(1)} %get-tuple-element.35.limits.refs_3_, ...), custom_call_target="tpu_custom_call" | custom-call | tf_op jit(solution)/shard_map/pallas_call | solution.py:442
  16.8 1.9 %collective-permute-done.e = f32[256,128]{1,0:T(8,128)S(1)} collective-permute-done((f32[256,128]{1,0:T(8,128)S(1)}, f32[256,128]{1,0:T(8,128)S(1)}, u32[]{:S(2)}, u32[]{:S(2)}) %collective-permute-start) | collective-permute-done | bytes 131104 | tf_op jit(solution)/shard_map/ppermute | solution.py:583
  18.9 1.1 %collective-permute-done.6.refs_2_ = f32[2,64,128]{2,1,0:T(8,128)S(1)} collective-permute-done((f32[2,64,128]{2,1,0:T(8,128)S(1)}, f32[2,64,128]{2,1,0:T(8,128)S(1)}, u32[]{:S(2)}, u32[]{:S(2)}) %collective-permute-start.6) | collective-permute-done | bytes 65568 | tf_op jit(solution)/shard_map/ppermute | solution.py:596
  20.0 3.5 %shard_map.103 = (f32[256,256]{1,0:T(8,128)S(1)}, f32[256,256]{1,0:T(8,128)S(1)}, f32[4,256,256]{2,1,0:T(8,128)S(1)}) custom-call(f32[2,256,256]{2,1,0:T(8,128)S(1)} %shard_map.96.refs_0_, f32[4,64,256]{2,1,0:T(8,128)S(1)} %collective-permute-done.2.refs_1_, f32[2,64,128]{2,1,0:T(8,128)S(1)} %collective-permute-done.6.refs_2_, ...), custom_call_target="tpu_custom_call" | custom-call | tf_op jit(solution)/shard_map/pallas_call | solution.py:442
  25.2 2.5 %collective-permute-start.11 = (f32[64,256]{1,0:T(8,128)S(1)}, f32[64,256]{1,0:T(8,128)S(1)}, u32[]{:S(2)}, u32[]{:S(2)}) collective-permute-start(f32[64,256]{1,0:T(8,128)S(1)} %get-tuple-element.59), channel_id=1, source_target_pairs={{0,1},{1,0},{2,3},{3,2},{4,5},{5,4},{6,7},{7,6},{8,9},{9,8},{10,11... | collective-permute-start | bytes 196616 | tf_op jit(solution)/shard_map/ppermute | solution.py:465
  27.8 1.4 %collective-permute-start.12 = (f32[64,256]{1,0:T(8,128)S(1)}, f32[64,256]{1,0:T(8,128)S(1)}, u32[]{:S(2)}, u32[]{:S(2)}) collective-permute-start(f32[64,256]{1,0:T(8,128)S(1)} %get-tuple-element.60), channel_id=1, source_target_pairs={{0,2},{1,3},{2,0},{3,1},{4,6},{5,7},{6,4},{7,5},{8,10},{9,11},{10,... | collective-permute-start | bytes 196616 | tf_op jit(solution)/shard_map/ppermute | solution.py:465
  29.3 0.9 %collective-permute-done.11.refs_1_ = f32[64,256]{1,0:T(8,128)S(1)} collective-permute-done((f32[64,256]{1,0:T(8,128)S(1)}, f32[64,256]{1,0:T(8,128)S(1)}, u32[]{:S(2)}, u32[]{:S(2)}) %collective-permute-start.11) | collective-permute-done | bytes 65568 | tf_op jit(solution)/shard_map/ppermute | solution.py:465
  30.2 1.9 %collective-permute-done.12.refs_2_ = f32[64,256]{1,0:T(8,128)S(1)} collective-permute-done((f32[64,256]{1,0:T(8,128)S(1)}, f32[64,256]{1,0:T(8,128)S(1)}, u32[]{:S(2)}, u32[]{:S(2)}) %collective-permute-start.12) | collective-permute-done | bytes 65568 | tf_op jit(solution)/shard_map/ppermute | solution.py:465
  32.0 2.3 %collective-permute-done.13.refs_3_ = f32[64,256]{1,0:T(8,128)S(1)} collective-permute-done((f32[64,256]{1,0:T(8,128)S(1)}, f32[64,256]{1,0:T(8,128)S(1)}, u32[]{:S(2)}, u32[]{:S(2)}) %collective-permute-start.13) | collective-permute-done | bytes 65568 | tf_op jit(solution)/shard_map/ppermute | solution.py:465
  34.4 2.4 %collective-permute-start.16 = (f32[64,256]{1,0:T(8,128)S(1)}, f32[64,256]{1,0:T(8,128)S(1)}, u32[]{:S(2)}, u32[]{:S(2)}) collective-permute-start(f32[64,256]{1,0:T(8,128)S(1)} %shard_map.108.refs_0_), channel_id=1, source_target_pairs={{0,12},{1,13},{2,14},{3,15},{4,8},{5,9},{6,10},{7,11},{8,4},{9,5},... | collective-permute-start | bytes 196616 | tf_op jit(solution)/shard_map/ppermute | solution.py:465
  36.8 0.7 %collective-permute-start.15 = (f32[64,256]{1,0:T(8,128)S(1)}, f32[64,256]{1,0:T(8,128)S(1)}, u32[]{:S(2)}, u32[]{:S(2)}) collective-permute-start(f32[64,256]{1,0:T(8,128)S(1)} %shard_map.108.refs_0_), channel_id=1, source_target_pairs={{0,8},{1,9},{2,10},{3,11},{4,12},{5,13},{6,14},{7,15},{8,0},{9,1},... | collective-permute-start | bytes 196616 | tf_op jit(solution)/shard_map/ppermute | solution.py:465
  37.5 1.3 %collective-permute-start.14 = (f32[64,256]{1,0:T(8,128)S(1)}, f32[64,256]{1,0:T(8,128)S(1)}, u32[]{:S(2)}, u32[]{:S(2)}) collective-permute-start(f32[64,256]{1,0:T(8,128)S(1)} %shard_map.108.refs_0_), channel_id=1, source_target_pairs={{0,4},{1,5},{2,6},{3,7},{4,0},{5,1},{6,2},{7,3},{8,12},{9,13},{10,... | collective-permute-start | bytes 196616 | tf_op jit(solution)/shard_map/ppermute | solution.py:465
  38.8 2.1 %collective-permute-done.16.refs_3_ = f32[64,256]{1,0:T(8,128)S(1)} collective-permute-done((f32[64,256]{1,0:T(8,128)S(1)}, f32[64,256]{1,0:T(8,128)S(1)}, u32[]{:S(2)}, u32[]{:S(2)}) %collective-permute-start.16) | collective-permute-done | bytes 65568 | tf_op jit(solution)/shard_map/ppermute | solution.py:465
  40.9 2.1 %collective-permute-done.15.refs_2_ = f32[64,256]{1,0:T(8,128)S(1)} collective-permute-done((f32[64,256]{1,0:T(8,128)S(1)}, f32[64,256]{1,0:T(8,128)S(1)}, u32[]{:S(2)}, u32[]{:S(2)}) %collective-permute-start.15) | collective-permute-done | bytes 65568 | tf_op jit(solution)/shard_map/ppermute | solution.py:465
  43.0 0.8 %collective-permute-start.19 = (f32[64,256]{1,0:T(8,128)S(1)}, f32[64,256]{1,0:T(8,128)S(1)}, u32[]{:S(2)}, u32[]{:S(2)}) collective-permute-start(f32[64,256]{1,0:T(8,128)S(1)} %shard_map.109.refs_0_), channel_id=1, source_target_pairs={{0,3},{1,2},{2,1},{3,0},{4,7},{5,6},{6,5},{7,4},{8,11},{9,10},{10,... | collective-permute-start | bytes 196616 | tf_op jit(solution)/shard_map/ppermute | solution.py:465
  43.7 1.6 %collective-permute-start.18 = (f32[64,256]{1,0:T(8,128)S(1)}, f32[64,256]{1,0:T(8,128)S(1)}, u32[]{:S(2)}, u32[]{:S(2)}) collective-permute-start(f32[64,256]{1,0:T(8,128)S(1)} %shard_map.109.refs_0_), channel_id=1, source_target_pairs={{0,2},{1,3},{2,0},{3,1},{4,6},{5,7},{6,4},{7,5},{8,10},{9,11},{10,... | collective-permute-start | bytes 196616 | tf_op jit(solution)/shard_map/ppermute | solution.py:465
  45.3 1.2 %collective-permute-start.17 = (f32[64,256]{1,0:T(8,128)S(1)}, f32[64,256]{1,0:T(8,128)S(1)}, u32[]{:S(2)}, u32[]{:S(2)}) collective-permute-start(f32[64,256]{1,0:T(8,128)S(1)} %shard_map.109.refs_0_), channel_id=1, source_target_pairs={{0,1},{1,0},{2,3},{3,2},{4,5},{5,4},{6,7},{7,6},{8,9},{9,8},{10,11... | collective-permute-start | bytes 196616 | tf_op jit(solution)/shard_map/ppermute | solution.py:465
  46.7 0.9 %collective-permute-start.8 = (f32[2,256,128]{2,1,0:T(8,128)S(1)}, f32[2,256,128]{2,1,0:T(8,128)S(1)}, u32[]{:S(2)}, u32[]{:S(2)}) collective-permute-start(f32[2,256,128]{2,1,0:T(8,128)S(1)} %get-tuple-element.54), channel_id=1, source_target_pairs={{0,1},{2,3},{4,5},{6,7},{8,9},{10,11},{12,13},{14,15},{1,0},{3,2},... | collective-permute-start | bytes 786440 | tf_op jit(solution)/shard_map/ppermute | solution.py:684
  47.6 0.7 %collective-permute-start.9 = (f32[2,256,128]{2,1,0:T(8,128)S(1)}, f32[2,256,128]{2,1,0:T(8,128)S(1)}, u32[]{:S(2)}, u32[]{:S(2)}) collective-permute-start(f32[2,256,128]{2,1,0:T(8,128)S(1)} %get-tuple-element.55), channel_id=1, source_target_pairs={{1,2},{3,4},{5,6},{7,8},{9,10},{11,12},{13,14},{2,1},{4,3},{6,5},{... | collective-permute-start | bytes 786440 | tf_op jit(solution)/shard_map/ppermute | solution.py:685
  48.3 0.7 %collective-permute-done.19.refs_3_ = f32[64,256]{1,0:T(8,128)S(1)} collective-permute-done((f32[64,256]{1,0:T(8,128)S(1)}, f32[64,256]{1,0:T(8,128)S(1)}, u32[]{:S(2)}, u32[]{:S(2)}) %collective-permute-start.19) | collective-permute-done | bytes 65568 | tf_op jit(solution)/shard_map/ppermute | solution.py:465
  48.9 1.4 %collective-permute-done.17.refs_1_ = f32[64,256]{1,0:T(8,128)S(1)} collective-permute-done((f32[64,256]{1,0:T(8,128)S(1)}, f32[64,256]{1,0:T(8,128)S(1)}, u32[]{:S(2)}, u32[]{:S(2)}) %collective-permute-start.17) | collective-permute-done | bytes 65568 | tf_op jit(solution)/shard_map/ppermute | solution.py:465
  50.4 0.7 %shard_map.111.started = f32[2,256,256]{2,1,0:T(8,128)} custom-call(f32[256,256]{1,0:T(8,128)S(1)} %shard_map.110.full), custom_call_target="tpu_custom_call" | custom-call | tf_op jit(solution)/shard_map/pallas_call | solution.py:555
  51.1 6.7 %collective-permute-done.8.e = f32[2,256,128]{2,1,0:T(8,128)S(1)} collective-permute-done((f32[2,256,128]{2,1,0:T(8,128)S(1)}, f32[2,256,128]{2,1,0:T(8,128)S(1)}, u32[]{:S(2)}, u32[]{:S(2)}) %collective-permute-start.8) | collective-permute-done | bytes 262176 | tf_op jit(solution)/shard_map/ppermute | solution.py:684
  57.9 1.2 %shard_map.106 = f32[4,256,256]{2,1,0:T(8,128)} custom-call(f32[4,256,256]{2,1,0:T(8,128)S(1)} %get-tuple-element.53.total, f32[2,256,128]{2,1,0:T(8,128)S(1)} %collective-permute-done.8.e, f32[2,256,128]{2,1,0:T(8,128)S(1)} %collective-permute-done.9.o), custom_call_target="tpu_custom_call" | custom-call | tf_op jit(solution)/shard_map/pallas_call | solution.py:442
  59.1 0.7 %shard_map.112 = f32[2,256,256]{2,1,0:T(8,128)} custom-call(f32[2,256,256]{2,1,0:T(8,128)} %shard_map.111.started, f32[256,256]{1,0:T(8,128)S(1)} %collective-permute-done.20.other), custom_call_target="tpu_custom_call", output_to_operand_aliasing={{}: (0, {})} | custom-call | tf_op jit(solution)/shard_map/pallas_call | solution.py:556
  (28 shorter events, 3.4 us)
Async XLA Ops:
  2.6 12.7 %collective-permute-start.2 = (f32[4,64,256]{2,1,0:T(8,128)S(1)}, f32[4,64,256]{2,1,0:T(8,128)S(1)}, u32[]{:S(2)}, u32[]{:S(2)}) collective-permute-start(f32[4,64,256]{2,1,0:T(8,128)S(1)} %get-tuple-element.36), channel_id=1, source_target_pairs={{0,16},{16,0},{1,17},{17,1},{2,18},{18,2},{3,19},{19,3},{4,20},{20... | collective-permute-start | bytes 786440 | tf_op jit(solution)/shard_map/ppermute | solution.py:585
  3.2 10.8 %collective-permute-start.3 = (f32[256,128]{1,0:T(8,128)S(1)}, f32[256,128]{1,0:T(8,128)S(1)}, u32[]{:S(2)}, u32[]{:S(2)}) collective-permute-start(f32[256,128]{1,0:T(8,128)S(1)} %get-tuple-element.37), channel_id=1, source_target_pairs={{0,1},{2,3},{4,5},{6,7},{8,9},{10,11},{12,13},{14,15},{1,0},{3,2},... | collective-permute-start | bytes 393224 | tf_op jit(solution)/shard_map/ppermute | solution.py:583
  5.7 8.2 %collective-permute-start.4 = (f32[256,128]{1,0:T(8,128)S(1)}, f32[256,128]{1,0:T(8,128)S(1)}, u32[]{:S(2)}, u32[]{:S(2)}) collective-permute-start(f32[256,128]{1,0:T(8,128)S(1)} %get-tuple-element.38), channel_id=1, source_target_pairs={{1,2},{3,4},{5,6},{7,8},{9,10},{11,12},{13,14},{2,1},{4,3},{6,5},{... | collective-permute-start | bytes 393224 | tf_op jit(solution)/shard_map/ppermute | solution.py:583
  6.4 12.3 %collective-permute-start = (f32[256,128]{1,0:T(8,128)S(1)}, f32[256,128]{1,0:T(8,128)S(1)}, u32[]{:S(2)}, u32[]{:S(2)}) collective-permute-start(f32[256,128]{1,0:T(8,128)S(1)} %get-tuple-element.33), channel_id=1, source_target_pairs={{0,1},{2,3},{4,5},{6,7},{8,9},{10,11},{12,13},{14,15},{1,0},{3,2},... | collective-permute-start | bytes 393224 | tf_op jit(solution)/shard_map/ppermute | solution.py:583
  10.7 8.0 %collective-permute-start.1 = (f32[256,128]{1,0:T(8,128)S(1)}, f32[256,128]{1,0:T(8,128)S(1)}, u32[]{:S(2)}, u32[]{:S(2)}) collective-permute-start(f32[256,128]{1,0:T(8,128)S(1)} %get-tuple-element.34), channel_id=1, source_target_pairs={{1,2},{3,4},{5,6},{7,8},{9,10},{11,12},{13,14},{2,1},{4,3},{6,5},{... | collective-permute-start | bytes 393224 | tf_op jit(solution)/shard_map/ppermute | solution.py:583
  14.0 1.3 %collective-permute-start.5 = (f32[2,64,128]{2,1,0:T(8,128)S(1)}, f32[2,64,128]{2,1,0:T(8,128)S(1)}, u32[]{:S(2)}, u32[]{:S(2)}) collective-permute-start(f32[2,64,128]{2,1,0:T(8,128)S(1)} %shard_map.99), channel_id=1, source_target_pairs={{0,16},{16,0},{1,17},{17,1},{2,18},{18,2},{3,19},{19,3},{4,20},{20... | collective-permute-start | bytes 196616 | tf_op jit(solution)/shard_map/ppermute | solution.py:596
  18.7 1.3 %collective-permute-start.6 = (f32[2,64,128]{2,1,0:T(8,128)S(1)}, f32[2,64,128]{2,1,0:T(8,128)S(1)}, u32[]{:S(2)}, u32[]{:S(2)}) collective-permute-start(f32[2,64,128]{2,1,0:T(8,128)S(1)} %shard_map.102), channel_id=1, source_target_pairs={{0,16},{16,0},{1,17},{17,1},{2,18},{18,2},{3,19},{19,3},{4,20},{20... | collective-permute-start | bytes 196616 | tf_op jit(solution)/shard_map/ppermute | solution.py:596
  23.6 1.6 %collective-permute-start.10 = (f32[256,256]{1,0:T(8,128)S(1)}, f32[256,256]{1,0:T(8,128)S(1)}, u32[]{:S(2)}, u32[]{:S(2)}) collective-permute-start(f32[256,256]{1,0:T(8,128)S(1)} %get-tuple-element.57), channel_id=1, source_target_pairs={{0,16},{16,0},{1,17},{17,1},{2,18},{18,2},{3,19},{19,3},{4,20},{20... | collective-permute-start | bytes 786440 | tf_op jit(solution)/shard_map/ppermute | solution.py:465
  24.2 22.4 %collective-permute-start.7 = (f32[4,64,384]{2,1,0:T(8,128)S(1)}, f32[4,64,384]{2,1,0:T(8,128)S(1)}, u32[]{:S(2)}, u32[]{:S(2)}) collective-permute-start(f32[4,64,384]{2,1,0:T(8,128)S(1)} %get-tuple-element.52), channel_id=1, source_target_pairs={{0,16},{16,0},{1,17},{17,1},{2,18},{18,2},{3,19},{19,3},{4,20},{20... | collective-permute-start | bytes 1179656 | tf_op jit(solution)/shard_map/ppermute | solution.py:675
  25.2 5.0 %collective-permute-start.11 = (f32[64,256]{1,0:T(8,128)S(1)}, f32[64,256]{1,0:T(8,128)S(1)}, u32[]{:S(2)}, u32[]{:S(2)}) collective-permute-start(f32[64,256]{1,0:T(8,128)S(1)} %get-tuple-element.59), channel_id=1, source_target_pairs={{0,1},{1,0},{2,3},{3,2},{4,5},{5,4},{6,7},{7,6},{8,9},{9,8},{10,11... | collective-permute-start | bytes 196616 | tf_op jit(solution)/shard_map/ppermute | solution.py:465
  27.8 4.3 %collective-permute-start.12 = (f32[64,256]{1,0:T(8,128)S(1)}, f32[64,256]{1,0:T(8,128)S(1)}, u32[]{:S(2)}, u32[]{:S(2)}) collective-permute-start(f32[64,256]{1,0:T(8,128)S(1)} %get-tuple-element.60), channel_id=1, source_target_pairs={{0,2},{1,3},{2,0},{3,1},{4,6},{5,7},{6,4},{7,5},{8,10},{9,11},{10,... | collective-permute-start | bytes 196616 | tf_op jit(solution)/shard_map/ppermute | solution.py:465
  29.2 5.2 %collective-permute-start.13 = (f32[64,256]{1,0:T(8,128)S(1)}, f32[64,256]{1,0:T(8,128)S(1)}, u32[]{:S(2)}, u32[]{:S(2)}) collective-permute-start(f32[64,256]{1,0:T(8,128)S(1)} %get-tuple-element.61), channel_id=1, source_target_pairs={{0,3},{1,2},{2,1},{3,0},{4,7},{5,6},{6,5},{7,4},{8,11},{9,10},{10,... | collective-permute-start | bytes 196616 | tf_op jit(solution)/shard_map/ppermute | solution.py:465
  34.4 6.5 %collective-permute-start.16 = (f32[64,256]{1,0:T(8,128)S(1)}, f32[64,256]{1,0:T(8,128)S(1)}, u32[]{:S(2)}, u32[]{:S(2)}) collective-permute-start(f32[64,256]{1,0:T(8,128)S(1)} %shard_map.108.refs_0_), channel_id=1, source_target_pairs={{0,12},{1,13},{2,14},{3,15},{4,8},{5,9},{6,10},{7,11},{8,4},{9,5},... | collective-permute-start | bytes 196616 | tf_op jit(solution)/shard_map/ppermute | solution.py:465
  36.8 6.1 %collective-permute-start.15 = (f32[64,256]{1,0:T(8,128)S(1)}, f32[64,256]{1,0:T(8,128)S(1)}, u32[]{:S(2)}, u32[]{:S(2)}) collective-permute-start(f32[64,256]{1,0:T(8,128)S(1)} %shard_map.108.refs_0_), channel_id=1, source_target_pairs={{0,8},{1,9},{2,10},{3,11},{4,12},{5,13},{6,14},{7,15},{8,0},{9,1},... | collective-permute-start | bytes 196616 | tf_op jit(solution)/shard_map/ppermute | solution.py:465
  37.5 5.5 %collective-permute-start.14 = (f32[64,256]{1,0:T(8,128)S(1)}, f32[64,256]{1,0:T(8,128)S(1)}, u32[]{:S(2)}, u32[]{:S(2)}) collective-permute-start(f32[64,256]{1,0:T(8,128)S(1)} %shard_map.108.refs_0_), channel_id=1, source_target_pairs={{0,4},{1,5},{2,6},{3,7},{4,0},{5,1},{6,2},{7,3},{8,12},{9,13},{10,... | collective-permute-start | bytes 196616 | tf_op jit(solution)/shard_map/ppermute | solution.py:465
  43.0 5.9 %collective-permute-start.19 = (f32[64,256]{1,0:T(8,128)S(1)}, f32[64,256]{1,0:T(8,128)S(1)}, u32[]{:S(2)}, u32[]{:S(2)}) collective-permute-start(f32[64,256]{1,0:T(8,128)S(1)} %shard_map.109.refs_0_), channel_id=1, source_target_pairs={{0,3},{1,2},{2,1},{3,0},{4,7},{5,6},{6,5},{7,4},{8,11},{9,10},{10,... | collective-permute-start | bytes 196616 | tf_op jit(solution)/shard_map/ppermute | solution.py:465
  43.7 5.2 %collective-permute-start.18 = (f32[64,256]{1,0:T(8,128)S(1)}, f32[64,256]{1,0:T(8,128)S(1)}, u32[]{:S(2)}, u32[]{:S(2)}) collective-permute-start(f32[64,256]{1,0:T(8,128)S(1)} %shard_map.109.refs_0_), channel_id=1, source_target_pairs={{0,2},{1,3},{2,0},{3,1},{4,6},{5,7},{6,4},{7,5},{8,10},{9,11},{10,... | collective-permute-start | bytes 196616 | tf_op jit(solution)/shard_map/ppermute | solution.py:465
  45.3 5.0 %collective-permute-start.17 = (f32[64,256]{1,0:T(8,128)S(1)}, f32[64,256]{1,0:T(8,128)S(1)}, u32[]{:S(2)}, u32[]{:S(2)}) collective-permute-start(f32[64,256]{1,0:T(8,128)S(1)} %shard_map.109.refs_0_), channel_id=1, source_target_pairs={{0,1},{1,0},{2,3},{3,2},{4,5},{5,4},{6,7},{7,6},{8,9},{9,8},{10,11... | collective-permute-start | bytes 196616 | tf_op jit(solution)/shard_map/ppermute | solution.py:465
  46.7 11.1 %collective-permute-start.8 = (f32[2,256,128]{2,1,0:T(8,128)S(1)}, f32[2,256,128]{2,1,0:T(8,128)S(1)}, u32[]{:S(2)}, u32[]{:S(2)}) collective-permute-start(f32[2,256,128]{2,1,0:T(8,128)S(1)} %get-tuple-element.54), channel_id=1, source_target_pairs={{0,1},{2,3},{4,5},{6,7},{8,9},{10,11},{12,13},{14,15},{1,0},{3,2},... | collective-permute-start | bytes 786440 | tf_op jit(solution)/shard_map/ppermute | solution.py:684
  47.6 10.3 %collective-permute-start.9 = (f32[2,256,128]{2,1,0:T(8,128)S(1)}, f32[2,256,128]{2,1,0:T(8,128)S(1)}, u32[]{:S(2)}, u32[]{:S(2)}) collective-permute-start(f32[2,256,128]{2,1,0:T(8,128)S(1)} %get-tuple-element.55), channel_id=1, source_target_pairs={{1,2},{3,4},{5,6},{7,8},{9,10},{11,12},{13,14},{2,1},{4,3},{6,5},{... | collective-permute-start | bytes 786440 | tf_op jit(solution)/shard_map/ppermute | solution.py:685
  50.3 8.8 %collective-permute-start.20 = (f32[256,256]{1,0:T(8,128)S(1)}, f32[256,256]{1,0:T(8,128)S(1)}, u32[]{:S(2)}, u32[]{:S(2)}) collective-permute-start(f32[256,256]{1,0:T(8,128)S(1)} %shard_map.110.full), channel_id=1, source_target_pairs={{0,16},{16,0},{1,17},{17,1},{2,18},{18,2},{3,19},{19,3},{4,20},{20... | collective-permute-start | bytes 786440 | tf_op jit(solution)/shard_map/ppermute | solution.py:465

commit v7 on v6

--- a/solution.py
+++ b/solution.py
@@ -211,26 +211,30 @@
 
 
 def prep_kernel(*refs):
-    hbm, (kr, ki, am, mats), loaded = refs[:6], refs[6:10], refs[10:13]
-    phase, amps, table, sems = refs[13:]
+    hbm, (kr, ki, mats), loaded = refs[:6], refs[6:9], refs[9:13]
+    phase, table, sems = refs[13:]
     n = phase.shape[0]
     h = n // 2
-    copies = copy_all(hbm, (phase, table, amps) + loaded, sems)
+    first = pltpu.make_async_copy(hbm[0], phase, sems.at[0])
+    first.start()
     order = [even_odd(n, axis) for axis in range(2)]
-    copies[0].wait()
+    first.wait()
+    copies = copy_all(hbm[1:], (table,) + loaded, sems)
     angle = reorder(phase[...], order)
     kr[...], ki[...] = cos_sin(angle)
-    copies[1].wait()
+    copies[0].wait()
     for i in range(2):
         mats[i] = table[i]
         mats[2 + i, :h, :h] = table[i, :h, :h]
         mats[2 + i, :h, h:] = -table[i, :h, h:]
         mats[2 + i, h:, :h] = -table[i, h:, :h]
         mats[2 + i, h:, h:] = table[i, h:, h:]
-    copies[2].wait()
-    am[...] = reorder(amps[...], order)
-    for copy in copies[3:]:
+    for copy in copies[1:]:
         copy.wait()
+
+
+def reorder_kernel(x, after, out):
+    out[...] = reorder(x[...], [even_odd(x.shape[0], axis) for axis in range(2)])
 
 
 def roll_kernel(margin, offs, probe, pr):
@@ -606,16 +610,15 @@
         )
         return main
 
-    loads = (phase, mats, amplitudes.reshape(n, n), tw_left, tw_right, probe)
-    kr, ki, am, mats, tw_left, tw_right, pr = call(
+    loads = (phase, mats, tw_left, tw_right, probe, amplitudes.reshape(n, n))
+    kr, ki, mats, tw_left, tw_right, pr, am = call(
         prep_kernel,
-        [(n, n)] * 3
+        [(n, n)] * 2
         + [jax.ShapeDtypeStruct((4, n, n), BF16)]
-        + [jax.ShapeDtypeStruct(x.shape, x.dtype) for x in loads[3:]],
+        + [jax.ShapeDtypeStruct(x.shape, x.dtype) for x in loads[2:]],
         [HBM] * len(loads),
         *[in_hbm(x) for x in loads],
         scratch=[
-            pltpu.VMEM((n, n), F32),
             pltpu.VMEM((n, n), F32),
             pltpu.VMEM((2, n, n), BF16),
             pltpu.SemaphoreType.DMA((len(loads),)),
@@ -640,6 +643,7 @@
         tw_right,
     )
     cut(1, arrive)
+    (am,) = call(reorder_kernel, [(n, n)], [VMEM] * 2, am, arrive)
     main = merge(1)
     keep, give, grads = call(
         functools.partial(back_kernel, n_row, margin),

time: 60.1 us -> 60.6 us (level); the launches traced: 59.8 us -> 59.7 us
  waiting for transfers between devices: 21.8 us -> 21.1 us
    ppermute x2, waiting for transfers between devices: 1.37 us -> 0.74 us  [cut(): corners[s].append(lax.ppermute(parts[i], 'row', pairs))]
    pallas_call x16 -> x17, Pallas kernels: 12.5 us -> 12.9 us  [call(): pl.pallas_call(kernel, out_shape=shapes, in_specs=in_specs, out_specs=[SM...]
where the time goes in v7:
time: 60.6 us; the launch traced here: 59.7 us
  starting transfers between devices  23.5 us (39%)
  waiting for transfers between devices  21.1 us (35%)
  Pallas kernels  14.3 us (24%)
  between operations  0.81 us (1%)
    pallas_call x17, Pallas kernels, call(): pl.pallas_call(kernel, out_shape=shapes, in_specs=in_specs, out_specs=[SM...  12.9 us
    ppermute x11, starting transfers between devices, swap(): return lax.ppermute(value, axis, [(i, i ^ distance) for i in range(count)])  12.4 us
    ppermute x11, waiting for transfers between devices, swap(): return lax.ppermute(value, axis, [(i, i ^ distance) for i in range(count)])  11.5 us
    ppermute x4, starting transfers between devices, whole(): strips.append(lax.ppermute(packed[i], 'col', col_rounds[i % 2]))  8.15 us
    ppermute x1, waiting for transfers between devices, whole(): send_e = lax.ppermute(send_e, 'col', col_rounds[0])  6.62 us
    ppermute x4, waiting for transfers between devices, whole(): strips.append(lax.ppermute(packed[i], 'col', col_rounds[i % 2]))  2.19 us
  transfers between devices with their start and end apart: 21, of which 12 were waited for; matrix products, arithmetic and copies ran while one was open for 0% of the time, Pallas kernels for 13%

profile of v7, /device:TPU:0, one launch (start us, length us, event | category | flops | bytes accessed | tf_op | source)
XLA Modules:
  0.0 59.7 jit_solution(7067730535947394353)
XLA Ops:
  0.6 2.0 %shard_map.95 = (f32[4,256,256]{2,1,0:T(8,128)S(1)}, s32[1,2]{1,0:T(1,128)S(1)}, s32[2,8,128]{2,1,0:T(8,128)S(1)}, f32[256,128]{1,0:T(8,128)S(1)}, f32[256,128]{...) custom-call(f32[4,256,256]{2,1,0:T(8,128)} %bitcast.4, s32[1,2]{1,0:T(1,128)} %bitcast.7), custom_call_target="tpu_custom_call" | custom-call | tf_op jit(solution)/shard_map/pallas_call | solution.py:446
  2.6 0.6 collective-permute-start.2
  3.2 2.6 %collective-permute-start.3 = (f32[256,128]{1,0:T(8,128)S(1)}, f32[256,128]{1,0:T(8,128)S(1)}, u32[]{:S(2)}, u32[]{:S(2)}) collective-permute-start(f32[256,128]{1,0:T(8,128)S(1)} %get-tuple-element.37), channel_id=1, source_target_pairs={{0,1},{2,3},{4,5},{6,7},{8,9},{10,11},{12,13},{14,15},{1,0},{3,2},... | collective-permute-start | bytes 393224 | tf_op jit(solution)/shard_map/ppermute | solution.py:587
  5.7 0.7 %collective-permute-start.4 = (f32[256,128]{1,0:T(8,128)S(1)}, f32[256,128]{1,0:T(8,128)S(1)}, u32[]{:S(2)}, u32[]{:S(2)}) collective-permute-start(f32[256,128]{1,0:T(8,128)S(1)} %get-tuple-element.38), channel_id=1, source_target_pairs={{1,2},{3,4},{5,6},{7,8},{9,10},{11,12},{13,14},{2,1},{4,3},{6,5},{... | collective-permute-start | bytes 393224 | tf_op jit(solution)/shard_map/ppermute | solution.py:587
  6.4 4.3 %collective-permute-start = (f32[256,128]{1,0:T(8,128)S(1)}, f32[256,128]{1,0:T(8,128)S(1)}, u32[]{:S(2)}, u32[]{:S(2)}) collective-permute-start(f32[256,128]{1,0:T(8,128)S(1)} %get-tuple-element.33), channel_id=1, source_target_pairs={{0,1},{2,3},{4,5},{6,7},{8,9},{10,11},{12,13},{14,15},{1,0},{3,2},... | collective-permute-start | bytes 393224 | tf_op jit(solution)/shard_map/ppermute | solution.py:587
  10.7 0.7 %collective-permute-start.1 = (f32[256,128]{1,0:T(8,128)S(1)}, f32[256,128]{1,0:T(8,128)S(1)}, u32[]{:S(2)}, u32[]{:S(2)}) collective-permute-start(f32[256,128]{1,0:T(8,128)S(1)} %get-tuple-element.34), channel_id=1, source_target_pairs={{1,2},{3,4},{5,6},{7,8},{9,10},{11,12},{13,14},{2,1},{4,3},{6,5},{... | collective-permute-start | bytes 393224 | tf_op jit(solution)/shard_map/ppermute | solution.py:587
  11.3 2.3 %shard_map.98 = (f32[256,256]{1,0:T(8,128)S(1)}, f32[256,256]{1,0:T(8,128)S(1)}, bf16[4,256,256]{2,1,0:T(8,128)(2,1)S(1)}, f32[2,128,128]{2,1,0:T(8,128)S(1)}, f...) custom-call(f32[256,256]{1,0:T(8,128)} %refs_0_.1, ...), custom_call_target="tpu_custom_call" | custom-call | tf_op jit(solution)/shard_map/pallas_call | solution.py:446
  13.7 0.8 %shard_map.100.refs_4_.refs_5_ = f32[2,256,256]{2,1,0:T(8,128)S(1)} custom-call(s32[1,2]{1,0:T(1,128)S(1)} %get-tuple-element.40.offs, f32[2,256,256]{2,1,0:T(8,128)S(1)} %get-tuple-element.41.probe), custom_call_target="tpu_custom_call" | custom-call | tf_op jit(solution)/shard_map/pallas_call | solution.py:446
  15.0 1.5 %shard_map.101 = (f32[2,256,256]{2,1,0:T(8,128)S(1)}, f32[2,256,256]{2,1,0:T(8,128)S(1)}) custom-call(f32[2,256,256]{2,1,0:T(8,128)S(1)} %shard_map.97.refs_0_, f32[4,64,256]{2,1,0:T(8,128)S(1)} %collective-permute-done.2.refs_1_, f32[2,64,128]{2,1,0:T(8,128)S(1)} %collective-permute-done.5.refs_2_, s32[2,8,128]{2,1,0:T(8,128)S(1)} %get-tuple-element.35.limits.refs_3_, ...), custom_call_target="tpu_custom_call" | custom-call | tf_op jit(solution)/shard_map/pallas_call | solution.py:446
  16.5 2.2 %collective-permute-done.e = f32[256,128]{1,0:T(8,128)S(1)} collective-permute-done((f32[256,128]{1,0:T(8,128)S(1)}, f32[256,128]{1,0:T(8,128)S(1)}, u32[]{:S(2)}, u32[]{:S(2)}) %collective-permute-start) | collective-permute-done | bytes 131104 | tf_op jit(solution)/shard_map/ppermute | solution.py:587
  18.9 0.6 %shard_map.103.refs_8_ = f32[256,256]{1,0:T(8,128)S(1)} custom-call(f32[256,256]{1,0:T(8,128)S(1)} %get-tuple-element.47.x, f32[2,256,256]{2,1,0:T(8,128)S(1)} %get-tuple-element.46.after.refs_10_), custom_call_target="tpu_custom_call" | custom-call | tf_op jit(solution)/shard_map/pallas_call | solution.py:446
  20.0 3.6 %shard_map.104 = (f32[256,256]{1,0:T(8,128)S(1)}, f32[256,256]{1,0:T(8,128)S(1)}, f32[4,256,256]{2,1,0:T(8,128)S(1)}) custom-call(f32[2,256,256]{2,1,0:T(8,128)S(1)} %shard_map.96.refs_0_, f32[4,64,256]{2,1,0:T(8,128)S(1)} %collective-permute-done.2.refs_1_, f32[2,64,128]{2,1,0:T(8,128)S(1)} %collective-permute-done.6.refs_2_, ...), custom_call_target="tpu_custom_call" | custom-call | tf_op jit(solution)/shard_map/pallas_call | solution.py:446
  24.6 0.6 collective-permute-done.10.other
  25.2 2.5 %collective-permute-start.11 = (f32[64,256]{1,0:T(8,128)S(1)}, f32[64,256]{1,0:T(8,128)S(1)}, u32[]{:S(2)}, u32[]{:S(2)}) collective-permute-start(f32[64,256]{1,0:T(8,128)S(1)} %get-tuple-element.59), channel_id=1, source_target_pairs={{0,1},{1,0},{2,3},{3,2},{4,5},{5,4},{6,7},{7,6},{8,9},{9,8},{10,11... | collective-permute-start | bytes 196616 | tf_op jit(solution)/shard_map/ppermute | solution.py:469
  27.8 1.1 %collective-permute-start.12 = (f32[64,256]{1,0:T(8,128)S(1)}, f32[64,256]{1,0:T(8,128)S(1)}, u32[]{:S(2)}, u32[]{:S(2)}) collective-permute-start(f32[64,256]{1,0:T(8,128)S(1)} %get-tuple-element.60), channel_id=1, source_target_pairs={{0,2},{1,3},{2,0},{3,1},{4,6},{5,7},{6,4},{7,5},{8,10},{9,11},{10,... | collective-permute-start | bytes 196616 | tf_op jit(solution)/shard_map/ppermute | solution.py:469
  29.3 0.9 %collective-permute-done.11.refs_1_ = f32[64,256]{1,0:T(8,128)S(1)} collective-permute-done((f32[64,256]{1,0:T(8,128)S(1)}, f32[64,256]{1,0:T(8,128)S(1)}, u32[]{:S(2)}, u32[]{:S(2)}) %collective-permute-start.11) | collective-permute-done | bytes 65568 | tf_op jit(solution)/shard_map/ppermute | solution.py:469
  30.2 1.9 %collective-permute-done.12.refs_2_ = f32[64,256]{1,0:T(8,128)S(1)} collective-permute-done((f32[64,256]{1,0:T(8,128)S(1)}, f32[64,256]{1,0:T(8,128)S(1)}, u32[]{:S(2)}, u32[]{:S(2)}) %collective-permute-start.12) | collective-permute-done | bytes 65568 | tf_op jit(solution)/shard_map/ppermute | solution.py:469
  32.0 2.0 %collective-permute-done.13.refs_3_ = f32[64,256]{1,0:T(8,128)S(1)} collective-permute-done((f32[64,256]{1,0:T(8,128)S(1)}, f32[64,256]{1,0:T(8,128)S(1)}, u32[]{:S(2)}, u32[]{:S(2)}) %collective-permute-start.13) | collective-permute-done | bytes 65568 | tf_op jit(solution)/shard_map/ppermute | solution.py:469
  34.1 2.8 %collective-permute-start.16 = (f32[64,256]{1,0:T(8,128)S(1)}, f32[64,256]{1,0:T(8,128)S(1)}, u32[]{:S(2)}, u32[]{:S(2)}) collective-permute-start(f32[64,256]{1,0:T(8,128)S(1)} %shard_map.109.refs_0_), channel_id=1, source_target_pairs={{0,12},{1,13},{2,14},{3,15},{4,8},{5,9},{6,10},{7,11},{8,4},{9,5},... | collective-permute-start | bytes 196616 | tf_op jit(solution)/shard_map/ppermute | solution.py:469
  37.2 1.4 %collective-permute-start.14 = (f32[64,256]{1,0:T(8,128)S(1)}, f32[64,256]{1,0:T(8,128)S(1)}, u32[]{:S(2)}, u32[]{:S(2)}) collective-permute-start(f32[64,256]{1,0:T(8,128)S(1)} %shard_map.109.refs_0_), channel_id=1, source_target_pairs={{0,4},{1,5},{2,6},{3,7},{4,0},{5,1},{6,2},{7,3},{8,12},{9,13},{10,... | collective-permute-start | bytes 196616 | tf_op jit(solution)/shard_map/ppermute | solution.py:469
  38.5 1.7 %collective-permute-done.16.refs_3_ = f32[64,256]{1,0:T(8,128)S(1)} collective-permute-done((f32[64,256]{1,0:T(8,128)S(1)}, f32[64,256]{1,0:T(8,128)S(1)}, u32[]{:S(2)}, u32[]{:S(2)}) %collective-permute-start.16) | collective-permute-done | bytes 65568 | tf_op jit(solution)/shard_map/ppermute | solution.py:469
  40.3 2.4 %collective-permute-done.15.refs_2_ = f32[64,256]{1,0:T(8,128)S(1)} collective-permute-done((f32[64,256]{1,0:T(8,128)S(1)}, f32[64,256]{1,0:T(8,128)S(1)}, u32[]{:S(2)}, u32[]{:S(2)}) %collective-permute-start.15) | collective-permute-done | bytes 65568 | tf_op jit(solution)/shard_map/ppermute | solution.py:469
  42.7 1.1 %collective-permute-start.19 = (f32[64,256]{1,0:T(8,128)S(1)}, f32[64,256]{1,0:T(8,128)S(1)}, u32[]{:S(2)}, u32[]{:S(2)}) collective-permute-start(f32[64,256]{1,0:T(8,128)S(1)} %shard_map.110.refs_0_), channel_id=1, source_target_pairs={{0,3},{1,2},{2,1},{3,0},{4,7},{5,6},{6,5},{7,4},{8,11},{9,10},{10,... | collective-permute-start | bytes 196616 | tf_op jit(solution)/shard_map/ppermute | solution.py:469
  43.7 1.6 %collective-permute-start.18 = (f32[64,256]{1,0:T(8,128)S(1)}, f32[64,256]{1,0:T(8,128)S(1)}, u32[]{:S(2)}, u32[]{:S(2)}) collective-permute-start(f32[64,256]{1,0:T(8,128)S(1)} %shard_map.110.refs_0_), channel_id=1, source_target_pairs={{0,2},{1,3},{2,0},{3,1},{4,6},{5,7},{6,4},{7,5},{8,10},{9,11},{10,... | collective-permute-start | bytes 196616 | tf_op jit(solution)/shard_map/ppermute | solution.py:469
  45.3 0.9 %collective-permute-start.17 = (f32[64,256]{1,0:T(8,128)S(1)}, f32[64,256]{1,0:T(8,128)S(1)}, u32[]{:S(2)}, u32[]{:S(2)}) collective-permute-start(f32[64,256]{1,0:T(8,128)S(1)} %shard_map.110.refs_0_), channel_id=1, source_target_pairs={{0,1},{1,0},{2,3},{3,2},{4,5},{5,4},{6,7},{7,6},{8,9},{9,8},{10,11... | collective-permute-start | bytes 196616 | tf_op jit(solution)/shard_map/ppermute | solution.py:469
  46.4 1.2 %collective-permute-start.8 = (f32[2,256,128]{2,1,0:T(8,128)S(1)}, f32[2,256,128]{2,1,0:T(8,128)S(1)}, u32[]{:S(2)}, u32[]{:S(2)}) collective-permute-start(f32[2,256,128]{2,1,0:T(8,128)S(1)} %get-tuple-element.54), channel_id=1, source_target_pairs={{0,1},{2,3},{4,5},{6,7},{8,9},{10,11},{12,13},{14,15},{1,0},{3,2},... | collective-permute-start | bytes 786440 | tf_op jit(solution)/shard_map/ppermute | solution.py:688
  47.6 0.7 %collective-permute-start.9 = (f32[2,256,128]{2,1,0:T(8,128)S(1)}, f32[2,256,128]{2,1,0:T(8,128)S(1)}, u32[]{:S(2)}, u32[]{:S(2)}) collective-permute-start(f32[2,256,128]{2,1,0:T(8,128)S(1)} %get-tuple-element.55), channel_id=1, source_target_pairs={{1,2},{3,4},{5,6},{7,8},{9,10},{11,12},{13,14},{2,1},{4,3},{6,5},{... | collective-permute-start | bytes 786440 | tf_op jit(solution)/shard_map/ppermute | solution.py:689
  48.7 1.6 %collective-permute-done.17.refs_1_ = f32[64,256]{1,0:T(8,128)S(1)} collective-permute-done((f32[64,256]{1,0:T(8,128)S(1)}, f32[64,256]{1,0:T(8,128)S(1)}, u32[]{:S(2)}, u32[]{:S(2)}) %collective-permute-start.17) | collective-permute-done | bytes 65568 | tf_op jit(solution)/shard_map/ppermute | solution.py:469
  50.4 0.7 %shard_map.112.started = f32[2,256,256]{2,1,0:T(8,128)} custom-call(f32[256,256]{1,0:T(8,128)S(1)} %shard_map.111.full), custom_call_target="tpu_custom_call" | custom-call | tf_op jit(solution)/shard_map/pallas_call | solution.py:559
  51.1 6.6 %collective-permute-done.8.e = f32[2,256,128]{2,1,0:T(8,128)S(1)} collective-permute-done((f32[2,256,128]{2,1,0:T(8,128)S(1)}, f32[2,256,128]{2,1,0:T(8,128)S(1)}, u32[]{:S(2)}, u32[]{:S(2)}) %collective-permute-start.8) | collective-permute-done | bytes 262176 | tf_op jit(solution)/shard_map/ppermute | solution.py:688
  57.8 1.2 %shard_map.107 = f32[4,256,256]{2,1,0:T(8,128)} custom-call(f32[4,256,256]{2,1,0:T(8,128)S(1)} %get-tuple-element.53.total, f32[2,256,128]{2,1,0:T(8,128)S(1)} %collective-permute-done.8.e, f32[2,256,128]{2,1,0:T(8,128)S(1)} %collective-permute-done.9.o), custom_call_target="tpu_custom_call" | custom-call | tf_op jit(solution)/shard_map/pallas_call | solution.py:446
  59.0 0.7 %shard_map.113 = f32[2,256,256]{2,1,0:T(8,128)} custom-call(f32[2,256,256]{2,1,0:T(8,128)} %shard_map.112.started, f32[256,256]{1,0:T(8,128)S(1)} %collective-permute-done.20.other), custom_call_target="tpu_custom_call", output_to_operand_aliasing={{}: (0, {})} | custom-call | tf_op jit(solution)/shard_map/pallas_call | solution.py:560
  (29 shorter events, 3.7 us)
Async XLA Ops:
  2.6 12.4 %collective-permute-start.2 = (f32[4,64,256]{2,1,0:T(8,128)S(1)}, f32[4,64,256]{2,1,0:T(8,128)S(1)}, u32[]{:S(2)}, u32[]{:S(2)}) collective-permute-start(f32[4,64,256]{2,1,0:T(8,128)S(1)} %get-tuple-element.36), channel_id=1, source_target_pairs={{0,16},{16,0},{1,17},{17,1},{2,18},{18,2},{3,19},{19,3},{4,20},{20... | collective-permute-start | bytes 786440 | tf_op jit(solution)/shard_map/ppermute | solution.py:589
  3.2 10.5 %collective-permute-start.3 = (f32[256,128]{1,0:T(8,128)S(1)}, f32[256,128]{1,0:T(8,128)S(1)}, u32[]{:S(2)}, u32[]{:S(2)}) collective-permute-start(f32[256,128]{1,0:T(8,128)S(1)} %get-tuple-element.37), channel_id=1, source_target_pairs={{0,1},{2,3},{4,5},{6,7},{8,9},{10,11},{12,13},{14,15},{1,0},{3,2},... | collective-permute-start | bytes 393224 | tf_op jit(solution)/shard_map/ppermute | solution.py:587
  5.7 7.9 %collective-permute-start.4 = (f32[256,128]{1,0:T(8,128)S(1)}, f32[256,128]{1,0:T(8,128)S(1)}, u32[]{:S(2)}, u32[]{:S(2)}) collective-permute-start(f32[256,128]{1,0:T(8,128)S(1)} %get-tuple-element.38), channel_id=1, source_target_pairs={{1,2},{3,4},{5,6},{7,8},{9,10},{11,12},{13,14},{2,1},{4,3},{6,5},{... | collective-permute-start | bytes 393224 | tf_op jit(solution)/shard_map/ppermute | solution.py:587
  6.4 12.3 %collective-permute-start = (f32[256,128]{1,0:T(8,128)S(1)}, f32[256,128]{1,0:T(8,128)S(1)}, u32[]{:S(2)}, u32[]{:S(2)}) collective-permute-start(f32[256,128]{1,0:T(8,128)S(1)} %get-tuple-element.33), channel_id=1, source_target_pairs={{0,1},{2,3},{4,5},{6,7},{8,9},{10,11},{12,13},{14,15},{1,0},{3,2},... | collective-permute-start | bytes 393224 | tf_op jit(solution)/shard_map/ppermute | solution.py:587
  10.7 8.0 %collective-permute-start.1 = (f32[256,128]{1,0:T(8,128)S(1)}, f32[256,128]{1,0:T(8,128)S(1)}, u32[]{:S(2)}, u32[]{:S(2)}) collective-permute-start(f32[256,128]{1,0:T(8,128)S(1)} %get-tuple-element.34), channel_id=1, source_target_pairs={{1,2},{3,4},{5,6},{7,8},{9,10},{11,12},{13,14},{2,1},{4,3},{6,5},{... | collective-permute-start | bytes 393224 | tf_op jit(solution)/shard_map/ppermute | solution.py:587
  13.7 1.3 %collective-permute-start.5 = (f32[2,64,128]{2,1,0:T(8,128)S(1)}, f32[2,64,128]{2,1,0:T(8,128)S(1)}, u32[]{:S(2)}, u32[]{:S(2)}) collective-permute-start(f32[2,64,128]{2,1,0:T(8,128)S(1)} %shard_map.99), channel_id=1, source_target_pairs={{0,16},{16,0},{1,17},{17,1},{2,18},{18,2},{3,19},{19,3},{4,20},{20... | collective-permute-start | bytes 196616 | tf_op jit(solution)/shard_map/ppermute | solution.py:600
  18.7 1.3 %collective-permute-start.6 = (f32[2,64,128]{2,1,0:T(8,128)S(1)}, f32[2,64,128]{2,1,0:T(8,128)S(1)}, u32[]{:S(2)}, u32[]{:S(2)}) collective-permute-start(f32[2,64,128]{2,1,0:T(8,128)S(1)} %shard_map.102), channel_id=1, source_target_pairs={{0,16},{16,0},{1,17},{17,1},{2,18},{18,2},{3,19},{19,3},{4,20},{20... | collective-permute-start | bytes 196616 | tf_op jit(solution)/shard_map/ppermute | solution.py:600
  23.6 1.6 %collective-permute-start.10 = (f32[256,256]{1,0:T(8,128)S(1)}, f32[256,256]{1,0:T(8,128)S(1)}, u32[]{:S(2)}, u32[]{:S(2)}) collective-permute-start(f32[256,256]{1,0:T(8,128)S(1)} %get-tuple-element.57), channel_id=1, source_target_pairs={{0,16},{16,0},{1,17},{17,1},{2,18},{18,2},{3,19},{19,3},{4,20},{20... | collective-permute-start | bytes 786440 | tf_op jit(solution)/shard_map/ppermute | solution.py:469
  24.2 22.1 %collective-permute-start.7 = (f32[4,64,384]{2,1,0:T(8,128)S(1)}, f32[4,64,384]{2,1,0:T(8,128)S(1)}, u32[]{:S(2)}, u32[]{:S(2)}) collective-permute-start(f32[4,64,384]{2,1,0:T(8,128)S(1)} %get-tuple-element.52), channel_id=1, source_target_pairs={{0,16},{16,0},{1,17},{17,1},{2,18},{18,2},{3,19},{19,3},{4,20},{20... | collective-permute-start | bytes 1179656 | tf_op jit(solution)/shard_map/ppermute | solution.py:679
  25.2 5.0 %collective-permute-start.11 = (f32[64,256]{1,0:T(8,128)S(1)}, f32[64,256]{1,0:T(8,128)S(1)}, u32[]{:S(2)}, u32[]{:S(2)}) collective-permute-start(f32[64,256]{1,0:T(8,128)S(1)} %get-tuple-element.59), channel_id=1, source_target_pairs={{0,1},{1,0},{2,3},{3,2},{4,5},{5,4},{6,7},{7,6},{8,9},{9,8},{10,11... | collective-permute-start | bytes 196616 | tf_op jit(solution)/shard_map/ppermute | solution.py:469
  27.8 4.3 %collective-permute-start.12 = (f32[64,256]{1,0:T(8,128)S(1)}, f32[64,256]{1,0:T(8,128)S(1)}, u32[]{:S(2)}, u32[]{:S(2)}) collective-permute-start(f32[64,256]{1,0:T(8,128)S(1)} %get-tuple-element.60), channel_id=1, source_target_pairs={{0,2},{1,3},{2,0},{3,1},{4,6},{5,7},{6,4},{7,5},{8,10},{9,11},{10,... | collective-permute-start | bytes 196616 | tf_op jit(solution)/shard_map/ppermute | solution.py:469
  28.9 5.2 %collective-permute-start.13 = (f32[64,256]{1,0:T(8,128)S(1)}, f32[64,256]{1,0:T(8,128)S(1)}, u32[]{:S(2)}, u32[]{:S(2)}) collective-permute-start(f32[64,256]{1,0:T(8,128)S(1)} %get-tuple-element.61), channel_id=1, source_target_pairs={{0,3},{1,2},{2,1},{3,0},{4,7},{5,6},{6,5},{7,4},{8,11},{9,10},{10,... | collective-permute-start | bytes 196616 | tf_op jit(solution)/shard_map/ppermute | solution.py:469
  34.1 6.2 %collective-permute-start.16 = (f32[64,256]{1,0:T(8,128)S(1)}, f32[64,256]{1,0:T(8,128)S(1)}, u32[]{:S(2)}, u32[]{:S(2)}) collective-permute-start(f32[64,256]{1,0:T(8,128)S(1)} %shard_map.109.refs_0_), channel_id=1, source_target_pairs={{0,12},{1,13},{2,14},{3,15},{4,8},{5,9},{6,10},{7,11},{8,4},{9,5},... | collective-permute-start | bytes 196616 | tf_op jit(solution)/shard_map/ppermute | solution.py:469
  36.8 5.8 %collective-permute-start.15 = (f32[64,256]{1,0:T(8,128)S(1)}, f32[64,256]{1,0:T(8,128)S(1)}, u32[]{:S(2)}, u32[]{:S(2)}) collective-permute-start(f32[64,256]{1,0:T(8,128)S(1)} %shard_map.109.refs_0_), channel_id=1, source_target_pairs={{0,8},{1,9},{2,10},{3,11},{4,12},{5,13},{6,14},{7,15},{8,0},{9,1},... | collective-permute-start | bytes 196616 | tf_op jit(solution)/shard_map/ppermute | solution.py:469
  37.2 5.5 %collective-permute-start.14 = (f32[64,256]{1,0:T(8,128)S(1)}, f32[64,256]{1,0:T(8,128)S(1)}, u32[]{:S(2)}, u32[]{:S(2)}) collective-permute-start(f32[64,256]{1,0:T(8,128)S(1)} %shard_map.109.refs_0_), channel_id=1, source_target_pairs={{0,4},{1,5},{2,6},{3,7},{4,0},{5,1},{6,2},{7,3},{8,12},{9,13},{10,... | collective-permute-start | bytes 196616 | tf_op jit(solution)/shard_map/ppermute | solution.py:469
  42.7 5.6 %collective-permute-start.19 = (f32[64,256]{1,0:T(8,128)S(1)}, f32[64,256]{1,0:T(8,128)S(1)}, u32[]{:S(2)}, u32[]{:S(2)}) collective-permute-start(f32[64,256]{1,0:T(8,128)S(1)} %shard_map.110.refs_0_), channel_id=1, source_target_pairs={{0,3},{1,2},{2,1},{3,0},{4,7},{5,6},{6,5},{7,4},{8,11},{9,10},{10,... | collective-permute-start | bytes 196616 | tf_op jit(solution)/shard_map/ppermute | solution.py:469
  43.7 4.9 %collective-permute-start.18 = (f32[64,256]{1,0:T(8,128)S(1)}, f32[64,256]{1,0:T(8,128)S(1)}, u32[]{:S(2)}, u32[]{:S(2)}) collective-permute-start(f32[64,256]{1,0:T(8,128)S(1)} %shard_map.110.refs_0_), channel_id=1, source_target_pairs={{0,2},{1,3},{2,0},{3,1},{4,6},{5,7},{6,4},{7,5},{8,10},{9,11},{10,... | collective-permute-start | bytes 196616 | tf_op jit(solution)/shard_map/ppermute | solution.py:469
  45.3 5.0 %collective-permute-start.17 = (f32[64,256]{1,0:T(8,128)S(1)}, f32[64,256]{1,0:T(8,128)S(1)}, u32[]{:S(2)}, u32[]{:S(2)}) collective-permute-start(f32[64,256]{1,0:T(8,128)S(1)} %shard_map.110.refs_0_), channel_id=1, source_target_pairs={{0,1},{1,0},{2,3},{3,2},{4,5},{5,4},{6,7},{7,6},{8,9},{9,8},{10,11... | collective-permute-start | bytes 196616 | tf_op jit(solution)/shard_map/ppermute | solution.py:469
  46.4 11.3 %collective-permute-start.8 = (f32[2,256,128]{2,1,0:T(8,128)S(1)}, f32[2,256,128]{2,1,0:T(8,128)S(1)}, u32[]{:S(2)}, u32[]{:S(2)}) collective-permute-start(f32[2,256,128]{2,1,0:T(8,128)S(1)} %get-tuple-element.54), channel_id=1, source_target_pairs={{0,1},{2,3},{4,5},{6,7},{8,9},{10,11},{12,13},{14,15},{1,0},{3,2},... | collective-permute-start | bytes 786440 | tf_op jit(solution)/shard_map/ppermute | solution.py:688
  47.6 10.2 %collective-permute-start.9 = (f32[2,256,128]{2,1,0:T(8,128)S(1)}, f32[2,256,128]{2,1,0:T(8,128)S(1)}, u32[]{:S(2)}, u32[]{:S(2)}) collective-permute-start(f32[2,256,128]{2,1,0:T(8,128)S(1)} %get-tuple-element.55), channel_id=1, source_target_pairs={{1,2},{3,4},{5,6},{7,8},{9,10},{11,12},{13,14},{2,1},{4,3},{6,5},{... | collective-permute-start | bytes 786440 | tf_op jit(solution)/shard_map/ppermute | solution.py:689
  50.3 8.6 %collective-permute-start.20 = (f32[256,256]{1,0:T(8,128)S(1)}, f32[256,256]{1,0:T(8,128)S(1)}, u32[]{:S(2)}, u32[]{:S(2)}) collective-permute-start(f32[256,256]{1,0:T(8,128)S(1)} %shard_map.111.full), channel_id=1, source_target_pairs={{0,16},{16,0},{1,17},{17,1},{2,18},{18,2},{3,19},{19,3},{4,20},{20... | collective-permute-start | bytes 786440 | tf_op jit(solution)/shard_map/ppermute | solution.py:469

commit v8 on v7

--- a/solution.py
+++ b/solution.py
@@ -168,7 +168,7 @@
 
 
 def pack_kernel(margin, obj_hbm, offs_hbm, obj, offs, limits, *refs):
-    strips, rows, sems = refs[:4], refs[4:-1], refs[-1]
+    evens, odds, rows, sems = refs[:2], refs[2], refs[3:-1], refs[-1]
     n = obj.shape[1]
     copies = copy_all(
         (obj_hbm.at[0:2], obj_hbm.at[2:4], offs_hbm), (obj.at[0:2], obj.at[2:4], offs), sems
@@ -177,8 +177,8 @@
     for s in range(2):
         copies[s].wait()
         low, high = pack_cols(obj[2 * s], obj[2 * s + 1])
-        strips[2 * s][...] = jnp.where(even, high, low)
-        strips[2 * s + 1][...] = jnp.where(even, low, high)
+        evens[s][...] = jnp.where(even, high, low)
+        odds[s] = jnp.where(even, low, high)
     for which, out in enumerate(rows):
         out[...] = obj[:, pl.ds(row_start(which, n, margin), margin), :]
     copies[2].wait()
@@ -186,11 +186,11 @@
         limits[i] = jnp.full(limits.shape[1:], offs[0, i] - margin, jnp.int32)
 
 
-def corner_kernel(margin, e, o, after, *outs):
+def corner_kernel(s, margin, e, o, after, *outs):
     for which, out in enumerate(outs):
         rows = pl.ds(row_start(which, e.shape[0], margin), margin)
         out[0] = e[rows, :]
-        out[1] = o[rows, :]
+        out[1] = o[s, rows, :]
 
 
 def even_odd(n, axis):
@@ -271,7 +271,7 @@
 
 def merge_kernel(s, obj, e, o, limits, out):
     own = [obj[2 * s], obj[2 * s + 1]]
-    out[0], out[1] = merge_cols(own, e[...], o[...], limits)
+    out[0], out[1] = merge_cols(own, e[...], o[s], limits)
 
 
 def window_of(main, s, halos, corners, limits, margin):
@@ -571,29 +571,32 @@
 
     row_rounds, col_rounds = edges("row"), edges("col")
     n_row = len(row_rounds)
-    obj, offs, limits, *packed = call(
+    obj, offs, limits, even0, even1, odds, *rows = call(
         functools.partial(pack_kernel, margin),
         [(4, n, n), jax.ShapeDtypeStruct((1, 2), jnp.int32)]
         + [jax.ShapeDtypeStruct((2, 8, h), jnp.int32)]
-        + [(n, h)] * 4
+        + [(n, h), (n, h), (2, n, h)]
         + [(4, margin, n)] * n_row,
         [HBM, HBM],
         in_hbm(object_field.reshape(4, tile, tile)),
         in_hbm(offsets.reshape(1, 2)),
         scratch=[pltpu.SemaphoreType.DMA((3,))],
     )
-    strips, halos, corners = [], [], [[], []]
-    for i in range(4):
-        strips.append(lax.ppermute(packed[i], "col", col_rounds[i % 2]))
+    halos, corners = [], [[], []]
+    even0 = lax.ppermute(even0, "col", col_rounds[0])
+    odds = lax.ppermute(odds, "col", col_rounds[1])
+    even1 = lax.ppermute(even1, "col", col_rounds[0])
     for i, pairs in enumerate(row_rounds):
-        halos.append(lax.ppermute(packed[4 + i], "row", pairs))
+        halos.append(lax.ppermute(rows[i], "row", pairs))
+    evens = (even0, even1)
 
     def cut(s, after):
         parts = call(
-            functools.partial(corner_kernel, margin),
+            functools.partial(corner_kernel, s, margin),
             [(2, margin, h)] * n_row,
             [VMEM] * 3,
-            *strips[2 * s : 2 * s + 2],
+            evens[s],
+            odds,
             after,
         )
         for i, pairs in enumerate(row_rounds):
@@ -605,7 +608,8 @@
             [(2, n, n)],
             [VMEM] * 4,
             obj,
-            *strips[2 * s : 2 * s + 2],
+            evens[s],
+            odds,
             limits,
         )
         return main
@@ -624,9 +628,11 @@
             pltpu.SemaphoreType.DMA((len(loads),)),
         ],
     )
-    cut(0, kr)
     (pr,) = call(functools.partial(roll_kernel, margin), [(2, n, n)], [SMEM, VMEM], offs, pr)
+    (am,) = call(reorder_kernel, [(n, n)], [VMEM] * 2, am, pr)
+    cut(0, am)
     main = merge(0)
+    cut(1, main)
     w1, arrive = call(
         functools.partial(arrive_kernel, n_row, margin),
         [(2, n, n), (2, n, n)],
@@ -642,8 +648,6 @@
         tw_left,
         tw_right,
     )
-    cut(1, arrive)
-    (am,) = call(reorder_kernel, [(n, n)], [VMEM] * 2, am, arrive)
     main = merge(1)
     keep, give, grads = call(
         functools.partial(back_kernel, n_row, margin),

time: 60.6 us -> 62 us (1.023)
  waiting for transfers between devices: 21.1 us -> 25.5 us
  starting transfers between devices: 23.5 us -> 20.9 us
    ppermute x5 -> x4, waiting for transfers between devices: 2.2 us -> 7.45 us  [the longest x1 6.02 us: whole(): even0 = lax.ppermute(even0, 'col', col_rounds[0])]
    ppermute x5 -> x4, starting transfers between devices: 8.71 us -> 6.59 us  [the longest x1 5.27 us: whole(): even0 = lax.ppermute(even0, 'col', col_rounds[0])]
    ppermute x2, waiting for transfers between devices: 0.74 us -> 0.01 us  [cut(): corners[s].append(lax.ppermute(parts[i], 'row', pairs))]
  transfers between devices with their start and end apart: 21 -> 20, of which waited for: 12 -> 11; matrix products, arithmetic and copies ran while one was open for 0% -> 0% of each run, Pallas kernels for 13% -> 13%
where the time goes in v8:
time: 62 us; the launch traced here: 61.5 us
  waiting for transfers between devices  25.5 us (41%)
  starting transfers between devices  20.9 us (34%)
  Pallas kernels  14.3 us (23%)
  between operations  0.8 us (1%)
    pallas_call x17, Pallas kernels, call(): pl.pallas_call(kernel, out_shape=shapes, in_specs=in_specs, out_specs=[SM...  12.9 us
    ppermute x11, starting transfers between devices, swap(): return lax.ppermute(value, axis, [(i, i ^ distance) for i in range(count)])  12.6 us
    ppermute x11, waiting for transfers between devices, swap(): return lax.ppermute(value, axis, [(i, i ^ distance) for i in range(count)])  11 us
    ppermute x1, waiting for transfers between devices, whole(): send_e = lax.ppermute(send_e, 'col', col_rounds[0])  7.03 us
    ppermute x1, waiting for transfers between devices, whole(): even0 = lax.ppermute(even0, 'col', col_rounds[0])  6.02 us
    ppermute x1, starting transfers between devices, whole(): even0 = lax.ppermute(even0, 'col', col_rounds[0])  5.27 us
    ppermute x1, waiting for transfers between devices, whole(): even1 = lax.ppermute(even1, 'col', col_rounds[0])  1.42 us
  transfers between devices with their start and end apart: 20, of which 11 were waited for; matrix products, arithmetic and copies ran while one was open for 0% of the time, Pallas kernels for 13%

profile of v8, /device:TPU:0, one launch (start us, length us, event | category | flops | bytes accessed | tf_op | source)
XLA Modules:
  0.0 61.5 jit_solution(10293130939077079465)
XLA Ops:
  0.6 2.0 %shard_map.95 = (f32[4,256,256]{2,1,0:T(8,128)S(1)}, s32[1,2]{1,0:T(1,128)S(1)}, s32[2,8,128]{2,1,0:T(8,128)S(1)}, f32[256,128]{1,0:T(8,128)S(1)}, f32[256,128]{...) custom-call(f32[4,256,256]{2,1,0:T(8,128)} %bitcast.4, s32[1,2]{1,0:T(1,128)} %bitcast.7), custom_call_target="tpu_custom_call" | custom-call | tf_op jit(solution)/shard_map/pallas_call | solution.py:446
  2.6 0.7 %collective-permute-start.1 = (f32[2,256,128]{2,1,0:T(8,128)S(1)}, f32[2,256,128]{2,1,0:T(8,128)S(1)}, u32[]{:S(2)}, u32[]{:S(2)}) collective-permute-start(f32[2,256,128]{2,1,0:T(8,128)S(1)} %get-tuple-element.33), channel_id=1, source_target_pairs={{1,2},{3,4},{5,6},{7,8},{9,10},{11,12},{13,14},{2,1},{4,3},{6,5},{... | collective-permute-start | bytes 786440 | tf_op jit(solution)/shard_map/ppermute | solution.py:587
  3.3 0.6 collective-permute-start.2
  3.9 5.3 %collective-permute-start.3 = (f32[256,128]{1,0:T(8,128)S(1)}, f32[256,128]{1,0:T(8,128)S(1)}, u32[]{:S(2)}, u32[]{:S(2)}) collective-permute-start(f32[256,128]{1,0:T(8,128)S(1)} %get-tuple-element.36), channel_id=1, source_target_pairs={{0,1},{2,3},{4,5},{6,7},{8,9},{10,11},{12,13},{14,15},{1,0},{3,2},... | collective-permute-start | bytes 393224 | tf_op jit(solution)/shard_map/ppermute | solution.py:586
  9.2 2.3 %shard_map.99 = (f32[256,256]{1,0:T(8,128)S(1)}, f32[256,256]{1,0:T(8,128)S(1)}, bf16[4,256,256]{2,1,0:T(8,128)(2,1)S(1)}, f32[2,128,128]{2,1,0:T(8,128)S(1)}, f...) custom-call(f32[256,256]{1,0:T(8,128)} %refs_0_.1, ...), custom_call_target="tpu_custom_call" | custom-call | tf_op jit(solution)/shard_map/pallas_call | solution.py:446
  11.5 0.8 %shard_map.100.after.refs_4_.refs_5_ = f32[2,256,256]{2,1,0:T(8,128)S(1)} custom-call(s32[1,2]{1,0:T(1,128)S(1)} %get-tuple-element.37.offs, f32[2,256,256]{2,1,0:T(8,128)S(1)} %get-tuple-element.38.probe), custom_call_target="tpu_custom_call" | custom-call | tf_op jit(solution)/shard_map/pallas_call | solution.py:446
  12.3 0.6 %shard_map.101.after.refs_8_ = f32[256,256]{1,0:T(8,128)S(1)} custom-call(f32[256,256]{1,0:T(8,128)S(1)} %get-tuple-element.41.x, f32[2,256,256]{2,1,0:T(8,128)S(1)} %shard_map.100.after.refs_4_.refs_5_), custom_call_target="tpu_custom_call" | custom-call | tf_op jit(solution)/shard_map/pallas_call | solution.py:446
  12.9 6.0 %collective-permute-done.3.e = f32[256,128]{1,0:T(8,128)S(1)} collective-permute-done((f32[256,128]{1,0:T(8,128)S(1)}, f32[256,128]{1,0:T(8,128)S(1)}, u32[]{:S(2)}, u32[]{:S(2)}) %collective-permute-start.3) | collective-permute-done | bytes 131104 | tf_op jit(solution)/shard_map/ppermute | solution.py:586
  19.2 1.4 %collective-permute-done.e = f32[256,128]{1,0:T(8,128)S(1)} collective-permute-done((f32[256,128]{1,0:T(8,128)S(1)}, f32[256,128]{1,0:T(8,128)S(1)}, u32[]{:S(2)}, u32[]{:S(2)}) %collective-permute-start) | collective-permute-done | bytes 131104 | tf_op jit(solution)/shard_map/ppermute | solution.py:588
  20.8 1.5 %shard_map.103 = (f32[2,256,256]{2,1,0:T(8,128)S(1)}, f32[2,256,256]{2,1,0:T(8,128)S(1)}) custom-call(f32[2,256,256]{2,1,0:T(8,128)S(1)} %shard_map.97.after.refs_0_, f32[4,64,256]{2,1,0:T(8,128)S(1)} %collective-permute-done.2.refs_1_, f32[2,64,128]{2,1,0:T(8,128)S(1)} %collective-permute-done.5.refs_2_, s32[2,8,128]{2,1,0:T(8,128)S(1)} %get-tuple-element.34.limits.refs_3_, ...), custom_call_target="tpu_custom_call" | custom-call | tf_op jit(solution)/shard_map/pallas_call | solution.py:446
  22.3 3.6 %shard_map.104 = (f32[256,256]{1,0:T(8,128)S(1)}, f32[256,256]{1,0:T(8,128)S(1)}, f32[4,256,256]{2,1,0:T(8,128)S(1)}) custom-call(f32[2,256,256]{2,1,0:T(8,128)S(1)} %shard_map.96.refs_0_, f32[4,64,256]{2,1,0:T(8,128)S(1)} %collective-permute-done.2.refs_1_, f32[2,64,128]{2,1,0:T(8,128)S(1)} %collective-permute-done.4.refs_2_, ...), custom_call_target="tpu_custom_call" | custom-call | tf_op jit(solution)/shard_map/pallas_call | solution.py:446
  25.9 0.6 collective-permute-start.9
  26.9 0.7 %collective-permute-done.9.other = f32[256,256]{1,0:T(8,128)S(1)} collective-permute-done((f32[256,256]{1,0:T(8,128)S(1)}, f32[256,256]{1,0:T(8,128)S(1)}, u32[]{:S(2)}, u32[]{:S(2)}) %collective-permute-start.9) | collective-permute-done | bytes 262176 | tf_op jit(solution)/shard_map/ppermute | solution.py:469
  27.7 2.5 %collective-permute-start.10 = (f32[64,256]{1,0:T(8,128)S(1)}, f32[64,256]{1,0:T(8,128)S(1)}, u32[]{:S(2)}, u32[]{:S(2)}) collective-permute-start(f32[64,256]{1,0:T(8,128)S(1)} %get-tuple-element.57), channel_id=1, source_target_pairs={{0,1},{1,0},{2,3},{3,2},{4,5},{5,4},{6,7},{7,6},{8,9},{9,8},{10,11... | collective-permute-start | bytes 196616 | tf_op jit(solution)/shard_map/ppermute | solution.py:469
  30.1 1.5 %collective-permute-start.12 = (f32[64,256]{1,0:T(8,128)S(1)}, f32[64,256]{1,0:T(8,128)S(1)}, u32[]{:S(2)}, u32[]{:S(2)}) collective-permute-start(f32[64,256]{1,0:T(8,128)S(1)} %get-tuple-element.59), channel_id=1, source_target_pairs={{0,3},{1,2},{2,1},{3,0},{4,7},{5,6},{6,5},{7,4},{8,11},{9,10},{10,... | collective-permute-start | bytes 196616 | tf_op jit(solution)/shard_map/ppermute | solution.py:469
  31.7 1.1 %collective-permute-done.10.refs_1_ = f32[64,256]{1,0:T(8,128)S(1)} collective-permute-done((f32[64,256]{1,0:T(8,128)S(1)}, f32[64,256]{1,0:T(8,128)S(1)}, u32[]{:S(2)}, u32[]{:S(2)}) %collective-permute-start.10) | collective-permute-done | bytes 65568 | tf_op jit(solution)/shard_map/ppermute | solution.py:469
  32.8 3.0 %collective-permute-done.11.refs_2_ = f32[64,256]{1,0:T(8,128)S(1)} collective-permute-done((f32[64,256]{1,0:T(8,128)S(1)}, f32[64,256]{1,0:T(8,128)S(1)}, u32[]{:S(2)}, u32[]{:S(2)}) %collective-permute-start.11) | collective-permute-done | bytes 65568 | tf_op jit(solution)/shard_map/ppermute | solution.py:469
  35.8 2.8 %collective-permute-start.15 = (f32[64,256]{1,0:T(8,128)S(1)}, f32[64,256]{1,0:T(8,128)S(1)}, u32[]{:S(2)}, u32[]{:S(2)}) collective-permute-start(f32[64,256]{1,0:T(8,128)S(1)} %shard_map.109.refs_0_), channel_id=1, source_target_pairs={{0,12},{1,13},{2,14},{3,15},{4,8},{5,9},{6,10},{7,11},{8,4},{9,5},... | collective-permute-start | bytes 196616 | tf_op jit(solution)/shard_map/ppermute | solution.py:469
  38.9 1.3 %collective-permute-start.13 = (f32[64,256]{1,0:T(8,128)S(1)}, f32[64,256]{1,0:T(8,128)S(1)}, u32[]{:S(2)}, u32[]{:S(2)}) collective-permute-start(f32[64,256]{1,0:T(8,128)S(1)} %shard_map.109.refs_0_), channel_id=1, source_target_pairs={{0,4},{1,5},{2,6},{3,7},{4,0},{5,1},{6,2},{7,3},{8,12},{9,13},{10,... | collective-permute-start | bytes 196616 | tf_op jit(solution)/shard_map/ppermute | solution.py:469
  40.3 2.0 %collective-permute-done.15.refs_3_ = f32[64,256]{1,0:T(8,128)S(1)} collective-permute-done((f32[64,256]{1,0:T(8,128)S(1)}, f32[64,256]{1,0:T(8,128)S(1)}, u32[]{:S(2)}, u32[]{:S(2)}) %collective-permute-start.15) | collective-permute-done | bytes 65568 | tf_op jit(solution)/shard_map/ppermute | solution.py:469
  42.3 2.2 %collective-permute-done.14.refs_2_ = f32[64,256]{1,0:T(8,128)S(1)} collective-permute-done((f32[64,256]{1,0:T(8,128)S(1)}, f32[64,256]{1,0:T(8,128)S(1)}, u32[]{:S(2)}, u32[]{:S(2)}) %collective-permute-start.14) | collective-permute-done | bytes 65568 | tf_op jit(solution)/shard_map/ppermute | solution.py:469
  44.5 1.3 %collective-permute-start.18 = (f32[64,256]{1,0:T(8,128)S(1)}, f32[64,256]{1,0:T(8,128)S(1)}, u32[]{:S(2)}, u32[]{:S(2)}) collective-permute-start(f32[64,256]{1,0:T(8,128)S(1)} %shard_map.110.refs_0_), channel_id=1, source_target_pairs={{0,3},{1,2},{2,1},{3,0},{4,7},{5,6},{6,5},{7,4},{8,11},{9,10},{10,... | collective-permute-start | bytes 196616 | tf_op jit(solution)/shard_map/ppermute | solution.py:469
  45.8 1.0 %collective-permute-start.17 = (f32[64,256]{1,0:T(8,128)S(1)}, f32[64,256]{1,0:T(8,128)S(1)}, u32[]{:S(2)}, u32[]{:S(2)}) collective-permute-start(f32[64,256]{1,0:T(8,128)S(1)} %shard_map.110.refs_0_), channel_id=1, source_target_pairs={{0,2},{1,3},{2,0},{3,1},{4,6},{5,7},{6,4},{7,5},{8,10},{9,11},{10,... | collective-permute-start | bytes 196616 | tf_op jit(solution)/shard_map/ppermute | solution.py:469
  46.8 1.3 %collective-permute-start.16 = (f32[64,256]{1,0:T(8,128)S(1)}, f32[64,256]{1,0:T(8,128)S(1)}, u32[]{:S(2)}, u32[]{:S(2)}) collective-permute-start(f32[64,256]{1,0:T(8,128)S(1)} %shard_map.110.refs_0_), channel_id=1, source_target_pairs={{0,1},{1,0},{2,3},{3,2},{4,5},{5,4},{6,7},{7,6},{8,9},{9,8},{10,11... | collective-permute-start | bytes 196616 | tf_op jit(solution)/shard_map/ppermute | solution.py:469
  48.2 0.8 %collective-permute-start.7 = (f32[2,256,128]{2,1,0:T(8,128)S(1)}, f32[2,256,128]{2,1,0:T(8,128)S(1)}, u32[]{:S(2)}, u32[]{:S(2)}) collective-permute-start(f32[2,256,128]{2,1,0:T(8,128)S(1)} %get-tuple-element.52), channel_id=1, source_target_pairs={{0,1},{2,3},{4,5},{6,7},{8,9},{10,11},{12,13},{14,15},{1,0},{3,2},... | collective-permute-start | bytes 786440 | tf_op jit(solution)/shard_map/ppermute | solution.py:692
  49.0 0.7 %collective-permute-start.8 = (f32[2,256,128]{2,1,0:T(8,128)S(1)}, f32[2,256,128]{2,1,0:T(8,128)S(1)}, u32[]{:S(2)}, u32[]{:S(2)}) collective-permute-start(f32[2,256,128]{2,1,0:T(8,128)S(1)} %get-tuple-element.53), channel_id=1, source_target_pairs={{1,2},{3,4},{5,6},{7,8},{9,10},{11,12},{13,14},{2,1},{4,3},{6,5},{... | collective-permute-start | bytes 786440 | tf_op jit(solution)/shard_map/ppermute | solution.py:693
  49.7 0.7 %collective-permute-done.18.refs_3_ = f32[64,256]{1,0:T(8,128)S(1)} collective-permute-done((f32[64,256]{1,0:T(8,128)S(1)}, f32[64,256]{1,0:T(8,128)S(1)}, u32[]{:S(2)}, u32[]{:S(2)}) %collective-permute-start.18) | collective-permute-done | bytes 65568 | tf_op jit(solution)/shard_map/ppermute | solution.py:469
  50.6 1.1 %collective-permute-done.16.refs_1_ = f32[64,256]{1,0:T(8,128)S(1)} collective-permute-done((f32[64,256]{1,0:T(8,128)S(1)}, f32[64,256]{1,0:T(8,128)S(1)}, u32[]{:S(2)}, u32[]{:S(2)}) %collective-permute-start.16) | collective-permute-done | bytes 65568 | tf_op jit(solution)/shard_map/ppermute | solution.py:469
  51.8 0.7 %shard_map.112.started = f32[2,256,256]{2,1,0:T(8,128)} custom-call(f32[256,256]{1,0:T(8,128)S(1)} %shard_map.111.full), custom_call_target="tpu_custom_call" | custom-call | tf_op jit(solution)/shard_map/pallas_call | solution.py:559
  52.6 7.0 %collective-permute-done.7.e = f32[2,256,128]{2,1,0:T(8,128)S(1)} collective-permute-done((f32[2,256,128]{2,1,0:T(8,128)S(1)}, f32[2,256,128]{2,1,0:T(8,128)S(1)}, u32[]{:S(2)}, u32[]{:S(2)}) %collective-permute-start.7) | collective-permute-done | bytes 262176 | tf_op jit(solution)/shard_map/ppermute | solution.py:692
  59.6 1.2 %shard_map.107 = f32[4,256,256]{2,1,0:T(8,128)} custom-call(f32[4,256,256]{2,1,0:T(8,128)S(1)} %get-tuple-element.51.total, f32[2,256,128]{2,1,0:T(8,128)S(1)} %collective-permute-done.7.e, f32[2,256,128]{2,1,0:T(8,128)S(1)} %collective-permute-done.8.o), custom_call_target="tpu_custom_call" | custom-call | tf_op jit(solution)/shard_map/pallas_call | solution.py:446
  60.8 0.7 %shard_map.113 = f32[2,256,256]{2,1,0:T(8,128)} custom-call(f32[2,256,256]{2,1,0:T(8,128)} %shard_map.112.started, f32[256,256]{1,0:T(8,128)S(1)} %collective-permute-done.19.other), custom_call_target="tpu_custom_call", output_to_operand_aliasing={{}: (0, {})} | custom-call | tf_op jit(solution)/shard_map/pallas_call | solution.py:560
  (27 shorter events, 1.8 us)
Async XLA Ops:
  2.6 16.3 %collective-permute-start.1 = (f32[2,256,128]{2,1,0:T(8,128)S(1)}, f32[2,256,128]{2,1,0:T(8,128)S(1)}, u32[]{:S(2)}, u32[]{:S(2)}) collective-permute-start(f32[2,256,128]{2,1,0:T(8,128)S(1)} %get-tuple-element.33), channel_id=1, source_target_pairs={{1,2},{3,4},{5,6},{7,8},{9,10},{11,12},{13,14},{2,1},{4,3},{6,5},{... | collective-permute-start | bytes 786440 | tf_op jit(solution)/shard_map/ppermute | solution.py:587
  3.3 17.5 %collective-permute-start.2 = (f32[4,64,256]{2,1,0:T(8,128)S(1)}, f32[4,64,256]{2,1,0:T(8,128)S(1)}, u32[]{:S(2)}, u32[]{:S(2)}) collective-permute-start(f32[4,64,256]{2,1,0:T(8,128)S(1)} %get-tuple-element.35), channel_id=1, source_target_pairs={{0,16},{16,0},{1,17},{17,1},{2,18},{18,2},{3,19},{19,3},{4,20},{20... | collective-permute-start | bytes 786440 | tf_op jit(solution)/shard_map/ppermute | solution.py:590
  3.9 15.1 %collective-permute-start.3 = (f32[256,128]{1,0:T(8,128)S(1)}, f32[256,128]{1,0:T(8,128)S(1)}, u32[]{:S(2)}, u32[]{:S(2)}) collective-permute-start(f32[256,128]{1,0:T(8,128)S(1)} %get-tuple-element.36), channel_id=1, source_target_pairs={{0,1},{2,3},{4,5},{6,7},{8,9},{10,11},{12,13},{14,15},{1,0},{3,2},... | collective-permute-start | bytes 393224 | tf_op jit(solution)/shard_map/ppermute | solution.py:586
  9.1 11.5 %collective-permute-start = (f32[256,128]{1,0:T(8,128)S(1)}, f32[256,128]{1,0:T(8,128)S(1)}, u32[]{:S(2)}, u32[]{:S(2)}) collective-permute-start(f32[256,128]{1,0:T(8,128)S(1)} %get-tuple-element.32), channel_id=1, source_target_pairs={{0,1},{2,3},{4,5},{6,7},{8,9},{10,11},{12,13},{14,15},{1,0},{3,2},... | collective-permute-start | bytes 393224 | tf_op jit(solution)/shard_map/ppermute | solution.py:588
  18.9 1.9 %collective-permute-start.5 = (f32[2,64,128]{2,1,0:T(8,128)S(1)}, f32[2,64,128]{2,1,0:T(8,128)S(1)}, u32[]{:S(2)}, u32[]{:S(2)}) collective-permute-start(f32[2,64,128]{2,1,0:T(8,128)S(1)} %shard_map.102), channel_id=1, source_target_pairs={{0,16},{16,0},{1,17},{17,1},{2,18},{18,2},{3,19},{19,3},{4,20},{20... | collective-permute-start | bytes 196616 | tf_op jit(solution)/shard_map/ppermute | solution.py:603
  20.6 1.7 %collective-permute-start.4 = (f32[2,64,128]{2,1,0:T(8,128)S(1)}, f32[2,64,128]{2,1,0:T(8,128)S(1)}, u32[]{:S(2)}, u32[]{:S(2)}) collective-permute-start(f32[2,64,128]{2,1,0:T(8,128)S(1)} %shard_map.98), channel_id=1, source_target_pairs={{0,16},{16,0},{1,17},{17,1},{2,18},{18,2},{3,19},{19,3},{4,20},{20... | collective-permute-start | bytes 196616 | tf_op jit(solution)/shard_map/ppermute | solution.py:603
  25.9 1.7 %collective-permute-start.9 = (f32[256,256]{1,0:T(8,128)S(1)}, f32[256,256]{1,0:T(8,128)S(1)}, u32[]{:S(2)}, u32[]{:S(2)}) collective-permute-start(f32[256,256]{1,0:T(8,128)S(1)} %get-tuple-element.55), channel_id=1, source_target_pairs={{0,16},{16,0},{1,17},{17,1},{2,18},{18,2},{3,19},{19,3},{4,20},{20... | collective-permute-start | bytes 786440 | tf_op jit(solution)/shard_map/ppermute | solution.py:469
  26.8 21.2 %collective-permute-start.6 = (f32[4,64,384]{2,1,0:T(8,128)S(1)}, f32[4,64,384]{2,1,0:T(8,128)S(1)}, u32[]{:S(2)}, u32[]{:S(2)}) collective-permute-start(f32[4,64,384]{2,1,0:T(8,128)S(1)} %get-tuple-element.50), channel_id=1, source_target_pairs={{0,16},{16,0},{1,17},{17,1},{2,18},{18,2},{3,19},{19,3},{4,20},{20... | collective-permute-start | bytes 1179656 | tf_op jit(solution)/shard_map/ppermute | solution.py:683
  27.7 5.1 %collective-permute-start.10 = (f32[64,256]{1,0:T(8,128)S(1)}, f32[64,256]{1,0:T(8,128)S(1)}, u32[]{:S(2)}, u32[]{:S(2)}) collective-permute-start(f32[64,256]{1,0:T(8,128)S(1)} %get-tuple-element.57), channel_id=1, source_target_pairs={{0,1},{1,0},{2,3},{3,2},{4,5},{5,4},{6,7},{7,6},{8,9},{9,8},{10,11... | collective-permute-start | bytes 196616 | tf_op jit(solution)/shard_map/ppermute | solution.py:469
  30.1 5.7 %collective-permute-start.11 = (f32[64,256]{1,0:T(8,128)S(1)}, f32[64,256]{1,0:T(8,128)S(1)}, u32[]{:S(2)}, u32[]{:S(2)}) collective-permute-start(f32[64,256]{1,0:T(8,128)S(1)} %get-tuple-element.58), channel_id=1, source_target_pairs={{0,2},{1,3},{2,0},{3,1},{4,6},{5,7},{6,4},{7,5},{8,10},{9,11},{10,... | collective-permute-start | bytes 196616 | tf_op jit(solution)/shard_map/ppermute | solution.py:469
  30.1 5.7 %collective-permute-start.12 = (f32[64,256]{1,0:T(8,128)S(1)}, f32[64,256]{1,0:T(8,128)S(1)}, u32[]{:S(2)}, u32[]{:S(2)}) collective-permute-start(f32[64,256]{1,0:T(8,128)S(1)} %get-tuple-element.59), channel_id=1, source_target_pairs={{0,3},{1,2},{2,1},{3,0},{4,7},{5,6},{6,5},{7,4},{8,11},{9,10},{10,... | collective-permute-start | bytes 196616 | tf_op jit(solution)/shard_map/ppermute | solution.py:469
  35.8 6.4 %collective-permute-start.15 = (f32[64,256]{1,0:T(8,128)S(1)}, f32[64,256]{1,0:T(8,128)S(1)}, u32[]{:S(2)}, u32[]{:S(2)}) collective-permute-start(f32[64,256]{1,0:T(8,128)S(1)} %shard_map.109.refs_0_), channel_id=1, source_target_pairs={{0,12},{1,13},{2,14},{3,15},{4,8},{5,9},{6,10},{7,11},{8,4},{9,5},... | collective-permute-start | bytes 196616 | tf_op jit(solution)/shard_map/ppermute | solution.py:469
  38.6 5.9 %collective-permute-start.14 = (f32[64,256]{1,0:T(8,128)S(1)}, f32[64,256]{1,0:T(8,128)S(1)}, u32[]{:S(2)}, u32[]{:S(2)}) collective-permute-start(f32[64,256]{1,0:T(8,128)S(1)} %shard_map.109.refs_0_), channel_id=1, source_target_pairs={{0,8},{1,9},{2,10},{3,11},{4,12},{5,13},{6,14},{7,15},{8,0},{9,1},... | collective-permute-start | bytes 196616 | tf_op jit(solution)/shard_map/ppermute | solution.py:469
  38.9 5.5 %collective-permute-start.13 = (f32[64,256]{1,0:T(8,128)S(1)}, f32[64,256]{1,0:T(8,128)S(1)}, u32[]{:S(2)}, u32[]{:S(2)}) collective-permute-start(f32[64,256]{1,0:T(8,128)S(1)} %shard_map.109.refs_0_), channel_id=1, source_target_pairs={{0,4},{1,5},{2,6},{3,7},{4,0},{5,1},{6,2},{7,3},{8,12},{9,13},{10,... | collective-permute-start | bytes 196616 | tf_op jit(solution)/shard_map/ppermute | solution.py:469
  44.5 5.9 %collective-permute-start.18 = (f32[64,256]{1,0:T(8,128)S(1)}, f32[64,256]{1,0:T(8,128)S(1)}, u32[]{:S(2)}, u32[]{:S(2)}) collective-permute-start(f32[64,256]{1,0:T(8,128)S(1)} %shard_map.110.refs_0_), channel_id=1, source_target_pairs={{0,3},{1,2},{2,1},{3,0},{4,7},{5,6},{6,5},{7,4},{8,11},{9,10},{10,... | collective-permute-start | bytes 196616 | tf_op jit(solution)/shard_map/ppermute | solution.py:469
  45.8 4.8 %collective-permute-start.17 = (f32[64,256]{1,0:T(8,128)S(1)}, f32[64,256]{1,0:T(8,128)S(1)}, u32[]{:S(2)}, u32[]{:S(2)}) collective-permute-start(f32[64,256]{1,0:T(8,128)S(1)} %shard_map.110.refs_0_), channel_id=1, source_target_pairs={{0,2},{1,3},{2,0},{3,1},{4,6},{5,7},{6,4},{7,5},{8,10},{9,11},{10,... | collective-permute-start | bytes 196616 | tf_op jit(solution)/shard_map/ppermute | solution.py:469
  46.8 5.0 %collective-permute-start.16 = (f32[64,256]{1,0:T(8,128)S(1)}, f32[64,256]{1,0:T(8,128)S(1)}, u32[]{:S(2)}, u32[]{:S(2)}) collective-permute-start(f32[64,256]{1,0:T(8,128)S(1)} %shard_map.110.refs_0_), channel_id=1, source_target_pairs={{0,1},{1,0},{2,3},{3,2},{4,5},{5,4},{6,7},{7,6},{8,9},{9,8},{10,11... | collective-permute-start | bytes 196616 | tf_op jit(solution)/shard_map/ppermute | solution.py:469
  48.2 11.4 %collective-permute-start.7 = (f32[2,256,128]{2,1,0:T(8,128)S(1)}, f32[2,256,128]{2,1,0:T(8,128)S(1)}, u32[]{:S(2)}, u32[]{:S(2)}) collective-permute-start(f32[2,256,128]{2,1,0:T(8,128)S(1)} %get-tuple-element.52), channel_id=1, source_target_pairs={{0,1},{2,3},{4,5},{6,7},{8,9},{10,11},{12,13},{14,15},{1,0},{3,2},... | collective-permute-start | bytes 786440 | tf_op jit(solution)/shard_map/ppermute | solution.py:692
  49.0 10.6 %collective-permute-start.8 = (f32[2,256,128]{2,1,0:T(8,128)S(1)}, f32[2,256,128]{2,1,0:T(8,128)S(1)}, u32[]{:S(2)}, u32[]{:S(2)}) collective-permute-start(f32[2,256,128]{2,1,0:T(8,128)S(1)} %get-tuple-element.53), channel_id=1, source_target_pairs={{1,2},{3,4},{5,6},{7,8},{9,10},{11,12},{13,14},{2,1},{4,3},{6,5},{... | collective-permute-start | bytes 786440 | tf_op jit(solution)/shard_map/ppermute | solution.py:693
  51.8 9.1 %collective-permute-start.19 = (f32[256,256]{1,0:T(8,128)S(1)}, f32[256,256]{1,0:T(8,128)S(1)}, u32[]{:S(2)}, u32[]{:S(2)}) collective-permute-start(f32[256,256]{1,0:T(8,128)S(1)} %shard_map.111.full), channel_id=1, source_target_pairs={{0,16},{16,0},{1,17},{17,1},{2,18},{18,2},{3,19},{19,3},{4,20},{20... | collective-permute-start | bytes 786440 | tf_op jit(solution)/shard_map/ppermute | solution.py:469

commit v9 on v7

--- a/solution.py
+++ b/solution.py
@@ -168,7 +168,7 @@
 
 
 def pack_kernel(margin, obj_hbm, offs_hbm, obj, offs, limits, *refs):
-    strips, rows, sems = refs[:4], refs[4:-1], refs[-1]
+    evens, odds, rows, sems = refs[:2], refs[2:4], refs[4:-1], refs[-1]
     n = obj.shape[1]
     copies = copy_all(
         (obj_hbm.at[0:2], obj_hbm.at[2:4], offs_hbm), (obj.at[0:2], obj.at[2:4], offs), sems
@@ -177,8 +177,8 @@
     for s in range(2):
         copies[s].wait()
         low, high = pack_cols(obj[2 * s], obj[2 * s + 1])
-        strips[2 * s][...] = jnp.where(even, high, low)
-        strips[2 * s + 1][...] = jnp.where(even, low, high)
+        evens[s][...] = jnp.where(even, high, low)
+        odds[s][...] = jnp.where(even, low, high)
     for which, out in enumerate(rows):
         out[...] = obj[:, pl.ds(row_start(which, n, margin), margin), :]
     copies[2].wait()
@@ -215,11 +215,9 @@
     phase, table, sems = refs[13:]
     n = phase.shape[0]
     h = n // 2
-    first = pltpu.make_async_copy(hbm[0], phase, sems.at[0])
-    first.start()
+    phase = hbm[0]
+    copies = copy_all(hbm[1:], (table,) + loaded, sems)
     order = [even_odd(n, axis) for axis in range(2)]
-    first.wait()
-    copies = copy_all(hbm[1:], (table,) + loaded, sems)
     angle = reorder(phase[...], order)
     kr[...], ki[...] = cos_sin(angle)
     copies[0].wait()
@@ -571,7 +569,7 @@
 
     row_rounds, col_rounds = edges("row"), edges("col")
     n_row = len(row_rounds)
-    obj, offs, limits, *packed = call(
+    obj, offs, limits, even0, even1, odd0, odd1, *rows = call(
         functools.partial(pack_kernel, margin),
         [(4, n, n), jax.ShapeDtypeStruct((1, 2), jnp.int32)]
         + [jax.ShapeDtypeStruct((2, 8, h), jnp.int32)]
@@ -582,18 +580,22 @@
         in_hbm(offsets.reshape(1, 2)),
         scratch=[pltpu.SemaphoreType.DMA((3,))],
     )
-    strips, halos, corners = [], [], [[], []]
-    for i in range(4):
-        strips.append(lax.ppermute(packed[i], "col", col_rounds[i % 2]))
+    halos, corners = [], [[], []]
+    even0 = lax.ppermute(even0, "col", col_rounds[0])
+    even1 = lax.ppermute(even1, "col", col_rounds[0])
+    odd0 = lax.ppermute(odd0, "col", col_rounds[1])
+    odd1 = lax.ppermute(odd1, "col", col_rounds[1])
     for i, pairs in enumerate(row_rounds):
-        halos.append(lax.ppermute(packed[4 + i], "row", pairs))
+        halos.append(lax.ppermute(rows[i], "row", pairs))
+    evens, odds = (even0, even1), (odd0, odd1)
 
     def cut(s, after):
         parts = call(
             functools.partial(corner_kernel, margin),
             [(2, margin, h)] * n_row,
             [VMEM] * 3,
-            *strips[2 * s : 2 * s + 2],
+            evens[s],
+            odds[s],
             after,
         )
         for i, pairs in enumerate(row_rounds):
@@ -605,7 +607,8 @@
             [(2, n, n)],
             [VMEM] * 4,
             obj,
-            *strips[2 * s : 2 * s + 2],
+            evens[s],
+            odds[s],
             limits,
         )
         return main
@@ -616,8 +619,9 @@
         [(n, n)] * 2
         + [jax.ShapeDtypeStruct((4, n, n), BF16)]
         + [jax.ShapeDtypeStruct(x.shape, x.dtype) for x in loads[2:]],
-        [HBM] * len(loads),
-        *[in_hbm(x) for x in loads],
+        [VMEM] + [HBM] * (len(loads) - 1),
+        loads[0],
+        *[in_hbm(x) for x in loads[1:]],
         scratch=[
             pltpu.VMEM((n, n), F32),
             pltpu.VMEM((2, n, n), BF16),

time: 60.6 us -> 60.2 us (level)
  Pallas kernels: 14.3 us -> 13.4 us
    ppermute x5, waiting for transfers between devices: 2.2 us -> 3.13 us  [the longest x1 3.12 us: whole(): even1 = lax.ppermute(even1, 'col', col_rounds[0])]
    pallas_call x17, Pallas kernels: 12.9 us -> 12 us  [call(): pl.pallas_call(kernel, out_shape=shapes, in_specs=in_specs, out_specs=[SM...]
  transfers between devices with their start and end apart: 21 -> 21, of which waited for: 12 -> 11; matrix products, arithmetic and copies ran while one was open for 0% -> 0% of each run, Pallas kernels for 13% -> 12%
where the time goes in v9:
time: 60.2 us; the launch traced here: 59.4 us
  starting transfers between devices  23.9 us (40%)
  waiting for transfers between devices  21.3 us (35%)
  Pallas kernels  13.4 us (22%)
  between operations  0.83 us (1%)
    ppermute x11, starting transfers between devices, swap(): return lax.ppermute(value, axis, [(i, i ^ distance) for i in range(count)])  12.4 us
    pallas_call x17, Pallas kernels, call(): pl.pallas_call(kernel, out_shape=shapes, in_specs=in_specs, out_specs=[SM...  12 us
    ppermute x11, waiting for transfers between devices, swap(): return lax.ppermute(value, axis, [(i, i ^ distance) for i in range(count)])  11.1 us
    ppermute x1, waiting for transfers between devices, whole(): send_e = lax.ppermute(send_e, 'col', col_rounds[0])  6.34 us
    ppermute x1, starting transfers between devices, whole(): even1 = lax.ppermute(even1, 'col', col_rounds[0])  4.29 us
    ppermute x1, waiting for transfers between devices, whole(): even1 = lax.ppermute(even1, 'col', col_rounds[0])  3.12 us
    ppermute x1, starting transfers between devices, whole(): even0 = lax.ppermute(even0, 'col', col_rounds[0])  2.55 us
    ppermute x1, starting transfers between devices, whole(): send_e = lax.ppermute(send_e, 'col', col_rounds[0])  1.59 us
  transfers between devices with their start and end apart: 21, of which 11 were waited for; matrix products, arithmetic and copies ran while one was open for 0% of the time, Pallas kernels for 12%

profile of v9, /device:TPU:0, one launch (start us, length us, event | category | flops | bytes accessed | tf_op | source)
XLA Modules:
  0.0 59.4 jit_solution(3603980586436555837)
XLA Ops:
  0.6 2.0 %shard_map.95 = (f32[4,256,256]{2,1,0:T(8,128)S(1)}, s32[1,2]{1,0:T(1,128)S(1)}, s32[2,8,128]{2,1,0:T(8,128)S(1)}, f32[256,128]{1,0:T(8,128)S(1)}, f32[256,128]{...) custom-call(f32[4,256,256]{2,1,0:T(8,128)} %bitcast.4, s32[1,2]{1,0:T(1,128)} %bitcast.7), custom_call_target="tpu_custom_call" | custom-call | tf_op jit(solution)/shard_map/pallas_call | solution.py:444
  2.7 0.6 collective-permute-start.2
  3.2 2.6 %collective-permute-start.3 = (f32[256,128]{1,0:T(8,128)S(1)}, f32[256,128]{1,0:T(8,128)S(1)}, u32[]{:S(2)}, u32[]{:S(2)}) collective-permute-start(f32[256,128]{1,0:T(8,128)S(1)} %get-tuple-element.37), channel_id=1, source_target_pairs={{0,1},{2,3},{4,5},{6,7},{8,9},{10,11},{12,13},{14,15},{1,0},{3,2},... | collective-permute-start | bytes 393224 | tf_op jit(solution)/shard_map/ppermute | solution.py:584
  5.8 0.7 %collective-permute-start.4 = (f32[256,128]{1,0:T(8,128)S(1)}, f32[256,128]{1,0:T(8,128)S(1)}, u32[]{:S(2)}, u32[]{:S(2)}) collective-permute-start(f32[256,128]{1,0:T(8,128)S(1)} %get-tuple-element.38), channel_id=1, source_target_pairs={{1,2},{3,4},{5,6},{7,8},{9,10},{11,12},{13,14},{2,1},{4,3},{6,5},{... | collective-permute-start | bytes 393224 | tf_op jit(solution)/shard_map/ppermute | solution.py:586
  6.4 4.3 %collective-permute-start = (f32[256,128]{1,0:T(8,128)S(1)}, f32[256,128]{1,0:T(8,128)S(1)}, u32[]{:S(2)}, u32[]{:S(2)}) collective-permute-start(f32[256,128]{1,0:T(8,128)S(1)} %get-tuple-element.33), channel_id=1, source_target_pairs={{0,1},{2,3},{4,5},{6,7},{8,9},{10,11},{12,13},{14,15},{1,0},{3,2},... | collective-permute-start | bytes 393224 | tf_op jit(solution)/shard_map/ppermute | solution.py:585
  10.7 0.7 %collective-permute-start.1 = (f32[256,128]{1,0:T(8,128)S(1)}, f32[256,128]{1,0:T(8,128)S(1)}, u32[]{:S(2)}, u32[]{:S(2)}) collective-permute-start(f32[256,128]{1,0:T(8,128)S(1)} %get-tuple-element.34), channel_id=1, source_target_pairs={{1,2},{3,4},{5,6},{7,8},{9,10},{11,12},{13,14},{2,1},{4,3},{6,5},{... | collective-permute-start | bytes 393224 | tf_op jit(solution)/shard_map/ppermute | solution.py:587
  11.4 1.3 %shard_map.98 = (f32[256,256]{1,0:T(8,128)S(1)}, f32[256,256]{1,0:T(8,128)S(1)}, bf16[4,256,256]{2,1,0:T(8,128)(2,1)S(1)}, f32[2,128,128]{2,1,0:T(8,128)S(1)}, f...) custom-call(f32[256,256]{1,0:T(8,128)S(1)} %copy-done, ...), custom_call_target="tpu_custom_call" | custom-call | tf_op jit(solution)/shard_map/pallas_call | solution.py:444
  12.9 0.8 %shard_map.100.refs_4_.refs_5_ = f32[2,256,256]{2,1,0:T(8,128)S(1)} custom-call(s32[1,2]{1,0:T(1,128)S(1)} %get-tuple-element.40.offs, f32[2,256,256]{2,1,0:T(8,128)S(1)} %get-tuple-element.41.probe), custom_call_target="tpu_custom_call" | custom-call | tf_op jit(solution)/shard_map/pallas_call | solution.py:444
  14.1 1.5 %shard_map.101 = (f32[2,256,256]{2,1,0:T(8,128)S(1)}, f32[2,256,256]{2,1,0:T(8,128)S(1)}) custom-call(f32[2,256,256]{2,1,0:T(8,128)S(1)} %shard_map.97.refs_0_, f32[4,64,256]{2,1,0:T(8,128)S(1)} %collective-permute-done.2.refs_1_, f32[2,64,128]{2,1,0:T(8,128)S(1)} %collective-permute-done.5.refs_2_, s32[2,8,128]{2,1,0:T(8,128)S(1)} %get-tuple-element.35.limits.refs_3_, ...), custom_call_target="tpu_custom_call" | custom-call | tf_op jit(solution)/shard_map/pallas_call | solution.py:444
  15.6 3.1 %collective-permute-done.e = f32[256,128]{1,0:T(8,128)S(1)} collective-permute-done((f32[256,128]{1,0:T(8,128)S(1)}, f32[256,128]{1,0:T(8,128)S(1)}, u32[]{:S(2)}, u32[]{:S(2)}) %collective-permute-start) | collective-permute-done | bytes 131104 | tf_op jit(solution)/shard_map/ppermute | solution.py:585
  19.0 0.6 %shard_map.103.refs_8_ = f32[256,256]{1,0:T(8,128)S(1)} custom-call(f32[256,256]{1,0:T(8,128)S(1)} %get-tuple-element.47.x, f32[2,256,256]{2,1,0:T(8,128)S(1)} %get-tuple-element.46.after.refs_10_), custom_call_target="tpu_custom_call" | custom-call | tf_op jit(solution)/shard_map/pallas_call | solution.py:444
  19.6 0.4 collective-permute-done.6.refs_2_
  20.1 3.6 %shard_map.104 = (f32[256,256]{1,0:T(8,128)S(1)}, f32[256,256]{1,0:T(8,128)S(1)}, f32[4,256,256]{2,1,0:T(8,128)S(1)}) custom-call(f32[2,256,256]{2,1,0:T(8,128)S(1)} %shard_map.96.refs_0_, f32[4,64,256]{2,1,0:T(8,128)S(1)} %collective-permute-done.2.refs_1_, f32[2,64,128]{2,1,0:T(8,128)S(1)} %collective-permute-done.6.refs_2_, ...), custom_call_target="tpu_custom_call" | custom-call | tf_op jit(solution)/shard_map/pallas_call | solution.py:444
  24.6 0.6 %collective-permute-done.10.other = f32[256,256]{1,0:T(8,128)S(1)} collective-permute-done((f32[256,256]{1,0:T(8,128)S(1)}, f32[256,256]{1,0:T(8,128)S(1)}, u32[]{:S(2)}, u32[]{:S(2)}) %collective-permute-start.10) | collective-permute-done | bytes 262176 | tf_op jit(solution)/shard_map/ppermute | solution.py:467
  25.3 2.5 %collective-permute-start.11 = (f32[64,256]{1,0:T(8,128)S(1)}, f32[64,256]{1,0:T(8,128)S(1)}, u32[]{:S(2)}, u32[]{:S(2)}) collective-permute-start(f32[64,256]{1,0:T(8,128)S(1)} %get-tuple-element.59), channel_id=1, source_target_pairs={{0,1},{1,0},{2,3},{3,2},{4,5},{5,4},{6,7},{7,6},{8,9},{9,8},{10,11... | collective-permute-start | bytes 196616 | tf_op jit(solution)/shard_map/ppermute | solution.py:467
  28.0 1.4 %collective-permute-start.13 = (f32[64,256]{1,0:T(8,128)S(1)}, f32[64,256]{1,0:T(8,128)S(1)}, u32[]{:S(2)}, u32[]{:S(2)}) collective-permute-start(f32[64,256]{1,0:T(8,128)S(1)} %get-tuple-element.61), channel_id=1, source_target_pairs={{0,3},{1,2},{2,1},{3,0},{4,7},{5,6},{6,5},{7,4},{8,11},{9,10},{10,... | collective-permute-start | bytes 196616 | tf_op jit(solution)/shard_map/ppermute | solution.py:467
  29.3 0.9 %collective-permute-done.11.refs_1_ = f32[64,256]{1,0:T(8,128)S(1)} collective-permute-done((f32[64,256]{1,0:T(8,128)S(1)}, f32[64,256]{1,0:T(8,128)S(1)}, u32[]{:S(2)}, u32[]{:S(2)}) %collective-permute-start.11) | collective-permute-done | bytes 65568 | tf_op jit(solution)/shard_map/ppermute | solution.py:467
  30.2 3.2 %collective-permute-done.12.refs_2_ = f32[64,256]{1,0:T(8,128)S(1)} collective-permute-done((f32[64,256]{1,0:T(8,128)S(1)}, f32[64,256]{1,0:T(8,128)S(1)}, u32[]{:S(2)}, u32[]{:S(2)}) %collective-permute-start.12) | collective-permute-done | bytes 65568 | tf_op jit(solution)/shard_map/ppermute | solution.py:467
  33.4 3.4 %collective-permute-start.16 = (f32[64,256]{1,0:T(8,128)S(1)}, f32[64,256]{1,0:T(8,128)S(1)}, u32[]{:S(2)}, u32[]{:S(2)}) collective-permute-start(f32[64,256]{1,0:T(8,128)S(1)} %shard_map.109.refs_0_), channel_id=1, source_target_pairs={{0,12},{1,13},{2,14},{3,15},{4,8},{5,9},{6,10},{7,11},{8,4},{9,5},... | collective-permute-start | bytes 196616 | tf_op jit(solution)/shard_map/ppermute | solution.py:467
  36.9 1.0 %collective-permute-start.14 = (f32[64,256]{1,0:T(8,128)S(1)}, f32[64,256]{1,0:T(8,128)S(1)}, u32[]{:S(2)}, u32[]{:S(2)}) collective-permute-start(f32[64,256]{1,0:T(8,128)S(1)} %shard_map.109.refs_0_), channel_id=1, source_target_pairs={{0,4},{1,5},{2,6},{3,7},{4,0},{5,1},{6,2},{7,3},{8,12},{9,13},{10,... | collective-permute-start | bytes 196616 | tf_op jit(solution)/shard_map/ppermute | solution.py:467
  37.9 1.7 %collective-permute-done.16.refs_3_ = f32[64,256]{1,0:T(8,128)S(1)} collective-permute-done((f32[64,256]{1,0:T(8,128)S(1)}, f32[64,256]{1,0:T(8,128)S(1)}, u32[]{:S(2)}, u32[]{:S(2)}) %collective-permute-start.16) | collective-permute-done | bytes 65568 | tf_op jit(solution)/shard_map/ppermute | solution.py:467
  39.6 2.7 %collective-permute-done.15.refs_2_ = f32[64,256]{1,0:T(8,128)S(1)} collective-permute-done((f32[64,256]{1,0:T(8,128)S(1)}, f32[64,256]{1,0:T(8,128)S(1)}, u32[]{:S(2)}, u32[]{:S(2)}) %collective-permute-start.15) | collective-permute-done | bytes 65568 | tf_op jit(solution)/shard_map/ppermute | solution.py:467
  42.3 1.5 %collective-permute-start.19 = (f32[64,256]{1,0:T(8,128)S(1)}, f32[64,256]{1,0:T(8,128)S(1)}, u32[]{:S(2)}, u32[]{:S(2)}) collective-permute-start(f32[64,256]{1,0:T(8,128)S(1)} %shard_map.110.refs_0_), channel_id=1, source_target_pairs={{0,3},{1,2},{2,1},{3,0},{4,7},{5,6},{6,5},{7,4},{8,11},{9,10},{10,... | collective-permute-start | bytes 196616 | tf_op jit(solution)/shard_map/ppermute | solution.py:467
  43.8 1.6 %collective-permute-start.18 = (f32[64,256]{1,0:T(8,128)S(1)}, f32[64,256]{1,0:T(8,128)S(1)}, u32[]{:S(2)}, u32[]{:S(2)}) collective-permute-start(f32[64,256]{1,0:T(8,128)S(1)} %shard_map.110.refs_0_), channel_id=1, source_target_pairs={{0,2},{1,3},{2,0},{3,1},{4,6},{5,7},{6,4},{7,5},{8,10},{9,11},{10,... | collective-permute-start | bytes 196616 | tf_op jit(solution)/shard_map/ppermute | solution.py:467
  45.4 0.5 collective-permute-start.17
  46.0 1.6 %collective-permute-start.8 = (f32[2,256,128]{2,1,0:T(8,128)S(1)}, f32[2,256,128]{2,1,0:T(8,128)S(1)}, u32[]{:S(2)}, u32[]{:S(2)}) collective-permute-start(f32[2,256,128]{2,1,0:T(8,128)S(1)} %get-tuple-element.54), channel_id=1, source_target_pairs={{0,1},{2,3},{4,5},{6,7},{8,9},{10,11},{12,13},{14,15},{1,0},{3,2},... | collective-permute-start | bytes 786440 | tf_op jit(solution)/shard_map/ppermute | solution.py:692
  47.6 0.7 %collective-permute-start.9 = (f32[2,256,128]{2,1,0:T(8,128)S(1)}, f32[2,256,128]{2,1,0:T(8,128)S(1)}, u32[]{:S(2)}, u32[]{:S(2)}) collective-permute-start(f32[2,256,128]{2,1,0:T(8,128)S(1)} %get-tuple-element.55), channel_id=1, source_target_pairs={{1,2},{3,4},{5,6},{7,8},{9,10},{11,12},{13,14},{2,1},{4,3},{6,5},{... | collective-permute-start | bytes 786440 | tf_op jit(solution)/shard_map/ppermute | solution.py:693
  48.5 1.8 %collective-permute-done.17.refs_1_ = f32[64,256]{1,0:T(8,128)S(1)} collective-permute-done((f32[64,256]{1,0:T(8,128)S(1)}, f32[64,256]{1,0:T(8,128)S(1)}, u32[]{:S(2)}, u32[]{:S(2)}) %collective-permute-start.17) | collective-permute-done | bytes 65568 | tf_op jit(solution)/shard_map/ppermute | solution.py:467
  50.4 0.7 %shard_map.112.started = f32[2,256,256]{2,1,0:T(8,128)} custom-call(f32[256,256]{1,0:T(8,128)S(1)} %shard_map.111.full), custom_call_target="tpu_custom_call" | custom-call | tf_op jit(solution)/shard_map/pallas_call | solution.py:557
  51.2 6.3 %collective-permute-done.8.e = f32[2,256,128]{2,1,0:T(8,128)S(1)} collective-permute-done((f32[2,256,128]{2,1,0:T(8,128)S(1)}, f32[2,256,128]{2,1,0:T(8,128)S(1)}, u32[]{:S(2)}, u32[]{:S(2)}) %collective-permute-start.8) | collective-permute-done | bytes 262176 | tf_op jit(solution)/shard_map/ppermute | solution.py:692
  57.5 1.2 %shard_map.107 = f32[4,256,256]{2,1,0:T(8,128)} custom-call(f32[4,256,256]{2,1,0:T(8,128)S(1)} %get-tuple-element.53.total, f32[2,256,128]{2,1,0:T(8,128)S(1)} %collective-permute-done.8.e, f32[2,256,128]{2,1,0:T(8,128)S(1)} %collective-permute-done.9.o), custom_call_target="tpu_custom_call" | custom-call | tf_op jit(solution)/shard_map/pallas_call | solution.py:444
  58.7 0.7 %shard_map.113 = f32[2,256,256]{2,1,0:T(8,128)} custom-call(f32[2,256,256]{2,1,0:T(8,128)} %shard_map.112.started, f32[256,256]{1,0:T(8,128)S(1)} %collective-permute-done.20.other), custom_call_target="tpu_custom_call", output_to_operand_aliasing={{}: (0, {})} | custom-call | tf_op jit(solution)/shard_map/pallas_call | solution.py:558
  (31 shorter events, 2.5 us)
Async XLA Ops:
  0.6 10.8 %copy-start = (f32[256,256]{1,0:T(8,128)S(1)}, f32[256,256]{1,0:T(8,128)}, u32[]{:S(2)}) copy-start(f32[256,256]{1,0:T(8,128)} %refs_0_.1) | copy-start | bytes 786436
  2.7 11.4 %collective-permute-start.2 = (f32[4,64,256]{2,1,0:T(8,128)S(1)}, f32[4,64,256]{2,1,0:T(8,128)S(1)}, u32[]{:S(2)}, u32[]{:S(2)}) collective-permute-start(f32[4,64,256]{2,1,0:T(8,128)S(1)} %get-tuple-element.36), channel_id=1, source_target_pairs={{0,16},{16,0},{1,17},{17,1},{2,18},{18,2},{3,19},{19,3},{4,20},{20... | collective-permute-start | bytes 786440 | tf_op jit(solution)/shard_map/ppermute | solution.py:589
  3.2 9.5 %collective-permute-start.3 = (f32[256,128]{1,0:T(8,128)S(1)}, f32[256,128]{1,0:T(8,128)S(1)}, u32[]{:S(2)}, u32[]{:S(2)}) collective-permute-start(f32[256,128]{1,0:T(8,128)S(1)} %get-tuple-element.37), channel_id=1, source_target_pairs={{0,1},{2,3},{4,5},{6,7},{8,9},{10,11},{12,13},{14,15},{1,0},{3,2},... | collective-permute-start | bytes 393224 | tf_op jit(solution)/shard_map/ppermute | solution.py:584
  5.8 7.0 %collective-permute-start.4 = (f32[256,128]{1,0:T(8,128)S(1)}, f32[256,128]{1,0:T(8,128)S(1)}, u32[]{:S(2)}, u32[]{:S(2)}) collective-permute-start(f32[256,128]{1,0:T(8,128)S(1)} %get-tuple-element.38), channel_id=1, source_target_pairs={{1,2},{3,4},{5,6},{7,8},{9,10},{11,12},{13,14},{2,1},{4,3},{6,5},{... | collective-permute-start | bytes 393224 | tf_op jit(solution)/shard_map/ppermute | solution.py:586
  6.4 12.3 %collective-permute-start = (f32[256,128]{1,0:T(8,128)S(1)}, f32[256,128]{1,0:T(8,128)S(1)}, u32[]{:S(2)}, u32[]{:S(2)}) collective-permute-start(f32[256,128]{1,0:T(8,128)S(1)} %get-tuple-element.33), channel_id=1, source_target_pairs={{0,1},{2,3},{4,5},{6,7},{8,9},{10,11},{12,13},{14,15},{1,0},{3,2},... | collective-permute-start | bytes 393224 | tf_op jit(solution)/shard_map/ppermute | solution.py:585
  10.7 8.0 %collective-permute-start.1 = (f32[256,128]{1,0:T(8,128)S(1)}, f32[256,128]{1,0:T(8,128)S(1)}, u32[]{:S(2)}, u32[]{:S(2)}) collective-permute-start(f32[256,128]{1,0:T(8,128)S(1)} %get-tuple-element.34), channel_id=1, source_target_pairs={{1,2},{3,4},{5,6},{7,8},{9,10},{11,12},{13,14},{2,1},{4,3},{6,5},{... | collective-permute-start | bytes 393224 | tf_op jit(solution)/shard_map/ppermute | solution.py:587
  12.8 1.3 %collective-permute-start.5 = (f32[2,64,128]{2,1,0:T(8,128)S(1)}, f32[2,64,128]{2,1,0:T(8,128)S(1)}, u32[]{:S(2)}, u32[]{:S(2)}) collective-permute-start(f32[2,64,128]{2,1,0:T(8,128)S(1)} %shard_map.99), channel_id=1, source_target_pairs={{0,16},{16,0},{1,17},{17,1},{2,18},{18,2},{3,19},{19,3},{4,20},{20... | collective-permute-start | bytes 196616 | tf_op jit(solution)/shard_map/ppermute | solution.py:602
  18.7 1.3 %collective-permute-start.6 = (f32[2,64,128]{2,1,0:T(8,128)S(1)}, f32[2,64,128]{2,1,0:T(8,128)S(1)}, u32[]{:S(2)}, u32[]{:S(2)}) collective-permute-start(f32[2,64,128]{2,1,0:T(8,128)S(1)} %shard_map.102), channel_id=1, source_target_pairs={{0,16},{16,0},{1,17},{17,1},{2,18},{18,2},{3,19},{19,3},{4,20},{20... | collective-permute-start | bytes 196616 | tf_op jit(solution)/shard_map/ppermute | solution.py:602
  23.6 1.6 %collective-permute-start.10 = (f32[256,256]{1,0:T(8,128)S(1)}, f32[256,256]{1,0:T(8,128)S(1)}, u32[]{:S(2)}, u32[]{:S(2)}) collective-permute-start(f32[256,256]{1,0:T(8,128)S(1)} %get-tuple-element.57), channel_id=1, source_target_pairs={{0,16},{16,0},{1,17},{17,1},{2,18},{18,2},{3,19},{19,3},{4,20},{20... | collective-permute-start | bytes 786440 | tf_op jit(solution)/shard_map/ppermute | solution.py:467
  24.2 21.6 %collective-permute-start.7 = (f32[4,64,384]{2,1,0:T(8,128)S(1)}, f32[4,64,384]{2,1,0:T(8,128)S(1)}, u32[]{:S(2)}, u32[]{:S(2)}) collective-permute-start(f32[4,64,384]{2,1,0:T(8,128)S(1)} %get-tuple-element.52), channel_id=1, source_target_pairs={{0,16},{16,0},{1,17},{17,1},{2,18},{18,2},{3,19},{19,3},{4,20},{20... | collective-permute-start | bytes 1179656 | tf_op jit(solution)/shard_map/ppermute | solution.py:683
  25.3 5.0 %collective-permute-start.11 = (f32[64,256]{1,0:T(8,128)S(1)}, f32[64,256]{1,0:T(8,128)S(1)}, u32[]{:S(2)}, u32[]{:S(2)}) collective-permute-start(f32[64,256]{1,0:T(8,128)S(1)} %get-tuple-element.59), channel_id=1, source_target_pairs={{0,1},{1,0},{2,3},{3,2},{4,5},{5,4},{6,7},{7,6},{8,9},{9,8},{10,11... | collective-permute-start | bytes 196616 | tf_op jit(solution)/shard_map/ppermute | solution.py:467
  27.8 5.6 %collective-permute-start.12 = (f32[64,256]{1,0:T(8,128)S(1)}, f32[64,256]{1,0:T(8,128)S(1)}, u32[]{:S(2)}, u32[]{:S(2)}) collective-permute-start(f32[64,256]{1,0:T(8,128)S(1)} %get-tuple-element.60), channel_id=1, source_target_pairs={{0,2},{1,3},{2,0},{3,1},{4,6},{5,7},{6,4},{7,5},{8,10},{9,11},{10,... | collective-permute-start | bytes 196616 | tf_op jit(solution)/shard_map/ppermute | solution.py:467
  28.0 5.4 %collective-permute-start.13 = (f32[64,256]{1,0:T(8,128)S(1)}, f32[64,256]{1,0:T(8,128)S(1)}, u32[]{:S(2)}, u32[]{:S(2)}) collective-permute-start(f32[64,256]{1,0:T(8,128)S(1)} %get-tuple-element.61), channel_id=1, source_target_pairs={{0,3},{1,2},{2,1},{3,0},{4,7},{5,6},{6,5},{7,4},{8,11},{9,10},{10,... | collective-permute-start | bytes 196616 | tf_op jit(solution)/shard_map/ppermute | solution.py:467
  33.4 6.1 %collective-permute-start.16 = (f32[64,256]{1,0:T(8,128)S(1)}, f32[64,256]{1,0:T(8,128)S(1)}, u32[]{:S(2)}, u32[]{:S(2)}) collective-permute-start(f32[64,256]{1,0:T(8,128)S(1)} %shard_map.109.refs_0_), channel_id=1, source_target_pairs={{0,12},{1,13},{2,14},{3,15},{4,8},{5,9},{6,10},{7,11},{8,4},{9,5},... | collective-permute-start | bytes 196616 | tf_op jit(solution)/shard_map/ppermute | solution.py:467
  36.9 5.4 %collective-permute-start.15 = (f32[64,256]{1,0:T(8,128)S(1)}, f32[64,256]{1,0:T(8,128)S(1)}, u32[]{:S(2)}, u32[]{:S(2)}) collective-permute-start(f32[64,256]{1,0:T(8,128)S(1)} %shard_map.109.refs_0_), channel_id=1, source_target_pairs={{0,8},{1,9},{2,10},{3,11},{4,12},{5,13},{6,14},{7,15},{8,0},{9,1},... | collective-permute-start | bytes 196616 | tf_op jit(solution)/shard_map/ppermute | solution.py:467
  36.9 5.4 %collective-permute-start.14 = (f32[64,256]{1,0:T(8,128)S(1)}, f32[64,256]{1,0:T(8,128)S(1)}, u32[]{:S(2)}, u32[]{:S(2)}) collective-permute-start(f32[64,256]{1,0:T(8,128)S(1)} %shard_map.109.refs_0_), channel_id=1, source_target_pairs={{0,4},{1,5},{2,6},{3,7},{4,0},{5,1},{6,2},{7,3},{8,12},{9,13},{10,... | collective-permute-start | bytes 196616 | tf_op jit(solution)/shard_map/ppermute | solution.py:467
  42.3 6.0 %collective-permute-start.19 = (f32[64,256]{1,0:T(8,128)S(1)}, f32[64,256]{1,0:T(8,128)S(1)}, u32[]{:S(2)}, u32[]{:S(2)}) collective-permute-start(f32[64,256]{1,0:T(8,128)S(1)} %shard_map.110.refs_0_), channel_id=1, source_target_pairs={{0,3},{1,2},{2,1},{3,0},{4,7},{5,6},{6,5},{7,4},{8,11},{9,10},{10,... | collective-permute-start | bytes 196616 | tf_op jit(solution)/shard_map/ppermute | solution.py:467
  43.8 4.7 %collective-permute-start.18 = (f32[64,256]{1,0:T(8,128)S(1)}, f32[64,256]{1,0:T(8,128)S(1)}, u32[]{:S(2)}, u32[]{:S(2)}) collective-permute-start(f32[64,256]{1,0:T(8,128)S(1)} %shard_map.110.refs_0_), channel_id=1, source_target_pairs={{0,2},{1,3},{2,0},{3,1},{4,6},{5,7},{6,4},{7,5},{8,10},{9,11},{10,... | collective-permute-start | bytes 196616 | tf_op jit(solution)/shard_map/ppermute | solution.py:467
  45.4 5.0 %collective-permute-start.17 = (f32[64,256]{1,0:T(8,128)S(1)}, f32[64,256]{1,0:T(8,128)S(1)}, u32[]{:S(2)}, u32[]{:S(2)}) collective-permute-start(f32[64,256]{1,0:T(8,128)S(1)} %shard_map.110.refs_0_), channel_id=1, source_target_pairs={{0,1},{1,0},{2,3},{3,2},{4,5},{5,4},{6,7},{7,6},{8,9},{9,8},{10,11... | collective-permute-start | bytes 196616 | tf_op jit(solution)/shard_map/ppermute | solution.py:467
  46.0 11.5 %collective-permute-start.8 = (f32[2,256,128]{2,1,0:T(8,128)S(1)}, f32[2,256,128]{2,1,0:T(8,128)S(1)}, u32[]{:S(2)}, u32[]{:S(2)}) collective-permute-start(f32[2,256,128]{2,1,0:T(8,128)S(1)} %get-tuple-element.54), channel_id=1, source_target_pairs={{0,1},{2,3},{4,5},{6,7},{8,9},{10,11},{12,13},{14,15},{1,0},{3,2},... | collective-permute-start | bytes 786440 | tf_op jit(solution)/shard_map/ppermute | solution.py:692
  47.6 9.9 %collective-permute-start.9 = (f32[2,256,128]{2,1,0:T(8,128)S(1)}, f32[2,256,128]{2,1,0:T(8,128)S(1)}, u32[]{:S(2)}, u32[]{:S(2)}) collective-permute-start(f32[2,256,128]{2,1,0:T(8,128)S(1)} %get-tuple-element.55), channel_id=1, source_target_pairs={{1,2},{3,4},{5,6},{7,8},{9,10},{11,12},{13,14},{2,1},{4,3},{6,5},{... | collective-permute-start | bytes 786440 | tf_op jit(solution)/shard_map/ppermute | solution.py:693
  50.4 8.4 %collective-permute-start.20 = (f32[256,256]{1,0:T(8,128)S(1)}, f32[256,256]{1,0:T(8,128)S(1)}, u32[]{:S(2)}, u32[]{:S(2)}) collective-permute-start(f32[256,256]{1,0:T(8,128)S(1)} %shard_map.111.full), channel_id=1, source_target_pairs={{0,16},{16,0},{1,17},{17,1},{2,18},{18,2},{3,19},{19,3},{4,20},{20... | collective-permute-start | bytes 786440 | tf_op jit(solution)/shard_map/ppermute | solution.py:467

commit v10 on v8

--- a/solution.py
+++ b/solution.py
@@ -177,7 +177,11 @@
     for s in range(2):
         copies[s].wait()
         low, high = pack_cols(obj[2 * s], obj[2 * s + 1])
-        evens[s][...] = jnp.where(even, high, low)
+        strip = jnp.where(even, high, low)
+        if s == 0:
+            evens[0][:n] = strip
+        else:
+            evens[0][n:], evens[1][...] = strip[: n // 2], strip[n // 2 :]
         odds[s] = jnp.where(even, low, high)
     for which, out in enumerate(rows):
         out[...] = obj[:, pl.ds(row_start(which, n, margin), margin), :]
@@ -186,11 +190,17 @@
         limits[i] = jnp.full(limits.shape[1:], offs[0, i] - margin, jnp.int32)
 
 
-def corner_kernel(s, margin, e, o, after, *outs):
+def corner_kernel(s, margin, *refs):
+    evens, o, outs = refs[: s + 1], refs[s + 1], refs[s + 3 :]
+    n = o.shape[1]
     for which, out in enumerate(outs):
-        rows = pl.ds(row_start(which, e.shape[0], margin), margin)
-        out[0] = e[rows, :]
-        out[1] = o[s, rows, :]
+        start = row_start(which, n, margin)
+        if s == 0:
+            out[0] = evens[0][pl.ds(start, margin), :]
+        else:
+            top, bottom = evens[0][n : n + margin], evens[1][n // 2 - margin :]
+            out[0] = jnp.where(start == 0, top, bottom)
+        out[1] = o[s, pl.ds(start, margin), :]
 
 
 def even_odd(n, axis):
@@ -269,9 +279,12 @@
     return out
 
 
-def merge_kernel(s, obj, e, o, limits, out):
+def merge_kernel(s, obj, *refs):
+    evens, (o, limits, out) = refs[: s + 1], refs[s + 1 :]
+    n = obj.shape[1]
+    e = cat([evens[0][n:], evens[1][...]], 0) if s else evens[0][:n]
     own = [obj[2 * s], obj[2 * s + 1]]
-    out[0], out[1] = merge_cols(own, e[...], o[s], limits)
+    out[0], out[1] = merge_cols(own, e, o[s], limits)
 
 
 def window_of(main, s, halos, corners, limits, margin):
@@ -575,7 +588,7 @@
         functools.partial(pack_kernel, margin),
         [(4, n, n), jax.ShapeDtypeStruct((1, 2), jnp.int32)]
         + [jax.ShapeDtypeStruct((2, 8, h), jnp.int32)]
-        + [(n, h), (n, h), (2, n, h)]
+        + [(n + n // 2, h), (n // 2, h), (2, n, h)]
         + [(4, margin, n)] * n_row,
         [HBM, HBM],
         in_hbm(object_field.reshape(4, tile, tile)),
@@ -594,8 +607,8 @@
         parts = call(
             functools.partial(corner_kernel, s, margin),
             [(2, margin, h)] * n_row,
-            [VMEM] * 3,
-            evens[s],
+            [VMEM] * (3 + s),
+            *evens[: s + 1],
             odds,
             after,
         )
@@ -606,9 +619,9 @@
         (main,) = call(
             functools.partial(merge_kernel, s),
             [(2, n, n)],
-            [VMEM] * 4,
+            [VMEM] * (4 + s),
             obj,
-            evens[s],
+            *evens[: s + 1],
             odds,
             limits,
         )

time: 62 us -> 61.7 us (level)
    ppermute x1, waiting for transfers between devices: 1.42 us -> 0.45 us  [whole(): even1 = lax.ppermute(even1, 'col', col_rounds[0])]
    ppermute x1, waiting for transfers between devices: 6.02 us -> 6.99 us  [whole(): even0 = lax.ppermute(even0, 'col', col_rounds[0])]
    ppermute x11, starting transfers between devices: 12.6 us -> 11.8 us  [swap(): return lax.ppermute(value, axis, [(i, i ^ distance) for i in range(count)])]
  transfers between devices with their start and end apart: 20 -> 20, of which waited for: 11 -> 12; matrix products, arithmetic and copies ran while one was open for 0% -> 0% of each run, Pallas kernels for 13% -> 13%
where the time goes in v10:
time: 61.7 us; the launch traced here: 61.3 us
  waiting for transfers between devices  25.2 us (41%)
  starting transfers between devices  21 us (34%)
  Pallas kernels  14.3 us (23%)
  between operations  0.79 us (1%)
    pallas_call x17, Pallas kernels, call(): pl.pallas_call(kernel, out_shape=shapes, in_specs=in_specs, out_specs=[SM...  12.9 us
    ppermute x11, starting transfers between devices, swap(): return lax.ppermute(value, axis, [(i, i ^ distance) for i in range(count)])  11.8 us
    ppermute x11, waiting for transfers between devices, swap(): return lax.ppermute(value, axis, [(i, i ^ distance) for i in range(count)])  10.7 us
    ppermute x1, waiting for transfers between devices, whole(): even0 = lax.ppermute(even0, 'col', col_rounds[0])  6.99 us
    ppermute x1, waiting for transfers between devices, whole(): send_e = lax.ppermute(send_e, 'col', col_rounds[0])  6.76 us
    ppermute x1, starting transfers between devices, whole(): even0 = lax.ppermute(even0, 'col', col_rounds[0])  5.75 us
    ppermute x1, starting transfers between devices, whole(): send_e = lax.ppermute(send_e, 'col', col_rounds[0])  1.27 us
  transfers between devices with their start and end apart: 20, of which 12 were waited for; matrix products, arithmetic and copies ran while one was open for 0% of the time, Pallas kernels for 13%

profile of v10, /device:TPU:0, one launch (start us, length us, event | category | flops | bytes accessed | tf_op | source)
XLA Modules:
  0.0 61.3 jit_solution(2157077965976223370)
XLA Ops:
  0.6 2.0 %shard_map.95 = (f32[4,256,256]{2,1,0:T(8,128)S(1)}, s32[1,2]{1,0:T(1,128)S(1)}, s32[2,8,128]{2,1,0:T(8,128)S(1)}, f32[384,128]{1,0:T(8,128)S(1)}, f32[128,128]{...) custom-call(f32[4,256,256]{2,1,0:T(8,128)} %bitcast.4, s32[1,2]{1,0:T(1,128)} %bitcast.7), custom_call_target="tpu_custom_call" | custom-call | tf_op jit(solution)/shard_map/pallas_call | solution.py:459
  2.6 0.7 %collective-permute-start.2 = (f32[2,256,128]{2,1,0:T(8,128)S(1)}, f32[2,256,128]{2,1,0:T(8,128)S(1)}, u32[]{:S(2)}, u32[]{:S(2)}) collective-permute-start(f32[2,256,128]{2,1,0:T(8,128)S(1)} %get-tuple-element.34), channel_id=1, source_target_pairs={{1,2},{3,4},{5,6},{7,8},{9,10},{11,12},{13,14},{2,1},{4,3},{6,5},{... | collective-permute-start | bytes 786440 | tf_op jit(solution)/shard_map/ppermute | solution.py:600
  3.3 5.8 %collective-permute-start = (f32[384,128]{1,0:T(8,128)S(1)}, f32[384,128]{1,0:T(8,128)S(1)}, u32[]{:S(2)}, u32[]{:S(2)}) collective-permute-start(f32[384,128]{1,0:T(8,128)S(1)} %get-tuple-element.32), channel_id=1, source_target_pairs={{0,1},{2,3},{4,5},{6,7},{8,9},{10,11},{12,13},{14,15},{1,0},{3,2},... | collective-permute-start | bytes 589832 | tf_op jit(solution)/shard_map/ppermute | solution.py:599
  9.2 2.3 %shard_map.99 = (f32[256,256]{1,0:T(8,128)S(1)}, f32[256,256]{1,0:T(8,128)S(1)}, bf16[4,256,256]{2,1,0:T(8,128)(2,1)S(1)}, f32[2,128,128]{2,1,0:T(8,128)S(1)}, f...) custom-call(f32[256,256]{1,0:T(8,128)} %refs_0_.1, ...), custom_call_target="tpu_custom_call" | custom-call | tf_op jit(solution)/shard_map/pallas_call | solution.py:459
  11.5 0.8 %shard_map.100.after.refs_4_.refs_5_ = f32[2,256,256]{2,1,0:T(8,128)S(1)} custom-call(s32[1,2]{1,0:T(1,128)S(1)} %get-tuple-element.37.offs, f32[2,256,256]{2,1,0:T(8,128)S(1)} %get-tuple-element.38.probe), custom_call_target="tpu_custom_call" | custom-call | tf_op jit(solution)/shard_map/pallas_call | solution.py:459
  12.3 0.6 %shard_map.101.refs_2_.refs_8_ = f32[256,256]{1,0:T(8,128)S(1)} custom-call(f32[256,256]{1,0:T(8,128)S(1)} %get-tuple-element.41.x, f32[2,256,256]{2,1,0:T(8,128)S(1)} %shard_map.100.after.refs_4_.refs_5_), custom_call_target="tpu_custom_call" | custom-call | tf_op jit(solution)/shard_map/pallas_call | solution.py:459
  12.9 7.0 %collective-permute-done.refs_0_ = f32[384,128]{1,0:T(8,128)S(1)} collective-permute-done((f32[384,128]{1,0:T(8,128)S(1)}, f32[384,128]{1,0:T(8,128)S(1)}, u32[]{:S(2)}, u32[]{:S(2)}) %collective-permute-start) | collective-permute-done | bytes 196640 | tf_op jit(solution)/shard_map/ppermute | solution.py:599
  20.2 0.4 collective-permute-done.1.refs_1_
  21.2 1.5 %shard_map.103 = (f32[2,256,256]{2,1,0:T(8,128)S(1)}, f32[2,256,256]{2,1,0:T(8,128)S(1)}) custom-call(f32[2,256,256]{2,1,0:T(8,128)S(1)} %shard_map.97.refs_3_.refs_0_, f32[4,64,256]{2,1,0:T(8,128)S(1)} %collective-permute-done.3.refs_1_, f32[2,64,128]{2,1,0:T(8,128)S(1)} %collective-permute-done.5.refs_2_, ...), custom_call_target="tpu_custom_call" | custom-call | tf_op jit(solution)/shard_map/pallas_call | solution.py:459
  22.8 3.6 %shard_map.104 = (f32[256,256]{1,0:T(8,128)S(1)}, f32[256,256]{1,0:T(8,128)S(1)}, f32[4,256,256]{2,1,0:T(8,128)S(1)}) custom-call(f32[2,256,256]{2,1,0:T(8,128)S(1)} %shard_map.96.refs_0_, f32[4,64,256]{2,1,0:T(8,128)S(1)} %collective-permute-done.3.refs_1_, f32[2,64,128]{2,1,0:T(8,128)S(1)} %collective-permute-done.4.refs_2_, ...), custom_call_target="tpu_custom_call" | custom-call | tf_op jit(solution)/shard_map/pallas_call | solution.py:459
  26.6 0.4 shard_map.105
  26.9 0.4 collective-permute-start.6
  27.4 0.6 collective-permute-done.9.other
  28.0 1.8 %collective-permute-start.10 = (f32[64,256]{1,0:T(8,128)S(1)}, f32[64,256]{1,0:T(8,128)S(1)}, u32[]{:S(2)}, u32[]{:S(2)}) collective-permute-start(f32[64,256]{1,0:T(8,128)S(1)} %get-tuple-element.57), channel_id=1, source_target_pairs={{0,1},{1,0},{2,3},{3,2},{4,5},{5,4},{6,7},{7,6},{8,9},{9,8},{10,11... | collective-permute-start | bytes 196616 | tf_op jit(solution)/shard_map/ppermute | solution.py:482
  30.0 1.5 %collective-permute-start.12 = (f32[64,256]{1,0:T(8,128)S(1)}, f32[64,256]{1,0:T(8,128)S(1)}, u32[]{:S(2)}, u32[]{:S(2)}) collective-permute-start(f32[64,256]{1,0:T(8,128)S(1)} %get-tuple-element.59), channel_id=1, source_target_pairs={{0,3},{1,2},{2,1},{3,0},{4,7},{5,6},{6,5},{7,4},{8,11},{9,10},{10,... | collective-permute-start | bytes 196616 | tf_op jit(solution)/shard_map/ppermute | solution.py:482
  31.5 0.8 %collective-permute-done.10.refs_1_ = f32[64,256]{1,0:T(8,128)S(1)} collective-permute-done((f32[64,256]{1,0:T(8,128)S(1)}, f32[64,256]{1,0:T(8,128)S(1)}, u32[]{:S(2)}, u32[]{:S(2)}) %collective-permute-start.10) | collective-permute-done | bytes 65568 | tf_op jit(solution)/shard_map/ppermute | solution.py:482
  32.3 3.0 %collective-permute-done.11.refs_2_ = f32[64,256]{1,0:T(8,128)S(1)} collective-permute-done((f32[64,256]{1,0:T(8,128)S(1)}, f32[64,256]{1,0:T(8,128)S(1)}, u32[]{:S(2)}, u32[]{:S(2)}) %collective-permute-start.11) | collective-permute-done | bytes 65568 | tf_op jit(solution)/shard_map/ppermute | solution.py:482
  35.4 3.5 %collective-permute-start.15 = (f32[64,256]{1,0:T(8,128)S(1)}, f32[64,256]{1,0:T(8,128)S(1)}, u32[]{:S(2)}, u32[]{:S(2)}) collective-permute-start(f32[64,256]{1,0:T(8,128)S(1)} %shard_map.109.refs_0_), channel_id=1, source_target_pairs={{0,12},{1,13},{2,14},{3,15},{4,8},{5,9},{6,10},{7,11},{8,4},{9,5},... | collective-permute-start | bytes 196616 | tf_op jit(solution)/shard_map/ppermute | solution.py:482
  38.9 0.9 %collective-permute-start.13 = (f32[64,256]{1,0:T(8,128)S(1)}, f32[64,256]{1,0:T(8,128)S(1)}, u32[]{:S(2)}, u32[]{:S(2)}) collective-permute-start(f32[64,256]{1,0:T(8,128)S(1)} %shard_map.109.refs_0_), channel_id=1, source_target_pairs={{0,4},{1,5},{2,6},{3,7},{4,0},{5,1},{6,2},{7,3},{8,12},{9,13},{10,... | collective-permute-start | bytes 196616 | tf_op jit(solution)/shard_map/ppermute | solution.py:482
  39.8 1.7 %collective-permute-done.15.refs_3_ = f32[64,256]{1,0:T(8,128)S(1)} collective-permute-done((f32[64,256]{1,0:T(8,128)S(1)}, f32[64,256]{1,0:T(8,128)S(1)}, u32[]{:S(2)}, u32[]{:S(2)}) %collective-permute-start.15) | collective-permute-done | bytes 65568 | tf_op jit(solution)/shard_map/ppermute | solution.py:482
  41.5 2.6 %collective-permute-done.14.refs_2_ = f32[64,256]{1,0:T(8,128)S(1)} collective-permute-done((f32[64,256]{1,0:T(8,128)S(1)}, f32[64,256]{1,0:T(8,128)S(1)}, u32[]{:S(2)}, u32[]{:S(2)}) %collective-permute-start.14) | collective-permute-done | bytes 65568 | tf_op jit(solution)/shard_map/ppermute | solution.py:482
  44.1 1.6 %collective-permute-start.18 = (f32[64,256]{1,0:T(8,128)S(1)}, f32[64,256]{1,0:T(8,128)S(1)}, u32[]{:S(2)}, u32[]{:S(2)}) collective-permute-start(f32[64,256]{1,0:T(8,128)S(1)} %shard_map.110.refs_0_), channel_id=1, source_target_pairs={{0,3},{1,2},{2,1},{3,0},{4,7},{5,6},{6,5},{7,4},{8,11},{9,10},{10,... | collective-permute-start | bytes 196616 | tf_op jit(solution)/shard_map/ppermute | solution.py:482
  45.7 1.2 %collective-permute-start.17 = (f32[64,256]{1,0:T(8,128)S(1)}, f32[64,256]{1,0:T(8,128)S(1)}, u32[]{:S(2)}, u32[]{:S(2)}) collective-permute-start(f32[64,256]{1,0:T(8,128)S(1)} %shard_map.110.refs_0_), channel_id=1, source_target_pairs={{0,2},{1,3},{2,0},{3,1},{4,6},{5,7},{6,4},{7,5},{8,10},{9,11},{10,... | collective-permute-start | bytes 196616 | tf_op jit(solution)/shard_map/ppermute | solution.py:482
  46.8 0.8 %collective-permute-start.16 = (f32[64,256]{1,0:T(8,128)S(1)}, f32[64,256]{1,0:T(8,128)S(1)}, u32[]{:S(2)}, u32[]{:S(2)}) collective-permute-start(f32[64,256]{1,0:T(8,128)S(1)} %shard_map.110.refs_0_), channel_id=1, source_target_pairs={{0,1},{1,0},{2,3},{3,2},{4,5},{5,4},{6,7},{7,6},{8,9},{9,8},{10,11... | collective-permute-start | bytes 196616 | tf_op jit(solution)/shard_map/ppermute | solution.py:482
  47.8 1.3 %collective-permute-start.7 = (f32[2,256,128]{2,1,0:T(8,128)S(1)}, f32[2,256,128]{2,1,0:T(8,128)S(1)}, u32[]{:S(2)}, u32[]{:S(2)}) collective-permute-start(f32[2,256,128]{2,1,0:T(8,128)S(1)} %get-tuple-element.52), channel_id=1, source_target_pairs={{0,1},{2,3},{4,5},{6,7},{8,9},{10,11},{12,13},{14,15},{1,0},{3,2},... | collective-permute-start | bytes 786440 | tf_op jit(solution)/shard_map/ppermute | solution.py:705
  49.1 0.7 %collective-permute-start.8 = (f32[2,256,128]{2,1,0:T(8,128)S(1)}, f32[2,256,128]{2,1,0:T(8,128)S(1)}, u32[]{:S(2)}, u32[]{:S(2)}) collective-permute-start(f32[2,256,128]{2,1,0:T(8,128)S(1)} %get-tuple-element.53), channel_id=1, source_target_pairs={{1,2},{3,4},{5,6},{7,8},{9,10},{11,12},{13,14},{2,1},{4,3},{6,5},{... | collective-permute-start | bytes 786440 | tf_op jit(solution)/shard_map/ppermute | solution.py:706
  50.0 0.3 collective-permute-done.17.refs_2_
  50.3 1.5 %collective-permute-done.16.refs_1_ = f32[64,256]{1,0:T(8,128)S(1)} collective-permute-done((f32[64,256]{1,0:T(8,128)S(1)}, f32[64,256]{1,0:T(8,128)S(1)}, u32[]{:S(2)}, u32[]{:S(2)}) %collective-permute-start.16) | collective-permute-done | bytes 65568 | tf_op jit(solution)/shard_map/ppermute | solution.py:482
  51.9 0.7 %shard_map.112.started = f32[2,256,256]{2,1,0:T(8,128)} custom-call(f32[256,256]{1,0:T(8,128)S(1)} %shard_map.111.full), custom_call_target="tpu_custom_call" | custom-call | tf_op jit(solution)/shard_map/pallas_call | solution.py:572
  52.6 6.8 %collective-permute-done.7.e = f32[2,256,128]{2,1,0:T(8,128)S(1)} collective-permute-done((f32[2,256,128]{2,1,0:T(8,128)S(1)}, f32[2,256,128]{2,1,0:T(8,128)S(1)}, u32[]{:S(2)}, u32[]{:S(2)}) %collective-permute-start.7) | collective-permute-done | bytes 262176 | tf_op jit(solution)/shard_map/ppermute | solution.py:705
  59.4 1.2 %shard_map.107 = f32[4,256,256]{2,1,0:T(8,128)} custom-call(f32[4,256,256]{2,1,0:T(8,128)S(1)} %get-tuple-element.51.total, f32[2,256,128]{2,1,0:T(8,128)S(1)} %collective-permute-done.7.e, f32[2,256,128]{2,1,0:T(8,128)S(1)} %collective-permute-done.8.o), custom_call_target="tpu_custom_call" | custom-call | tf_op jit(solution)/shard_map/pallas_call | solution.py:459
  60.6 0.7 %shard_map.113 = f32[2,256,256]{2,1,0:T(8,128)} custom-call(f32[2,256,256]{2,1,0:T(8,128)} %shard_map.112.started, f32[256,256]{1,0:T(8,128)S(1)} %collective-permute-done.19.other), custom_call_target="tpu_custom_call", output_to_operand_aliasing={{}: (0, {})} | custom-call | tf_op jit(solution)/shard_map/pallas_call | solution.py:573
  (27 shorter events, 2.1 us)
Async XLA Ops:
  2.6 17.3 %collective-permute-start.2 = (f32[2,256,128]{2,1,0:T(8,128)S(1)}, f32[2,256,128]{2,1,0:T(8,128)S(1)}, u32[]{:S(2)}, u32[]{:S(2)}) collective-permute-start(f32[2,256,128]{2,1,0:T(8,128)S(1)} %get-tuple-element.34), channel_id=1, source_target_pairs={{1,2},{3,4},{5,6},{7,8},{9,10},{11,12},{13,14},{2,1},{4,3},{6,5},{... | collective-permute-start | bytes 786440 | tf_op jit(solution)/shard_map/ppermute | solution.py:600
  3.3 16.6 %collective-permute-start = (f32[384,128]{1,0:T(8,128)S(1)}, f32[384,128]{1,0:T(8,128)S(1)}, u32[]{:S(2)}, u32[]{:S(2)}) collective-permute-start(f32[384,128]{1,0:T(8,128)S(1)} %get-tuple-element.32), channel_id=1, source_target_pairs={{0,1},{2,3},{4,5},{6,7},{8,9},{10,11},{12,13},{14,15},{1,0},{3,2},... | collective-permute-start | bytes 589832 | tf_op jit(solution)/shard_map/ppermute | solution.py:599
  9.0 11.9 %collective-permute-start.3 = (f32[4,64,256]{2,1,0:T(8,128)S(1)}, f32[4,64,256]{2,1,0:T(8,128)S(1)}, u32[]{:S(2)}, u32[]{:S(2)}) collective-permute-start(f32[4,64,256]{2,1,0:T(8,128)S(1)} %get-tuple-element.36), channel_id=1, source_target_pairs={{0,16},{16,0},{1,17},{17,1},{2,18},{18,2},{3,19},{19,3},{4,20},{20... | collective-permute-start | bytes 786440 | tf_op jit(solution)/shard_map/ppermute | solution.py:603
  9.1 11.5 %collective-permute-start.1 = (f32[128,128]{1,0:T(8,128)S(1)}, f32[128,128]{1,0:T(8,128)S(1)}, u32[]{:S(2)}, u32[]{:S(2)}) collective-permute-start(f32[128,128]{1,0:T(8,128)S(1)} %get-tuple-element.33), channel_id=1, source_target_pairs={{0,1},{2,3},{4,5},{6,7},{8,9},{10,11},{12,13},{14,15},{1,0},{3,2},... | collective-permute-start | bytes 196616 | tf_op jit(solution)/shard_map/ppermute | solution.py:601
  19.9 1.3 %collective-permute-start.5 = (f32[2,64,128]{2,1,0:T(8,128)S(1)}, f32[2,64,128]{2,1,0:T(8,128)S(1)}, u32[]{:S(2)}, u32[]{:S(2)}) collective-permute-start(f32[2,64,128]{2,1,0:T(8,128)S(1)} %shard_map.102), channel_id=1, source_target_pairs={{0,16},{16,0},{1,17},{17,1},{2,18},{18,2},{3,19},{19,3},{4,20},{20... | collective-permute-start | bytes 196616 | tf_op jit(solution)/shard_map/ppermute | solution.py:616
  20.6 2.1 %collective-permute-start.4 = (f32[2,64,128]{2,1,0:T(8,128)S(1)}, f32[2,64,128]{2,1,0:T(8,128)S(1)}, u32[]{:S(2)}, u32[]{:S(2)}) collective-permute-start(f32[2,64,128]{2,1,0:T(8,128)S(1)} %shard_map.98), channel_id=1, source_target_pairs={{0,16},{16,0},{1,17},{17,1},{2,18},{18,2},{3,19},{19,3},{4,20},{20... | collective-permute-start | bytes 196616 | tf_op jit(solution)/shard_map/ppermute | solution.py:616
  26.3 1.6 %collective-permute-start.9 = (f32[256,256]{1,0:T(8,128)S(1)}, f32[256,256]{1,0:T(8,128)S(1)}, u32[]{:S(2)}, u32[]{:S(2)}) collective-permute-start(f32[256,256]{1,0:T(8,128)S(1)} %get-tuple-element.55), channel_id=1, source_target_pairs={{0,16},{16,0},{1,17},{17,1},{2,18},{18,2},{3,19},{19,3},{4,20},{20... | collective-permute-start | bytes 786440 | tf_op jit(solution)/shard_map/ppermute | solution.py:482
  26.9 20.7 %collective-permute-start.6 = (f32[4,64,384]{2,1,0:T(8,128)S(1)}, f32[4,64,384]{2,1,0:T(8,128)S(1)}, u32[]{:S(2)}, u32[]{:S(2)}) collective-permute-start(f32[4,64,384]{2,1,0:T(8,128)S(1)} %get-tuple-element.50), channel_id=1, source_target_pairs={{0,16},{16,0},{1,17},{17,1},{2,18},{18,2},{3,19},{19,3},{4,20},{20... | collective-permute-start | bytes 1179656 | tf_op jit(solution)/shard_map/ppermute | solution.py:696
  28.0 4.3 %collective-permute-start.10 = (f32[64,256]{1,0:T(8,128)S(1)}, f32[64,256]{1,0:T(8,128)S(1)}, u32[]{:S(2)}, u32[]{:S(2)}) collective-permute-start(f32[64,256]{1,0:T(8,128)S(1)} %get-tuple-element.57), channel_id=1, source_target_pairs={{0,1},{1,0},{2,3},{3,2},{4,5},{5,4},{6,7},{7,6},{8,9},{9,8},{10,11... | collective-permute-start | bytes 196616 | tf_op jit(solution)/shard_map/ppermute | solution.py:482
  29.8 5.5 %collective-permute-start.11 = (f32[64,256]{1,0:T(8,128)S(1)}, f32[64,256]{1,0:T(8,128)S(1)}, u32[]{:S(2)}, u32[]{:S(2)}) collective-permute-start(f32[64,256]{1,0:T(8,128)S(1)} %get-tuple-element.58), channel_id=1, source_target_pairs={{0,2},{1,3},{2,0},{3,1},{4,6},{5,7},{6,4},{7,5},{8,10},{9,11},{10,... | collective-permute-start | bytes 196616 | tf_op jit(solution)/shard_map/ppermute | solution.py:482
  30.0 5.3 %collective-permute-start.12 = (f32[64,256]{1,0:T(8,128)S(1)}, f32[64,256]{1,0:T(8,128)S(1)}, u32[]{:S(2)}, u32[]{:S(2)}) collective-permute-start(f32[64,256]{1,0:T(8,128)S(1)} %get-tuple-element.59), channel_id=1, source_target_pairs={{0,3},{1,2},{2,1},{3,0},{4,7},{5,6},{6,5},{7,4},{8,11},{9,10},{10,... | collective-permute-start | bytes 196616 | tf_op jit(solution)/shard_map/ppermute | solution.py:482
  35.4 6.1 %collective-permute-start.15 = (f32[64,256]{1,0:T(8,128)S(1)}, f32[64,256]{1,0:T(8,128)S(1)}, u32[]{:S(2)}, u32[]{:S(2)}) collective-permute-start(f32[64,256]{1,0:T(8,128)S(1)} %shard_map.109.refs_0_), channel_id=1, source_target_pairs={{0,12},{1,13},{2,14},{3,15},{4,8},{5,9},{6,10},{7,11},{8,4},{9,5},... | collective-permute-start | bytes 196616 | tf_op jit(solution)/shard_map/ppermute | solution.py:482
  38.9 5.2 %collective-permute-start.14 = (f32[64,256]{1,0:T(8,128)S(1)}, f32[64,256]{1,0:T(8,128)S(1)}, u32[]{:S(2)}, u32[]{:S(2)}) collective-permute-start(f32[64,256]{1,0:T(8,128)S(1)} %shard_map.109.refs_0_), channel_id=1, source_target_pairs={{0,8},{1,9},{2,10},{3,11},{4,12},{5,13},{6,14},{7,15},{8,0},{9,1},... | collective-permute-start | bytes 196616 | tf_op jit(solution)/shard_map/ppermute | solution.py:482
  38.9 5.2 %collective-permute-start.13 = (f32[64,256]{1,0:T(8,128)S(1)}, f32[64,256]{1,0:T(8,128)S(1)}, u32[]{:S(2)}, u32[]{:S(2)}) collective-permute-start(f32[64,256]{1,0:T(8,128)S(1)} %shard_map.109.refs_0_), channel_id=1, source_target_pairs={{0,4},{1,5},{2,6},{3,7},{4,0},{5,1},{6,2},{7,3},{8,12},{9,13},{10,... | collective-permute-start | bytes 196616 | tf_op jit(solution)/shard_map/ppermute | solution.py:482
  44.1 5.9 %collective-permute-start.18 = (f32[64,256]{1,0:T(8,128)S(1)}, f32[64,256]{1,0:T(8,128)S(1)}, u32[]{:S(2)}, u32[]{:S(2)}) collective-permute-start(f32[64,256]{1,0:T(8,128)S(1)} %shard_map.110.refs_0_), channel_id=1, source_target_pairs={{0,3},{1,2},{2,1},{3,0},{4,7},{5,6},{6,5},{7,4},{8,11},{9,10},{10,... | collective-permute-start | bytes 196616 | tf_op jit(solution)/shard_map/ppermute | solution.py:482
  45.7 4.7 %collective-permute-start.17 = (f32[64,256]{1,0:T(8,128)S(1)}, f32[64,256]{1,0:T(8,128)S(1)}, u32[]{:S(2)}, u32[]{:S(2)}) collective-permute-start(f32[64,256]{1,0:T(8,128)S(1)} %shard_map.110.refs_0_), channel_id=1, source_target_pairs={{0,2},{1,3},{2,0},{3,1},{4,6},{5,7},{6,4},{7,5},{8,10},{9,11},{10,... | collective-permute-start | bytes 196616 | tf_op jit(solution)/shard_map/ppermute | solution.py:482
  46.8 5.0 %collective-permute-start.16 = (f32[64,256]{1,0:T(8,128)S(1)}, f32[64,256]{1,0:T(8,128)S(1)}, u32[]{:S(2)}, u32[]{:S(2)}) collective-permute-start(f32[64,256]{1,0:T(8,128)S(1)} %shard_map.110.refs_0_), channel_id=1, source_target_pairs={{0,1},{1,0},{2,3},{3,2},{4,5},{5,4},{6,7},{7,6},{8,9},{9,8},{10,11... | collective-permute-start | bytes 196616 | tf_op jit(solution)/shard_map/ppermute | solution.py:482
  47.8 11.6 %collective-permute-start.7 = (f32[2,256,128]{2,1,0:T(8,128)S(1)}, f32[2,256,128]{2,1,0:T(8,128)S(1)}, u32[]{:S(2)}, u32[]{:S(2)}) collective-permute-start(f32[2,256,128]{2,1,0:T(8,128)S(1)} %get-tuple-element.52), channel_id=1, source_target_pairs={{0,1},{2,3},{4,5},{6,7},{8,9},{10,11},{12,13},{14,15},{1,0},{3,2},... | collective-permute-start | bytes 786440 | tf_op jit(solution)/shard_map/ppermute | solution.py:705
  49.1 10.3 %collective-permute-start.8 = (f32[2,256,128]{2,1,0:T(8,128)S(1)}, f32[2,256,128]{2,1,0:T(8,128)S(1)}, u32[]{:S(2)}, u32[]{:S(2)}) collective-permute-start(f32[2,256,128]{2,1,0:T(8,128)S(1)} %get-tuple-element.53), channel_id=1, source_target_pairs={{1,2},{3,4},{5,6},{7,8},{9,10},{11,12},{13,14},{2,1},{4,3},{6,5},{... | collective-permute-start | bytes 786440 | tf_op jit(solution)/shard_map/ppermute | solution.py:706
  51.8 8.8 %collective-permute-start.19 = (f32[256,256]{1,0:T(8,128)S(1)}, f32[256,256]{1,0:T(8,128)S(1)}, u32[]{:S(2)}, u32[]{:S(2)}) collective-permute-start(f32[256,256]{1,0:T(8,128)S(1)} %shard_map.111.full), channel_id=1, source_target_pairs={{0,16},{16,0},{1,17},{17,1},{2,18},{18,2},{3,19},{19,3},{4,20},{20... | collective-permute-start | bytes 786440 | tf_op jit(solution)/shard_map/ppermute | solution.py:482

commit v11 on v10

--- a/solution.py
+++ b/solution.py
@@ -167,12 +167,10 @@
     return pl.multiple_of(jnp.where(last, n - margin, 0), 8)
 
 
-def pack_kernel(margin, obj_hbm, offs_hbm, obj, offs, limits, *refs):
+def pack_kernel(margin, obj_hbm, obj, *refs):
     evens, odds, rows, sems = refs[:2], refs[2], refs[3:-1], refs[-1]
     n = obj.shape[1]
-    copies = copy_all(
-        (obj_hbm.at[0:2], obj_hbm.at[2:4], offs_hbm), (obj.at[0:2], obj.at[2:4], offs), sems
-    )
+    copies = copy_all((obj_hbm.at[0:2], obj_hbm.at[2:4]), (obj.at[0:2], obj.at[2:4]), sems)
     even = lax.axis_index("col") % 2 == 0
     for s in range(2):
         copies[s].wait()
@@ -185,9 +183,6 @@
         odds[s] = jnp.where(even, low, high)
     for which, out in enumerate(rows):
         out[...] = obj[:, pl.ds(row_start(which, n, margin), margin), :]
-    copies[2].wait()
-    for i in range(2):
-        limits[i] = jnp.full(limits.shape[1:], offs[0, i] - margin, jnp.int32)
 
 
 def corner_kernel(s, margin, *refs):
@@ -220,16 +215,16 @@
     return dot(a, order[0]) + (dot(b, order[0]) + dot(c, order[0]))
 
 
-def prep_kernel(*refs):
-    hbm, (kr, ki, mats), loaded = refs[:6], refs[6:9], refs[9:13]
-    phase, table, sems = refs[13:]
+def prep_kernel(margin, *refs):
+    hbm, (offs, limits, kr, ki, mats), loaded = refs[:7], refs[7:12], refs[12:16]
+    phase, table, sems = refs[16:]
     n = phase.shape[0]
     h = n // 2
     first = pltpu.make_async_copy(hbm[0], phase, sems.at[0])
     first.start()
     order = [even_odd(n, axis) for axis in range(2)]
     first.wait()
-    copies = copy_all(hbm[1:], (table,) + loaded, sems)
+    copies = copy_all(hbm[1:], (table,) + loaded + (offs,), sems)
     angle = reorder(phase[...], order)
     kr[...], ki[...] = cos_sin(angle)
     copies[0].wait()
@@ -241,6 +236,8 @@
         mats[2 + i, h:, h:] = table[i, h:, h:]
     for copy in copies[1:]:
         copy.wait()
+    for i in range(2):
+        limits[i] = jnp.full(limits.shape[1:], offs[0, i] - margin, jnp.int32)
 
 
 def reorder_kernel(x, after, out):
@@ -584,16 +581,14 @@
 
     row_rounds, col_rounds = edges("row"), edges("col")
     n_row = len(row_rounds)
-    obj, offs, limits, even0, even1, odds, *rows = call(
+    obj, even0, even1, odds, *rows = call(
         functools.partial(pack_kernel, margin),
-        [(4, n, n), jax.ShapeDtypeStruct((1, 2), jnp.int32)]
-        + [jax.ShapeDtypeStruct((2, 8, h), jnp.int32)]
+        [(4, n, n)]
         + [(n + n // 2, h), (n // 2, h), (2, n, h)]
         + [(4, margin, n)] * n_row,
-        [HBM, HBM],
+        [HBM],
         in_hbm(object_field.reshape(4, tile, tile)),
-        in_hbm(offsets.reshape(1, 2)),
-        scratch=[pltpu.SemaphoreType.DMA((3,))],
+        scratch=[pltpu.SemaphoreType.DMA((2,))],
     )
     halos, corners = [], [[], []]
     even0 = lax.ppermute(even0, "col", col_rounds[0])
@@ -628,11 +623,13 @@
         return main
 
     loads = (phase, mats, tw_left, tw_right, probe, amplitudes.reshape(n, n))
-    kr, ki, mats, tw_left, tw_right, pr, am = call(
-        prep_kernel,
-        [(n, n)] * 2
+    loads += (offsets.reshape(1, 2),)
+    offs, limits, kr, ki, mats, tw_left, tw_right, pr, am = call(
+        functools.partial(prep_kernel, margin),
+        [jax.ShapeDtypeStruct((1, 2), jnp.int32), jax.ShapeDtypeStruct((2, 8, h), jnp.int32)]
+        + [(n, n)] * 2
         + [jax.ShapeDtypeStruct((4, n, n), BF16)]
-        + [jax.ShapeDtypeStruct(x.shape, x.dtype) for x in loads[2:]],
+        + [jax.ShapeDtypeStruct(x.shape, x.dtype) for x in loads[2:-1]],
         [HBM] * len(loads),
         *[in_hbm(x) for x in loads],
         scratch=[

time: 61.7 us -> 61.1 us (level)
  waiting for transfers between devices: 25.2 us -> 24.5 us
  transfers between devices with their start and end apart: 20 -> 20, of which waited for: 12 -> 12; matrix products, arithmetic and copies ran while one was open for 0% -> 0% of each run, Pallas kernels for 13% -> 14%
where the time goes in v11:
time: 61.1 us; the launch traced here: 60.7 us
  waiting for transfers between devices  24.5 us (40%)
  starting transfers between devices  21 us (34%)
  Pallas kernels  14.3 us (23%)
  between operations  0.79 us (1%)
    pallas_call x17, Pallas kernels, call(): pl.pallas_call(kernel, out_shape=shapes, in_specs=in_specs, out_specs=[SM...  12.9 us
    ppermute x11, starting transfers between devices, swap(): return lax.ppermute(value, axis, [(i, i ^ distance) for i in range(count)])  11.9 us
    ppermute x11, waiting for transfers between devices, swap(): return lax.ppermute(value, axis, [(i, i ^ distance) for i in range(count)])  10.7 us
    ppermute x1, waiting for transfers between devices, whole(): send_e = lax.ppermute(send_e, 'col', col_rounds[0])  6.74 us
    ppermute x1, waiting for transfers between devices, whole(): even0 = lax.ppermute(even0, 'col', col_rounds[0])  6.38 us
    ppermute x1, starting transfers between devices, whole(): even0 = lax.ppermute(even0, 'col', col_rounds[0])  5.75 us
    ppermute x1, starting transfers between devices, whole(): send_e = lax.ppermute(send_e, 'col', col_rounds[0])  1.28 us
  transfers between devices with their start and end apart: 20, of which 12 were waited for; matrix products, arithmetic and copies ran while one was open for 0% of the time, Pallas kernels for 14%

profile of v11, /device:TPU:0, one launch (start us, length us, event | category | flops | bytes accessed | tf_op | source)
XLA Modules:
  0.0 60.7 jit_solution(6211575007755565357)
XLA Ops:
  0.6 1.4 %shard_map.95 = (f32[4,256,256]{2,1,0:T(8,128)S(1)}, f32[384,128]{1,0:T(8,128)S(1)}, f32[128,128]{1,0:T(8,128)S(1)}, f32[2,256,128]{2,1,0:T(8,128)S(1)}, f32[4,64,256]{2,1,0:T(8,128)S(1)}) custom-call(f32[4,256,256]{2,1,0:T(8,128)} %bitcast.4), custom_call_target="tpu_custom_call" | custom-call | tf_op jit(solution)/shard_map/pallas_call | solution.py:456
  2.0 0.7 %collective-permute-start.2 = (f32[2,256,128]{2,1,0:T(8,128)S(1)}, f32[2,256,128]{2,1,0:T(8,128)S(1)}, u32[]{:S(2)}, u32[]{:S(2)}) collective-permute-start(f32[2,256,128]{2,1,0:T(8,128)S(1)} %get-tuple-element.34), channel_id=1, source_target_pairs={{1,2},{3,4},{5,6},{7,8},{9,10},{11,12},{13,14},{2,1},{4,3},{6,5},{... | collective-permute-start | bytes 786440 | tf_op jit(solution)/shard_map/ppermute | solution.py:595
  2.7 5.8 %collective-permute-start = (f32[384,128]{1,0:T(8,128)S(1)}, f32[384,128]{1,0:T(8,128)S(1)}, u32[]{:S(2)}, u32[]{:S(2)}) collective-permute-start(f32[384,128]{1,0:T(8,128)S(1)} %get-tuple-element.32), channel_id=1, source_target_pairs={{0,1},{2,3},{4,5},{6,7},{8,9},{10,11},{12,13},{14,15},{1,0},{3,2},... | collective-permute-start | bytes 589832 | tf_op jit(solution)/shard_map/ppermute | solution.py:594
  8.6 2.9 %shard_map.96 = (s32[1,2]{1,0:T(1,128)S(1)}, s32[2,8,128]{2,1,0:T(8,128)S(1)}, f32[256,256]{1,0:T(8,128)S(1)}, f32[256,256]{1,0:T(8,128)S(1)}, bf16[4,256,256]{2...) custom-call(f32[256,256]{1,0:T(8,128)} %refs_0_.1, ...), custom_call_target="tpu_custom_call" | custom-call | tf_op jit(solution)/shard_map/pallas_call | solution.py:456
  11.5 0.8 %shard_map.100.after.refs_4_.refs_5_ = f32[2,256,256]{2,1,0:T(8,128)S(1)} custom-call(s32[1,2]{1,0:T(1,128)S(1)} %get-tuple-element.37.offs, f32[2,256,256]{2,1,0:T(8,128)S(1)} %get-tuple-element.38.probe), custom_call_target="tpu_custom_call" | custom-call | tf_op jit(solution)/shard_map/pallas_call | solution.py:456
  12.3 0.6 %shard_map.101.refs_2_.refs_8_ = f32[256,256]{1,0:T(8,128)S(1)} custom-call(f32[256,256]{1,0:T(8,128)S(1)} %get-tuple-element.41.x, f32[2,256,256]{2,1,0:T(8,128)S(1)} %shard_map.100.after.refs_4_.refs_5_), custom_call_target="tpu_custom_call" | custom-call | tf_op jit(solution)/shard_map/pallas_call | solution.py:456
  12.9 6.4 %collective-permute-done.refs_0_ = f32[384,128]{1,0:T(8,128)S(1)} collective-permute-done((f32[384,128]{1,0:T(8,128)S(1)}, f32[384,128]{1,0:T(8,128)S(1)}, u32[]{:S(2)}, u32[]{:S(2)}) %collective-permute-start) | collective-permute-done | bytes 196640 | tf_op jit(solution)/shard_map/ppermute | solution.py:594
  19.5 0.4 collective-permute-done.1.refs_1_
  20.6 1.5 %shard_map.103 = (f32[2,256,256]{2,1,0:T(8,128)S(1)}, f32[2,256,256]{2,1,0:T(8,128)S(1)}) custom-call(f32[2,256,256]{2,1,0:T(8,128)S(1)} %shard_map.98.refs_3_.refs_0_, f32[4,64,256]{2,1,0:T(8,128)S(1)} %collective-permute-done.3.refs_1_, f32[2,64,128]{2,1,0:T(8,128)S(1)} %collective-permute-done.5.refs_2_, ...), custom_call_target="tpu_custom_call" | custom-call | tf_op jit(solution)/shard_map/pallas_call | solution.py:456
  22.1 3.6 %shard_map.104 = (f32[256,256]{1,0:T(8,128)S(1)}, f32[256,256]{1,0:T(8,128)S(1)}, f32[4,256,256]{2,1,0:T(8,128)S(1)}) custom-call(f32[2,256,256]{2,1,0:T(8,128)S(1)} %shard_map.97.refs_0_, f32[4,64,256]{2,1,0:T(8,128)S(1)} %collective-permute-done.3.refs_1_, f32[2,64,128]{2,1,0:T(8,128)S(1)} %collective-permute-done.4.refs_2_, ...), custom_call_target="tpu_custom_call" | custom-call | tf_op jit(solution)/shard_map/pallas_call | solution.py:456
  25.9 0.4 shard_map.105
  26.3 0.4 collective-permute-start.6
  26.7 0.6 collective-permute-done.9.other
  27.4 1.8 %collective-permute-start.10 = (f32[64,256]{1,0:T(8,128)S(1)}, f32[64,256]{1,0:T(8,128)S(1)}, u32[]{:S(2)}, u32[]{:S(2)}) collective-permute-start(f32[64,256]{1,0:T(8,128)S(1)} %get-tuple-element.57), channel_id=1, source_target_pairs={{0,1},{1,0},{2,3},{3,2},{4,5},{5,4},{6,7},{7,6},{8,9},{9,8},{10,11... | collective-permute-start | bytes 196616 | tf_op jit(solution)/shard_map/ppermute | solution.py:479
  29.4 1.5 %collective-permute-start.12 = (f32[64,256]{1,0:T(8,128)S(1)}, f32[64,256]{1,0:T(8,128)S(1)}, u32[]{:S(2)}, u32[]{:S(2)}) collective-permute-start(f32[64,256]{1,0:T(8,128)S(1)} %get-tuple-element.59), channel_id=1, source_target_pairs={{0,3},{1,2},{2,1},{3,0},{4,7},{5,6},{6,5},{7,4},{8,11},{9,10},{10,... | collective-permute-start | bytes 196616 | tf_op jit(solution)/shard_map/ppermute | solution.py:479
  30.9 0.8 %collective-permute-done.10.refs_1_ = f32[64,256]{1,0:T(8,128)S(1)} collective-permute-done((f32[64,256]{1,0:T(8,128)S(1)}, f32[64,256]{1,0:T(8,128)S(1)}, u32[]{:S(2)}, u32[]{:S(2)}) %collective-permute-start.10) | collective-permute-done | bytes 65568 | tf_op jit(solution)/shard_map/ppermute | solution.py:479
  31.7 3.0 %collective-permute-done.11.refs_2_ = f32[64,256]{1,0:T(8,128)S(1)} collective-permute-done((f32[64,256]{1,0:T(8,128)S(1)}, f32[64,256]{1,0:T(8,128)S(1)}, u32[]{:S(2)}, u32[]{:S(2)}) %collective-permute-start.11) | collective-permute-done | bytes 65568 | tf_op jit(solution)/shard_map/ppermute | solution.py:479
  34.7 3.5 %collective-permute-start.15 = (f32[64,256]{1,0:T(8,128)S(1)}, f32[64,256]{1,0:T(8,128)S(1)}, u32[]{:S(2)}, u32[]{:S(2)}) collective-permute-start(f32[64,256]{1,0:T(8,128)S(1)} %shard_map.109.refs_0_), channel_id=1, source_target_pairs={{0,12},{1,13},{2,14},{3,15},{4,8},{5,9},{6,10},{7,11},{8,4},{9,5},... | collective-permute-start | bytes 196616 | tf_op jit(solution)/shard_map/ppermute | solution.py:479
  38.3 0.9 %collective-permute-start.13 = (f32[64,256]{1,0:T(8,128)S(1)}, f32[64,256]{1,0:T(8,128)S(1)}, u32[]{:S(2)}, u32[]{:S(2)}) collective-permute-start(f32[64,256]{1,0:T(8,128)S(1)} %shard_map.109.refs_0_), channel_id=1, source_target_pairs={{0,4},{1,5},{2,6},{3,7},{4,0},{5,1},{6,2},{7,3},{8,12},{9,13},{10,... | collective-permute-start | bytes 196616 | tf_op jit(solution)/shard_map/ppermute | solution.py:479
  39.2 1.7 %collective-permute-done.15.refs_3_ = f32[64,256]{1,0:T(8,128)S(1)} collective-permute-done((f32[64,256]{1,0:T(8,128)S(1)}, f32[64,256]{1,0:T(8,128)S(1)}, u32[]{:S(2)}, u32[]{:S(2)}) %collective-permute-start.15) | collective-permute-done | bytes 65568 | tf_op jit(solution)/shard_map/ppermute | solution.py:479
  40.9 2.5 %collective-permute-done.14.refs_2_ = f32[64,256]{1,0:T(8,128)S(1)} collective-permute-done((f32[64,256]{1,0:T(8,128)S(1)}, f32[64,256]{1,0:T(8,128)S(1)}, u32[]{:S(2)}, u32[]{:S(2)}) %collective-permute-start.14) | collective-permute-done | bytes 65568 | tf_op jit(solution)/shard_map/ppermute | solution.py:479
  43.5 1.6 %collective-permute-start.18 = (f32[64,256]{1,0:T(8,128)S(1)}, f32[64,256]{1,0:T(8,128)S(1)}, u32[]{:S(2)}, u32[]{:S(2)}) collective-permute-start(f32[64,256]{1,0:T(8,128)S(1)} %shard_map.110.refs_0_), channel_id=1, source_target_pairs={{0,3},{1,2},{2,1},{3,0},{4,7},{5,6},{6,5},{7,4},{8,11},{9,10},{10,... | collective-permute-start | bytes 196616 | tf_op jit(solution)/shard_map/ppermute | solution.py:479
  45.0 1.2 %collective-permute-start.17 = (f32[64,256]{1,0:T(8,128)S(1)}, f32[64,256]{1,0:T(8,128)S(1)}, u32[]{:S(2)}, u32[]{:S(2)}) collective-permute-start(f32[64,256]{1,0:T(8,128)S(1)} %shard_map.110.refs_0_), channel_id=1, source_target_pairs={{0,2},{1,3},{2,0},{3,1},{4,6},{5,7},{6,4},{7,5},{8,10},{9,11},{10,... | collective-permute-start | bytes 196616 | tf_op jit(solution)/shard_map/ppermute | solution.py:479
  46.2 0.8 %collective-permute-start.16 = (f32[64,256]{1,0:T(8,128)S(1)}, f32[64,256]{1,0:T(8,128)S(1)}, u32[]{:S(2)}, u32[]{:S(2)}) collective-permute-start(f32[64,256]{1,0:T(8,128)S(1)} %shard_map.110.refs_0_), channel_id=1, source_target_pairs={{0,1},{1,0},{2,3},{3,2},{4,5},{5,4},{6,7},{7,6},{8,9},{9,8},{10,11... | collective-permute-start | bytes 196616 | tf_op jit(solution)/shard_map/ppermute | solution.py:479
  47.2 1.3 %collective-permute-start.7 = (f32[2,256,128]{2,1,0:T(8,128)S(1)}, f32[2,256,128]{2,1,0:T(8,128)S(1)}, u32[]{:S(2)}, u32[]{:S(2)}) collective-permute-start(f32[2,256,128]{2,1,0:T(8,128)S(1)} %get-tuple-element.52), channel_id=1, source_target_pairs={{0,1},{2,3},{4,5},{6,7},{8,9},{10,11},{12,13},{14,15},{1,0},{3,2},... | collective-permute-start | bytes 786440 | tf_op jit(solution)/shard_map/ppermute | solution.py:702
  48.5 0.7 %collective-permute-start.8 = (f32[2,256,128]{2,1,0:T(8,128)S(1)}, f32[2,256,128]{2,1,0:T(8,128)S(1)}, u32[]{:S(2)}, u32[]{:S(2)}) collective-permute-start(f32[2,256,128]{2,1,0:T(8,128)S(1)} %get-tuple-element.53), channel_id=1, source_target_pairs={{1,2},{3,4},{5,6},{7,8},{9,10},{11,12},{13,14},{2,1},{4,3},{6,5},{... | collective-permute-start | bytes 786440 | tf_op jit(solution)/shard_map/ppermute | solution.py:703
  49.4 0.3 collective-permute-done.17.refs_2_
  49.7 1.5 %collective-permute-done.16.refs_1_ = f32[64,256]{1,0:T(8,128)S(1)} collective-permute-done((f32[64,256]{1,0:T(8,128)S(1)}, f32[64,256]{1,0:T(8,128)S(1)}, u32[]{:S(2)}, u32[]{:S(2)}) %collective-permute-start.16) | collective-permute-done | bytes 65568 | tf_op jit(solution)/shard_map/ppermute | solution.py:479
  51.3 0.7 %shard_map.112.started = f32[2,256,256]{2,1,0:T(8,128)} custom-call(f32[256,256]{1,0:T(8,128)S(1)} %shard_map.111.full), custom_call_target="tpu_custom_call" | custom-call | tf_op jit(solution)/shard_map/pallas_call | solution.py:569
  52.0 6.7 %collective-permute-done.7.e = f32[2,256,128]{2,1,0:T(8,128)S(1)} collective-permute-done((f32[2,256,128]{2,1,0:T(8,128)S(1)}, f32[2,256,128]{2,1,0:T(8,128)S(1)}, u32[]{:S(2)}, u32[]{:S(2)}) %collective-permute-start.7) | collective-permute-done | bytes 262176 | tf_op jit(solution)/shard_map/ppermute | solution.py:702
  58.8 1.2 %shard_map.107 = f32[4,256,256]{2,1,0:T(8,128)} custom-call(f32[4,256,256]{2,1,0:T(8,128)S(1)} %get-tuple-element.51.total, f32[2,256,128]{2,1,0:T(8,128)S(1)} %collective-permute-done.7.e, f32[2,256,128]{2,1,0:T(8,128)S(1)} %collective-permute-done.8.o), custom_call_target="tpu_custom_call" | custom-call | tf_op jit(solution)/shard_map/pallas_call | solution.py:456
  60.0 0.7 %shard_map.113 = f32[2,256,256]{2,1,0:T(8,128)} custom-call(f32[2,256,256]{2,1,0:T(8,128)} %shard_map.112.started, f32[256,256]{1,0:T(8,128)S(1)} %collective-permute-done.19.other), custom_call_target="tpu_custom_call", output_to_operand_aliasing={{}: (0, {})} | custom-call | tf_op jit(solution)/shard_map/pallas_call | solution.py:570
  (27 shorter events, 2.0 us)
Async XLA Ops:
  2.0 17.3 %collective-permute-start.2 = (f32[2,256,128]{2,1,0:T(8,128)S(1)}, f32[2,256,128]{2,1,0:T(8,128)S(1)}, u32[]{:S(2)}, u32[]{:S(2)}) collective-permute-start(f32[2,256,128]{2,1,0:T(8,128)S(1)} %get-tuple-element.34), channel_id=1, source_target_pairs={{1,2},{3,4},{5,6},{7,8},{9,10},{11,12},{13,14},{2,1},{4,3},{6,5},{... | collective-permute-start | bytes 786440 | tf_op jit(solution)/shard_map/ppermute | solution.py:595
  2.7 16.6 %collective-permute-start = (f32[384,128]{1,0:T(8,128)S(1)}, f32[384,128]{1,0:T(8,128)S(1)}, u32[]{:S(2)}, u32[]{:S(2)}) collective-permute-start(f32[384,128]{1,0:T(8,128)S(1)} %get-tuple-element.32), channel_id=1, source_target_pairs={{0,1},{2,3},{4,5},{6,7},{8,9},{10,11},{12,13},{14,15},{1,0},{3,2},... | collective-permute-start | bytes 589832 | tf_op jit(solution)/shard_map/ppermute | solution.py:594
  8.4 11.9 %collective-permute-start.3 = (f32[4,64,256]{2,1,0:T(8,128)S(1)}, f32[4,64,256]{2,1,0:T(8,128)S(1)}, u32[]{:S(2)}, u32[]{:S(2)}) collective-permute-start(f32[4,64,256]{2,1,0:T(8,128)S(1)} %get-tuple-element.36), channel_id=1, source_target_pairs={{0,16},{16,0},{1,17},{17,1},{2,18},{18,2},{3,19},{19,3},{4,20},{20... | collective-permute-start | bytes 786440 | tf_op jit(solution)/shard_map/ppermute | solution.py:598
  8.4 11.5 %collective-permute-start.1 = (f32[128,128]{1,0:T(8,128)S(1)}, f32[128,128]{1,0:T(8,128)S(1)}, u32[]{:S(2)}, u32[]{:S(2)}) collective-permute-start(f32[128,128]{1,0:T(8,128)S(1)} %get-tuple-element.33), channel_id=1, source_target_pairs={{0,1},{2,3},{4,5},{6,7},{8,9},{10,11},{12,13},{14,15},{1,0},{3,2},... | collective-permute-start | bytes 196616 | tf_op jit(solution)/shard_map/ppermute | solution.py:596
  19.3 1.3 %collective-permute-start.5 = (f32[2,64,128]{2,1,0:T(8,128)S(1)}, f32[2,64,128]{2,1,0:T(8,128)S(1)}, u32[]{:S(2)}, u32[]{:S(2)}) collective-permute-start(f32[2,64,128]{2,1,0:T(8,128)S(1)} %shard_map.102), channel_id=1, source_target_pairs={{0,16},{16,0},{1,17},{17,1},{2,18},{18,2},{3,19},{19,3},{4,20},{20... | collective-permute-start | bytes 196616 | tf_op jit(solution)/shard_map/ppermute | solution.py:611
  20.0 2.1 %collective-permute-start.4 = (f32[2,64,128]{2,1,0:T(8,128)S(1)}, f32[2,64,128]{2,1,0:T(8,128)S(1)}, u32[]{:S(2)}, u32[]{:S(2)}) collective-permute-start(f32[2,64,128]{2,1,0:T(8,128)S(1)} %shard_map.99), channel_id=1, source_target_pairs={{0,16},{16,0},{1,17},{17,1},{2,18},{18,2},{3,19},{19,3},{4,20},{20... | collective-permute-start | bytes 196616 | tf_op jit(solution)/shard_map/ppermute | solution.py:611
  25.7 1.6 %collective-permute-start.9 = (f32[256,256]{1,0:T(8,128)S(1)}, f32[256,256]{1,0:T(8,128)S(1)}, u32[]{:S(2)}, u32[]{:S(2)}) collective-permute-start(f32[256,256]{1,0:T(8,128)S(1)} %get-tuple-element.55), channel_id=1, source_target_pairs={{0,16},{16,0},{1,17},{17,1},{2,18},{18,2},{3,19},{19,3},{4,20},{20... | collective-permute-start | bytes 786440 | tf_op jit(solution)/shard_map/ppermute | solution.py:479
  26.3 20.7 %collective-permute-start.6 = (f32[4,64,384]{2,1,0:T(8,128)S(1)}, f32[4,64,384]{2,1,0:T(8,128)S(1)}, u32[]{:S(2)}, u32[]{:S(2)}) collective-permute-start(f32[4,64,384]{2,1,0:T(8,128)S(1)} %get-tuple-element.50), channel_id=1, source_target_pairs={{0,16},{16,0},{1,17},{17,1},{2,18},{18,2},{3,19},{19,3},{4,20},{20... | collective-permute-start | bytes 1179656 | tf_op jit(solution)/shard_map/ppermute | solution.py:693
  27.4 4.3 %collective-permute-start.10 = (f32[64,256]{1,0:T(8,128)S(1)}, f32[64,256]{1,0:T(8,128)S(1)}, u32[]{:S(2)}, u32[]{:S(2)}) collective-permute-start(f32[64,256]{1,0:T(8,128)S(1)} %get-tuple-element.57), channel_id=1, source_target_pairs={{0,1},{1,0},{2,3},{3,2},{4,5},{5,4},{6,7},{7,6},{8,9},{9,8},{10,11... | collective-permute-start | bytes 196616 | tf_op jit(solution)/shard_map/ppermute | solution.py:479
  29.2 5.5 %collective-permute-start.11 = (f32[64,256]{1,0:T(8,128)S(1)}, f32[64,256]{1,0:T(8,128)S(1)}, u32[]{:S(2)}, u32[]{:S(2)}) collective-permute-start(f32[64,256]{1,0:T(8,128)S(1)} %get-tuple-element.58), channel_id=1, source_target_pairs={{0,2},{1,3},{2,0},{3,1},{4,6},{5,7},{6,4},{7,5},{8,10},{9,11},{10,... | collective-permute-start | bytes 196616 | tf_op jit(solution)/shard_map/ppermute | solution.py:479
  29.4 5.3 %collective-permute-start.12 = (f32[64,256]{1,0:T(8,128)S(1)}, f32[64,256]{1,0:T(8,128)S(1)}, u32[]{:S(2)}, u32[]{:S(2)}) collective-permute-start(f32[64,256]{1,0:T(8,128)S(1)} %get-tuple-element.59), channel_id=1, source_target_pairs={{0,3},{1,2},{2,1},{3,0},{4,7},{5,6},{6,5},{7,4},{8,11},{9,10},{10,... | collective-permute-start | bytes 196616 | tf_op jit(solution)/shard_map/ppermute | solution.py:479
  34.7 6.1 %collective-permute-start.15 = (f32[64,256]{1,0:T(8,128)S(1)}, f32[64,256]{1,0:T(8,128)S(1)}, u32[]{:S(2)}, u32[]{:S(2)}) collective-permute-start(f32[64,256]{1,0:T(8,128)S(1)} %shard_map.109.refs_0_), channel_id=1, source_target_pairs={{0,12},{1,13},{2,14},{3,15},{4,8},{5,9},{6,10},{7,11},{8,4},{9,5},... | collective-permute-start | bytes 196616 | tf_op jit(solution)/shard_map/ppermute | solution.py:479
  38.3 5.2 %collective-permute-start.14 = (f32[64,256]{1,0:T(8,128)S(1)}, f32[64,256]{1,0:T(8,128)S(1)}, u32[]{:S(2)}, u32[]{:S(2)}) collective-permute-start(f32[64,256]{1,0:T(8,128)S(1)} %shard_map.109.refs_0_), channel_id=1, source_target_pairs={{0,8},{1,9},{2,10},{3,11},{4,12},{5,13},{6,14},{7,15},{8,0},{9,1},... | collective-permute-start | bytes 196616 | tf_op jit(solution)/shard_map/ppermute | solution.py:479
  38.3 5.2 %collective-permute-start.13 = (f32[64,256]{1,0:T(8,128)S(1)}, f32[64,256]{1,0:T(8,128)S(1)}, u32[]{:S(2)}, u32[]{:S(2)}) collective-permute-start(f32[64,256]{1,0:T(8,128)S(1)} %shard_map.109.refs_0_), channel_id=1, source_target_pairs={{0,4},{1,5},{2,6},{3,7},{4,0},{5,1},{6,2},{7,3},{8,12},{9,13},{10,... | collective-permute-start | bytes 196616 | tf_op jit(solution)/shard_map/ppermute | solution.py:479
  43.5 5.9 %collective-permute-start.18 = (f32[64,256]{1,0:T(8,128)S(1)}, f32[64,256]{1,0:T(8,128)S(1)}, u32[]{:S(2)}, u32[]{:S(2)}) collective-permute-start(f32[64,256]{1,0:T(8,128)S(1)} %shard_map.110.refs_0_), channel_id=1, source_target_pairs={{0,3},{1,2},{2,1},{3,0},{4,7},{5,6},{6,5},{7,4},{8,11},{9,10},{10,... | collective-permute-start | bytes 196616 | tf_op jit(solution)/shard_map/ppermute | solution.py:479
  45.0 4.7 %collective-permute-start.17 = (f32[64,256]{1,0:T(8,128)S(1)}, f32[64,256]{1,0:T(8,128)S(1)}, u32[]{:S(2)}, u32[]{:S(2)}) collective-permute-start(f32[64,256]{1,0:T(8,128)S(1)} %shard_map.110.refs_0_), channel_id=1, source_target_pairs={{0,2},{1,3},{2,0},{3,1},{4,6},{5,7},{6,4},{7,5},{8,10},{9,11},{10,... | collective-permute-start | bytes 196616 | tf_op jit(solution)/shard_map/ppermute | solution.py:479
  46.2 5.0 %collective-permute-start.16 = (f32[64,256]{1,0:T(8,128)S(1)}, f32[64,256]{1,0:T(8,128)S(1)}, u32[]{:S(2)}, u32[]{:S(2)}) collective-permute-start(f32[64,256]{1,0:T(8,128)S(1)} %shard_map.110.refs_0_), channel_id=1, source_target_pairs={{0,1},{1,0},{2,3},{3,2},{4,5},{5,4},{6,7},{7,6},{8,9},{9,8},{10,11... | collective-permute-start | bytes 196616 | tf_op jit(solution)/shard_map/ppermute | solution.py:479
  47.2 11.6 %collective-permute-start.7 = (f32[2,256,128]{2,1,0:T(8,128)S(1)}, f32[2,256,128]{2,1,0:T(8,128)S(1)}, u32[]{:S(2)}, u32[]{:S(2)}) collective-permute-start(f32[2,256,128]{2,1,0:T(8,128)S(1)} %get-tuple-element.52), channel_id=1, source_target_pairs={{0,1},{2,3},{4,5},{6,7},{8,9},{10,11},{12,13},{14,15},{1,0},{3,2},... | collective-permute-start | bytes 786440 | tf_op jit(solution)/shard_map/ppermute | solution.py:702
  48.5 10.3 %collective-permute-start.8 = (f32[2,256,128]{2,1,0:T(8,128)S(1)}, f32[2,256,128]{2,1,0:T(8,128)S(1)}, u32[]{:S(2)}, u32[]{:S(2)}) collective-permute-start(f32[2,256,128]{2,1,0:T(8,128)S(1)} %get-tuple-element.53), channel_id=1, source_target_pairs={{1,2},{3,4},{5,6},{7,8},{9,10},{11,12},{13,14},{2,1},{4,3},{6,5},{... | collective-permute-start | bytes 786440 | tf_op jit(solution)/shard_map/ppermute | solution.py:703
  51.2 8.8 %collective-permute-start.19 = (f32[256,256]{1,0:T(8,128)S(1)}, f32[256,256]{1,0:T(8,128)S(1)}, u32[]{:S(2)}, u32[]{:S(2)}) collective-permute-start(f32[256,256]{1,0:T(8,128)S(1)} %shard_map.111.full), channel_id=1, source_target_pairs={{0,16},{16,0},{1,17},{17,1},{2,18},{18,2},{3,19},{19,3},{4,20},{20... | collective-permute-start | bytes 786440 | tf_op jit(solution)/shard_map/ppermute | solution.py:479

commit v12 on v11

--- a/solution.py
+++ b/solution.py
@@ -242,6 +242,13 @@
 
 def reorder_kernel(x, after, out):
     out[...] = reorder(x[...], [even_odd(x.shape[0], axis) for axis in range(2)])
+
+
+def roll_back_kernel(margin, offs, x, out):
+    n = x.shape[0]
+    sy = (margin - offs[0, 0] + n) % n
+    sx = (margin - offs[0, 1] + n) % n
+    out[...] = dyn_roll(dyn_roll(x[...], sy, 0), sx, 1)
 
 
 def roll_kernel(margin, offs, probe, pr):
@@ -357,10 +364,9 @@
     scalars.wait()
     sy = (margin - offs[0, 0] + n) % n
     sx = (margin - offs[0, 1] + n) % n
-    grad = [dyn_roll(dyn_roll(g, sy, 0), sx, 1) for g in grad]
     even = lax.axis_index("row") % 2 == 0
     keep[...] = jnp.where(even, grad[0], grad[1])
-    give[...] = jnp.where(even, grad[1], grad[0])
+    give[...] = dyn_roll(dyn_roll(jnp.where(even, grad[1], grad[0]), sy, 0), sx, 1)
 
 
 def divide_kernel(margin, grads, limits, own, strip, *sends):
@@ -511,24 +517,19 @@
     refs[-1][...] = pair_sum([r[...] for r in refs[:-1]])
 
 
-def join_kernel(stride, *refs):
-    parts, full = refs[:-1], refs[-1]
-    quad, chunk = len(parts), parts[0].shape[0]
+def write_kernel(stride, quad, mine, others, started, *refs):
+    parts, out, sems = refs[started:-2], refs[-2], refs[-1]
+    half = lax.axis_index("row") % 2
     place = lax.axis_index("col") // stride % quad
-    for j, part in enumerate(parts):
-        full[pl.ds(pl.multiple_of((place ^ j) * chunk, 8), chunk), :] = part[...]
-
-
-def half_kernel(full, out, sem):
-    copy = pltpu.make_async_copy(full, out.at[lax.axis_index("row") % 2], sem)
-    copy.start()
-    copy.wait()
-
-
-def other_kernel(started, other, out, sem):
-    copy = pltpu.make_async_copy(other, out.at[1 - lax.axis_index("row") % 2], sem)
-    copy.start()
-    copy.wait()
+    chunk = parts[0].shape[0]
+    copies = []
+    for i, (part, j) in enumerate(zip(parts, mine + others)):
+        rows = pl.ds(pl.multiple_of((place ^ j) * chunk, 8), chunk)
+        at = half if i < len(mine) else 1 - half
+        copies.append(pltpu.make_async_copy(part, out.at[at, rows, :], sems.at[i]))
+        copies[-1].start()
+    for copy in copies:
+        copy.wait()
 
 
 def reduce_probe(keep, give):
@@ -553,23 +554,27 @@
         for mask in masks[1:]:
             sums.append(swap(total, axis, mask))
         (total,) = call(sum_kernel, [(chunk, n)], [VMEM] * len(sums), *sums)
-    parts = [total]
+    parts, others = {0: total}, {}
     for j in range(1, quad):
-        parts.append(swap(total, "col", offsets[j]))
-    (full,) = call(
-        functools.partial(join_kernel, stride), [(n, n)], [VMEM] * quad, *parts
-    )
-    other = swap(full, "row", 1)
-    out = dict(
-        out_shape=jax.ShapeDtypeStruct((2, n, n), F32),
-        out_specs=HBM,
-        scratch_shapes=[pltpu.SemaphoreType.DMA(())],
-        compiler_params=pltpu.CompilerParams(vmem_limit_bytes=16 << 20),
-    )
-    grad = pl.pallas_call(half_kernel, in_specs=[VMEM], **out)(full)
-    return pl.pallas_call(
-        other_kernel, in_specs=[HBM, VMEM], input_output_aliases={0: 0}, **out
-    )(grad, other)
+        parts[j] = swap(total, "col", offsets[j])
+    for j in range(quad):
+        others[j] = swap(parts[j], "row", 1)
+
+    def write(mine, theirs, *started):
+        count = len(mine) + len(theirs)
+        return pl.pallas_call(
+            functools.partial(write_kernel, stride, quad, mine, theirs, len(started)),
+            out_shape=jax.ShapeDtypeStruct((2, n, n), F32),
+            in_specs=[HBM] * len(started) + [VMEM] * count,
+            out_specs=HBM,
+            scratch_shapes=[pltpu.SemaphoreType.DMA((count,))],
+            input_output_aliases={0: 0} if started else {},
+            compiler_params=pltpu.CompilerParams(vmem_limit_bytes=16 << 20),
+        )(*started, *[parts[j] for j in mine], *[others[j] for j in theirs])
+
+    order = [0] + list(range(quad - 1, 0, -1))
+    grad = write(order, order[:-1])
+    return write([], order[-1:], grad)
 
 
 def whole(object_field, probe, phase, amplitudes, offsets):
@@ -680,6 +685,7 @@
         scratch=[pltpu.SMEM((1, 2), jnp.int32), pltpu.SemaphoreType.DMA(())],
         mib=40,
     )
+    (keep,) = call(functools.partial(roll_back_kernel, margin), [(n, n)], [SMEM, VMEM], offs, keep)
     probe_grad = reduce_probe(keep, give)
     own, strip, *sends = call(
         functools.partial(divide_kernel, margin),

time: 61.1 us -> 58.4 us (0.956)
  waiting for transfers between devices: 24.5 us -> 21.8 us
  Pallas kernels: 14.3 us -> 15 us
    ppermute x1, waiting for transfers between devices: 6.74 us -> 0.01 us  [whole(): send_e = lax.ppermute(send_e, 'col', col_rounds[0])]
    ppermute x11 -> x14, waiting for transfers between devices: 10.7 us -> 14.6 us  [swap(): return lax.ppermute(value, axis, [(i, i ^ distance) for i in range(count)])]
    ppermute x11 -> x14, starting transfers between devices: 11.9 us -> 12 us  [swap(): return lax.ppermute(value, axis, [(i, i ^ distance) for i in range(count)])]
  transfers between devices with their start and end apart: 20 -> 23, of which waited for: 12 -> 11; matrix products, arithmetic and copies ran while one was open for 0% -> 0% of each run, Pallas kernels for 14% -> 15%
where the time goes in v12:
time: 58.4 us; the launch traced here: 58.2 us
  waiting for transfers between devices  21.8 us (37%)
  starting transfers between devices  20.7 us (35%)
  Pallas kernels  15 us (26%)
  between operations  0.84 us (1%)
    ppermute x14, waiting for transfers between devices, swap(): return lax.ppermute(value, axis, [(i, i ^ distance) for i in range(count)])  14.6 us
    pallas_call x17, Pallas kernels, call(): pl.pallas_call(kernel, out_shape=shapes, in_specs=in_specs, out_specs=[SM...  13.5 us
    ppermute x14, starting transfers between devices, swap(): return lax.ppermute(value, axis, [(i, i ^ distance) for i in range(count)])  12 us
    ppermute x1, waiting for transfers between devices, whole(): even0 = lax.ppermute(even0, 'col', col_rounds[0])  6.38 us
    ppermute x1, starting transfers between devices, whole(): even0 = lax.ppermute(even0, 'col', col_rounds[0])  5.75 us
    pallas_call x2, Pallas kernels, write(): pl.pallas_call(functools.partial(write_kernel, stride, quad, mine, theirs...  1.47 us
  transfers between devices with their start and end apart: 23, of which 11 were waited for; matrix products, arithmetic and copies ran while one was open for 0% of the time, Pallas kernels for 15%

profile of v12, /device:TPU:0, one launch (start us, length us, event | category | flops | bytes accessed | tf_op | source)
XLA Modules:
  0.0 58.2 jit_solution(12075141961685406314)
XLA Ops:
  0.6 1.4 %shard_map.95 = (f32[4,256,256]{2,1,0:T(8,128)S(1)}, f32[384,128]{1,0:T(8,128)S(1)}, f32[128,128]{1,0:T(8,128)S(1)}, f32[2,256,128]{2,1,0:T(8,128)S(1)}, f32[4,64,256]{2,1,0:T(8,128)S(1)}) custom-call(f32[4,256,256]{2,1,0:T(8,128)} %bitcast.4), custom_call_target="tpu_custom_call" | custom-call | tf_op jit(solution)/shard_map/pallas_call | solution.py:462
  2.0 0.7 %collective-permute-start.2 = (f32[2,256,128]{2,1,0:T(8,128)S(1)}, f32[2,256,128]{2,1,0:T(8,128)S(1)}, u32[]{:S(2)}, u32[]{:S(2)}) collective-permute-start(f32[2,256,128]{2,1,0:T(8,128)S(1)} %get-tuple-element.34), channel_id=1, source_target_pairs={{1,2},{3,4},{5,6},{7,8},{9,10},{11,12},{13,14},{2,1},{4,3},{6,5},{... | collective-permute-start | bytes 786440 | tf_op jit(solution)/shard_map/ppermute | solution.py:600
  2.7 5.8 %collective-permute-start = (f32[384,128]{1,0:T(8,128)S(1)}, f32[384,128]{1,0:T(8,128)S(1)}, u32[]{:S(2)}, u32[]{:S(2)}) collective-permute-start(f32[384,128]{1,0:T(8,128)S(1)} %get-tuple-element.32), channel_id=1, source_target_pairs={{0,1},{2,3},{4,5},{6,7},{8,9},{10,11},{12,13},{14,15},{1,0},{3,2},... | collective-permute-start | bytes 589832 | tf_op jit(solution)/shard_map/ppermute | solution.py:599
  8.6 2.9 %shard_map.96 = (s32[1,2]{1,0:T(1,128)S(1)}, s32[2,8,128]{2,1,0:T(8,128)S(1)}, f32[256,256]{1,0:T(8,128)S(1)}, f32[256,256]{1,0:T(8,128)S(1)}, bf16[4,256,256]{2...) custom-call(f32[256,256]{1,0:T(8,128)} %refs_0_.1, ...), custom_call_target="tpu_custom_call" | custom-call | tf_op jit(solution)/shard_map/pallas_call | solution.py:462
  11.5 0.8 %shard_map.100.after.refs_4_.refs_5_ = f32[2,256,256]{2,1,0:T(8,128)S(1)} custom-call(s32[1,2]{1,0:T(1,128)S(1)} %get-tuple-element.37.offs, f32[2,256,256]{2,1,0:T(8,128)S(1)} %get-tuple-element.38.probe), custom_call_target="tpu_custom_call" | custom-call | tf_op jit(solution)/shard_map/pallas_call | solution.py:462
  12.3 0.6 %shard_map.101.refs_2_.refs_8_ = f32[256,256]{1,0:T(8,128)S(1)} custom-call(f32[256,256]{1,0:T(8,128)S(1)} %get-tuple-element.41.x, f32[2,256,256]{2,1,0:T(8,128)S(1)} %shard_map.100.after.refs_4_.refs_5_), custom_call_target="tpu_custom_call" | custom-call | tf_op jit(solution)/shard_map/pallas_call | solution.py:462
  12.9 6.4 %collective-permute-done.refs_0_ = f32[384,128]{1,0:T(8,128)S(1)} collective-permute-done((f32[384,128]{1,0:T(8,128)S(1)}, f32[384,128]{1,0:T(8,128)S(1)}, u32[]{:S(2)}, u32[]{:S(2)}) %collective-permute-start) | collective-permute-done | bytes 196640 | tf_op jit(solution)/shard_map/ppermute | solution.py:599
  19.5 0.4 collective-permute-done.1.refs_1_
  20.6 1.5 %shard_map.103 = (f32[2,256,256]{2,1,0:T(8,128)S(1)}, f32[2,256,256]{2,1,0:T(8,128)S(1)}) custom-call(f32[2,256,256]{2,1,0:T(8,128)S(1)} %shard_map.98.refs_3_.refs_0_, f32[4,64,256]{2,1,0:T(8,128)S(1)} %collective-permute-done.3.refs_1_, f32[2,64,128]{2,1,0:T(8,128)S(1)} %collective-permute-done.5.refs_2_, ...), custom_call_target="tpu_custom_call" | custom-call | tf_op jit(solution)/shard_map/pallas_call | solution.py:462
  22.1 3.5 %shard_map.104 = (f32[256,256]{1,0:T(8,128)S(1)}, f32[256,256]{1,0:T(8,128)S(1)}, f32[4,256,256]{2,1,0:T(8,128)S(1)}) custom-call(f32[2,256,256]{2,1,0:T(8,128)S(1)} %shard_map.97.refs_0_, f32[4,64,256]{2,1,0:T(8,128)S(1)} %collective-permute-done.3.refs_1_, f32[2,64,128]{2,1,0:T(8,128)S(1)} %collective-permute-done.4.refs_2_, ...), custom_call_target="tpu_custom_call" | custom-call | tf_op jit(solution)/shard_map/pallas_call | solution.py:462
  25.6 0.4 shard_map.105
  26.6 0.7 %shard_map.108.keep = f32[256,256]{1,0:T(8,128)S(1)} custom-call(s32[1,2]{1,0:T(1,128)S(1)} %get-tuple-element.37.offs, f32[256,256]{1,0:T(8,128)S(1)} %get-tuple-element.54.x), custom_call_target="tpu_custom_call" | custom-call | tf_op jit(solution)/shard_map/pallas_call | solution.py:462
  27.3 0.9 %collective-permute-done.9.other = f32[256,256]{1,0:T(8,128)S(1)} collective-permute-done((f32[256,256]{1,0:T(8,128)S(1)}, f32[256,256]{1,0:T(8,128)S(1)}, u32[]{:S(2)}, u32[]{:S(2)}) %collective-permute-start.9) | collective-permute-done | bytes 262176 | tf_op jit(solution)/shard_map/ppermute | solution.py:485
  28.2 1.8 %collective-permute-start.10 = (f32[64,256]{1,0:T(8,128)S(1)}, f32[64,256]{1,0:T(8,128)S(1)}, u32[]{:S(2)}, u32[]{:S(2)}) collective-permute-start(f32[64,256]{1,0:T(8,128)S(1)} %get-tuple-element.57), channel_id=1, source_target_pairs={{0,1},{1,0},{2,3},{3,2},{4,5},{5,4},{6,7},{7,6},{8,9},{9,8},{10,11... | collective-permute-start | bytes 196616 | tf_op jit(solution)/shard_map/ppermute | solution.py:485
  30.3 1.5 %collective-permute-start.12 = (f32[64,256]{1,0:T(8,128)S(1)}, f32[64,256]{1,0:T(8,128)S(1)}, u32[]{:S(2)}, u32[]{:S(2)}) collective-permute-start(f32[64,256]{1,0:T(8,128)S(1)} %get-tuple-element.59), channel_id=1, source_target_pairs={{0,3},{1,2},{2,1},{3,0},{4,7},{5,6},{6,5},{7,4},{8,11},{9,10},{10,... | collective-permute-start | bytes 196616 | tf_op jit(solution)/shard_map/ppermute | solution.py:485
  31.8 0.8 %collective-permute-done.10.refs_1_ = f32[64,256]{1,0:T(8,128)S(1)} collective-permute-done((f32[64,256]{1,0:T(8,128)S(1)}, f32[64,256]{1,0:T(8,128)S(1)}, u32[]{:S(2)}, u32[]{:S(2)}) %collective-permute-start.10) | collective-permute-done | bytes 65568 | tf_op jit(solution)/shard_map/ppermute | solution.py:485
  32.5 3.0 %collective-permute-done.11.refs_2_ = f32[64,256]{1,0:T(8,128)S(1)} collective-permute-done((f32[64,256]{1,0:T(8,128)S(1)}, f32[64,256]{1,0:T(8,128)S(1)}, u32[]{:S(2)}, u32[]{:S(2)}) %collective-permute-start.11) | collective-permute-done | bytes 65568 | tf_op jit(solution)/shard_map/ppermute | solution.py:485
  35.6 3.5 %collective-permute-start.15 = (f32[64,256]{1,0:T(8,128)S(1)}, f32[64,256]{1,0:T(8,128)S(1)}, u32[]{:S(2)}, u32[]{:S(2)}) collective-permute-start(f32[64,256]{1,0:T(8,128)S(1)} %shard_map.110.refs_0_), channel_id=1, source_target_pairs={{0,12},{1,13},{2,14},{3,15},{4,8},{5,9},{6,10},{7,11},{8,4},{9,5},... | collective-permute-start | bytes 196616 | tf_op jit(solution)/shard_map/ppermute | solution.py:485
  39.1 0.9 %collective-permute-start.13 = (f32[64,256]{1,0:T(8,128)S(1)}, f32[64,256]{1,0:T(8,128)S(1)}, u32[]{:S(2)}, u32[]{:S(2)}) collective-permute-start(f32[64,256]{1,0:T(8,128)S(1)} %shard_map.110.refs_0_), channel_id=1, source_target_pairs={{0,4},{1,5},{2,6},{3,7},{4,0},{5,1},{6,2},{7,3},{8,12},{9,13},{10,... | collective-permute-start | bytes 196616 | tf_op jit(solution)/shard_map/ppermute | solution.py:485
  40.2 1.0 %collective-permute-start.7 = (f32[2,256,128]{2,1,0:T(8,128)S(1)}, f32[2,256,128]{2,1,0:T(8,128)S(1)}, u32[]{:S(2)}, u32[]{:S(2)}) collective-permute-start(f32[2,256,128]{2,1,0:T(8,128)S(1)} %get-tuple-element.52), channel_id=1, source_target_pairs={{0,1},{2,3},{4,5},{6,7},{8,9},{10,11},{12,13},{14,15},{1,0},{3,2},... | collective-permute-start | bytes 786440 | tf_op jit(solution)/shard_map/ppermute | solution.py:708
  41.2 0.7 %collective-permute-start.8 = (f32[2,256,128]{2,1,0:T(8,128)S(1)}, f32[2,256,128]{2,1,0:T(8,128)S(1)}, u32[]{:S(2)}, u32[]{:S(2)}) collective-permute-start(f32[2,256,128]{2,1,0:T(8,128)S(1)} %get-tuple-element.53), channel_id=1, source_target_pairs={{1,2},{3,4},{5,6},{7,8},{9,10},{11,12},{13,14},{2,1},{4,3},{6,5},{... | collective-permute-start | bytes 786440 | tf_op jit(solution)/shard_map/ppermute | solution.py:709
  41.9 2.4 %collective-permute-done.14.refs_2_ = f32[64,256]{1,0:T(8,128)S(1)} collective-permute-done((f32[64,256]{1,0:T(8,128)S(1)}, f32[64,256]{1,0:T(8,128)S(1)}, u32[]{:S(2)}, u32[]{:S(2)}) %collective-permute-start.14) | collective-permute-done | bytes 65568 | tf_op jit(solution)/shard_map/ppermute | solution.py:485
  44.4 1.5 %collective-permute-start.17 = (f32[64,256]{1,0:T(8,128)S(1)}, f32[64,256]{1,0:T(8,128)S(1)}, u32[]{:S(2)}, u32[]{:S(2)}) collective-permute-start(f32[64,256]{1,0:T(8,128)S(1)} %shard_map.111.refs_0_), channel_id=1, source_target_pairs={{0,2},{1,3},{2,0},{3,1},{4,6},{5,7},{6,4},{7,5},{8,10},{9,11},{10,... | collective-permute-start | bytes 196616 | tf_op jit(solution)/shard_map/ppermute | solution.py:485
  45.9 1.3 %collective-permute-start.16 = (f32[64,256]{1,0:T(8,128)S(1)}, f32[64,256]{1,0:T(8,128)S(1)}, u32[]{:S(2)}, u32[]{:S(2)}) collective-permute-start(f32[64,256]{1,0:T(8,128)S(1)} %shard_map.111.refs_0_), channel_id=1, source_target_pairs={{0,3},{1,2},{2,1},{3,0},{4,7},{5,6},{6,5},{7,4},{8,11},{9,10},{10,... | collective-permute-start | bytes 196616 | tf_op jit(solution)/shard_map/ppermute | solution.py:485
  47.2 0.7 %collective-permute-start.18 = (f32[64,256]{1,0:T(8,128)S(1)}, f32[64,256]{1,0:T(8,128)S(1)}, u32[]{:S(2)}, u32[]{:S(2)}) collective-permute-start(f32[64,256]{1,0:T(8,128)S(1)} %shard_map.111.refs_0_), channel_id=1, source_target_pairs={{0,1},{1,0},{2,3},{3,2},{4,5},{5,4},{6,7},{7,6},{8,9},{9,8},{10,11... | collective-permute-start | bytes 196616 | tf_op jit(solution)/shard_map/ppermute | solution.py:485
  47.9 2.4 %collective-permute-done.17.refs_2_ = f32[64,256]{1,0:T(8,128)S(1)} collective-permute-done((f32[64,256]{1,0:T(8,128)S(1)}, f32[64,256]{1,0:T(8,128)S(1)}, u32[]{:S(2)}, u32[]{:S(2)}) %collective-permute-start.17) | collective-permute-done | bytes 65568 | tf_op jit(solution)/shard_map/ppermute | solution.py:485
  50.4 2.3 %collective-permute-done.16.refs_1_ = f32[64,256]{1,0:T(8,128)S(1)} collective-permute-done((f32[64,256]{1,0:T(8,128)S(1)}, f32[64,256]{1,0:T(8,128)S(1)}, u32[]{:S(2)}, u32[]{:S(2)}) %collective-permute-start.16) | collective-permute-done | bytes 65568 | tf_op jit(solution)/shard_map/ppermute | solution.py:485
  52.7 2.4 %collective-permute-done.18.refs_3_ = f32[64,256]{1,0:T(8,128)S(1)} collective-permute-done((f32[64,256]{1,0:T(8,128)S(1)}, f32[64,256]{1,0:T(8,128)S(1)}, u32[]{:S(2)}, u32[]{:S(2)}) %collective-permute-start.18) | collective-permute-done | bytes 65568 | tf_op jit(solution)/shard_map/ppermute | solution.py:485
  55.1 0.8 %shard_map.112.refs_0_ = f32[2,256,256]{2,1,0:T(8,128)} custom-call(f32[64,256]{1,0:T(8,128)S(1)} %shard_map.111.refs_0_, f32[64,256]{1,0:T(8,128)S(1)} %collective-permute-done.16.refs_1_, f32[64,256]{1,0:T(8,128)S(1)} %collective-permute-done.17.refs_2_, f32[64,256]{1,0:T(8,128)S(1)} %collective-permute-done.18.refs_3_, ...), custom_call_target="tpu_custom_call" | custom-call | tf_op jit(solution)/shard_map/pallas_call | solution.py:565
  56.0 0.4 collective-permute-done.22.refs_1_
  56.4 0.6 %shard_map.113 = f32[2,256,256]{2,1,0:T(8,128)} custom-call(f32[2,256,256]{2,1,0:T(8,128)} %shard_map.112.refs_0_, f32[64,256]{1,0:T(8,128)S(1)} %collective-permute-done.22.refs_1_), custom_call_target="tpu_custom_call", output_to_operand_aliasing={{}: (0, {})} | custom-call | tf_op jit(solution)/shard_map/pallas_call | solution.py:565
  57.0 1.2 %shard_map.107 = f32[4,256,256]{2,1,0:T(8,128)} custom-call(f32[4,256,256]{2,1,0:T(8,128)S(1)} %get-tuple-element.51.total, f32[2,256,128]{2,1,0:T(8,128)S(1)} %collective-permute-done.7.e, f32[2,256,128]{2,1,0:T(8,128)S(1)} %collective-permute-done.8.o), custom_call_target="tpu_custom_call" | custom-call | tf_op jit(solution)/shard_map/pallas_call | solution.py:462
  (33 shorter events, 2.1 us)
Async XLA Ops:
  2.0 17.3 %collective-permute-start.2 = (f32[2,256,128]{2,1,0:T(8,128)S(1)}, f32[2,256,128]{2,1,0:T(8,128)S(1)}, u32[]{:S(2)}, u32[]{:S(2)}) collective-permute-start(f32[2,256,128]{2,1,0:T(8,128)S(1)} %get-tuple-element.34), channel_id=1, source_target_pairs={{1,2},{3,4},{5,6},{7,8},{9,10},{11,12},{13,14},{2,1},{4,3},{6,5},{... | collective-permute-start | bytes 786440 | tf_op jit(solution)/shard_map/ppermute | solution.py:600
  2.7 16.6 %collective-permute-start = (f32[384,128]{1,0:T(8,128)S(1)}, f32[384,128]{1,0:T(8,128)S(1)}, u32[]{:S(2)}, u32[]{:S(2)}) collective-permute-start(f32[384,128]{1,0:T(8,128)S(1)} %get-tuple-element.32), channel_id=1, source_target_pairs={{0,1},{2,3},{4,5},{6,7},{8,9},{10,11},{12,13},{14,15},{1,0},{3,2},... | collective-permute-start | bytes 589832 | tf_op jit(solution)/shard_map/ppermute | solution.py:599
  8.4 11.9 %collective-permute-start.3 = (f32[4,64,256]{2,1,0:T(8,128)S(1)}, f32[4,64,256]{2,1,0:T(8,128)S(1)}, u32[]{:S(2)}, u32[]{:S(2)}) collective-permute-start(f32[4,64,256]{2,1,0:T(8,128)S(1)} %get-tuple-element.36), channel_id=1, source_target_pairs={{0,16},{16,0},{1,17},{17,1},{2,18},{18,2},{3,19},{19,3},{4,20},{20... | collective-permute-start | bytes 786440 | tf_op jit(solution)/shard_map/ppermute | solution.py:603
  8.4 11.5 %collective-permute-start.1 = (f32[128,128]{1,0:T(8,128)S(1)}, f32[128,128]{1,0:T(8,128)S(1)}, u32[]{:S(2)}, u32[]{:S(2)}) collective-permute-start(f32[128,128]{1,0:T(8,128)S(1)} %get-tuple-element.33), channel_id=1, source_target_pairs={{0,1},{2,3},{4,5},{6,7},{8,9},{10,11},{12,13},{14,15},{1,0},{3,2},... | collective-permute-start | bytes 196616 | tf_op jit(solution)/shard_map/ppermute | solution.py:601
  19.3 1.3 %collective-permute-start.5 = (f32[2,64,128]{2,1,0:T(8,128)S(1)}, f32[2,64,128]{2,1,0:T(8,128)S(1)}, u32[]{:S(2)}, u32[]{:S(2)}) collective-permute-start(f32[2,64,128]{2,1,0:T(8,128)S(1)} %shard_map.102), channel_id=1, source_target_pairs={{0,16},{16,0},{1,17},{17,1},{2,18},{18,2},{3,19},{19,3},{4,20},{20... | collective-permute-start | bytes 196616 | tf_op jit(solution)/shard_map/ppermute | solution.py:616
  20.0 2.1 %collective-permute-start.4 = (f32[2,64,128]{2,1,0:T(8,128)S(1)}, f32[2,64,128]{2,1,0:T(8,128)S(1)}, u32[]{:S(2)}, u32[]{:S(2)}) collective-permute-start(f32[2,64,128]{2,1,0:T(8,128)S(1)} %shard_map.99), channel_id=1, source_target_pairs={{0,16},{16,0},{1,17},{17,1},{2,18},{18,2},{3,19},{19,3},{4,20},{20... | collective-permute-start | bytes 196616 | tf_op jit(solution)/shard_map/ppermute | solution.py:616
  26.0 14.0 %collective-permute-start.6 = (f32[4,64,384]{2,1,0:T(8,128)S(1)}, f32[4,64,384]{2,1,0:T(8,128)S(1)}, u32[]{:S(2)}, u32[]{:S(2)}) collective-permute-start(f32[4,64,384]{2,1,0:T(8,128)S(1)} %get-tuple-element.50), channel_id=1, source_target_pairs={{0,16},{16,0},{1,17},{17,1},{2,18},{18,2},{3,19},{19,3},{4,20},{20... | collective-permute-start | bytes 1179656 | tf_op jit(solution)/shard_map/ppermute | solution.py:699
  26.2 1.9 %collective-permute-start.9 = (f32[256,256]{1,0:T(8,128)S(1)}, f32[256,256]{1,0:T(8,128)S(1)}, u32[]{:S(2)}, u32[]{:S(2)}) collective-permute-start(f32[256,256]{1,0:T(8,128)S(1)} %get-tuple-element.55), channel_id=1, source_target_pairs={{0,16},{16,0},{1,17},{17,1},{2,18},{18,2},{3,19},{19,3},{4,20},{20... | collective-permute-start | bytes 786440 | tf_op jit(solution)/shard_map/ppermute | solution.py:485
  28.2 4.3 %collective-permute-start.10 = (f32[64,256]{1,0:T(8,128)S(1)}, f32[64,256]{1,0:T(8,128)S(1)}, u32[]{:S(2)}, u32[]{:S(2)}) collective-permute-start(f32[64,256]{1,0:T(8,128)S(1)} %get-tuple-element.57), channel_id=1, source_target_pairs={{0,1},{1,0},{2,3},{3,2},{4,5},{5,4},{6,7},{7,6},{8,9},{9,8},{10,11... | collective-permute-start | bytes 196616 | tf_op jit(solution)/shard_map/ppermute | solution.py:485
  30.1 5.5 %collective-permute-start.11 = (f32[64,256]{1,0:T(8,128)S(1)}, f32[64,256]{1,0:T(8,128)S(1)}, u32[]{:S(2)}, u32[]{:S(2)}) collective-permute-start(f32[64,256]{1,0:T(8,128)S(1)} %get-tuple-element.58), channel_id=1, source_target_pairs={{0,2},{1,3},{2,0},{3,1},{4,6},{5,7},{6,4},{7,5},{8,10},{9,11},{10,... | collective-permute-start | bytes 196616 | tf_op jit(solution)/shard_map/ppermute | solution.py:485
  30.3 5.3 %collective-permute-start.12 = (f32[64,256]{1,0:T(8,128)S(1)}, f32[64,256]{1,0:T(8,128)S(1)}, u32[]{:S(2)}, u32[]{:S(2)}) collective-permute-start(f32[64,256]{1,0:T(8,128)S(1)} %get-tuple-element.59), channel_id=1, source_target_pairs={{0,3},{1,2},{2,1},{3,0},{4,7},{5,6},{6,5},{7,4},{8,11},{9,10},{10,... | collective-permute-start | bytes 196616 | tf_op jit(solution)/shard_map/ppermute | solution.py:485
  35.6 6.3 %collective-permute-start.15 = (f32[64,256]{1,0:T(8,128)S(1)}, f32[64,256]{1,0:T(8,128)S(1)}, u32[]{:S(2)}, u32[]{:S(2)}) collective-permute-start(f32[64,256]{1,0:T(8,128)S(1)} %shard_map.110.refs_0_), channel_id=1, source_target_pairs={{0,12},{1,13},{2,14},{3,15},{4,8},{5,9},{6,10},{7,11},{8,4},{9,5},... | collective-permute-start | bytes 196616 | tf_op jit(solution)/shard_map/ppermute | solution.py:485
  39.1 5.2 %collective-permute-start.14 = (f32[64,256]{1,0:T(8,128)S(1)}, f32[64,256]{1,0:T(8,128)S(1)}, u32[]{:S(2)}, u32[]{:S(2)}) collective-permute-start(f32[64,256]{1,0:T(8,128)S(1)} %shard_map.110.refs_0_), channel_id=1, source_target_pairs={{0,8},{1,9},{2,10},{3,11},{4,12},{5,13},{6,14},{7,15},{8,0},{9,1},... | collective-permute-start | bytes 196616 | tf_op jit(solution)/shard_map/ppermute | solution.py:485
  39.1 5.2 %collective-permute-start.13 = (f32[64,256]{1,0:T(8,128)S(1)}, f32[64,256]{1,0:T(8,128)S(1)}, u32[]{:S(2)}, u32[]{:S(2)}) collective-permute-start(f32[64,256]{1,0:T(8,128)S(1)} %shard_map.110.refs_0_), channel_id=1, source_target_pairs={{0,4},{1,5},{2,6},{3,7},{4,0},{5,1},{6,2},{7,3},{8,12},{9,13},{10,... | collective-permute-start | bytes 196616 | tf_op jit(solution)/shard_map/ppermute | solution.py:485
  40.2 16.8 %collective-permute-start.7 = (f32[2,256,128]{2,1,0:T(8,128)S(1)}, f32[2,256,128]{2,1,0:T(8,128)S(1)}, u32[]{:S(2)}, u32[]{:S(2)}) collective-permute-start(f32[2,256,128]{2,1,0:T(8,128)S(1)} %get-tuple-element.52), channel_id=1, source_target_pairs={{0,1},{2,3},{4,5},{6,7},{8,9},{10,11},{12,13},{14,15},{1,0},{3,2},... | collective-permute-start | bytes 786440 | tf_op jit(solution)/shard_map/ppermute | solution.py:708
  41.2 15.8 %collective-permute-start.8 = (f32[2,256,128]{2,1,0:T(8,128)S(1)}, f32[2,256,128]{2,1,0:T(8,128)S(1)}, u32[]{:S(2)}, u32[]{:S(2)}) collective-permute-start(f32[2,256,128]{2,1,0:T(8,128)S(1)} %get-tuple-element.53), channel_id=1, source_target_pairs={{1,2},{3,4},{5,6},{7,8},{9,10},{11,12},{13,14},{2,1},{4,3},{6,5},{... | collective-permute-start | bytes 786440 | tf_op jit(solution)/shard_map/ppermute | solution.py:709
  44.3 2.9 %collective-permute-start.19 = (f32[64,256]{1,0:T(8,128)S(1)}, f32[64,256]{1,0:T(8,128)S(1)}, u32[]{:S(2)}, u32[]{:S(2)}) collective-permute-start(f32[64,256]{1,0:T(8,128)S(1)} %shard_map.111.refs_0_), channel_id=1, source_target_pairs={{0,16},{16,0},{1,17},{17,1},{2,18},{18,2},{3,19},{19,3},{4,20},{20... | collective-permute-start | bytes 196616 | tf_op jit(solution)/shard_map/ppermute | solution.py:485
  44.4 6.0 %collective-permute-start.17 = (f32[64,256]{1,0:T(8,128)S(1)}, f32[64,256]{1,0:T(8,128)S(1)}, u32[]{:S(2)}, u32[]{:S(2)}) collective-permute-start(f32[64,256]{1,0:T(8,128)S(1)} %shard_map.111.refs_0_), channel_id=1, source_target_pairs={{0,2},{1,3},{2,0},{3,1},{4,6},{5,7},{6,4},{7,5},{8,10},{9,11},{10,... | collective-permute-start | bytes 196616 | tf_op jit(solution)/shard_map/ppermute | solution.py:485
  45.9 6.8 %collective-permute-start.16 = (f32[64,256]{1,0:T(8,128)S(1)}, f32[64,256]{1,0:T(8,128)S(1)}, u32[]{:S(2)}, u32[]{:S(2)}) collective-permute-start(f32[64,256]{1,0:T(8,128)S(1)} %shard_map.111.refs_0_), channel_id=1, source_target_pairs={{0,3},{1,2},{2,1},{3,0},{4,7},{5,6},{6,5},{7,4},{8,11},{9,10},{10,... | collective-permute-start | bytes 196616 | tf_op jit(solution)/shard_map/ppermute | solution.py:485
  47.2 7.9 %collective-permute-start.18 = (f32[64,256]{1,0:T(8,128)S(1)}, f32[64,256]{1,0:T(8,128)S(1)}, u32[]{:S(2)}, u32[]{:S(2)}) collective-permute-start(f32[64,256]{1,0:T(8,128)S(1)} %shard_map.111.refs_0_), channel_id=1, source_target_pairs={{0,1},{1,0},{2,3},{3,2},{4,5},{5,4},{6,7},{7,6},{8,9},{9,8},{10,11... | collective-permute-start | bytes 196616 | tf_op jit(solution)/shard_map/ppermute | solution.py:485
  50.4 4.7 %collective-permute-start.21 = (f32[64,256]{1,0:T(8,128)S(1)}, f32[64,256]{1,0:T(8,128)S(1)}, u32[]{:S(2)}, u32[]{:S(2)}) collective-permute-start(f32[64,256]{1,0:T(8,128)S(1)} %collective-permute-done.17.refs_2_), channel_id=1, source_target_pairs={{0,16},{16,0},{1,17},{17,1},{2,18},{18,2},{3,19},{19,3},{4,20},{20... | collective-permute-start | bytes 196616 | tf_op jit(solution)/shard_map/ppermute | solution.py:485
  52.7 2.4 %collective-permute-start.20 = (f32[64,256]{1,0:T(8,128)S(1)}, f32[64,256]{1,0:T(8,128)S(1)}, u32[]{:S(2)}, u32[]{:S(2)}) collective-permute-start(f32[64,256]{1,0:T(8,128)S(1)} %collective-permute-done.16.refs_1_), channel_id=1, source_target_pairs={{0,16},{16,0},{1,17},{17,1},{2,18},{18,2},{3,19},{19,3},{4,20},{20... | collective-permute-start | bytes 196616 | tf_op jit(solution)/shard_map/ppermute | solution.py:485
  55.1 1.3 %collective-permute-start.22 = (f32[64,256]{1,0:T(8,128)S(1)}, f32[64,256]{1,0:T(8,128)S(1)}, u32[]{:S(2)}, u32[]{:S(2)}) collective-permute-start(f32[64,256]{1,0:T(8,128)S(1)} %collective-permute-done.18.refs_3_), channel_id=1, source_target_pairs={{0,16},{16,0},{1,17},{17,1},{2,18},{18,2},{3,19},{19,3},{4,20},{20... | collective-permute-start | bytes 196616 | tf_op jit(solution)/shard_map/ppermute | solution.py:485

commit v13 on v11

--- a/solution.py
+++ b/solution.py
@@ -27,15 +27,10 @@
 def dft_constants(n):
     h = n // 2
     k = np.arange(h)
-    angle = 2.0 * np.pi * ((k[:, None] * k[None, :]) % h) / h
-    scale = 1.0 / np.sqrt(n)
-    c, s = np.cos(angle) * scale, np.sin(angle) * scale
-    d = np.block([[c, s], [-s, c]])
-    mats = np.stack(split_np(d))
-    w = np.exp(-2j * np.pi * k / n)
-    tw_left = np.stack([np.tile(w.real[:, None], (1, h)), np.tile(w.imag[:, None], (1, h))])
-    tw_right = np.stack([np.tile(w.real[None], (8, 1)), np.tile(w.imag[None], (8, 1))])
-    return mats, tw_left.astype(np.float32), tw_right.astype(np.float32)
+    even = np.exp(-2j * np.pi * ((k[:, None] * k[None, :]) % h) / h) / np.sqrt(n)
+    odd = even * np.exp(-2j * np.pi * k / n)[None, :]
+    real = [np.block([[m.real, -m.imag], [m.imag, m.real]]) for m in (even, odd)]
+    return np.stack(split_np(real[0])), np.stack(split_np(real[1]) + split_np(real[1].T))
 
 
 def split(x):
@@ -70,48 +65,32 @@
 
 
 class Dft:
-    def __init__(self, mats, tw_left, tw_right, n):
-        self.mats, self.n, self.h = mats, n, n // 2
-        self.tw_left, self.tw_right = tw_left, tw_right
-
-    def wl(self, width):
-        parts = width // self.tw_left.shape[2]
-        return [cat([self.tw_left[i]] * parts, 1) for i in range(2)]
-
-    def wr(self):
-        return [self.tw_right[i, 0:1] for i in range(2)]
+    def __init__(self, mats, n):
+        self.mats, self.h = mats, n // 2
 
     def left(self, x):
-        h, w = self.h, x[0].shape[1]
-        total = [p[:h] + p[h:] for p in x]
-        odd = product([p[:h] - p[h:] for p in x], self.wl(w))
-        u = left_dot(self.mats, 0, cat(total, 0))
-        v = left_dot(self.mats, 0, cat(odd, 0))
+        h = self.h
+        u = left_dot(self.mats, 0, cat([p[:h] + p[h:] for p in x], 0))
+        v = left_dot(self.mats, 4, cat([p[:h] - p[h:] for p in x], 0))
         return [cat([u[:h], v[:h]], 0), cat([u[h:], v[h:]], 0)]
 
     def right(self, x):
-        h, m = self.h, x[0].shape[0]
-        total = [p[:, :h] + p[:, h:] for p in x]
-        odd = product([p[:, :h] - p[:, h:] for p in x], self.wr())
-        u = right_dot(cat(total, 1), self.mats, 2)
-        v = right_dot(cat(odd, 1), self.mats, 2)
+        h = self.h
+        u = right_dot(cat([p[:, :h] + p[:, h:] for p in x], 1), self.mats, 2)
+        v = right_dot(cat([p[:, :h] - p[:, h:] for p in x], 1), self.mats, 6)
         return [cat([u[:, :h], v[:, :h]], 1), cat([u[:, h:], v[:, h:]], 1)]
 
     def right_inverse(self, x):
-        h, m = self.h, x[0].shape[0]
+        h = self.h
         u = right_dot(cat([p[:, :h] for p in x], 1), self.mats, 0)
-        v = right_dot(cat([p[:, h:] for p in x], 1), self.mats, 0)
-        even = [u[:, :h], u[:, h:]]
-        odd = conj_product(self.wr(), [v[:, :h], v[:, h:]])
-        return [cat([e + o, e - o], 1) for e, o in zip(even, odd)]
+        v = right_dot(cat([p[:, h:] for p in x], 1), self.mats, 4)
+        return [cat([e + o, e - o], 1) for e, o in ((u[:, :h], v[:, :h]), (u[:, h:], v[:, h:]))]
 
     def left_inverse(self, x):
-        h, w = self.h, x[0].shape[1]
+        h = self.h
         u = left_dot(self.mats, 2, cat([p[:h] for p in x], 0))
-        v = left_dot(self.mats, 2, cat([p[h:] for p in x], 0))
-        even = [u[:h], u[h:]]
-        odd = conj_product(self.wl(w), [v[:h], v[h:]])
-        return [cat([e + o, e - o], 0) for e, o in zip(even, odd)]
+        v = left_dot(self.mats, 6, cat([p[h:] for p in x], 0))
+        return [cat([e + o, e - o], 0) for e, o in ((u[:h], v[:h]), (u[h:], v[h:]))]
 
 
 SIN = [(-1.0) ** i / math.factorial(2 * i + 1) for i in range(7)]
@@ -216,15 +195,15 @@
 
 
 def prep_kernel(margin, *refs):
-    hbm, (offs, limits, kr, ki, mats), loaded = refs[:7], refs[7:12], refs[12:16]
-    phase, table, sems = refs[16:]
+    hbm, (offs, limits, kr, ki, mats, *loaded) = refs[:6], refs[6:13]
+    phase, table, sems = refs[13:]
     n = phase.shape[0]
     h = n // 2
     first = pltpu.make_async_copy(hbm[0], phase, sems.at[0])
     first.start()
     order = [even_odd(n, axis) for axis in range(2)]
     first.wait()
-    copies = copy_all(hbm[1:], (table,) + loaded + (offs,), sems)
+    copies = copy_all(hbm[1:], (table, mats.at[4:8], *loaded, offs), sems)
     angle = reorder(phase[...], order)
     kr[...], ki[...] = cos_sin(angle)
     copies[0].wait()
@@ -323,9 +302,9 @@
 
 def arrive_kernel(n_row, margin, *refs):
     main, halos, corners, refs = unpack(n_row, refs)
-    limits, pr, kr, ki, mats, twl, twr, w1, arrive = refs
+    limits, pr, kr, ki, mats, w1, arrive = refs
     n = main.shape[1]
-    dft = Dft(mats, twl[...], twr[...], n)
+    dft = Dft(mats, n)
     win = window_of(main, 0, halos, corners, limits, margin)
     w1[0], w1[1] = win
     x = dft.left(product([pr[0], pr[1]], win))
@@ -335,12 +314,12 @@
 
 def back_kernel(n_row, margin, *refs):
     main, halos, corners, refs = unpack(n_row, refs)
-    limits, offs_hbm, pr, kr, ki, am, w1, arrive, mats, twl, twr = refs[:11]
-    keep, give, grads, offs, sem = refs[11:]
+    limits, offs_hbm, pr, kr, ki, am, w1, arrive, mats = refs[:9]
+    keep, give, grads, offs, sem = refs[9:]
     scalars = pltpu.make_async_copy(offs_hbm, offs, sem)
     scalars.start()
     n = main.shape[1]
-    dft = Dft(mats, twl[...], twr[...], n)
+    dft = Dft(mats, n)
     win = window_of(main, 1, halos, corners, limits, margin)
     x = dft.left(product([arrive[0], arrive[1]], win))
     far = dft.right(x)
@@ -577,7 +556,7 @@
     n = probe.shape[1]
     h = n // 2
     margin = n // 4
-    mats, tw_left, tw_right = [jnp.asarray(t) for t in dft_constants(n)]
+    even, odd = [jnp.asarray(t) for t in dft_constants(n)]
 
     row_rounds, col_rounds = edges("row"), edges("col")
     n_row = len(row_rounds)
@@ -622,14 +601,13 @@
         )
         return main
 
-    loads = (phase, mats, tw_left, tw_right, probe, amplitudes.reshape(n, n))
-    loads += (offsets.reshape(1, 2),)
-    offs, limits, kr, ki, mats, tw_left, tw_right, pr, am = call(
+    loads = (phase, even, odd, probe, amplitudes.reshape(n, n), offsets.reshape(1, 2))
+    offs, limits, kr, ki, mats, pr, am = call(
         functools.partial(prep_kernel, margin),
         [jax.ShapeDtypeStruct((1, 2), jnp.int32), jax.ShapeDtypeStruct((2, 8, h), jnp.int32)]
         + [(n, n)] * 2
-        + [jax.ShapeDtypeStruct((4, n, n), BF16)]
-        + [jax.ShapeDtypeStruct(x.shape, x.dtype) for x in loads[2:-1]],
+        + [jax.ShapeDtypeStruct((8, n, n), BF16)]
+        + [jax.ShapeDtypeStruct(x.shape, x.dtype) for x in loads[3:-1]],
         [HBM] * len(loads),
         *[in_hbm(x) for x in loads],
         scratch=[
@@ -646,7 +624,7 @@
     w1, arrive = call(
         functools.partial(arrive_kernel, n_row, margin),
         [(2, n, n), (2, n, n)],
-        [VMEM] * (8 + 2 * n_row),
+        [VMEM] * (6 + 2 * n_row),
         main,
         *halos,
         *corners[0],
@@ -655,14 +633,12 @@
         kr,
         ki,
         mats,
-        tw_left,
-        tw_right,
     )
     main = merge(1)
     keep, give, grads = call(
         functools.partial(back_kernel, n_row, margin),
         [(n, n), (n, n), (4, n, n)],
-        [VMEM] * (2 + 2 * n_row) + [HBM] + [VMEM] * 9,
+        [VMEM] * (2 + 2 * n_row) + [HBM] + [VMEM] * 7,
         main,
         *halos,
         *corners[1],
@@ -675,8 +651,6 @@
         w1,
         arrive,
         mats,
-        tw_left,
-        tw_right,
         scratch=[pltpu.SMEM((1, 2), jnp.int32), pltpu.SemaphoreType.DMA(())],
         mib=40,
     )

time: 61.1 us -> 61.1 us (level)
  no operation moved by 1% of the time
where the time goes in v13:
time: 61.1 us; the launch traced here: 60.7 us
  waiting for transfers between devices  24.5 us (40%)
  starting transfers between devices  21 us (34%)
  Pallas kernels  14.4 us (24%)
  between operations  0.79 us (1%)
    pallas_call x17, Pallas kernels, call(): pl.pallas_call(kernel, out_shape=shapes, in_specs=in_specs, out_specs=[SM...  12.9 us
    ppermute x11, starting transfers between devices, swap(): return lax.ppermute(value, axis, [(i, i ^ distance) for i in range(count)])  11.9 us
    ppermute x11, waiting for transfers between devices, swap(): return lax.ppermute(value, axis, [(i, i ^ distance) for i in range(count)])  10.7 us
    ppermute x1, waiting for transfers between devices, whole(): send_e = lax.ppermute(send_e, 'col', col_rounds[0])  6.74 us
    ppermute x1, waiting for transfers between devices, whole(): even0 = lax.ppermute(even0, 'col', col_rounds[0])  6.32 us
    ppermute x1, starting transfers between devices, whole(): even0 = lax.ppermute(even0, 'col', col_rounds[0])  5.75 us
    ppermute x1, starting transfers between devices, whole(): send_e = lax.ppermute(send_e, 'col', col_rounds[0])  1.28 us
  transfers between devices with their start and end apart: 20, of which 12 were waited for; matrix products, arithmetic and copies ran while one was open for 0% of the time, Pallas kernels for 14%

profile of v13, /device:TPU:0, one launch (start us, length us, event | category | flops | bytes accessed | tf_op | source)
XLA Modules:
  0.0 60.7 jit_solution(8519615868680174023)
XLA Ops:
  0.6 1.4 %shard_map.86 = (f32[4,256,256]{2,1,0:T(8,128)S(1)}, f32[384,128]{1,0:T(8,128)S(1)}, f32[128,128]{1,0:T(8,128)S(1)}, f32[2,256,128]{2,1,0:T(8,128)S(1)}, f32[4,64,256]{2,1,0:T(8,128)S(1)}) custom-call(f32[4,256,256]{2,1,0:T(8,128)} %bitcast.4), custom_call_target="tpu_custom_call" | custom-call | tf_op jit(solution)/shard_map/pallas_call | solution.py:435
  2.0 0.7 %collective-permute-start.2 = (f32[2,256,128]{2,1,0:T(8,128)S(1)}, f32[2,256,128]{2,1,0:T(8,128)S(1)}, u32[]{:S(2)}, u32[]{:S(2)}) collective-permute-start(f32[2,256,128]{2,1,0:T(8,128)S(1)} %get-tuple-element.32), channel_id=1, source_target_pairs={{1,2},{3,4},{5,6},{7,8},{9,10},{11,12},{13,14},{2,1},{4,3},{6,5},{... | collective-permute-start | bytes 786440 | tf_op jit(solution)/shard_map/ppermute | solution.py:574
  2.7 5.8 %collective-permute-start = (f32[384,128]{1,0:T(8,128)S(1)}, f32[384,128]{1,0:T(8,128)S(1)}, u32[]{:S(2)}, u32[]{:S(2)}) collective-permute-start(f32[384,128]{1,0:T(8,128)S(1)} %get-tuple-element.30), channel_id=1, source_target_pairs={{0,1},{2,3},{4,5},{6,7},{8,9},{10,11},{12,13},{14,15},{1,0},{3,2},... | collective-permute-start | bytes 589832 | tf_op jit(solution)/shard_map/ppermute | solution.py:573
  8.6 2.9 %shard_map.87 = (s32[1,2]{1,0:T(1,128)S(1)}, s32[2,8,128]{2,1,0:T(8,128)S(1)}, f32[256,256]{1,0:T(8,128)S(1)}, f32[256,256]{1,0:T(8,128)S(1)}, bf16[8,256,256]{2...) custom-call(f32[256,256]{1,0:T(8,128)} %refs_0_.1, ...), custom_call_target="tpu_custom_call" | custom-call | tf_op jit(solution)/shard_map/pallas_call | solution.py:435
  11.6 0.8 %shard_map.91.after.refs_4_.refs_5_ = f32[2,256,256]{2,1,0:T(8,128)S(1)} custom-call(s32[1,2]{1,0:T(1,128)S(1)} %get-tuple-element.35.offs, f32[2,256,256]{2,1,0:T(8,128)S(1)} %get-tuple-element.36.probe), custom_call_target="tpu_custom_call" | custom-call | tf_op jit(solution)/shard_map/pallas_call | solution.py:435
  12.3 0.6 %shard_map.92.refs_2_.refs_8_ = f32[256,256]{1,0:T(8,128)S(1)} custom-call(f32[256,256]{1,0:T(8,128)S(1)} %get-tuple-element.39.x, f32[2,256,256]{2,1,0:T(8,128)S(1)} %shard_map.91.after.refs_4_.refs_5_), custom_call_target="tpu_custom_call" | custom-call | tf_op jit(solution)/shard_map/pallas_call | solution.py:435
  13.0 6.3 %collective-permute-done.refs_0_ = f32[384,128]{1,0:T(8,128)S(1)} collective-permute-done((f32[384,128]{1,0:T(8,128)S(1)}, f32[384,128]{1,0:T(8,128)S(1)}, u32[]{:S(2)}, u32[]{:S(2)}) %collective-permute-start) | collective-permute-done | bytes 196640 | tf_op jit(solution)/shard_map/ppermute | solution.py:573
  19.5 0.4 collective-permute-done.1.refs_1_
  20.6 1.5 %shard_map.94 = (f32[2,256,256]{2,1,0:T(8,128)S(1)}, f32[2,256,256]{2,1,0:T(8,128)S(1)}) custom-call(f32[2,256,256]{2,1,0:T(8,128)S(1)} %shard_map.89.refs_3_.refs_0_, f32[4,64,256]{2,1,0:T(8,128)S(1)} %collective-permute-done.3.refs_1_, f32[2,64,128]{2,1,0:T(8,128)S(1)} %collective-permute-done.5.refs_2_, ...), custom_call_target="tpu_custom_call" | custom-call | tf_op jit(solution)/shard_map/pallas_call | solution.py:435
  22.1 3.6 %shard_map.95 = (f32[256,256]{1,0:T(8,128)S(1)}, f32[256,256]{1,0:T(8,128)S(1)}, f32[4,256,256]{2,1,0:T(8,128)S(1)}) custom-call(f32[2,256,256]{2,1,0:T(8,128)S(1)} %shard_map.88.refs_0_, f32[4,64,256]{2,1,0:T(8,128)S(1)} %collective-permute-done.3.refs_1_, f32[2,64,128]{2,1,0:T(8,128)S(1)} %collective-permute-done.4.refs_2_, ...), custom_call_target="tpu_custom_call" | custom-call | tf_op jit(solution)/shard_map/pallas_call | solution.py:435
  25.9 0.4 shard_map.96
  26.3 0.4 collective-permute-start.6
  26.7 0.6 collective-permute-done.9.other
  27.4 1.9 %collective-permute-start.10 = (f32[64,256]{1,0:T(8,128)S(1)}, f32[64,256]{1,0:T(8,128)S(1)}, u32[]{:S(2)}, u32[]{:S(2)}) collective-permute-start(f32[64,256]{1,0:T(8,128)S(1)} %get-tuple-element.53), channel_id=1, source_target_pairs={{0,1},{1,0},{2,3},{3,2},{4,5},{5,4},{6,7},{7,6},{8,9},{9,8},{10,11... | collective-permute-start | bytes 196616 | tf_op jit(solution)/shard_map/ppermute | solution.py:458
  29.4 1.5 %collective-permute-start.12 = (f32[64,256]{1,0:T(8,128)S(1)}, f32[64,256]{1,0:T(8,128)S(1)}, u32[]{:S(2)}, u32[]{:S(2)}) collective-permute-start(f32[64,256]{1,0:T(8,128)S(1)} %get-tuple-element.55), channel_id=1, source_target_pairs={{0,3},{1,2},{2,1},{3,0},{4,7},{5,6},{6,5},{7,4},{8,11},{9,10},{10,... | collective-permute-start | bytes 196616 | tf_op jit(solution)/shard_map/ppermute | solution.py:458
  30.9 0.8 %collective-permute-done.10.refs_1_ = f32[64,256]{1,0:T(8,128)S(1)} collective-permute-done((f32[64,256]{1,0:T(8,128)S(1)}, f32[64,256]{1,0:T(8,128)S(1)}, u32[]{:S(2)}, u32[]{:S(2)}) %collective-permute-start.10) | collective-permute-done | bytes 65568 | tf_op jit(solution)/shard_map/ppermute | solution.py:458
  31.7 3.0 %collective-permute-done.11.refs_2_ = f32[64,256]{1,0:T(8,128)S(1)} collective-permute-done((f32[64,256]{1,0:T(8,128)S(1)}, f32[64,256]{1,0:T(8,128)S(1)}, u32[]{:S(2)}, u32[]{:S(2)}) %collective-permute-start.11) | collective-permute-done | bytes 65568 | tf_op jit(solution)/shard_map/ppermute | solution.py:458
  34.7 3.5 %collective-permute-start.15 = (f32[64,256]{1,0:T(8,128)S(1)}, f32[64,256]{1,0:T(8,128)S(1)}, u32[]{:S(2)}, u32[]{:S(2)}) collective-permute-start(f32[64,256]{1,0:T(8,128)S(1)} %shard_map.100.refs_0_), channel_id=1, source_target_pairs={{0,12},{1,13},{2,14},{3,15},{4,8},{5,9},{6,10},{7,11},{8,4},{9,5},... | collective-permute-start | bytes 196616 | tf_op jit(solution)/shard_map/ppermute | solution.py:458
  38.3 0.9 %collective-permute-start.13 = (f32[64,256]{1,0:T(8,128)S(1)}, f32[64,256]{1,0:T(8,128)S(1)}, u32[]{:S(2)}, u32[]{:S(2)}) collective-permute-start(f32[64,256]{1,0:T(8,128)S(1)} %shard_map.100.refs_0_), channel_id=1, source_target_pairs={{0,4},{1,5},{2,6},{3,7},{4,0},{5,1},{6,2},{7,3},{8,12},{9,13},{10,... | collective-permute-start | bytes 196616 | tf_op jit(solution)/shard_map/ppermute | solution.py:458
  39.2 1.7 %collective-permute-done.15.refs_3_ = f32[64,256]{1,0:T(8,128)S(1)} collective-permute-done((f32[64,256]{1,0:T(8,128)S(1)}, f32[64,256]{1,0:T(8,128)S(1)}, u32[]{:S(2)}, u32[]{:S(2)}) %collective-permute-start.15) | collective-permute-done | bytes 65568 | tf_op jit(solution)/shard_map/ppermute | solution.py:458
  40.9 2.6 %collective-permute-done.14.refs_2_ = f32[64,256]{1,0:T(8,128)S(1)} collective-permute-done((f32[64,256]{1,0:T(8,128)S(1)}, f32[64,256]{1,0:T(8,128)S(1)}, u32[]{:S(2)}, u32[]{:S(2)}) %collective-permute-start.14) | collective-permute-done | bytes 65568 | tf_op jit(solution)/shard_map/ppermute | solution.py:458
  43.5 1.6 %collective-permute-start.18 = (f32[64,256]{1,0:T(8,128)S(1)}, f32[64,256]{1,0:T(8,128)S(1)}, u32[]{:S(2)}, u32[]{:S(2)}) collective-permute-start(f32[64,256]{1,0:T(8,128)S(1)} %shard_map.101.refs_0_), channel_id=1, source_target_pairs={{0,3},{1,2},{2,1},{3,0},{4,7},{5,6},{6,5},{7,4},{8,11},{9,10},{10,... | collective-permute-start | bytes 196616 | tf_op jit(solution)/shard_map/ppermute | solution.py:458
  45.0 1.2 %collective-permute-start.17 = (f32[64,256]{1,0:T(8,128)S(1)}, f32[64,256]{1,0:T(8,128)S(1)}, u32[]{:S(2)}, u32[]{:S(2)}) collective-permute-start(f32[64,256]{1,0:T(8,128)S(1)} %shard_map.101.refs_0_), channel_id=1, source_target_pairs={{0,2},{1,3},{2,0},{3,1},{4,6},{5,7},{6,4},{7,5},{8,10},{9,11},{10,... | collective-permute-start | bytes 196616 | tf_op jit(solution)/shard_map/ppermute | solution.py:458
  46.2 0.8 %collective-permute-start.16 = (f32[64,256]{1,0:T(8,128)S(1)}, f32[64,256]{1,0:T(8,128)S(1)}, u32[]{:S(2)}, u32[]{:S(2)}) collective-permute-start(f32[64,256]{1,0:T(8,128)S(1)} %shard_map.101.refs_0_), channel_id=1, source_target_pairs={{0,1},{1,0},{2,3},{3,2},{4,5},{5,4},{6,7},{7,6},{8,9},{9,8},{10,11... | collective-permute-start | bytes 196616 | tf_op jit(solution)/shard_map/ppermute | solution.py:458
  47.2 1.3 %collective-permute-start.7 = (f32[2,256,128]{2,1,0:T(8,128)S(1)}, f32[2,256,128]{2,1,0:T(8,128)S(1)}, u32[]{:S(2)}, u32[]{:S(2)}) collective-permute-start(f32[2,256,128]{2,1,0:T(8,128)S(1)} %get-tuple-element.48), channel_id=1, source_target_pairs={{0,1},{2,3},{4,5},{6,7},{8,9},{10,11},{12,13},{14,15},{1,0},{3,2},... | collective-permute-start | bytes 786440 | tf_op jit(solution)/shard_map/ppermute | solution.py:676
  48.5 0.7 %collective-permute-start.8 = (f32[2,256,128]{2,1,0:T(8,128)S(1)}, f32[2,256,128]{2,1,0:T(8,128)S(1)}, u32[]{:S(2)}, u32[]{:S(2)}) collective-permute-start(f32[2,256,128]{2,1,0:T(8,128)S(1)} %get-tuple-element.49), channel_id=1, source_target_pairs={{1,2},{3,4},{5,6},{7,8},{9,10},{11,12},{13,14},{2,1},{4,3},{6,5},{... | collective-permute-start | bytes 786440 | tf_op jit(solution)/shard_map/ppermute | solution.py:677
  49.4 0.3 collective-permute-done.17.refs_2_
  49.7 1.5 %collective-permute-done.16.refs_1_ = f32[64,256]{1,0:T(8,128)S(1)} collective-permute-done((f32[64,256]{1,0:T(8,128)S(1)}, f32[64,256]{1,0:T(8,128)S(1)}, u32[]{:S(2)}, u32[]{:S(2)}) %collective-permute-start.16) | collective-permute-done | bytes 65568 | tf_op jit(solution)/shard_map/ppermute | solution.py:458
  51.3 0.7 %shard_map.103.started = f32[2,256,256]{2,1,0:T(8,128)} custom-call(f32[256,256]{1,0:T(8,128)S(1)} %shard_map.102.full), custom_call_target="tpu_custom_call" | custom-call | tf_op jit(solution)/shard_map/pallas_call | solution.py:548
  52.0 6.7 %collective-permute-done.7.e = f32[2,256,128]{2,1,0:T(8,128)S(1)} collective-permute-done((f32[2,256,128]{2,1,0:T(8,128)S(1)}, f32[2,256,128]{2,1,0:T(8,128)S(1)}, u32[]{:S(2)}, u32[]{:S(2)}) %collective-permute-start.7) | collective-permute-done | bytes 262176 | tf_op jit(solution)/shard_map/ppermute | solution.py:676
  58.8 1.2 %shard_map.98 = f32[4,256,256]{2,1,0:T(8,128)} custom-call(f32[4,256,256]{2,1,0:T(8,128)S(1)} %get-tuple-element.47.total, f32[2,256,128]{2,1,0:T(8,128)S(1)} %collective-permute-done.7.e, f32[2,256,128]{2,1,0:T(8,128)S(1)} %collective-permute-done.8.o), custom_call_target="tpu_custom_call" | custom-call | tf_op jit(solution)/shard_map/pallas_call | solution.py:435
  60.0 0.7 %shard_map.104 = f32[2,256,256]{2,1,0:T(8,128)} custom-call(f32[2,256,256]{2,1,0:T(8,128)} %shard_map.103.started, f32[256,256]{1,0:T(8,128)S(1)} %collective-permute-done.19.other), custom_call_target="tpu_custom_call", output_to_operand_aliasing={{}: (0, {})} | custom-call | tf_op jit(solution)/shard_map/pallas_call | solution.py:549
  (27 shorter events, 2.0 us)
Async XLA Ops:
  2.0 17.3 %collective-permute-start.2 = (f32[2,256,128]{2,1,0:T(8,128)S(1)}, f32[2,256,128]{2,1,0:T(8,128)S(1)}, u32[]{:S(2)}, u32[]{:S(2)}) collective-permute-start(f32[2,256,128]{2,1,0:T(8,128)S(1)} %get-tuple-element.32), channel_id=1, source_target_pairs={{1,2},{3,4},{5,6},{7,8},{9,10},{11,12},{13,14},{2,1},{4,3},{6,5},{... | collective-permute-start | bytes 786440 | tf_op jit(solution)/shard_map/ppermute | solution.py:574
  2.7 16.6 %collective-permute-start = (f32[384,128]{1,0:T(8,128)S(1)}, f32[384,128]{1,0:T(8,128)S(1)}, u32[]{:S(2)}, u32[]{:S(2)}) collective-permute-start(f32[384,128]{1,0:T(8,128)S(1)} %get-tuple-element.30), channel_id=1, source_target_pairs={{0,1},{2,3},{4,5},{6,7},{8,9},{10,11},{12,13},{14,15},{1,0},{3,2},... | collective-permute-start | bytes 589832 | tf_op jit(solution)/shard_map/ppermute | solution.py:573
  8.4 11.9 %collective-permute-start.3 = (f32[4,64,256]{2,1,0:T(8,128)S(1)}, f32[4,64,256]{2,1,0:T(8,128)S(1)}, u32[]{:S(2)}, u32[]{:S(2)}) collective-permute-start(f32[4,64,256]{2,1,0:T(8,128)S(1)} %get-tuple-element.34), channel_id=1, source_target_pairs={{0,16},{16,0},{1,17},{17,1},{2,18},{18,2},{3,19},{19,3},{4,20},{20... | collective-permute-start | bytes 786440 | tf_op jit(solution)/shard_map/ppermute | solution.py:577
  8.4 11.5 %collective-permute-start.1 = (f32[128,128]{1,0:T(8,128)S(1)}, f32[128,128]{1,0:T(8,128)S(1)}, u32[]{:S(2)}, u32[]{:S(2)}) collective-permute-start(f32[128,128]{1,0:T(8,128)S(1)} %get-tuple-element.31), channel_id=1, source_target_pairs={{0,1},{2,3},{4,5},{6,7},{8,9},{10,11},{12,13},{14,15},{1,0},{3,2},... | collective-permute-start | bytes 196616 | tf_op jit(solution)/shard_map/ppermute | solution.py:575
  19.3 1.3 %collective-permute-start.5 = (f32[2,64,128]{2,1,0:T(8,128)S(1)}, f32[2,64,128]{2,1,0:T(8,128)S(1)}, u32[]{:S(2)}, u32[]{:S(2)}) collective-permute-start(f32[2,64,128]{2,1,0:T(8,128)S(1)} %shard_map.93), channel_id=1, source_target_pairs={{0,16},{16,0},{1,17},{17,1},{2,18},{18,2},{3,19},{19,3},{4,20},{20... | collective-permute-start | bytes 196616 | tf_op jit(solution)/shard_map/ppermute | solution.py:590
  20.0 2.1 %collective-permute-start.4 = (f32[2,64,128]{2,1,0:T(8,128)S(1)}, f32[2,64,128]{2,1,0:T(8,128)S(1)}, u32[]{:S(2)}, u32[]{:S(2)}) collective-permute-start(f32[2,64,128]{2,1,0:T(8,128)S(1)} %shard_map.90), channel_id=1, source_target_pairs={{0,16},{16,0},{1,17},{17,1},{2,18},{18,2},{3,19},{19,3},{4,20},{20... | collective-permute-start | bytes 196616 | tf_op jit(solution)/shard_map/ppermute | solution.py:590
  25.7 1.6 %collective-permute-start.9 = (f32[256,256]{1,0:T(8,128)S(1)}, f32[256,256]{1,0:T(8,128)S(1)}, u32[]{:S(2)}, u32[]{:S(2)}) collective-permute-start(f32[256,256]{1,0:T(8,128)S(1)} %get-tuple-element.51), channel_id=1, source_target_pairs={{0,16},{16,0},{1,17},{17,1},{2,18},{18,2},{3,19},{19,3},{4,20},{20... | collective-permute-start | bytes 786440 | tf_op jit(solution)/shard_map/ppermute | solution.py:458
  26.3 20.7 %collective-permute-start.6 = (f32[4,64,384]{2,1,0:T(8,128)S(1)}, f32[4,64,384]{2,1,0:T(8,128)S(1)}, u32[]{:S(2)}, u32[]{:S(2)}) collective-permute-start(f32[4,64,384]{2,1,0:T(8,128)S(1)} %get-tuple-element.46), channel_id=1, source_target_pairs={{0,16},{16,0},{1,17},{17,1},{2,18},{18,2},{3,19},{19,3},{4,20},{20... | collective-permute-start | bytes 1179656 | tf_op jit(solution)/shard_map/ppermute | solution.py:667
  27.4 4.3 %collective-permute-start.10 = (f32[64,256]{1,0:T(8,128)S(1)}, f32[64,256]{1,0:T(8,128)S(1)}, u32[]{:S(2)}, u32[]{:S(2)}) collective-permute-start(f32[64,256]{1,0:T(8,128)S(1)} %get-tuple-element.53), channel_id=1, source_target_pairs={{0,1},{1,0},{2,3},{3,2},{4,5},{5,4},{6,7},{7,6},{8,9},{9,8},{10,11... | collective-permute-start | bytes 196616 | tf_op jit(solution)/shard_map/ppermute | solution.py:458
  29.2 5.5 %collective-permute-start.11 = (f32[64,256]{1,0:T(8,128)S(1)}, f32[64,256]{1,0:T(8,128)S(1)}, u32[]{:S(2)}, u32[]{:S(2)}) collective-permute-start(f32[64,256]{1,0:T(8,128)S(1)} %get-tuple-element.54), channel_id=1, source_target_pairs={{0,2},{1,3},{2,0},{3,1},{4,6},{5,7},{6,4},{7,5},{8,10},{9,11},{10,... | collective-permute-start | bytes 196616 | tf_op jit(solution)/shard_map/ppermute | solution.py:458
  29.4 5.3 %collective-permute-start.12 = (f32[64,256]{1,0:T(8,128)S(1)}, f32[64,256]{1,0:T(8,128)S(1)}, u32[]{:S(2)}, u32[]{:S(2)}) collective-permute-start(f32[64,256]{1,0:T(8,128)S(1)} %get-tuple-element.55), channel_id=1, source_target_pairs={{0,3},{1,2},{2,1},{3,0},{4,7},{5,6},{6,5},{7,4},{8,11},{9,10},{10,... | collective-permute-start | bytes 196616 | tf_op jit(solution)/shard_map/ppermute | solution.py:458
  34.7 6.1 %collective-permute-start.15 = (f32[64,256]{1,0:T(8,128)S(1)}, f32[64,256]{1,0:T(8,128)S(1)}, u32[]{:S(2)}, u32[]{:S(2)}) collective-permute-start(f32[64,256]{1,0:T(8,128)S(1)} %shard_map.100.refs_0_), channel_id=1, source_target_pairs={{0,12},{1,13},{2,14},{3,15},{4,8},{5,9},{6,10},{7,11},{8,4},{9,5},... | collective-permute-start | bytes 196616 | tf_op jit(solution)/shard_map/ppermute | solution.py:458
  38.3 5.2 %collective-permute-start.14 = (f32[64,256]{1,0:T(8,128)S(1)}, f32[64,256]{1,0:T(8,128)S(1)}, u32[]{:S(2)}, u32[]{:S(2)}) collective-permute-start(f32[64,256]{1,0:T(8,128)S(1)} %shard_map.100.refs_0_), channel_id=1, source_target_pairs={{0,8},{1,9},{2,10},{3,11},{4,12},{5,13},{6,14},{7,15},{8,0},{9,1},... | collective-permute-start | bytes 196616 | tf_op jit(solution)/shard_map/ppermute | solution.py:458
  38.3 5.2 %collective-permute-start.13 = (f32[64,256]{1,0:T(8,128)S(1)}, f32[64,256]{1,0:T(8,128)S(1)}, u32[]{:S(2)}, u32[]{:S(2)}) collective-permute-start(f32[64,256]{1,0:T(8,128)S(1)} %shard_map.100.refs_0_), channel_id=1, source_target_pairs={{0,4},{1,5},{2,6},{3,7},{4,0},{5,1},{6,2},{7,3},{8,12},{9,13},{10,... | collective-permute-start | bytes 196616 | tf_op jit(solution)/shard_map/ppermute | solution.py:458
  43.5 5.9 %collective-permute-start.18 = (f32[64,256]{1,0:T(8,128)S(1)}, f32[64,256]{1,0:T(8,128)S(1)}, u32[]{:S(2)}, u32[]{:S(2)}) collective-permute-start(f32[64,256]{1,0:T(8,128)S(1)} %shard_map.101.refs_0_), channel_id=1, source_target_pairs={{0,3},{1,2},{2,1},{3,0},{4,7},{5,6},{6,5},{7,4},{8,11},{9,10},{10,... | collective-permute-start | bytes 196616 | tf_op jit(solution)/shard_map/ppermute | solution.py:458
  45.0 4.7 %collective-permute-start.17 = (f32[64,256]{1,0:T(8,128)S(1)}, f32[64,256]{1,0:T(8,128)S(1)}, u32[]{:S(2)}, u32[]{:S(2)}) collective-permute-start(f32[64,256]{1,0:T(8,128)S(1)} %shard_map.101.refs_0_), channel_id=1, source_target_pairs={{0,2},{1,3},{2,0},{3,1},{4,6},{5,7},{6,4},{7,5},{8,10},{9,11},{10,... | collective-permute-start | bytes 196616 | tf_op jit(solution)/shard_map/ppermute | solution.py:458
  46.2 5.0 %collective-permute-start.16 = (f32[64,256]{1,0:T(8,128)S(1)}, f32[64,256]{1,0:T(8,128)S(1)}, u32[]{:S(2)}, u32[]{:S(2)}) collective-permute-start(f32[64,256]{1,0:T(8,128)S(1)} %shard_map.101.refs_0_), channel_id=1, source_target_pairs={{0,1},{1,0},{2,3},{3,2},{4,5},{5,4},{6,7},{7,6},{8,9},{9,8},{10,11... | collective-permute-start | bytes 196616 | tf_op jit(solution)/shard_map/ppermute | solution.py:458
  47.2 11.6 %collective-permute-start.7 = (f32[2,256,128]{2,1,0:T(8,128)S(1)}, f32[2,256,128]{2,1,0:T(8,128)S(1)}, u32[]{:S(2)}, u32[]{:S(2)}) collective-permute-start(f32[2,256,128]{2,1,0:T(8,128)S(1)} %get-tuple-element.48), channel_id=1, source_target_pairs={{0,1},{2,3},{4,5},{6,7},{8,9},{10,11},{12,13},{14,15},{1,0},{3,2},... | collective-permute-start | bytes 786440 | tf_op jit(solution)/shard_map/ppermute | solution.py:676
  48.5 10.3 %collective-permute-start.8 = (f32[2,256,128]{2,1,0:T(8,128)S(1)}, f32[2,256,128]{2,1,0:T(8,128)S(1)}, u32[]{:S(2)}, u32[]{:S(2)}) collective-permute-start(f32[2,256,128]{2,1,0:T(8,128)S(1)} %get-tuple-element.49), channel_id=1, source_target_pairs={{1,2},{3,4},{5,6},{7,8},{9,10},{11,12},{13,14},{2,1},{4,3},{6,5},{... | collective-permute-start | bytes 786440 | tf_op jit(solution)/shard_map/ppermute | solution.py:677
  51.2 8.8 %collective-permute-start.19 = (f32[256,256]{1,0:T(8,128)S(1)}, f32[256,256]{1,0:T(8,128)S(1)}, u32[]{:S(2)}, u32[]{:S(2)}) collective-permute-start(f32[256,256]{1,0:T(8,128)S(1)} %shard_map.102.full), channel_id=1, source_target_pairs={{0,16},{16,0},{1,17},{17,1},{2,18},{18,2},{3,19},{19,3},{4,20},{20... | collective-permute-start | bytes 786440 | tf_op jit(solution)/shard_map/ppermute | solution.py:458

commit v14 on v13

--- a/solution.py
+++ b/solution.py
@@ -44,12 +44,16 @@
 
 def left_dot(mats, which, x):
     high, low = split(x)
-    return dot(mats[which], high) + (dot(mats[which], low) + dot(mats[which + 1], high))
+    n = x.shape[0]
+    y = dot(mats[which : which + 2].reshape(2 * n, n), high)
+    return y[:n] + (y[n:] + dot(mats[which], low))
 
 
 def right_dot(x, mats, which):
     high, low = split(x)
-    return dot(high, mats[which]) + (dot(low, mats[which]) + dot(high, mats[which + 1]))
+    m = x.shape[0]
+    y = dot(jnp.concatenate([high, low], axis=0), mats[which])
+    return y[:m] + (y[m:] + dot(high, mats[which + 1]))
 
 
 def cat(parts, axis):

time: 61.1 us -> 61.1 us (level)
  no operation moved by 1% of the time
where the time goes in v14:
time: 61.1 us; the launch traced here: 60.7 us
  waiting for transfers between devices  24.5 us (40%)
  starting transfers between devices  21 us (34%)
  Pallas kernels  14.4 us (24%)
  between operations  0.8 us (1%)
    pallas_call x17, Pallas kernels, call(): pl.pallas_call(kernel, out_shape=shapes, in_specs=in_specs, out_specs=[SM...  12.9 us
    ppermute x11, starting transfers between devices, swap(): return lax.ppermute(value, axis, [(i, i ^ distance) for i in range(count)])  11.8 us
    ppermute x11, waiting for transfers between devices, swap(): return lax.ppermute(value, axis, [(i, i ^ distance) for i in range(count)])  10.7 us
    ppermute x1, waiting for transfers between devices, whole(): send_e = lax.ppermute(send_e, 'col', col_rounds[0])  6.74 us
    ppermute x1, waiting for transfers between devices, whole(): even0 = lax.ppermute(even0, 'col', col_rounds[0])  6.32 us
    ppermute x1, starting transfers between devices, whole(): even0 = lax.ppermute(even0, 'col', col_rounds[0])  5.75 us
    ppermute x1, starting transfers between devices, whole(): send_e = lax.ppermute(send_e, 'col', col_rounds[0])  1.28 us
  transfers between devices with their start and end apart: 20, of which 12 were waited for; matrix products, arithmetic and copies ran while one was open for 0% of the time, Pallas kernels for 14%

profile of v14, /device:TPU:0, one launch (start us, length us, event | category | flops | bytes accessed | tf_op | source)
XLA Modules:
  0.0 60.7 jit_solution(7938253709008503708)
XLA Ops:
  0.6 1.4 %shard_map.86 = (f32[4,256,256]{2,1,0:T(8,128)S(1)}, f32[384,128]{1,0:T(8,128)S(1)}, f32[128,128]{1,0:T(8,128)S(1)}, f32[2,256,128]{2,1,0:T(8,128)S(1)}, f32[4,64,256]{2,1,0:T(8,128)S(1)}) custom-call(f32[4,256,256]{2,1,0:T(8,128)} %bitcast.4), custom_call_target="tpu_custom_call" | custom-call | tf_op jit(solution)/shard_map/pallas_call | solution.py:439
  2.0 0.7 %collective-permute-start.2 = (f32[2,256,128]{2,1,0:T(8,128)S(1)}, f32[2,256,128]{2,1,0:T(8,128)S(1)}, u32[]{:S(2)}, u32[]{:S(2)}) collective-permute-start(f32[2,256,128]{2,1,0:T(8,128)S(1)} %get-tuple-element.32), channel_id=1, source_target_pairs={{1,2},{3,4},{5,6},{7,8},{9,10},{11,12},{13,14},{2,1},{4,3},{6,5},{... | collective-permute-start | bytes 786440 | tf_op jit(solution)/shard_map/ppermute | solution.py:578
  2.7 5.8 %collective-permute-start = (f32[384,128]{1,0:T(8,128)S(1)}, f32[384,128]{1,0:T(8,128)S(1)}, u32[]{:S(2)}, u32[]{:S(2)}) collective-permute-start(f32[384,128]{1,0:T(8,128)S(1)} %get-tuple-element.30), channel_id=1, source_target_pairs={{0,1},{2,3},{4,5},{6,7},{8,9},{10,11},{12,13},{14,15},{1,0},{3,2},... | collective-permute-start | bytes 589832 | tf_op jit(solution)/shard_map/ppermute | solution.py:577
  8.6 2.9 %shard_map.87 = (s32[1,2]{1,0:T(1,128)S(1)}, s32[2,8,128]{2,1,0:T(8,128)S(1)}, f32[256,256]{1,0:T(8,128)S(1)}, f32[256,256]{1,0:T(8,128)S(1)}, bf16[8,256,256]{2...) custom-call(f32[256,256]{1,0:T(8,128)} %refs_0_.1, ...), custom_call_target="tpu_custom_call" | custom-call | tf_op jit(solution)/shard_map/pallas_call | solution.py:439
  11.6 0.8 %shard_map.91.after.refs_4_.refs_5_ = f32[2,256,256]{2,1,0:T(8,128)S(1)} custom-call(s32[1,2]{1,0:T(1,128)S(1)} %get-tuple-element.35.offs, f32[2,256,256]{2,1,0:T(8,128)S(1)} %get-tuple-element.36.probe), custom_call_target="tpu_custom_call" | custom-call | tf_op jit(solution)/shard_map/pallas_call | solution.py:439
  12.3 0.6 %shard_map.92.refs_2_.refs_8_ = f32[256,256]{1,0:T(8,128)S(1)} custom-call(f32[256,256]{1,0:T(8,128)S(1)} %get-tuple-element.39.x, f32[2,256,256]{2,1,0:T(8,128)S(1)} %shard_map.91.after.refs_4_.refs_5_), custom_call_target="tpu_custom_call" | custom-call | tf_op jit(solution)/shard_map/pallas_call | solution.py:439
  13.0 6.3 %collective-permute-done.refs_0_ = f32[384,128]{1,0:T(8,128)S(1)} collective-permute-done((f32[384,128]{1,0:T(8,128)S(1)}, f32[384,128]{1,0:T(8,128)S(1)}, u32[]{:S(2)}, u32[]{:S(2)}) %collective-permute-start) | collective-permute-done | bytes 196640 | tf_op jit(solution)/shard_map/ppermute | solution.py:577
  19.5 0.4 collective-permute-done.1.refs_1_
  20.6 1.5 %shard_map.94 = (f32[2,256,256]{2,1,0:T(8,128)S(1)}, f32[2,256,256]{2,1,0:T(8,128)S(1)}) custom-call(f32[2,256,256]{2,1,0:T(8,128)S(1)} %shard_map.89.refs_3_.refs_0_, f32[4,64,256]{2,1,0:T(8,128)S(1)} %collective-permute-done.3.refs_1_, f32[2,64,128]{2,1,0:T(8,128)S(1)} %collective-permute-done.5.refs_2_, ...), custom_call_target="tpu_custom_call" | custom-call | tf_op jit(solution)/shard_map/pallas_call | solution.py:439
  22.2 3.6 %shard_map.95 = (f32[256,256]{1,0:T(8,128)S(1)}, f32[256,256]{1,0:T(8,128)S(1)}, f32[4,256,256]{2,1,0:T(8,128)S(1)}) custom-call(f32[2,256,256]{2,1,0:T(8,128)S(1)} %shard_map.88.refs_0_, f32[4,64,256]{2,1,0:T(8,128)S(1)} %collective-permute-done.3.refs_1_, f32[2,64,128]{2,1,0:T(8,128)S(1)} %collective-permute-done.4.refs_2_, ...), custom_call_target="tpu_custom_call" | custom-call | tf_op jit(solution)/shard_map/pallas_call | solution.py:439
  25.9 0.4 shard_map.96
  26.3 0.4 collective-permute-start.6
  26.7 0.6 collective-permute-done.9.other
  27.4 1.8 %collective-permute-start.10 = (f32[64,256]{1,0:T(8,128)S(1)}, f32[64,256]{1,0:T(8,128)S(1)}, u32[]{:S(2)}, u32[]{:S(2)}) collective-permute-start(f32[64,256]{1,0:T(8,128)S(1)} %get-tuple-element.53), channel_id=1, source_target_pairs={{0,1},{1,0},{2,3},{3,2},{4,5},{5,4},{6,7},{7,6},{8,9},{9,8},{10,11... | collective-permute-start | bytes 196616 | tf_op jit(solution)/shard_map/ppermute | solution.py:462
  29.4 1.5 %collective-permute-start.12 = (f32[64,256]{1,0:T(8,128)S(1)}, f32[64,256]{1,0:T(8,128)S(1)}, u32[]{:S(2)}, u32[]{:S(2)}) collective-permute-start(f32[64,256]{1,0:T(8,128)S(1)} %get-tuple-element.55), channel_id=1, source_target_pairs={{0,3},{1,2},{2,1},{3,0},{4,7},{5,6},{6,5},{7,4},{8,11},{9,10},{10,... | collective-permute-start | bytes 196616 | tf_op jit(solution)/shard_map/ppermute | solution.py:462
  30.9 0.8 %collective-permute-done.10.refs_1_ = f32[64,256]{1,0:T(8,128)S(1)} collective-permute-done((f32[64,256]{1,0:T(8,128)S(1)}, f32[64,256]{1,0:T(8,128)S(1)}, u32[]{:S(2)}, u32[]{:S(2)}) %collective-permute-start.10) | collective-permute-done | bytes 65568 | tf_op jit(solution)/shard_map/ppermute | solution.py:462
  31.7 3.0 %collective-permute-done.11.refs_2_ = f32[64,256]{1,0:T(8,128)S(1)} collective-permute-done((f32[64,256]{1,0:T(8,128)S(1)}, f32[64,256]{1,0:T(8,128)S(1)}, u32[]{:S(2)}, u32[]{:S(2)}) %collective-permute-start.11) | collective-permute-done | bytes 65568 | tf_op jit(solution)/shard_map/ppermute | solution.py:462
  34.7 3.5 %collective-permute-start.15 = (f32[64,256]{1,0:T(8,128)S(1)}, f32[64,256]{1,0:T(8,128)S(1)}, u32[]{:S(2)}, u32[]{:S(2)}) collective-permute-start(f32[64,256]{1,0:T(8,128)S(1)} %shard_map.100.refs_0_), channel_id=1, source_target_pairs={{0,12},{1,13},{2,14},{3,15},{4,8},{5,9},{6,10},{7,11},{8,4},{9,5},... | collective-permute-start | bytes 196616 | tf_op jit(solution)/shard_map/ppermute | solution.py:462
  38.3 0.9 %collective-permute-start.13 = (f32[64,256]{1,0:T(8,128)S(1)}, f32[64,256]{1,0:T(8,128)S(1)}, u32[]{:S(2)}, u32[]{:S(2)}) collective-permute-start(f32[64,256]{1,0:T(8,128)S(1)} %shard_map.100.refs_0_), channel_id=1, source_target_pairs={{0,4},{1,5},{2,6},{3,7},{4,0},{5,1},{6,2},{7,3},{8,12},{9,13},{10,... | collective-permute-start | bytes 196616 | tf_op jit(solution)/shard_map/ppermute | solution.py:462
  39.2 1.7 %collective-permute-done.15.refs_3_ = f32[64,256]{1,0:T(8,128)S(1)} collective-permute-done((f32[64,256]{1,0:T(8,128)S(1)}, f32[64,256]{1,0:T(8,128)S(1)}, u32[]{:S(2)}, u32[]{:S(2)}) %collective-permute-start.15) | collective-permute-done | bytes 65568 | tf_op jit(solution)/shard_map/ppermute | solution.py:462
  40.9 2.6 %collective-permute-done.14.refs_2_ = f32[64,256]{1,0:T(8,128)S(1)} collective-permute-done((f32[64,256]{1,0:T(8,128)S(1)}, f32[64,256]{1,0:T(8,128)S(1)}, u32[]{:S(2)}, u32[]{:S(2)}) %collective-permute-start.14) | collective-permute-done | bytes 65568 | tf_op jit(solution)/shard_map/ppermute | solution.py:462
  43.5 1.6 %collective-permute-start.18 = (f32[64,256]{1,0:T(8,128)S(1)}, f32[64,256]{1,0:T(8,128)S(1)}, u32[]{:S(2)}, u32[]{:S(2)}) collective-permute-start(f32[64,256]{1,0:T(8,128)S(1)} %shard_map.101.refs_0_), channel_id=1, source_target_pairs={{0,3},{1,2},{2,1},{3,0},{4,7},{5,6},{6,5},{7,4},{8,11},{9,10},{10,... | collective-permute-start | bytes 196616 | tf_op jit(solution)/shard_map/ppermute | solution.py:462
  45.0 1.2 %collective-permute-start.17 = (f32[64,256]{1,0:T(8,128)S(1)}, f32[64,256]{1,0:T(8,128)S(1)}, u32[]{:S(2)}, u32[]{:S(2)}) collective-permute-start(f32[64,256]{1,0:T(8,128)S(1)} %shard_map.101.refs_0_), channel_id=1, source_target_pairs={{0,2},{1,3},{2,0},{3,1},{4,6},{5,7},{6,4},{7,5},{8,10},{9,11},{10,... | collective-permute-start | bytes 196616 | tf_op jit(solution)/shard_map/ppermute | solution.py:462
  46.2 0.8 %collective-permute-start.16 = (f32[64,256]{1,0:T(8,128)S(1)}, f32[64,256]{1,0:T(8,128)S(1)}, u32[]{:S(2)}, u32[]{:S(2)}) collective-permute-start(f32[64,256]{1,0:T(8,128)S(1)} %shard_map.101.refs_0_), channel_id=1, source_target_pairs={{0,1},{1,0},{2,3},{3,2},{4,5},{5,4},{6,7},{7,6},{8,9},{9,8},{10,11... | collective-permute-start | bytes 196616 | tf_op jit(solution)/shard_map/ppermute | solution.py:462
  47.2 1.3 %collective-permute-start.7 = (f32[2,256,128]{2,1,0:T(8,128)S(1)}, f32[2,256,128]{2,1,0:T(8,128)S(1)}, u32[]{:S(2)}, u32[]{:S(2)}) collective-permute-start(f32[2,256,128]{2,1,0:T(8,128)S(1)} %get-tuple-element.48), channel_id=1, source_target_pairs={{0,1},{2,3},{4,5},{6,7},{8,9},{10,11},{12,13},{14,15},{1,0},{3,2},... | collective-permute-start | bytes 786440 | tf_op jit(solution)/shard_map/ppermute | solution.py:680
  48.5 0.7 %collective-permute-start.8 = (f32[2,256,128]{2,1,0:T(8,128)S(1)}, f32[2,256,128]{2,1,0:T(8,128)S(1)}, u32[]{:S(2)}, u32[]{:S(2)}) collective-permute-start(f32[2,256,128]{2,1,0:T(8,128)S(1)} %get-tuple-element.49), channel_id=1, source_target_pairs={{1,2},{3,4},{5,6},{7,8},{9,10},{11,12},{13,14},{2,1},{4,3},{6,5},{... | collective-permute-start | bytes 786440 | tf_op jit(solution)/shard_map/ppermute | solution.py:681
  49.4 0.3 collective-permute-done.17.refs_2_
  49.7 1.5 %collective-permute-done.16.refs_1_ = f32[64,256]{1,0:T(8,128)S(1)} collective-permute-done((f32[64,256]{1,0:T(8,128)S(1)}, f32[64,256]{1,0:T(8,128)S(1)}, u32[]{:S(2)}, u32[]{:S(2)}) %collective-permute-start.16) | collective-permute-done | bytes 65568 | tf_op jit(solution)/shard_map/ppermute | solution.py:462
  51.3 0.7 %shard_map.103.started = f32[2,256,256]{2,1,0:T(8,128)} custom-call(f32[256,256]{1,0:T(8,128)S(1)} %shard_map.102.full), custom_call_target="tpu_custom_call" | custom-call | tf_op jit(solution)/shard_map/pallas_call | solution.py:552
  52.0 6.7 %collective-permute-done.7.e = f32[2,256,128]{2,1,0:T(8,128)S(1)} collective-permute-done((f32[2,256,128]{2,1,0:T(8,128)S(1)}, f32[2,256,128]{2,1,0:T(8,128)S(1)}, u32[]{:S(2)}, u32[]{:S(2)}) %collective-permute-start.7) | collective-permute-done | bytes 262176 | tf_op jit(solution)/shard_map/ppermute | solution.py:680
  58.8 1.2 %shard_map.98 = f32[4,256,256]{2,1,0:T(8,128)} custom-call(f32[4,256,256]{2,1,0:T(8,128)S(1)} %get-tuple-element.47.total, f32[2,256,128]{2,1,0:T(8,128)S(1)} %collective-permute-done.7.e, f32[2,256,128]{2,1,0:T(8,128)S(1)} %collective-permute-done.8.o), custom_call_target="tpu_custom_call" | custom-call | tf_op jit(solution)/shard_map/pallas_call | solution.py:439
  60.0 0.7 %shard_map.104 = f32[2,256,256]{2,1,0:T(8,128)} custom-call(f32[2,256,256]{2,1,0:T(8,128)} %shard_map.103.started, f32[256,256]{1,0:T(8,128)S(1)} %collective-permute-done.19.other), custom_call_target="tpu_custom_call", output_to_operand_aliasing={{}: (0, {})} | custom-call | tf_op jit(solution)/shard_map/pallas_call | solution.py:553
  (27 shorter events, 2.0 us)
Async XLA Ops:
  2.0 17.3 %collective-permute-start.2 = (f32[2,256,128]{2,1,0:T(8,128)S(1)}, f32[2,256,128]{2,1,0:T(8,128)S(1)}, u32[]{:S(2)}, u32[]{:S(2)}) collective-permute-start(f32[2,256,128]{2,1,0:T(8,128)S(1)} %get-tuple-element.32), channel_id=1, source_target_pairs={{1,2},{3,4},{5,6},{7,8},{9,10},{11,12},{13,14},{2,1},{4,3},{6,5},{... | collective-permute-start | bytes 786440 | tf_op jit(solution)/shard_map/ppermute | solution.py:578
  2.7 16.6 %collective-permute-start = (f32[384,128]{1,0:T(8,128)S(1)}, f32[384,128]{1,0:T(8,128)S(1)}, u32[]{:S(2)}, u32[]{:S(2)}) collective-permute-start(f32[384,128]{1,0:T(8,128)S(1)} %get-tuple-element.30), channel_id=1, source_target_pairs={{0,1},{2,3},{4,5},{6,7},{8,9},{10,11},{12,13},{14,15},{1,0},{3,2},... | collective-permute-start | bytes 589832 | tf_op jit(solution)/shard_map/ppermute | solution.py:577
  8.4 11.9 %collective-permute-start.3 = (f32[4,64,256]{2,1,0:T(8,128)S(1)}, f32[4,64,256]{2,1,0:T(8,128)S(1)}, u32[]{:S(2)}, u32[]{:S(2)}) collective-permute-start(f32[4,64,256]{2,1,0:T(8,128)S(1)} %get-tuple-element.34), channel_id=1, source_target_pairs={{0,16},{16,0},{1,17},{17,1},{2,18},{18,2},{3,19},{19,3},{4,20},{20... | collective-permute-start | bytes 786440 | tf_op jit(solution)/shard_map/ppermute | solution.py:581
  8.4 11.5 %collective-permute-start.1 = (f32[128,128]{1,0:T(8,128)S(1)}, f32[128,128]{1,0:T(8,128)S(1)}, u32[]{:S(2)}, u32[]{:S(2)}) collective-permute-start(f32[128,128]{1,0:T(8,128)S(1)} %get-tuple-element.31), channel_id=1, source_target_pairs={{0,1},{2,3},{4,5},{6,7},{8,9},{10,11},{12,13},{14,15},{1,0},{3,2},... | collective-permute-start | bytes 196616 | tf_op jit(solution)/shard_map/ppermute | solution.py:579
  19.3 1.3 %collective-permute-start.5 = (f32[2,64,128]{2,1,0:T(8,128)S(1)}, f32[2,64,128]{2,1,0:T(8,128)S(1)}, u32[]{:S(2)}, u32[]{:S(2)}) collective-permute-start(f32[2,64,128]{2,1,0:T(8,128)S(1)} %shard_map.93), channel_id=1, source_target_pairs={{0,16},{16,0},{1,17},{17,1},{2,18},{18,2},{3,19},{19,3},{4,20},{20... | collective-permute-start | bytes 196616 | tf_op jit(solution)/shard_map/ppermute | solution.py:594
  20.0 2.1 %collective-permute-start.4 = (f32[2,64,128]{2,1,0:T(8,128)S(1)}, f32[2,64,128]{2,1,0:T(8,128)S(1)}, u32[]{:S(2)}, u32[]{:S(2)}) collective-permute-start(f32[2,64,128]{2,1,0:T(8,128)S(1)} %shard_map.90), channel_id=1, source_target_pairs={{0,16},{16,0},{1,17},{17,1},{2,18},{18,2},{3,19},{19,3},{4,20},{20... | collective-permute-start | bytes 196616 | tf_op jit(solution)/shard_map/ppermute | solution.py:594
  25.7 1.6 %collective-permute-start.9 = (f32[256,256]{1,0:T(8,128)S(1)}, f32[256,256]{1,0:T(8,128)S(1)}, u32[]{:S(2)}, u32[]{:S(2)}) collective-permute-start(f32[256,256]{1,0:T(8,128)S(1)} %get-tuple-element.51), channel_id=1, source_target_pairs={{0,16},{16,0},{1,17},{17,1},{2,18},{18,2},{3,19},{19,3},{4,20},{20... | collective-permute-start | bytes 786440 | tf_op jit(solution)/shard_map/ppermute | solution.py:462
  26.3 20.7 %collective-permute-start.6 = (f32[4,64,384]{2,1,0:T(8,128)S(1)}, f32[4,64,384]{2,1,0:T(8,128)S(1)}, u32[]{:S(2)}, u32[]{:S(2)}) collective-permute-start(f32[4,64,384]{2,1,0:T(8,128)S(1)} %get-tuple-element.46), channel_id=1, source_target_pairs={{0,16},{16,0},{1,17},{17,1},{2,18},{18,2},{3,19},{19,3},{4,20},{20... | collective-permute-start | bytes 1179656 | tf_op jit(solution)/shard_map/ppermute | solution.py:671
  27.4 4.3 %collective-permute-start.10 = (f32[64,256]{1,0:T(8,128)S(1)}, f32[64,256]{1,0:T(8,128)S(1)}, u32[]{:S(2)}, u32[]{:S(2)}) collective-permute-start(f32[64,256]{1,0:T(8,128)S(1)} %get-tuple-element.53), channel_id=1, source_target_pairs={{0,1},{1,0},{2,3},{3,2},{4,5},{5,4},{6,7},{7,6},{8,9},{9,8},{10,11... | collective-permute-start | bytes 196616 | tf_op jit(solution)/shard_map/ppermute | solution.py:462
  29.2 5.5 %collective-permute-start.11 = (f32[64,256]{1,0:T(8,128)S(1)}, f32[64,256]{1,0:T(8,128)S(1)}, u32[]{:S(2)}, u32[]{:S(2)}) collective-permute-start(f32[64,256]{1,0:T(8,128)S(1)} %get-tuple-element.54), channel_id=1, source_target_pairs={{0,2},{1,3},{2,0},{3,1},{4,6},{5,7},{6,4},{7,5},{8,10},{9,11},{10,... | collective-permute-start | bytes 196616 | tf_op jit(solution)/shard_map/ppermute | solution.py:462
  29.4 5.3 %collective-permute-start.12 = (f32[64,256]{1,0:T(8,128)S(1)}, f32[64,256]{1,0:T(8,128)S(1)}, u32[]{:S(2)}, u32[]{:S(2)}) collective-permute-start(f32[64,256]{1,0:T(8,128)S(1)} %get-tuple-element.55), channel_id=1, source_target_pairs={{0,3},{1,2},{2,1},{3,0},{4,7},{5,6},{6,5},{7,4},{8,11},{9,10},{10,... | collective-permute-start | bytes 196616 | tf_op jit(solution)/shard_map/ppermute | solution.py:462
  34.7 6.1 %collective-permute-start.15 = (f32[64,256]{1,0:T(8,128)S(1)}, f32[64,256]{1,0:T(8,128)S(1)}, u32[]{:S(2)}, u32[]{:S(2)}) collective-permute-start(f32[64,256]{1,0:T(8,128)S(1)} %shard_map.100.refs_0_), channel_id=1, source_target_pairs={{0,12},{1,13},{2,14},{3,15},{4,8},{5,9},{6,10},{7,11},{8,4},{9,5},... | collective-permute-start | bytes 196616 | tf_op jit(solution)/shard_map/ppermute | solution.py:462
  38.3 5.2 %collective-permute-start.14 = (f32[64,256]{1,0:T(8,128)S(1)}, f32[64,256]{1,0:T(8,128)S(1)}, u32[]{:S(2)}, u32[]{:S(2)}) collective-permute-start(f32[64,256]{1,0:T(8,128)S(1)} %shard_map.100.refs_0_), channel_id=1, source_target_pairs={{0,8},{1,9},{2,10},{3,11},{4,12},{5,13},{6,14},{7,15},{8,0},{9,1},... | collective-permute-start | bytes 196616 | tf_op jit(solution)/shard_map/ppermute | solution.py:462
  38.3 5.2 %collective-permute-start.13 = (f32[64,256]{1,0:T(8,128)S(1)}, f32[64,256]{1,0:T(8,128)S(1)}, u32[]{:S(2)}, u32[]{:S(2)}) collective-permute-start(f32[64,256]{1,0:T(8,128)S(1)} %shard_map.100.refs_0_), channel_id=1, source_target_pairs={{0,4},{1,5},{2,6},{3,7},{4,0},{5,1},{6,2},{7,3},{8,12},{9,13},{10,... | collective-permute-start | bytes 196616 | tf_op jit(solution)/shard_map/ppermute | solution.py:462
  43.5 5.9 %collective-permute-start.18 = (f32[64,256]{1,0:T(8,128)S(1)}, f32[64,256]{1,0:T(8,128)S(1)}, u32[]{:S(2)}, u32[]{:S(2)}) collective-permute-start(f32[64,256]{1,0:T(8,128)S(1)} %shard_map.101.refs_0_), channel_id=1, source_target_pairs={{0,3},{1,2},{2,1},{3,0},{4,7},{5,6},{6,5},{7,4},{8,11},{9,10},{10,... | collective-permute-start | bytes 196616 | tf_op jit(solution)/shard_map/ppermute | solution.py:462
  45.0 4.7 %collective-permute-start.17 = (f32[64,256]{1,0:T(8,128)S(1)}, f32[64,256]{1,0:T(8,128)S(1)}, u32[]{:S(2)}, u32[]{:S(2)}) collective-permute-start(f32[64,256]{1,0:T(8,128)S(1)} %shard_map.101.refs_0_), channel_id=1, source_target_pairs={{0,2},{1,3},{2,0},{3,1},{4,6},{5,7},{6,4},{7,5},{8,10},{9,11},{10,... | collective-permute-start | bytes 196616 | tf_op jit(solution)/shard_map/ppermute | solution.py:462
  46.2 5.0 %collective-permute-start.16 = (f32[64,256]{1,0:T(8,128)S(1)}, f32[64,256]{1,0:T(8,128)S(1)}, u32[]{:S(2)}, u32[]{:S(2)}) collective-permute-start(f32[64,256]{1,0:T(8,128)S(1)} %shard_map.101.refs_0_), channel_id=1, source_target_pairs={{0,1},{1,0},{2,3},{3,2},{4,5},{5,4},{6,7},{7,6},{8,9},{9,8},{10,11... | collective-permute-start | bytes 196616 | tf_op jit(solution)/shard_map/ppermute | solution.py:462
  47.2 11.6 %collective-permute-start.7 = (f32[2,256,128]{2,1,0:T(8,128)S(1)}, f32[2,256,128]{2,1,0:T(8,128)S(1)}, u32[]{:S(2)}, u32[]{:S(2)}) collective-permute-start(f32[2,256,128]{2,1,0:T(8,128)S(1)} %get-tuple-element.48), channel_id=1, source_target_pairs={{0,1},{2,3},{4,5},{6,7},{8,9},{10,11},{12,13},{14,15},{1,0},{3,2},... | collective-permute-start | bytes 786440 | tf_op jit(solution)/shard_map/ppermute | solution.py:680
  48.5 10.3 %collective-permute-start.8 = (f32[2,256,128]{2,1,0:T(8,128)S(1)}, f32[2,256,128]{2,1,0:T(8,128)S(1)}, u32[]{:S(2)}, u32[]{:S(2)}) collective-permute-start(f32[2,256,128]{2,1,0:T(8,128)S(1)} %get-tuple-element.49), channel_id=1, source_target_pairs={{1,2},{3,4},{5,6},{7,8},{9,10},{11,12},{13,14},{2,1},{4,3},{6,5},{... | collective-permute-start | bytes 786440 | tf_op jit(solution)/shard_map/ppermute | solution.py:681
  51.2 8.8 %collective-permute-start.19 = (f32[256,256]{1,0:T(8,128)S(1)}, f32[256,256]{1,0:T(8,128)S(1)}, u32[]{:S(2)}, u32[]{:S(2)}) collective-permute-start(f32[256,256]{1,0:T(8,128)S(1)} %shard_map.102.full), channel_id=1, source_target_pairs={{0,16},{16,0},{1,17},{17,1},{2,18},{18,2},{3,19},{19,3},{4,20},{20... | collective-permute-start | bytes 786440 | tf_op jit(solution)/shard_map/ppermute | solution.py:462
